TPU v7x, 256 devices: a whole 4x4x8 slice. The times are simulated.
256 devices in a mesh: ep: 32 (over z, y), tp: 8 (over x, core).
Axes of the slice: x: 4, y: 4, z: 8, core: 2. Of those that a mesh axis runs over, the one named last changes fastest.
Arguments:
- tokens: bfloat16 [4096, 2048], P('ep', 'tp'), may hold values from -200 to 200
- norm_gain: bfloat16 [2048], P('tp'), may hold values from 0.099609375 to 1.8984375
- router_logits: float32 [4096, 64], P('ep'), may hold values from -8 to 400
- routes: int32 [4096, 8], P('ep'), may hold values from 0 to 63, all different within a row; in each aligned block of 128 rows (0 to 127, 128 to 255, ...) at most 32 rows name the same one
- gate_proj: bfloat16 [64, 2048, 1024], P('ep', None, 'tp'), may hold values from -0.125 to 0.125
- up_proj: bfloat16 [64, 2048, 1024], P('ep', None, 'tp'), may hold values from -0.125 to 0.125
- down_proj: bfloat16 [64, 1024, 2048], P('ep', 'tp'), may hold values from -0.1875 to 0.1875
Outputs:
- mixed: bfloat16 [4096, 2048], P('ep', 'tp')
Inputs may be any that keep to these rules, and one draw needn't show every extreme that they name: `routes`: within each aligned block of 128 rows (the tokens of one index of ep) no expert is named by more than 32 rows, a bound that some block reaches; a row names 8 different experts.
All inputs are finite; a program needn't handle non-finite values.
Results may differ from a plain program's by a relative error of at most 0.0071.
Values may be sent and summed in bfloat16 or wider, within the bound.
No kernel may reach another device: no remote copies, remote signals or barrier semaphores. Data moves between devices by JAX's collectives and lax.ppermute only.
A program may use at most 128 MiB of HBM per device.

v0:
```python
import jax
import jax.numpy as jnp
from jax import lax
from jax.sharding import PartitionSpec as P

epsilon = 1e-05


def on_device(tokens, norm_gain, router_logits, routes, gate_proj, up_proj, down_proj):
    ep_count = lax.axis_size("ep")
    group_size = tokens.shape[0]
    width = tokens.shape[1]
    top_count = routes.shape[1]
    local_experts = gate_proj.shape[0]
    expert_count = local_experts * ep_count
    capacity = 2 * group_size * top_count // expert_count
    slot_count = expert_count * capacity
    expert_iota = jnp.arange(expert_count, dtype=jnp.int32)
    flat_routes = routes.reshape(-1)
    route_hits = (flat_routes[:, None] == expert_iota[None, :]).astype(jnp.int32)
    position = jnp.sum((jnp.cumsum(route_hits, axis=0) - route_hits) * route_hits, axis=1)
    slot_grid = (flat_routes * capacity + position).reshape(group_size, top_count)
    chosen = jnp.sum(
        jnp.where(routes[:, :, None] == expert_iota[None, None, :], router_logits[:, None, :], 0.0),
        axis=-1,
    )
    gates = jax.nn.softmax(chosen, axis=-1)
    matches = jnp.arange(slot_count, dtype=jnp.int32)[:, None, None] == slot_grid[None, :, :]
    dispatch_table = jnp.any(matches, axis=-1).astype(jnp.bfloat16)
    whole, gain_all = (
        lax.all_gather(tokens, "tp", axis=1, tiled=True),
        lax.all_gather(norm_gain, "tp", axis=0, tiled=True),
    )
    floated = whole.astype(jnp.float32)
    mean_square = jnp.mean(floated * floated, axis=-1, keepdims=True)
    normed = (floated * lax.rsqrt(mean_square + epsilon) * gain_all.astype(jnp.float32)).astype(
        jnp.bfloat16
    )
    outgoing = jnp.dot(dispatch_table, normed, preferred_element_type=jnp.float32).astype(
        jnp.bfloat16
    )
    arrived = lax.all_to_all(outgoing, "ep", split_axis=0, concat_axis=0, tiled=True)
    arrived = arrived.reshape(ep_count, local_experts, capacity, arrived.shape[1])
    gate_val = jnp.einsum("slcd,ldh->slch", arrived, gate_proj, preferred_element_type=jnp.float32)
    up_val = jnp.einsum("slcd,ldh->slch", arrived, up_proj, preferred_element_type=jnp.float32)
    hidden = (jax.nn.silu(gate_val) * up_val).astype(jnp.bfloat16)
    term = jnp.einsum("slch,lhd->dslc", hidden, down_proj, preferred_element_type=jnp.float32)
    summed = lax.psum_scatter(
        term.reshape(width * lax.axis_size("tp"), slot_count), "tp", scatter_dimension=0, tiled=True
    )
    returned = lax.all_to_all(
        summed.astype(jnp.bfloat16), "ep", split_axis=1, concat_axis=1, tiled=True
    )
    slot_rows = jnp.transpose(returned)
    picked = slot_rows[slot_grid].astype(jnp.float32)
    mixed = jnp.sum(gates[:, :, None] * picked, axis=1)
    return mixed.astype(jnp.bfloat16)


def solution(mesh):
    return jax.shard_map(
        on_device,
        mesh=mesh,
        in_specs=(
            P("ep", "tp"),
            P("tp"),
            P("ep", None),
            P("ep", None),
            P("ep", None, "tp"),
            P("ep", None, "tp"),
            P("ep", "tp", None),
        ),
        out_specs=P("ep", "tp"),
        check_vma=False,
    )
```

profile of v0, /device:TPU:8, one launch (start us, length us, event | category | flops | bytes accessed | tf_op | source)
XLA Modules:
  0.0 431.7 jit_solution(2664050021449953185)
XLA Ops:
  6.5 0.0 copy-start
  6.5 0.0 reduce-scatter.2.cloned.1.call-start
  6.5 0.9 copy.44
  7.4 0.1 eq.59
  7.5 0.1 eq.55
  7.6 18.0 %reduce-window.6 = s32[64,8,128]{2,1,0:T(8,128)S(1)} reduce-window(s32[64,8,128]{2,1,0:T(8,128)S(1)} %fusion.39, s32[]{:T(128)} %constant.12.clone.1), window={size=1x1x128 pad=0_0x0_0x127_0}, to_apply=%region_3.4 | reduce-window | flops 8323072 | bytes 524292 | tf_op jit(solution)/shard_map/reduce-window
  25.6 0.1 slice.10
  25.8 0.1 copy.46
  26.0 0.1 copy.47
  26.0 0.1 broadcast_add_fusion
  26.2 0.1 fusion.38
  26.3 0.1 reduce_sum.50
  26.4 0.7 compare_select_fusion
  27.1 7.4 %fusion = pred[2048,128]{1,0:T(8,128)(4,1)S(1)} fusion(s32[128,8]{0,1:T(8,128)S(1)} %get-tuple-element.6), kind=kLoop, calls=%fused_computation.2 | loop fusion | flops 3932160 | bytes 266240 | tf_op jit(solution)/shard_map/reduce_or | solution.py:29
  34.5 13.7 %all_gather.6 = bf16[128,2048]{1,0:T(8,128)(2,1)S(1)} all-gather(bf16[128,256]{1,0:T(8,128)(2,1)} %param.7), channel_id=1, replica_groups=mesh['ep'=32,'tp'=8] {'tp'}, dimensions={1}, use_global_device_ids=true | all-gather | bytes 589824 | tf_op jit(solution)/shard_map/all_gather | solution.py:31
  48.2 0.2 fusion.19
  48.4 0.7 reshape.97
  49.1 10.2 %all-gather = bf16[8,1,256]{2,1,0:T(2,128)(2,1)S(1)} all-gather(bf16[1,1,256]{2,1,0:T(2,128)(2,1)S(1)} %reshape.97), channel_id=1, replica_groups=mesh['ep'=32,'tp'=8] {'tp'}, dimensions={0}, use_global_device_ids=true | all-gather | bytes 4608 | tf_op jit(solution)/shard_map/all_gather | solution.py:32
  59.3 2.4 convolution_convert_fusion
  61.7 0.0 copy-start.5
  61.7 197.5 %all_to_all.21 = bf16[32,64,2048]{2,1,0:T(8,128)(2,1)S(1)} all-to-all(bf16[32,64,2048]{2,1,0:T(8,128)(2,1)S(1)} %bitcast.59), channel_id=1, replica_groups=mesh['ep'=32,'tp'=8] {'ep'}, dimensions={0} | all-to-all | bytes 16777216 | tf_op jit(solution)/shard_map/all_to_all | solution.py:42
  259.2 0.0 copy-start.1
  259.2 0.0 copy-start.2
  259.2 3.2 copy-done.1
  262.4 0.0 copy-done.5
  262.4 2.3 fusion.5
  264.7 0.0 copy-done
  264.7 0.0 copy-done.2
  264.7 14.1 %convolution_bitcast_fusion = f32[2048,32,2,32]{0,3,1,2:T(8,128)} fusion(bf16[32,2,32,2048]{3,2,1,0:T(8,128)(2,1)} %bitcast.61, bf16[2,128,2048]{2,1,0:T(8,128)(2,1)S(1)} %copy-done, bf16[2,2048,128]{2,1,0:T(8,128)(2,1)S(1)} %copy-done.2, f32[32,2,32,128]{3,2,0,1:T(8,128)S(1)} %fusion.5), kind=kOutput, calls=%fused_computation.8 | convolution fusion | flops 2149056512 | bytes 28311552 | tf_op jit(solution)/shard_map/slch,lhd->dslc/dot_general | solution.py:47
  278.9 11.6 %copy.51 = f32[2048,32,2,32]{0,3,2,1:T(8,128)} copy(f32[2048,32,2,32]{0,3,1,2:T(8,128)} %convolution_bitcast_fusion) | data formatting | bytes 33554432 | tf_op jit(solution)/shard_map/slch,lhd->dslc/transpose | solution.py:47
  290.5 0.0 copy-start.3
  290.5 0.0 copy-start.4
  290.5 0.0 reduce-scatter.2.cloned.1.call-update
  290.5 89.0 %reduce-scatter.2.cloned.1.call-done = f32[256,2048]{0,1:T(8,128)} async-done(((f32[2048,2048]{0,1:T(8,128)}), f32[256,2048]{0,1:T(8,128)}) %reduce-scatter.2.cloned.1.call-update) | async-done | bytes 2097168 | tf_op jit(solution)/shard_map/reduce_scatter | solution.py:48
  379.5 2.7 convert_element_type.39
  382.2 10.2 %all-to-all-start.1 = ((bf16[256,32,64]{0,2,1:T(8,128)(2,1)}), bf16[256,32,64]{0,2,1:T(8,128)(2,1)S(1)}, u32[]{:S(2)}, u32[]{:S(2)}) async-start(bf16[256,32,64]{0,2,1:T(8,128)(2,1)} %bitcast.15), calls=%async_computation.2 | async-start | bytes 2097152 | tf_op jit(solution)/shard_map/all_to_all | solution.py:51
  392.4 0.1 copy.52
  392.5 0.1 reshape.88
  392.5 0.0 copy-done.3
  392.6 0.0 copy-done.4
  392.7 0.1 copy.43
  392.8 27.1 %all-to-all-done.1 = bf16[256,32,64]{0,2,1:T(8,128)(2,1)S(1)} async-done(((bf16[256,32,64]{0,2,1:T(8,128)(2,1)}), bf16[256,32,64]{0,2,1:T(8,128)(2,1)S(1)}, u32[]{:S(2)}, u32[]{:S(2)}) %all-to-all-start.1) | async-done | bytes 1048608 | tf_op jit(solution)/shard_map/all_to_all | solution.py:51
  419.9 3.9 gather_fusion
  423.8 1.0 fusion.22
  (11 shorter events, 0.2 us)
Async XLA Ops:
  6.5 258.2 %copy-start = (bf16[2,128,2048]{2,1,0:T(8,128)(2,1)S(1)}, bf16[2,128,2048]{2,1,0:T(8,128)(2,1)}, u32[]{:S(2)}) copy-start(bf16[2,128,2048]{2,1,0:T(8,128)(2,1)} %param.13) | copy-start | bytes 3145732
  6.5 373.0 %reduce-scatter.2.cloned.1.call-start = ((), (), s32[]{:S(2)}) async-start(), calls=%async_computation.3 | async-start | bytes 18874368 | tf_op jit(solution)/shard_map/reduce_scatter | solution.py:48
  61.7 200.7 %copy-start.5 = (bf16[2,2048,128]{2,1,0:T(8,128)(2,1)S(1)}, bf16[2,2048,128]{2,1,0:T(8,128)(2,1)}, u32[]{:S(2)}) copy-start(bf16[2,2048,128]{2,1,0:T(8,128)(2,1)} %param.11) | copy-start | bytes 3145732
  259.2 3.2 copy-start.1
  259.2 5.6 %copy-start.2 = (bf16[2,2048,128]{2,1,0:T(8,128)(2,1)S(1)}, bf16[2,2048,128]{2,1,0:T(8,128)(2,1)}, u32[]{:S(2)}) copy-start(bf16[2,2048,128]{2,1,0:T(8,128)(2,1)} %param.12) | copy-start | bytes 3145732
  290.5 102.1 %copy-start.3 = (s32[128,8]{0,1:T(8,128)S(1)}, s32[128,8]{0,1:T(8,128)}, u32[]{:S(2)}) copy-start(s32[128,8]{0,1:T(8,128)} %param.10) | copy-start | bytes 12292
  290.5 102.1 %copy-start.4 = (f32[128,64]{0,1:T(8,128)S(1)}, f32[128,64]{0,1:T(8,128)}, u32[]{:S(2)}) copy-start(f32[128,64]{0,1:T(8,128)} %param.9) | copy-start | bytes 98308
  382.2 37.7 %all-to-all-start.1 = ((bf16[256,32,64]{0,2,1:T(8,128)(2,1)}), bf16[256,32,64]{0,2,1:T(8,128)(2,1)S(1)}, u32[]{:S(2)}, u32[]{:S(2)}) async-start(bf16[256,32,64]{0,2,1:T(8,128)(2,1)} %bitcast.15), calls=%async_computation.2 | async-start | bytes 2097152 | tf_op jit(solution)/shard_map/all_to_all | solution.py:51
Sparse Core Ops, SparseCore 0:
  290.6 88.8 reduce-scatter.1
where the time goes:
time: 432 us
  blocking collectives  221 us (51%)
  waiting for transfers between devices  116 us (27%)
  other arithmetic  30.4 us (7%)
  local copies, waits for them, and re-layouts  21.3 us (5%)
  matrix products  18.8 us (4%)
  between operations  13.6 us (3%)
  starting transfers between devices  10.2 us (2%)
    all_to_all x1, blocking collectives, on_device(): lax.all_to_all(outgoing, 'ep', split_axis=0, concat_axis=0, tiled=True)  197 us
    reduce_scatter x1, waiting for transfers between devices, on_device(): lax.psum_scatter(term.reshape(width * lax.axis_size('tp'), slot_count), '...  89 us
    all_to_all x1, waiting for transfers between devices, on_device(): lax.all_to_all(summed.astype(jnp.bfloat16), 'ep', split_axis=1, concat_ax...  27.1 us
    another operation x3, other arithmetic  18.2 us
    dot_general x1, matrix products, on_device(): jnp.einsum('slch,lhd->dslc', hidden, down_proj, preferred_element_type=jn...  14.1 us
    all_gather x1, blocking collectives, on_device(): lax.all_gather(tokens, 'tp', axis=1, tiled=True)  13.7 us
    transpose x1, local copies, waits for them, and re-layouts, on_device(): jnp.einsum('slch,lhd->dslc', hidden, down_proj, preferred_element_type=jn...  11.6 us
    all_gather x1, blocking collectives, on_device(): lax.all_gather(norm_gain, 'tp', axis=0, tiled=True)  10.2 us
  transfers between devices with their start and end apart: 2, of which 2 were waited for; matrix products, arithmetic and copies ran while one was open for 0% of the time, Pallas kernels for 0%

commit v1 on v0

v1 whole, which is shorter than its diff:
```python
import jax
import jax.numpy as jnp
from jax import lax
from jax.sharding import Mesh, PartitionSpec as P

epsilon = 1e-05
chip_cores = 2


def on_device(tokens, norm_gain, router_logits, routes, gate_proj, up_proj, down_proj):
    bf16, f32 = jnp.bfloat16, jnp.float32
    ep_count = lax.axis_size("ep")
    row_count = lax.axis_size("x")
    group_size, width = tokens.shape
    top_count = routes.shape[1]
    expert_count = gate_proj.shape[0] * ep_count
    capacity = 2 * group_size * top_count // expert_count
    core = lax.axis_index("core")
    row = lax.axis_index("x")

    def swap(own):
        keep = lax.dynamic_index_in_dim(own, core, 0, keepdims=False)
        give = lax.dynamic_index_in_dim(own, 1 - core, 0, keepdims=False)
        return keep, lax.ppermute(give, "core", [(0, 1), (1, 0)])

    gate_w = jnp.concatenate(swap(gate_proj), axis=1)
    up_w = jnp.concatenate(swap(up_proj), axis=1)
    down_w = jnp.concatenate(swap(down_proj), axis=0)

    expert_iota = jnp.arange(expert_count, dtype=jnp.int32)
    hits = jnp.any(routes[:, :, None] == expert_iota[None, None, :], axis=1)
    earlier = jnp.tril(jnp.ones((group_size, group_size), bf16), -1)
    position = jnp.dot(earlier, hits.astype(bf16), preferred_element_type=f32)
    shifted = jnp.where(hits, router_logits, -jnp.inf)
    shifted = jnp.exp(shifted - jnp.max(shifted, axis=1, keepdims=True))
    gates = shifted / jnp.sum(shifted, axis=1, keepdims=True)

    def of_core(table):
        return lax.dynamic_index_in_dim(
            table.reshape(group_size, ep_count, chip_cores), core, 2, keepdims=False
        )

    slot = jnp.where(of_core(hits), of_core(position), -1.0)
    gates = of_core(gates)
    slot_iota = jnp.arange(capacity, dtype=jnp.int32).astype(f32)

    stacked = jnp.concatenate([tokens, jnp.broadcast_to(norm_gain[None, :], (16, width))], axis=0)
    whole = lax.all_gather(stacked, ("x", "core"), axis=0, tiled=False)
    floated = whole[:, :group_size].astype(f32)
    mean_square = jnp.sum(floated * floated, axis=(0, 2)) / (width * whole.shape[0])
    mine = lax.dynamic_slice_in_dim(whole, row * chip_cores, chip_cores, 0)
    normed = (
        mine[:, :group_size].astype(f32)
        * lax.rsqrt(mean_square + epsilon)[None, :, None]
        * mine[:, group_size : group_size + 1].astype(f32)
    ).astype(bf16)
    normed = jnp.concatenate([normed[0], normed[1]], axis=1)

    table = (slot.T[:, None, :] == slot_iota[None, :, None]).astype(bf16)
    outgoing = jnp.dot(
        table.reshape(ep_count * capacity, group_size), normed, preferred_element_type=f32
    ).astype(bf16)
    arrived = lax.all_to_all(
        outgoing.reshape(ep_count, capacity, -1), "ep", split_axis=0, concat_axis=0, tiled=True
    ).reshape(ep_count * capacity, -1)
    rows = lax.all_gather(arrived, "x", axis=0, tiled=False)
    part = rows.shape[2]
    gate_val = jnp.einsum(
        "frd,fdh->rh", rows, gate_w.reshape(row_count, part, -1), preferred_element_type=f32
    )
    up_val = jnp.einsum(
        "frd,fdh->rh", rows, up_w.reshape(row_count, part, -1), preferred_element_type=f32
    )
    hidden = (jax.nn.silu(gate_val) * up_val).astype(bf16)
    term = jnp.einsum(
        "rh,hfd->frd", hidden, down_w.reshape(-1, row_count, part), preferred_element_type=f32
    ).astype(bf16)
    summed = lax.psum_scatter(term, "x", scatter_dimension=0, tiled=False)
    returned = lax.all_to_all(
        summed.reshape(ep_count, capacity, -1), "ep", split_axis=0, concat_axis=0, tiled=True
    ).reshape(ep_count * capacity, -1)

    weight = jnp.where(slot[:, :, None] == slot_iota[None, None, :], gates[:, :, None], 0.0)
    weight = weight.reshape(group_size, ep_count * capacity)
    high = lax.reduce_precision(weight, 8, 7)
    both = jnp.concatenate([high.astype(bf16), (weight - high).astype(bf16)], axis=0)
    mixed = jnp.dot(both, returned, preferred_element_type=f32)
    mixed = mixed[:group_size] + mixed[group_size:]
    keep = lax.dynamic_slice_in_dim(mixed, core * width, width, 1)
    give = lax.dynamic_slice_in_dim(mixed, (1 - core) * width, width, 1)
    return (keep + lax.ppermute(give, "core", [(0, 1), (1, 0)])).astype(bf16)


def solution(mesh):
    ep_count, tp_count = mesh.devices.shape
    fine = Mesh(
        mesh.devices.reshape(ep_count, tp_count // chip_cores, chip_cores), ("ep", "x", "core")
    )
    tp = ("x", "core")
    return jax.shard_map(
        on_device,
        mesh=fine,
        in_specs=(
            P("ep", tp),
            P(tp),
            P("ep", None),
            P("ep", None),
            P("ep", None, tp),
            P("ep", None, tp),
            P("ep", tp, None),
        ),
        out_specs=P("ep", tp),
        check_vma=False,
    )
```

time: 432 us -> 226 us (0.52)
  blocking collectives: 221 us -> 53.8 us
  other arithmetic: 30.4 us -> 3.16 us
  local copies, waits for them, and re-layouts: 21.3 us -> 7.56 us
  waiting for transfers between devices: 116 us -> 121 us
    all_to_all x1, blocking collectives: 197 us -> 40.2 us  [on_device(): lax.all_to_all(outgoing.reshape(ep_count, capacity, -1), 'ep', split_axis...]
    all_gather x0 -> x1, waiting for transfers between devices: none -> 42.1 us  [on_device(): rows = lax.all_gather(arrived, 'x', axis=0, tiled=False)]
    reduce_scatter x1, waiting for transfers between devices: 89 us -> 49.9 us  [on_device(): summed = lax.psum_scatter(term, 'x', scatter_dimension=0, tiled=False)]
    another operation x3 -> x0, other arithmetic: 18.2 us -> none
    transpose x1 -> x0, local copies, waits for them, and re-layouts: 11.6 us -> none  [on_device(): jnp.einsum('slch,lhd->dslc', hidden, down_proj, preferred_element_type=jn...]
    all_gather x2 -> x1, blocking collectives: 23.9 us -> 13.6 us  [on_device(): whole = lax.all_gather(stacked, ('x', 'core'), axis=0, tiled=False)]
    reduce_or x1, other arithmetic: 7.41 us -> 0.81 us  [on_device(): hits = jnp.any(routes[:, :, None] == expert_iota[None, None, :], axis=1)]
    unnamed x14 -> x7, local copies, waits for them, and re-layouts: 4.78 us -> 0.01 us
  transfers between devices with their start and end apart: 2 -> 7, of which waited for: 2 -> 4; matrix products, arithmetic and copies ran while one was open for 0% -> 4% of each run, Pallas kernels for 0% -> 0%
where the time goes in v1:
time: 226 us; the launch traced here: 225 us
  waiting for transfers between devices  121 us (54%)
  blocking collectives  53.8 us (24%)
  matrix products  14.7 us (7%)
  between operations  13.6 us (6%)
  starting transfers between devices  10.8 us (5%)
  local copies, waits for them, and re-layouts  7.56 us (3%)
  other arithmetic  3.16 us (1%)
    reduce_scatter x1, waiting for transfers between devices, on_device(): summed = lax.psum_scatter(term, 'x', scatter_dimension=0, tiled=False)  49.9 us
    all_gather x1, waiting for transfers between devices, on_device(): rows = lax.all_gather(arrived, 'x', axis=0, tiled=False)  42.1 us
    all_to_all x1, blocking collectives, on_device(): lax.all_to_all(outgoing.reshape(ep_count, capacity, -1), 'ep', split_axis...  40.2 us
    all_to_all x1, waiting for transfers between devices, on_device(): lax.all_to_all(summed.reshape(ep_count, capacity, -1), 'ep', split_axis=0...  27.8 us
    all_gather x1, blocking collectives, on_device(): whole = lax.all_gather(stacked, ('x', 'core'), axis=0, tiled=False)  13.6 us
    all_to_all x1, starting transfers between devices, on_device(): lax.all_to_all(summed.reshape(ep_count, capacity, -1), 'ep', split_axis=0...  10.2 us
    dot_general x1, matrix products, on_device(): jnp.einsum('rh,hfd->frd', hidden, down_w.reshape(-1, row_count, part), pr...  9.02 us
    dot_general x1, matrix products, on_device(): jnp.einsum('frd,fdh->rh', rows, gate_w.reshape(row_count, part, -1), pref...  4.6 us
  transfers between devices with their start and end apart: 7, of which 4 were waited for; matrix products, arithmetic and copies ran while one was open for 4% of the time, Pallas kernels for 0%

profile of v1, /device:TPU:8, one launch (start us, length us, event | category | flops | bytes accessed | tf_op | source)
XLA Modules:
  0.0 224.8 jit_solution(14102034705566823099)
XLA Ops:
  6.5 0.0 copy-start
  6.5 0.0 all-gather.3.cloned.1.call-start
  6.6 0.8 fusion.26
  7.4 0.1 eq.62
  7.5 0.7 broadcast_in_dim.55
  8.2 0.8 pad_maximum_fusion
  9.0 0.0 copy-start.1
  9.0 13.6 %all-gather = bf16[1152,256]{1,0:T(8,128)(2,1)S(1)} all-gather(bf16[144,256]{1,0:T(8,128)(2,1)S(1)} %pad_maximum_fusion), channel_id=2, replica_groups=mesh['ep'=32,'x'=4,'core'=2] {'x','core'}, dimensions={0}, use_global_device_ids=true | all-gather | bytes 663552 | tf_op jit(solution)/shard_map/all_gather | solution.py:48
  22.6 0.2 multiply_reduce_fusion
  22.9 0.1 multiply_convert_fusion
  23.0 0.2 fusion.32
  23.3 0.2 bitcast_compare_fusion
  23.5 0.4 convolution_convert_fusion
  23.9 40.2 %all_to_all.10 = bf16[32,32,512]{2,1,0:T(8,128)(2,1)} all-to-all(bf16[32,32,512]{2,1,0:T(8,128)(2,1)S(1)} %bitcast.73), channel_id=1, replica_groups=mesh['ep'=32,'x'=4,'core'=2] {'ep'}, dimensions={0} | all-to-all | bytes 2097152 | tf_op jit(solution)/shard_map/all_to_all | solution.py:63
  64.1 0.0 all-gather.3.cloned.1.call-update
  64.1 0.0 reduce-scatter.2.cloned.1.call-start
  64.2 0.0 copy-done
  64.2 0.9 constant_dynamic-slice_fusion.4
  65.1 0.0 collective-permute-start
  65.1 0.0 copy-done.1
  65.1 0.9 constant_dynamic-slice_fusion.2
  66.0 0.5 collective-permute-start.1
  66.5 2.1 constant_dynamic-slice_fusion.1
  68.6 0.0 collective-permute-start.2
  68.6 0.3 copy.32
  68.8 0.0 collective-permute-done
  68.9 0.3 copy.33
  69.1 0.0 collective-permute-done.1
  69.1 42.1 %all-gather.3.cloned.1.call-done = bf16[4,1024,512]{2,1,0:T(8,128)(2,1)} async-done(((bf16[1,1024,512]{2,1,0:T(8,128)(2,1)}), bf16[4,1024,512]{2,1,0:T(8,128)(2,1)}) %all-gather.3.cloned.1.call-update) | async-done | bytes 4194320 | tf_op jit(solution)/shard_map/all_gather | solution.py:66
  111.2 4.6 %convolution_bitcast_fusion.1 = f32[1024,256]{1,0:T(8,128)} fusion(bf16[4,1024,512]{2,1,0:T(8,128)(2,1)} %all-gather.3.cloned.1.call-done, bf16[4,512,128]{2,1,0:T(8,128)(2,1)} %bitcast.19, bf16[4,512,128]{2,1,0:T(8,128)(2,1)S(1)} %bitcast.82), kind=kOutput, calls=%fused_computation.4 | convolution fusion | flops 1075838976 | bytes 6291456 | tf_op jit(solution)/shard_map/frd,fdh->rh/dot_general | solution.py:68
  115.8 0.0 collective-permute-done.2
  115.8 9.0 %convert_bitcast_fusion = bf16[4,1024,512]{1,2,0:T(8,128)(2,1)} fusion(bf16[4,1024,512]{2,1,0:T(8,128)(2,1)} %all-gather.3.cloned.1.call-done, bf16[128,4,512]{0,2,1:T(8,128)(2,1)S(1)} %bitcast.80, bf16[128,4,512]{0,2,1:T(8,128)(2,1)S(1)} %bitcast.79, bf16[4,512,128]{2,1,0:T(8,128)(2,1)} %bitcast.23, bf16[4,512,128]{2,1,0:T(8,128)(2,1)S(1)} %bitcast.81, ...), kind=kOutput, calls=%fused_computation | convolution fusion | flops 2155347968 | bytes 11534336 | tf_op jit(solution)/shard_map/rh,hfd->frd/dot_general | solution.py:75
  124.8 0.0 copy-start.2
  124.8 0.0 reduce-scatter.2.cloned.1.call-update
  124.8 49.9 %reduce-scatter.2.cloned.1.call-done = bf16[1,1024,512]{1,2,0:T(8,128)(2,1)} async-done(((bf16[4,1024,512]{1,2,0:T(8,128)(2,1)}), bf16[1,1024,512]{1,2,0:T(8,128)(2,1)}) %reduce-scatter.2.cloned.1.call-update) | async-done | bytes 1048592 | tf_op jit(solution)/shard_map/reduce_scatter | solution.py:78
  174.7 2.3 %copy.34 = bf16[1,1024,512]{2,1,0:T(8,128)(2,1)} copy(bf16[1,1024,512]{1,2,0:T(8,128)(2,1)} %reduce-scatter.2.cloned.1.call-done) | data formatting | bytes 2097152 | tf_op jit(solution)/shard_map/reduce_scatter | solution.py:78
  177.0 10.2 %all-to-all-start.1 = ((bf16[32,32,512]{2,1,0:T(8,128)(2,1)}), bf16[32,32,512]{2,1,0:T(8,128)(2,1)S(1)}, u32[]{:S(2)}, u32[]{:S(2)}) async-start(bf16[32,32,512]{2,1,0:T(8,128)(2,1)} %bitcast.27), calls=%async_computation.2 | async-start | bytes 2097152 | tf_op jit(solution)/shard_map/all_to_all | solution.py:79
  187.2 0.0 copy-done.2
  187.3 0.2 reduce-precision_convert_fusion
  187.5 27.8 %all-to-all-done.1 = bf16[32,32,512]{2,1,0:T(8,128)(2,1)S(1)} async-done(((bf16[32,32,512]{2,1,0:T(8,128)(2,1)}), bf16[32,32,512]{2,1,0:T(8,128)(2,1)S(1)}, u32[]{:S(2)}, u32[]{:S(2)}) %all-to-all-start.1) | async-done | bytes 1048608 | tf_op jit(solution)/shard_map/all_to_all | solution.py:79
  215.3 0.4 fusion.21
  215.8 0.1 collective-permute-start.3
  215.9 1.3 collective-permute-done.3
  217.3 0.6 add_convert_fusion
  (17 shorter events, 0.3 us)
Async XLA Ops:
  6.5 57.6 %copy-start = (bf16[2,128,2048]{2,1,0:T(8,128)(2,1)S(1)}, bf16[2,128,2048]{2,1,0:T(8,128)(2,1)}, u32[]{:S(2)}) copy-start(bf16[2,128,2048]{2,1,0:T(8,128)(2,1)} %param.13) | copy-start | bytes 3145732
  6.5 104.7 %all-gather.3.cloned.1.call-start = ((), (), s32[]{:S(2)}) async-start(), calls=%async_computation.3 | async-start | bytes 5242880 | tf_op jit(solution)/shard_map/all_gather | solution.py:66
  9.0 56.1 %copy-start.1 = (bf16[2,2048,128]{2,1,0:T(8,128)(2,1)S(1)}, bf16[2,2048,128]{2,1,0:T(8,128)(2,1)}, u32[]{:S(2)}) copy-start(bf16[2,2048,128]{2,1,0:T(8,128)(2,1)} %param.11) | copy-start | bytes 3145732
  64.1 110.6 %reduce-scatter.2.cloned.1.call-start = ((), (), s32[]{:S(2)}) async-start(), calls=%async_computation.4 | async-start | bytes 5242880 | tf_op jit(solution)/shard_map/reduce_scatter | solution.py:78
  65.1 3.7 %collective-permute-start = (bf16[128,2048]{1,0:T(8,128)(2,1)}, bf16[128,2048]{1,0:T(8,128)(2,1)S(1)}, u32[]{:S(2)}, u32[]{:S(2)}) collective-permute-start(bf16[128,2048]{1,0:T(8,128)(2,1)} %get-tuple-element.10), channel_id=1, source_target_pairs={{0,1},{1,0},{2,3},{3,2},{4,5},{5,4},{6,7},{7,6},{8,9},{9,8},{10,11... | collective-permute-start | bytes 1572872 | tf_op jit(solution)/shard_map/ppermute | solution.py:24
  66.0 3.1 %collective-permute-start.1 = (bf16[2048,128]{1,0:T(8,128)(2,1)}, bf16[2048,128]{1,0:T(8,128)(2,1)}, u32[]{:S(2)}, u32[]{:S(2)}) collective-permute-start(bf16[2048,128]{1,0:T(8,128)(2,1)} %get-tuple-element.6), channel_id=1, source_target_pairs={{0,1},{1,0},{2,3},{3,2},{4,5},{5,4},{6,7},{7,6},{8,9},{9,8},{10,11... | collective-permute-start | bytes 1572872 | tf_op jit(solution)/shard_map/ppermute | solution.py:24
  68.6 47.2 %collective-permute-start.2 = (bf16[2048,128]{1,0:T(8,128)(2,1)}, bf16[2048,128]{1,0:T(8,128)(2,1)}, u32[]{:S(2)}, u32[]{:S(2)}) collective-permute-start(bf16[2048,128]{1,0:T(8,128)(2,1)} %get-tuple-element.8), channel_id=1, source_target_pairs={{0,1},{1,0},{2,3},{3,2},{4,5},{5,4},{6,7},{7,6},{8,9},{9,8},{10,11... | collective-permute-start | bytes 1572872 | tf_op jit(solution)/shard_map/ppermute | solution.py:24
  124.8 62.4 %copy-start.2 = (f32[128,64]{0,1:T(8,128)S(1)}, f32[128,64]{0,1:T(8,128)}, u32[]{:S(2)}) copy-start(f32[128,64]{0,1:T(8,128)} %param.9) | copy-start | bytes 98308
  177.0 38.3 %all-to-all-start.1 = ((bf16[32,32,512]{2,1,0:T(8,128)(2,1)}), bf16[32,32,512]{2,1,0:T(8,128)(2,1)S(1)}, u32[]{:S(2)}, u32[]{:S(2)}) async-start(bf16[32,32,512]{2,1,0:T(8,128)(2,1)} %bitcast.27), calls=%async_computation.2 | async-start | bytes 2097152 | tf_op jit(solution)/shard_map/all_to_all | solution.py:79
  215.8 1.4 collective-permute-start.3
Sparse Core Ops, SparseCore 0:
  64.2 46.9 all-gather.2
  125.0 49.7 reduce-scatter.1

commit v2 on v1

v2 whole, which is shorter than its diff:
```python
import jax
import jax.numpy as jnp
from jax import lax
from jax.experimental import pallas as pl
from jax.experimental.pallas import tpu as pltpu
from jax.sharding import Mesh, PartitionSpec as P

epsilon = 1e-05
chip_cores = 2
other_core = [(0, 1), (1, 0)]
near_chip = [(0, 1), (1, 0), (2, 3), (3, 2)]
cross_chip = [(0, 3), (3, 0), (1, 2), (2, 1)]


def ffn_kernel(core_ref, arrived, across, *refs):
    joined, downs, (keep, give, hidden) = refs[:4], refs[4:8], refs[8:]
    core = core_ref[0]
    f32 = jnp.float32
    rows, held = arrived.shape
    block = 256
    unit = downs[0].shape[0]

    def at(j, parity):
        return pl.ds(pl.multiple_of((2 * j + parity) * block, block), block)

    for k in range(4):
        both = jnp.zeros((rows, 2 * unit), f32)
        for j in range(held // block):
            lanes = pl.ds(j * block, block)
            both += jnp.dot(arrived[:, lanes], joined[k][at(j, core), :], preferred_element_type=f32)
            both += jnp.dot(
                across[:, lanes], joined[k][at(j, 1 - core), :], preferred_element_type=f32
            )
        gate_val, up_val = both[:, :unit], both[:, unit:]
        silu = gate_val / (1.0 + jnp.exp(-gate_val))
        hidden[:, pl.ds(k * unit, unit)] = (silu * up_val).astype(hidden.dtype)
    for parity, out in ((core, keep), (1 - core, give)):
        for j in range(held // block):
            total = jnp.zeros((rows, block), f32)
            for k in range(4):
                total += jnp.dot(
                    hidden[:, pl.ds(k * unit, unit)],
                    downs[k][:, at(j, parity)],
                    preferred_element_type=f32,
                )
            out[:, pl.ds(j * block, block)] = total.astype(out.dtype)


def expert_rows(core, arrived, across, shards):
    rows, held = arrived.shape
    unit, width = shards[0][1].shape
    whole = pl.BlockSpec(memory_space=pltpu.VMEM)
    return pl.pallas_call(
        ffn_kernel,
        out_shape=(
            jax.ShapeDtypeStruct((rows, held), jnp.float32),
            jax.ShapeDtypeStruct((rows, held), jnp.bfloat16),
        ),
        in_specs=[pl.BlockSpec(memory_space=pltpu.SMEM)] + [whole] * 10,
        out_specs=(whole, whole),
        scratch_shapes=[pltpu.VMEM((rows, 4 * unit), jnp.bfloat16)],
        compiler_params=pltpu.CompilerParams(vmem_limit_bytes=40 * 2**20),
        cost_estimate=pl.CostEstimate(
            flops=2 * rows * width * 4 * unit * 3, bytes_accessed=12 * 2**20, transcendentals=0
        ),
    )(
        core.reshape(1).astype(jnp.int32),
        arrived,
        across,
        *[one[0] for one in shards],
        *[one[1] for one in shards],
    )


def on_device(tokens, norm_gain, router_logits, routes, gate_proj, up_proj, down_proj):
    bf16, f32 = jnp.bfloat16, jnp.float32
    ep_count = lax.axis_size("ep")
    row_count = lax.axis_size("x")
    group_size, width = tokens.shape
    local_experts = gate_proj.shape[0]
    top_count = routes.shape[1]
    expert_count = local_experts * ep_count
    capacity = 2 * group_size * top_count // expert_count
    share = capacity // (row_count // local_experts)
    core = lax.axis_index("core")
    row = lax.axis_index("x")
    kind = row // local_experts
    half = row % local_experts

    def pick(at):
        joined = jnp.concatenate([gate_proj, up_proj], axis=2)
        return (
            lax.dynamic_index_in_dim(joined, at, 0, keepdims=False),
            lax.dynamic_index_in_dim(down_proj, at, 0, keepdims=False),
        )

    def send(arrays, pairs):
        return tuple(lax.ppermute(one, "x", pairs) for one in arrays)

    own = pick(kind)
    crossed = send(pick(1 - kind), cross_chip)
    near = send(own, near_chip)
    relayed = send(crossed, near_chip)
    shards = (own, near, crossed, relayed)

    expert_iota = jnp.arange(expert_count, dtype=jnp.int32)
    hits = jnp.any(routes[:, :, None] == expert_iota[None, None, :], axis=1)
    earlier = jnp.tril(jnp.ones((group_size, group_size), bf16), -1)
    position = jnp.dot(earlier, hits.astype(bf16), preferred_element_type=f32)
    shifted = jnp.where(hits, router_logits, -jnp.inf)
    shifted = jnp.exp(shifted - jnp.max(shifted, axis=1, keepdims=True))
    gates = shifted / jnp.sum(shifted, axis=1, keepdims=True)

    def of_kind(table):
        return lax.dynamic_index_in_dim(
            table.reshape(group_size, ep_count, local_experts), kind, 2, keepdims=False
        )

    slot = jnp.where(of_kind(hits), of_kind(position), -1.0)
    gates = of_kind(gates)
    slot_iota = (jnp.arange(share, dtype=jnp.int32) + half * share).astype(f32)

    stacked = jnp.concatenate([tokens, jnp.broadcast_to(norm_gain[None, :], (16, width))], axis=0)
    whole = lax.all_gather(stacked, ("x", "core"), axis=0, tiled=False)
    floated = whole[:, :group_size].astype(f32)
    mean_square = jnp.sum(floated * floated, axis=(0, 2)) / (width * whole.shape[0])
    mine = lax.dynamic_index_in_dim(
        whole.reshape(row_count, chip_cores, -1, width), core, 1, keepdims=False
    )
    normed = (
        mine[:, :group_size].astype(f32)
        * lax.rsqrt(mean_square + epsilon)[None, :, None]
        * mine[:, group_size : group_size + 1].astype(f32)
    ).astype(bf16)
    normed = jnp.concatenate([normed[j] for j in range(row_count)], axis=1)

    table = (slot.T[:, None, :] == slot_iota[None, :, None]).astype(bf16)
    outgoing = jnp.dot(
        table.reshape(ep_count * share, group_size), normed, preferred_element_type=f32
    ).astype(bf16)
    arrived = lax.all_to_all(
        outgoing.reshape(ep_count, share, -1), "ep", split_axis=0, concat_axis=0, tiled=True
    ).reshape(ep_count * share, -1)
    across = lax.ppermute(arrived, "core", other_core)
    keep, give = expert_rows(core, arrived, across, shards)
    summed = keep + lax.ppermute(give, "core", other_core).astype(f32)
    returned = lax.all_to_all(
        summed.astype(bf16).reshape(ep_count, share, -1), "ep", split_axis=0, concat_axis=0, tiled=True
    ).reshape(ep_count * share, -1)

    weight = jnp.where(slot[:, :, None] == slot_iota[None, None, :], gates[:, :, None], 0.0)
    weight = weight.reshape(group_size, ep_count * share)
    high = lax.reduce_precision(weight, 8, 7)
    both = jnp.concatenate([high.astype(bf16), (weight - high).astype(bf16)], axis=0)
    mixed = jnp.dot(both, returned, preferred_element_type=f32)
    mixed = mixed[:group_size] + mixed[group_size:]

    def block_of(step):
        return lax.dynamic_slice_in_dim(mixed, ((row + step) % row_count) * width, width, 1)

    result = block_of(0)
    for step in range(1, row_count):
        pairs = [(at, (at + step) % row_count) for at in range(row_count)]
        result = result + lax.ppermute(block_of(step), "x", pairs)
    return result.astype(bf16)


def solution(mesh):
    ep_count, tp_count = mesh.devices.shape
    fine = Mesh(
        mesh.devices.reshape(ep_count, tp_count // chip_cores, chip_cores), ("ep", "x", "core")
    )
    tp = ("x", "core")
    return jax.shard_map(
        on_device,
        mesh=fine,
        in_specs=(
            P("ep", tp),
            P(tp),
            P("ep", None),
            P("ep", None),
            P("ep", None, tp),
            P("ep", None, tp),
            P("ep", tp, None),
        ),
        out_specs=P("ep", tp),
        check_vma=False,
    )
```

time: 226 us -> 164 us (0.73)
  blocking collectives: 53.8 us -> 13.5 us
  starting transfers between devices: 10.8 us -> 31.5 us
  waiting for transfers between devices: 121 us -> 103 us
  between operations: 13.6 us -> 0.32 us
  matrix products: 14.7 us -> 2.04 us
  Pallas kernels: 0 us -> 6.4 us
  local copies, waits for them, and re-layouts: 7.56 us -> 2.37 us
    ppermute x4 -> x11, waiting for transfers between devices: 1.34 us -> 74.6 us  [the longest x6 66.1 us: send(): return tuple((lax.ppermute(one, 'x', pairs) for one in arrays))]
    reduce_scatter x1 -> x0, waiting for transfers between devices: 49.9 us -> none  [on_device(): summed = lax.psum_scatter(term, 'x', scatter_dimension=0, tiled=False)]
    all_gather x1 -> x0, waiting for transfers between devices: 42.1 us -> none  [on_device(): rows = lax.all_gather(arrived, 'x', axis=0, tiled=False)]
    all_to_all x1 -> x0, blocking collectives: 40.2 us -> none  [on_device(): lax.all_to_all(outgoing.reshape(ep_count, capacity, -1), 'ep', split_axis...]
    dot_general x3 -> x1, matrix products: 14 us -> 1.39 us  [on_device(): jnp.dot(table.reshape(ep_count * share, group_size), normed, preferred_el...]
    all_to_all x1 -> x2, starting transfers between devices: 10.2 us -> 21.7 us  [the longest x1 11.8 us: on_device(): lax.all_to_all(outgoing.reshape(ep_count, share, -1), 'ep', split_axis=0,...]
    ppermute x4 -> x11, starting transfers between devices: 0.61 us -> 9.8 us  [the longest x6 5.47 us: send(): return tuple((lax.ppermute(one, 'x', pairs) for one in arrays))]
    pallas_call x0 -> x1, Pallas kernels: none -> 6.4 us  [expert_rows(): pl.pallas_call(ffn_kernel, out_shape=(jax.ShapeDtypeStruct((rows, held),...]
  transfers between devices with their start and end apart: 7 -> 13, of which waited for: 4 -> 9; matrix products, arithmetic and copies ran while one was open for 4% -> 1% of each run, Pallas kernels for 0% -> 0%
where the time goes in v2:
time: 164 us
  waiting for transfers between devices  103 us (63%)
  starting transfers between devices  31.5 us (19%)
  blocking collectives  13.5 us (8%)
  Pallas kernels  6.4 us (4%)
  other arithmetic  4.36 us (3%)
  local copies, waits for them, and re-layouts  2.37 us (1%)
  matrix products  2.04 us (1%)
    ppermute x6, waiting for transfers between devices, send(): return tuple((lax.ppermute(one, 'x', pairs) for one in arrays))  66.1 us
    all_to_all x1, waiting for transfers between devices, on_device(): lax.all_to_all(summed.astype(bf16).reshape(ep_count, share, -1), 'ep', sp...  28 us
    all_gather x1, blocking collectives, on_device(): whole = lax.all_gather(stacked, ('x', 'core'), axis=0, tiled=False)  13.5 us
    all_to_all x1, starting transfers between devices, on_device(): lax.all_to_all(outgoing.reshape(ep_count, share, -1), 'ep', split_axis=0,...  11.8 us
    all_to_all x1, starting transfers between devices, on_device(): lax.all_to_all(summed.astype(bf16).reshape(ep_count, share, -1), 'ep', sp...  9.91 us
    pallas_call x1, Pallas kernels, expert_rows(): pl.pallas_call(ffn_kernel, out_shape=(jax.ShapeDtypeStruct((rows, held),...  6.4 us
    ppermute x3, waiting for transfers between devices, on_device(): result = result + lax.ppermute(block_of(step), 'x', pairs)  5.84 us
    ppermute x6, starting transfers between devices, send(): return tuple((lax.ppermute(one, 'x', pairs) for one in arrays))  5.47 us
  transfers between devices with their start and end apart: 13, of which 9 were waited for; matrix products, arithmetic and copies ran while one was open for 1% of the time, Pallas kernels for 0%

profile of v2, /device:TPU:8, one launch (start us, length us, event | category | flops | bytes accessed | tf_op | source)
XLA Modules:
  0.0 163.6 jit_solution(8757397606536543521)
XLA Ops:
  0.0 0.7 fusion.12
  0.8 0.1 eq.64
  0.9 0.7 broadcast_in_dim.55
  1.5 0.8 pad_maximum_fusion
  2.4 13.5 %all-gather = bf16[1152,256]{1,0:T(8,128)(2,1)S(1)} all-gather(bf16[144,256]{1,0:T(8,128)(2,1)S(1)} %pad_maximum_fusion), channel_id=2, replica_groups=mesh['ep'=32,'x'=4,'core'=2] {'x','core'}, dimensions={0}, use_global_device_ids=true | all-gather | bytes 663552 | tf_op jit(solution)/shard_map/all_gather | solution.py:124
  16.0 0.2 multiply_reduce_fusion
  16.2 0.1 multiply_convert_fusion
  16.3 0.0 copy-start
  16.4 0.2 fusion.15
  16.6 0.1 bitcast_compare_fusion
  16.7 1.4 convolution_convert_fusion
  18.1 0.0 copy-start.1
  18.1 11.8 %all-to-all-start = ((bf16[32,16,1024]{2,1,0:T(8,128)(2,1)}), bf16[32,16,1024]{2,1,0:T(8,128)(2,1)S(1)}, u32[]{:S(2)}, u32[]{:S(2)}) async-start(bf16[32,16,1024]{2,1,0:T(8,128)(2,1)} %bitcast.17), calls=%async_computation | async-start | bytes 2097152 | tf_op jit(solution)/shard_map/all_to_all | solution.py:141
  30.0 0.0 copy-done
  30.0 0.2 constant_dynamic-update-slice_fusion.1
  30.2 0.0 copy-done.1
  30.2 0.2 constant_dynamic-update-slice_fusion
  30.5 0.0 copy-start.2
  30.5 0.1 dynamic-slice_bitcast_fusion
  30.6 2.5 %collective-permute-start.2 = (bf16[2048,256]{1,0:T(8,128)(2,1)S(1)}, bf16[2048,256]{1,0:T(8,128)(2,1)}, u32[]{:S(2)}, u32[]{:S(2)}) collective-permute-start(bf16[2048,256]{1,0:T(8,128)(2,1)S(1)} %get-tuple-element.9), channel_id=1, source_target_pairs={{0,6},{6,0},{2,4},{4,2},{1,7},{7,1},{3,5},{5,3},{8,14},{14,8},{10,... | collective-permute-start | bytes 3145736 | tf_op jit(solution)/shard_map/ppermute | solution.py:98
  33.1 0.0 collective-permute-start.1
  33.1 0.0 copy-done.2
  33.1 0.9 dynamic-slice_bitcast_fusion.2
  34.0 1.4 collective-permute-start.5
  35.4 22.7 %collective-permute-done.2.refs_2_ = bf16[2048,256]{1,0:T(8,128)(2,1)} collective-permute-done((bf16[2048,256]{1,0:T(8,128)(2,1)S(1)}, bf16[2048,256]{1,0:T(8,128)(2,1)}, u32[]{:S(2)}, u32[]{:S(2)}) %collective-permute-start.2) | collective-permute-done | bytes 1048608 | tf_op jit(solution)/shard_map/ppermute | solution.py:98
  58.1 0.0 collective-permute-start.3
  58.1 0.5 all-to-all-done
  58.6 0.0 collective-permute-start
  58.6 1.5 collective-permute-start.4
  60.1 7.9 %collective-permute-done.5.refs_6_ = bf16[128,2048]{1,0:T(8,128)(2,1)S(1)} collective-permute-done((bf16[128,2048]{1,0:T(8,128)(2,1)}, bf16[128,2048]{1,0:T(8,128)(2,1)S(1)}, u32[]{:S(2)}, u32[]{:S(2)}) %collective-permute-start.5) | collective-permute-done | bytes 524320 | tf_op jit(solution)/shard_map/ppermute | solution.py:98
  68.0 0.0 collective-permute-start.6
  68.0 27.6 %collective-permute-done.4.refs_5_ = bf16[128,2048]{1,0:T(8,128)(2,1)S(1)} collective-permute-done((bf16[128,2048]{1,0:T(8,128)(2,1)S(1)}, bf16[128,2048]{1,0:T(8,128)(2,1)S(1)}, u32[]{:S(2)}, u32[]{:S(2)}) %collective-permute-start.4) | collective-permute-done | bytes 524320 | tf_op jit(solution)/shard_map/ppermute | solution.py:98
  95.6 0.0 collective-permute-done.1.refs_1_
  95.6 7.9 %collective-permute-done.6.refs_7_ = bf16[128,2048]{1,0:T(8,128)(2,1)S(1)} collective-permute-done((bf16[128,2048]{1,0:T(8,128)(2,1)S(1)}, bf16[128,2048]{1,0:T(8,128)(2,1)S(1)}, u32[]{:S(2)}, u32[]{:S(2)}) %collective-permute-start.6) | collective-permute-done | bytes 524320 | tf_op jit(solution)/shard_map/ppermute | solution.py:98
  103.5 0.0 collective-permute-done.3.refs_3_
  103.5 0.0 collective-permute-done.across
  103.5 6.4 %shard_map.73 = (f32[512,1024]{1,0:T(8,128)S(1)}, bf16[512,1024]{1,0:T(8,128)(2,1)S(1)}) custom-call(s32[1]{0:T(128)} %bitcast.7.core_ref, bf16[512,1024]{1,0:T(8,128)(2,1)S(1)} %bitcast.58, bf16[512,1024]{1,0:T(8,128)(2,1)S(1)} %collective-permute-done.across, bf16[2048,256]{1,0:T(8,128)(2,1)S(1)} %get-tuple-element.10.refs_0_, ...), custom_call_target="tpu_custom_call" | custom-call | flops 3221225472 | bytes 12582912 | tf_op jit(solution)/shard_map/pallas_call | solution.py:53
  109.9 0.1 collective-permute-start.7
  110.0 2.6 %collective-permute-done.7 = bf16[512,1024]{1,0:T(8,128)(2,1)S(1)} collective-permute-done((bf16[512,1024]{1,0:T(8,128)(2,1)S(1)}, bf16[512,1024]{1,0:T(8,128)(2,1)S(1)}, u32[]{:S(2)}, u32[]{:S(2)}) %collective-permute-start.7) | collective-permute-done | bytes 1048608 | tf_op jit(solution)/shard_map/ppermute | solution.py:146
  112.7 1.3 add_convert_fusion
  114.0 0.0 copy-start.3
  114.0 9.9 %all-to-all-start.1 = ((bf16[32,16,1024]{2,1,0:T(8,128)(2,1)}), bf16[32,16,1024]{2,1,0:T(8,128)(2,1)S(1)}, u32[]{:S(2)}, u32[]{:S(2)}) async-start(bf16[32,16,1024]{2,1,0:T(8,128)(2,1)} %bitcast.23), calls=%async_computation.1 | async-start | bytes 2097152 | tf_op jit(solution)/shard_map/all_to_all | solution.py:147
  124.0 0.0 copy-done.3
  124.1 0.1 reduce-precision_convert_fusion
  124.3 28.0 %all-to-all-done.1 = bf16[32,16,1024]{2,1,0:T(8,128)(2,1)S(1)} async-done(((bf16[32,16,1024]{2,1,0:T(8,128)(2,1)}), bf16[32,16,1024]{2,1,0:T(8,128)(2,1)S(1)}, u32[]{:S(2)}, u32[]{:S(2)}) %all-to-all-start.1) | async-done | bytes 1048608 | tf_op jit(solution)/shard_map/all_to_all | solution.py:147
  152.3 0.5 fusion.1
  152.8 0.1 slice_add_fusion
  152.9 2.5 %collective-permute-start.10 = (f32[128,256]{1,0:T(8,128)S(1)}, f32[128,256]{1,0:T(8,128)S(1)}, u32[]{:S(2)}, u32[]{:S(2)}) collective-permute-start(f32[128,256]{1,0:T(8,128)S(1)} %get-tuple-element.14), channel_id=1, source_target_pairs={{0,6},{2,0},{4,2},{6,4},{1,7},{3,1},{5,3},{7,5},{8,14},{10,8},{12,... | collective-permute-start | bytes 393224 | tf_op jit(solution)/shard_map/ppermute | solution.py:164
  155.4 0.0 collective-permute-start.8
  155.4 1.7 %collective-permute-start.9 = (f32[128,256]{1,0:T(8,128)S(1)}, f32[128,256]{1,0:T(8,128)S(1)}, u32[]{:S(2)}, u32[]{:S(2)}) collective-permute-start(f32[128,256]{1,0:T(8,128)S(1)} %get-tuple-element.15), channel_id=1, source_target_pairs={{0,4},{2,6},{4,0},{6,2},{1,5},{3,7},{5,1},{7,3},{8,12},{10,14},{12... | collective-permute-start | bytes 393224 | tf_op jit(solution)/shard_map/ppermute | solution.py:164
  157.1 2.2 %collective-permute-done.10 = f32[128,256]{1,0:T(8,128)S(1)} collective-permute-done((f32[128,256]{1,0:T(8,128)S(1)}, f32[128,256]{1,0:T(8,128)S(1)}, u32[]{:S(2)}, u32[]{:S(2)}) %collective-permute-start.10) | collective-permute-done | bytes 131104 | tf_op jit(solution)/shard_map/ppermute | solution.py:164
  159.3 3.7 %collective-permute-done.8 = f32[128,256]{1,0:T(8,128)S(1)} collective-permute-done((f32[128,256]{1,0:T(8,128)S(1)}, f32[128,256]{1,0:T(8,128)S(1)}, u32[]{:S(2)}, u32[]{:S(2)}) %collective-permute-start.8) | collective-permute-done | bytes 131104 | tf_op jit(solution)/shard_map/ppermute | solution.py:164
  163.0 0.0 collective-permute-done.9
  163.0 0.7 add_convert_fusion.1
  (17 shorter events, 0.3 us)
Async XLA Ops:
  16.3 13.7 %copy-start = (bf16[2,2048,128]{2,1,0:T(8,128)(2,1)S(1)}, bf16[2,2048,128]{2,1,0:T(8,128)(2,1)}, u32[]{:S(2)}) copy-start(bf16[2,2048,128]{2,1,0:T(8,128)(2,1)} %param.11) | copy-start | bytes 3145732
  18.1 12.0 %copy-start.1 = (bf16[2,2048,128]{2,1,0:T(8,128)(2,1)S(1)}, bf16[2,2048,128]{2,1,0:T(8,128)(2,1)}, u32[]{:S(2)}) copy-start(bf16[2,2048,128]{2,1,0:T(8,128)(2,1)} %param.12) | copy-start | bytes 3145732
  18.1 40.4 %all-to-all-start = ((bf16[32,16,1024]{2,1,0:T(8,128)(2,1)}), bf16[32,16,1024]{2,1,0:T(8,128)(2,1)S(1)}, u32[]{:S(2)}, u32[]{:S(2)}) async-start(bf16[32,16,1024]{2,1,0:T(8,128)(2,1)} %bitcast.17), calls=%async_computation | async-start | bytes 2097152 | tf_op jit(solution)/shard_map/all_to_all | solution.py:141
  30.5 2.7 %copy-start.2 = (bf16[2,128,2048]{2,1,0:T(8,128)(2,1)S(1)}, bf16[2,128,2048]{2,1,0:T(8,128)(2,1)}, u32[]{:S(2)}) copy-start(bf16[2,128,2048]{2,1,0:T(8,128)(2,1)} %param.13) | copy-start | bytes 3145732
  30.6 27.5 %collective-permute-start.2 = (bf16[2048,256]{1,0:T(8,128)(2,1)S(1)}, bf16[2048,256]{1,0:T(8,128)(2,1)}, u32[]{:S(2)}, u32[]{:S(2)}) collective-permute-start(bf16[2048,256]{1,0:T(8,128)(2,1)S(1)} %get-tuple-element.9), channel_id=1, source_target_pairs={{0,6},{6,0},{2,4},{4,2},{1,7},{7,1},{3,5},{5,3},{8,14},{14,8},{10,... | collective-permute-start | bytes 3145736 | tf_op jit(solution)/shard_map/ppermute | solution.py:98
  33.1 62.5 %collective-permute-start.1 = (bf16[2048,256]{1,0:T(8,128)(2,1)S(1)}, bf16[2048,256]{1,0:T(8,128)(2,1)}, u32[]{:S(2)}, u32[]{:S(2)}) collective-permute-start(bf16[2048,256]{1,0:T(8,128)(2,1)S(1)} %get-tuple-element.10.refs_0_), channel_id=1, source_target_pairs={{0,2},{2,0},{4,6},{6,4},{1,3},{3,1},{5,7},{7,5},{8,10},{10,8},{12,... | collective-permute-start | bytes 3145736 | tf_op jit(solution)/shard_map/ppermute | solution.py:98
  34.0 34.0 %collective-permute-start.5 = (bf16[128,2048]{1,0:T(8,128)(2,1)}, bf16[128,2048]{1,0:T(8,128)(2,1)S(1)}, u32[]{:S(2)}, u32[]{:S(2)}) collective-permute-start(bf16[128,2048]{1,0:T(8,128)(2,1)} %get-tuple-element.11), channel_id=1, source_target_pairs={{0,6},{6,0},{2,4},{4,2},{1,7},{7,1},{3,5},{5,3},{8,14},{14,8},{10,... | collective-permute-start | bytes 1572872 | tf_op jit(solution)/shard_map/ppermute | solution.py:98
  58.1 45.5 %collective-permute-start.3 = (bf16[2048,256]{1,0:T(8,128)(2,1)}, bf16[2048,256]{1,0:T(8,128)(2,1)}, u32[]{:S(2)}, u32[]{:S(2)}) collective-permute-start(bf16[2048,256]{1,0:T(8,128)(2,1)} %collective-permute-done.2.refs_2_), channel_id=1, source_target_pairs={{0,2},{2,0},{4,6},{6,4},{1,3},{3,1},{5,7},{7,5},{8,10},{10,8},{12,... | collective-permute-start | bytes 3145736 | tf_op jit(solution)/shard_map/ppermute | solution.py:98
  58.6 45.0 %collective-permute-start = (bf16[512,1024]{1,0:T(8,128)(2,1)S(1)}, bf16[512,1024]{1,0:T(8,128)(2,1)S(1)}, u32[]{:S(2)}, u32[]{:S(2)}) collective-permute-start(bf16[512,1024]{1,0:T(8,128)(2,1)S(1)} %bitcast.57), channel_id=1, source_target_pairs={{0,1},{1,0},{2,3},{3,2},{4,5},{5,4},{6,7},{7,6},{8,9},{9,8},{10,11... | collective-permute-start | bytes 3145736 | tf_op jit(solution)/shard_map/ppermute | solution.py:144
  58.6 37.0 %collective-permute-start.4 = (bf16[128,2048]{1,0:T(8,128)(2,1)S(1)}, bf16[128,2048]{1,0:T(8,128)(2,1)S(1)}, u32[]{:S(2)}, u32[]{:S(2)}) collective-permute-start(bf16[128,2048]{1,0:T(8,128)(2,1)S(1)} %get-tuple-element.12.refs_4_), channel_id=1, source_target_pairs={{0,2},{2,0},{4,6},{6,4},{1,3},{3,1},{5,7},{7,5},{8,10},{10,8},{12,... | collective-permute-start | bytes 1572872 | tf_op jit(solution)/shard_map/ppermute | solution.py:98
  68.0 35.5 %collective-permute-start.6 = (bf16[128,2048]{1,0:T(8,128)(2,1)S(1)}, bf16[128,2048]{1,0:T(8,128)(2,1)S(1)}, u32[]{:S(2)}, u32[]{:S(2)}) collective-permute-start(bf16[128,2048]{1,0:T(8,128)(2,1)S(1)} %collective-permute-done.5.refs_6_), channel_id=1, source_target_pairs={{0,2},{2,0},{4,6},{6,4},{1,3},{3,1},{5,7},{7,5},{8,10},{10,8},{12,... | collective-permute-start | bytes 1572872 | tf_op jit(solution)/shard_map/ppermute | solution.py:98
  109.9 2.7 %collective-permute-start.7 = (bf16[512,1024]{1,0:T(8,128)(2,1)S(1)}, bf16[512,1024]{1,0:T(8,128)(2,1)S(1)}, u32[]{:S(2)}, u32[]{:S(2)}) collective-permute-start(bf16[512,1024]{1,0:T(8,128)(2,1)S(1)} %get-tuple-element.8), channel_id=1, source_target_pairs={{0,1},{1,0},{2,3},{3,2},{4,5},{5,4},{6,7},{7,6},{8,9},{9,8},{10,11... | collective-permute-start | bytes 3145736 | tf_op jit(solution)/shard_map/ppermute | solution.py:146
  114.0 10.0 %copy-start.3 = (f32[128,64]{0,1:T(8,128)S(1)}, f32[128,64]{0,1:T(8,128)}, u32[]{:S(2)}) copy-start(f32[128,64]{0,1:T(8,128)} %param.9) | copy-start | bytes 98308
  114.0 38.3 %all-to-all-start.1 = ((bf16[32,16,1024]{2,1,0:T(8,128)(2,1)}), bf16[32,16,1024]{2,1,0:T(8,128)(2,1)S(1)}, u32[]{:S(2)}, u32[]{:S(2)}) async-start(bf16[32,16,1024]{2,1,0:T(8,128)(2,1)} %bitcast.23), calls=%async_computation.1 | async-start | bytes 2097152 | tf_op jit(solution)/shard_map/all_to_all | solution.py:147
  152.9 6.4 %collective-permute-start.10 = (f32[128,256]{1,0:T(8,128)S(1)}, f32[128,256]{1,0:T(8,128)S(1)}, u32[]{:S(2)}, u32[]{:S(2)}) collective-permute-start(f32[128,256]{1,0:T(8,128)S(1)} %get-tuple-element.14), channel_id=1, source_target_pairs={{0,6},{2,0},{4,2},{6,4},{1,7},{3,1},{5,3},{7,5},{8,14},{10,8},{12,... | collective-permute-start | bytes 393224 | tf_op jit(solution)/shard_map/ppermute | solution.py:164
  155.4 7.6 %collective-permute-start.8 = (f32[128,256]{1,0:T(8,128)S(1)}, f32[128,256]{1,0:T(8,128)S(1)}, u32[]{:S(2)}, u32[]{:S(2)}) collective-permute-start(f32[128,256]{1,0:T(8,128)S(1)} %get-tuple-element.13), channel_id=1, source_target_pairs={{0,2},{2,4},{4,6},{6,0},{1,3},{3,5},{5,7},{7,1},{8,10},{10,12},{12... | collective-permute-start | bytes 393224 | tf_op jit(solution)/shard_map/ppermute | solution.py:164
  155.4 7.6 %collective-permute-start.9 = (f32[128,256]{1,0:T(8,128)S(1)}, f32[128,256]{1,0:T(8,128)S(1)}, u32[]{:S(2)}, u32[]{:S(2)}) collective-permute-start(f32[128,256]{1,0:T(8,128)S(1)} %get-tuple-element.15), channel_id=1, source_target_pairs={{0,4},{2,6},{4,0},{6,2},{1,5},{3,7},{5,1},{7,3},{8,12},{10,14},{12... | collective-permute-start | bytes 393224 | tf_op jit(solution)/shard_map/ppermute | solution.py:164

commit v3 on v2

--- a/solution.py
+++ b/solution.py
@@ -1,3 +1,4 @@
+import functools
 import jax
 import jax.numpy as jnp
 from jax import lax
@@ -7,69 +8,100 @@
 
 epsilon = 1e-05
 chip_cores = 2
+block = 256
 other_core = [(0, 1), (1, 0)]
 near_chip = [(0, 1), (1, 0), (2, 3), (3, 2)]
 cross_chip = [(0, 3), (3, 0), (1, 2), (2, 1)]
 
 
-def ffn_kernel(core_ref, arrived, across, *refs):
-    joined, downs, (keep, give, hidden) = refs[:4], refs[4:8], refs[8:]
+def pick_kernel(kind_ref, gate, up, down, own, other, sems):
+    depth, unit = gate.shape[1:]
+    copies = []
+    for turn, packed in enumerate((own, other)):
+        at = kind_ref[0] if turn == 0 else 1 - kind_ref[0]
+        pairs = [
+            (gate.at[at], packed.at[pl.ds(0, depth), pl.ds(0, unit)]),
+            (up.at[at], packed.at[pl.ds(0, depth), pl.ds(unit, unit)]),
+        ]
+        for j in range(depth // block):
+            rows = pl.ds(depth + j * unit, unit)
+            pairs.append((down.at[at, :, pl.ds(j * block, block)], packed.at[rows, :]))
+        for source, target in pairs:
+            copies.append(pltpu.make_async_copy(source, target, sems.at[len(copies)]))
+    for copy in copies:
+        copy.start()
+    for copy in copies:
+        copy.wait()
+
+
+def pick_shards(kind, gate, up, down):
+    anywhere = pl.BlockSpec(memory_space=pl.ANY)
+    depth, unit = gate.shape[1:]
+    packed = jax.ShapeDtypeStruct((depth + depth // block * unit, block), gate.dtype)
+    return pl.pallas_call(
+        pick_kernel,
+        out_shape=(packed, packed),
+        in_specs=[pl.BlockSpec(memory_space=pltpu.SMEM)] + [anywhere] * 3,
+        out_specs=(anywhere,) * 2,
+        scratch_shapes=[pltpu.SemaphoreType.DMA((2 * (2 + depth // block),))],
+        cost_estimate=pl.CostEstimate(flops=0, bytes_accessed=12 * 2**20, transcendentals=0),
+    )(kind.reshape(1).astype(jnp.int32), gate, up, down)
+
+
+def ffn_kernel(count, core_ref, arrived, across, *refs):
+    shards, added, (keep, give, hidden) = refs[:count], refs[count:-3], refs[-3:]
     core = core_ref[0]
     f32 = jnp.float32
     rows, held = arrived.shape
-    block = 256
-    unit = downs[0].shape[0]
+    depth = 2 * held
+    unit = block // 2
 
     def at(j, parity):
         return pl.ds(pl.multiple_of((2 * j + parity) * block, block), block)
 
-    for k in range(4):
-        both = jnp.zeros((rows, 2 * unit), f32)
+    def down_at(j, parity):
+        return pl.ds(pl.multiple_of(depth + (2 * j + parity) * unit, unit), unit)
+
+    for k, shard in enumerate(shards):
+        both = jnp.zeros((rows, block), f32)
         for j in range(held // block):
             lanes = pl.ds(j * block, block)
-            both += jnp.dot(arrived[:, lanes], joined[k][at(j, core), :], preferred_element_type=f32)
-            both += jnp.dot(
-                across[:, lanes], joined[k][at(j, 1 - core), :], preferred_element_type=f32
-            )
+            both += jnp.dot(arrived[:, lanes], shard[at(j, core), :], preferred_element_type=f32)
+            both += jnp.dot(across[:, lanes], shard[at(j, 1 - core), :], preferred_element_type=f32)
         gate_val, up_val = both[:, :unit], both[:, unit:]
         silu = gate_val / (1.0 + jnp.exp(-gate_val))
         hidden[:, pl.ds(k * unit, unit)] = (silu * up_val).astype(hidden.dtype)
-    for parity, out in ((core, keep), (1 - core, give)):
+    for which, (parity, out) in enumerate(((core, keep), (1 - core, give))):
         for j in range(held // block):
-            total = jnp.zeros((rows, block), f32)
-            for k in range(4):
+            lanes = pl.ds(j * block, block)
+            total = added[which][:, lanes] if added else jnp.zeros((rows, block), f32)
+            for k, shard in enumerate(shards):
                 total += jnp.dot(
                     hidden[:, pl.ds(k * unit, unit)],
-                    downs[k][:, at(j, parity)],
+                    shard[down_at(j, parity), :],
                     preferred_element_type=f32,
                 )
-            out[:, pl.ds(j * block, block)] = total.astype(out.dtype)
-
-
-def expert_rows(core, arrived, across, shards):
+            out[:, lanes] = total.astype(out.dtype)
+
+
+def expert_rows(core, arrived, across, shards, added, give_type):
     rows, held = arrived.shape
-    unit, width = shards[0][1].shape
+    unit, width, count = block // 2, 2 * held, len(shards)
     whole = pl.BlockSpec(memory_space=pltpu.VMEM)
     return pl.pallas_call(
-        ffn_kernel,
+        functools.partial(ffn_kernel, count),
         out_shape=(
             jax.ShapeDtypeStruct((rows, held), jnp.float32),
-            jax.ShapeDtypeStruct((rows, held), jnp.bfloat16),
+            jax.ShapeDtypeStruct((rows, held), give_type),
         ),
-        in_specs=[pl.BlockSpec(memory_space=pltpu.SMEM)] + [whole] * 10,
+        in_specs=[pl.BlockSpec(memory_space=pltpu.SMEM)] + [whole] * (2 + count + len(added)),
         out_specs=(whole, whole),
-        scratch_shapes=[pltpu.VMEM((rows, 4 * unit), jnp.bfloat16)],
+        scratch_shapes=[pltpu.VMEM((rows, count * unit), jnp.bfloat16)],
         compiler_params=pltpu.CompilerParams(vmem_limit_bytes=40 * 2**20),
         cost_estimate=pl.CostEstimate(
-            flops=2 * rows * width * 4 * unit * 3, bytes_accessed=12 * 2**20, transcendentals=0
+            flops=2 * rows * width * unit, bytes_accessed=2**20, transcendentals=0
         ),
-    )(
-        core.reshape(1).astype(jnp.int32),
-        arrived,
-        across,
-        *[one[0] for one in shards],
-        *[one[1] for one in shards],
-    )
+    )(core.reshape(1).astype(jnp.int32), arrived, across, *shards, *added)
 
 
 def on_device(tokens, norm_gain, router_logits, routes, gate_proj, up_proj, down_proj):
@@ -87,21 +119,13 @@
     kind = row // local_experts
     half = row % local_experts
 
-    def pick(at):
-        joined = jnp.concatenate([gate_proj, up_proj], axis=2)
-        return (
-            lax.dynamic_index_in_dim(joined, at, 0, keepdims=False),
-            lax.dynamic_index_in_dim(down_proj, at, 0, keepdims=False),
-        )
-
-    def send(arrays, pairs):
-        return tuple(lax.ppermute(one, "x", pairs) for one in arrays)
-
-    own = pick(kind)
-    crossed = send(pick(1 - kind), cross_chip)
-    near = send(own, near_chip)
-    relayed = send(crossed, near_chip)
-    shards = (own, near, crossed, relayed)
+    own, other = pick_shards(kind, gate_proj, up_proj, down_proj)
+    tokens, own, other = lax.optimization_barrier((tokens, own, other))
+
+    crossed = lax.ppermute(other, "x", cross_chip)
+    near = lax.ppermute(own, "x", near_chip)
+    crossed, near = lax.optimization_barrier((crossed, near))
+    relayed = lax.ppermute(crossed, "x", near_chip)
 
     expert_iota = jnp.arange(expert_count, dtype=jnp.int32)
     hits = jnp.any(routes[:, :, None] == expert_iota[None, None, :], axis=1)
@@ -142,7 +166,8 @@
         outgoing.reshape(ep_count, share, -1), "ep", split_axis=0, concat_axis=0, tiled=True
     ).reshape(ep_count * share, -1)
     across = lax.ppermute(arrived, "core", other_core)
-    keep, give = expert_rows(core, arrived, across, shards)
+    added = expert_rows(core, arrived, across, (own, near, crossed), (), f32)
+    keep, give = expert_rows(core, arrived, across, (relayed,), added, bf16)
     summed = keep + lax.ppermute(give, "core", other_core).astype(f32)
     returned = lax.all_to_all(
         summed.astype(bf16).reshape(ep_count, share, -1), "ep", split_axis=0, concat_axis=0, tiled=True

time: 164 us -> 251 us (1.53)
  Pallas kernels: 6.4 us -> 106 us
  waiting for transfers between devices: 103 us -> 66 us
  blocking collectives: 13.5 us -> 44.4 us
  starting transfers between devices: 31.5 us -> 28.5 us
    pallas_call x1 -> x3, Pallas kernels: 6.4 us -> 106 us  [the longest x1 96.6 us: pick_shards(): pl.pallas_call(pick_kernel, out_shape=(packed, packed), in_specs=[pl.Bloc...]
    ppermute x6 -> x3, waiting for transfers between devices: 66.1 us -> 0.01 us  [the longest x1 0.01 us: on_device(): crossed = lax.ppermute(other, 'x', cross_chip)]
    all_gather x1, blocking collectives: 13.5 us -> 44.4 us  [on_device(): whole = lax.all_gather(stacked, ('x', 'core'), axis=0, tiled=False)]
    all_to_all x1, waiting for transfers between devices: 0.48 us -> 28.5 us  [on_device(): lax.all_to_all(outgoing.reshape(ep_count, share, -1), 'ep', split_axis=0,...]
    ppermute x1, waiting for transfers between devices: 0.01 us -> 2.66 us  [on_device(): across = lax.ppermute(arrived, 'core', other_core)]
    ppermute x6 -> x3, starting transfers between devices: 5.47 us -> 3.16 us  [the longest x1 2.85 us: on_device(): crossed = lax.ppermute(other, 'x', cross_chip)]
  transfers between devices with their start and end apart: 13 -> 10, of which waited for: 9 -> 6; matrix products, arithmetic and copies ran while one was open for 1% -> 1% of each run, Pallas kernels for 0% -> 2%
where the time goes in v3:
time: 251 us
  Pallas kernels  106 us (42%)
  waiting for transfers between devices  66 us (26%)
  blocking collectives  44.4 us (18%)
  starting transfers between devices  28.5 us (11%)
  other arithmetic  2.81 us (1%)
    pallas_call x1, Pallas kernels, pick_shards(): pl.pallas_call(pick_kernel, out_shape=(packed, packed), in_specs=[pl.Bloc...  96.6 us
    all_gather x1, blocking collectives, on_device(): whole = lax.all_gather(stacked, ('x', 'core'), axis=0, tiled=False)  44.4 us
    all_to_all x1, waiting for transfers between devices, on_device(): lax.all_to_all(outgoing.reshape(ep_count, share, -1), 'ep', split_axis=0,...  28.5 us
    all_to_all x1, waiting for transfers between devices, on_device(): lax.all_to_all(summed.astype(bf16).reshape(ep_count, share, -1), 'ep', sp...  28 us
    all_to_all x1, starting transfers between devices, on_device(): lax.all_to_all(outgoing.reshape(ep_count, share, -1), 'ep', split_axis=0,...  11.7 us
    pallas_call x2, Pallas kernels, expert_rows(): pl.pallas_call(functools.partial(ffn_kernel, count), out_shape=(jax.Shape...  9.73 us
    all_to_all x1, starting transfers between devices, on_device(): lax.all_to_all(summed.astype(bf16).reshape(ep_count, share, -1), 'ep', sp...  9.21 us
  transfers between devices with their start and end apart: 10, of which 6 were waited for; matrix products, arithmetic and copies ran while one was open for 1% of the time, Pallas kernels for 2%

profile of v3, /device:TPU:8, one launch (start us, length us, event | category | flops | bytes accessed | tf_op | source)
XLA Modules:
  0.0 250.6 jit_solution(17588806766253824302)
XLA Ops:
  0.0 0.0 copy-start.2
  0.0 0.0 copy-start.4
  0.0 96.6 %shard_map.73 = (bf16[3072,256]{1,0:T(8,128)(2,1)}, bf16[3072,256]{1,0:T(8,128)(2,1)}) custom-call(s32[1]{0:T(128)} %bitcast.10.kind_ref, bf16[2,2048,128]{2,1,0:T(8,128)(2,1)} %gate.1, bf16[2,2048,128]{2,1,0:T(8,128)(2,1)} %up.1, bf16[2,128,2048]{2,1,0:T(8,128)(2,1)} %down.1), custom_call_target="tpu_custom_call" | custom-call | bytes 12582912 | tf_op jit(solution)/shard_map/pallas_call | solution.py:41
  96.6 0.0 copy-start.3
  96.6 2.8 %collective-permute-start.1 = (bf16[3072,256]{1,0:T(8,128)(2,1)}, bf16[3072,256]{1,0:T(8,128)(2,1)}, u32[]{:S(2)}, u32[]{:S(2)}) collective-permute-start(bf16[3072,256]{1,0:T(8,128)(2,1)} %get-tuple-element.19), channel_id=1, source_target_pairs={{0,6},{6,0},{2,4},{4,2},{1,7},{7,1},{3,5},{5,3},{8,14},{14,8},{10,... | collective-permute-start | bytes 4718600 | tf_op jit(solution)/shard_map/ppermute | solution.py:125
  99.4 0.2 collective-permute-start.2
  99.7 0.0 copy-done.4
  99.7 0.0 copy-done.2
  99.7 44.4 %all-gather = bf16[1152,256]{1,0:T(8,128)(2,1)S(1)} all-gather(bf16[144,256]{1,0:T(8,128)(2,1)S(1)} %pad_maximum_fusion), channel_id=2, replica_groups=mesh['ep'=32,'x'=4,'core'=2] {'x','core'}, dimensions={0}, use_global_device_ids=true | all-gather | bytes 663552 | tf_op jit(solution)/shard_map/all_gather | solution.py:148
  144.1 0.2 multiply_reduce_fusion
  144.3 0.1 multiply_convert_fusion
  144.4 0.0 copy-start
  144.5 0.0 copy-done.3
  144.6 0.1 eq.64
  144.7 0.2 fusion.15
  145.0 0.1 bitcast_compare_fusion
  145.1 1.4 convolution_convert_fusion
  146.5 11.7 %all-to-all-start = ((bf16[32,16,1024]{2,1,0:T(8,128)(2,1)}), bf16[32,16,1024]{2,1,0:T(8,128)(2,1)S(1)}, u32[]{:S(2)}, u32[]{:S(2)}) async-start(bf16[32,16,1024]{2,1,0:T(8,128)(2,1)} %bitcast.54), calls=%async_computation | async-start | bytes 2097152 | tf_op jit(solution)/shard_map/all_to_all | solution.py:165
  158.2 0.0 collective-permute-done.1.refs_2_
  158.2 0.0 collective-permute-done.2.refs_1_
  158.2 0.1 collective-permute-start.3
  158.3 28.5 %all-to-all-done = bf16[32,16,1024]{2,1,0:T(8,128)(2,1)S(1)} async-done(((bf16[32,16,1024]{2,1,0:T(8,128)(2,1)}), bf16[32,16,1024]{2,1,0:T(8,128)(2,1)S(1)}, u32[]{:S(2)}, u32[]{:S(2)}) %all-to-all-start) | async-done | bytes 1048608 | tf_op jit(solution)/shard_map/all_to_all | solution.py:165
  186.8 0.0 collective-permute-start
  186.8 2.7 %collective-permute-done.across = bf16[512,1024]{1,0:T(8,128)(2,1)S(1)} collective-permute-done((bf16[512,1024]{1,0:T(8,128)(2,1)S(1)}, bf16[512,1024]{1,0:T(8,128)(2,1)S(1)}, u32[]{:S(2)}, u32[]{:S(2)}) %collective-permute-start) | collective-permute-done | bytes 1048608 | tf_op jit(solution)/shard_map/ppermute | solution.py:168
  189.5 0.0 copy-done
  189.5 5.9 %shard_map.74 = (f32[512,1024]{1,0:T(8,128)S(1)}, f32[512,1024]{1,0:T(8,128)S(1)}) custom-call(s32[1]{0:T(128)} %bitcast.7.core_ref, bf16[512,1024]{1,0:T(8,128)(2,1)S(1)} %bitcast.51, bf16[512,1024]{1,0:T(8,128)(2,1)S(1)} %collective-permute-done.across, bf16[3072,256]{1,0:T(8,128)(2,1)S(1)} %copy-done, bf16[3072,256]{1,0:T(8,128)(2,1)} %collective-permute-done.2.refs_1_, ...), custom_call_target="tpu_custom_call" | custom-call | flops 268435456 | bytes 1048576 | tf_op jit(solution)/shard_map/pallas_call | solution.py:91
  195.4 0.0 collective-permute-done.3.refs_0_
  195.4 3.8 %shard_map.75 = (f32[512,1024]{1,0:T(8,128)S(1)}, bf16[512,1024]{1,0:T(8,128)(2,1)S(1)}) custom-call(s32[1]{0:T(128)} %bitcast.7.core_ref, bf16[512,1024]{1,0:T(8,128)(2,1)S(1)} %bitcast.52, bf16[512,1024]{1,0:T(8,128)(2,1)S(1)} %collective-permute-done.across, bf16[3072,256]{1,0:T(8,128)(2,1)} %collective-permute-done.3.refs_0_, ...), custom_call_target="tpu_custom_call" | custom-call | flops 268435456 | bytes 1048576 | tf_op jit(solution)/shard_map/pallas_call | solution.py:91
  199.2 0.2 collective-permute-start.4
  199.4 2.5 %collective-permute-done.4 = bf16[512,1024]{1,0:T(8,128)(2,1)S(1)} collective-permute-done((bf16[512,1024]{1,0:T(8,128)(2,1)S(1)}, bf16[512,1024]{1,0:T(8,128)(2,1)S(1)}, u32[]{:S(2)}, u32[]{:S(2)}) %collective-permute-start.4) | collective-permute-done | bytes 1048608 | tf_op jit(solution)/shard_map/ppermute | solution.py:171
  202.0 1.3 add_convert_fusion
  203.3 0.0 copy-start.1
  203.3 9.2 %all-to-all-start.1 = ((bf16[32,16,1024]{2,1,0:T(8,128)(2,1)}), bf16[32,16,1024]{2,1,0:T(8,128)(2,1)S(1)}, u32[]{:S(2)}, u32[]{:S(2)}) async-start(bf16[32,16,1024]{2,1,0:T(8,128)(2,1)} %bitcast.20), calls=%async_computation.1 | async-start | bytes 2097152 | tf_op jit(solution)/shard_map/all_to_all | solution.py:172
  212.5 0.0 copy-done.1
  212.7 0.1 reduce-precision_convert_fusion
  212.8 28.0 %all-to-all-done.1 = bf16[32,16,1024]{2,1,0:T(8,128)(2,1)S(1)} async-done(((bf16[32,16,1024]{2,1,0:T(8,128)(2,1)}), bf16[32,16,1024]{2,1,0:T(8,128)(2,1)S(1)}, u32[]{:S(2)}, u32[]{:S(2)}) %all-to-all-start.1) | async-done | bytes 1048608 | tf_op jit(solution)/shard_map/all_to_all | solution.py:172
  240.9 0.5 fusion.1
  241.3 0.1 slice_add_fusion
  241.4 0.4 collective-permute-start.5
  241.8 2.3 collective-permute-start.6
  244.1 1.5 collective-permute-start.7
  245.6 3.5 %collective-permute-done.5 = f32[128,256]{1,0:T(8,128)S(1)} collective-permute-done((f32[128,256]{1,0:T(8,128)S(1)}, f32[128,256]{1,0:T(8,128)S(1)}, u32[]{:S(2)}, u32[]{:S(2)}) %collective-permute-start.5) | collective-permute-done | bytes 131104 | tf_op jit(solution)/shard_map/ppermute | solution.py:189
  249.1 0.0 collective-permute-done.6
  249.1 0.9 collective-permute-done.7
  250.0 0.7 add_convert_fusion.1
  (20 shorter events, 0.3 us)
Async XLA Ops:
  0.0 99.7 %copy-start.2 = (bf16[128,256]{1,0:T(8,128)(2,1)S(1)}, bf16[128,256]{1,0:T(8,128)(2,1)}, u32[]{:S(2)}) copy-start(bf16[128,256]{1,0:T(8,128)(2,1)} %param.7) | copy-start | bytes 196612
  0.0 99.7 %copy-start.4 = (bf16[256]{0:T(256)(128)(2,1)S(1)}, bf16[256]{0:T(256)(128)(2,1)}, u32[]{:S(2)}) copy-start(bf16[256]{0:T(256)(128)(2,1)} %param.8) | copy-start | bytes 1540
  96.6 47.9 %copy-start.3 = (s32[128,8]{0,1:T(8,128)S(1)}, s32[128,8]{0,1:T(8,128)}, u32[]{:S(2)}) copy-start(s32[128,8]{0,1:T(8,128)} %param.10) | copy-start | bytes 12292
  96.6 61.6 %collective-permute-start.1 = (bf16[3072,256]{1,0:T(8,128)(2,1)}, bf16[3072,256]{1,0:T(8,128)(2,1)}, u32[]{:S(2)}, u32[]{:S(2)}) collective-permute-start(bf16[3072,256]{1,0:T(8,128)(2,1)} %get-tuple-element.19), channel_id=1, source_target_pairs={{0,6},{6,0},{2,4},{4,2},{1,7},{7,1},{3,5},{5,3},{8,14},{14,8},{10,... | collective-permute-start | bytes 4718600 | tf_op jit(solution)/shard_map/ppermute | solution.py:125
  99.4 58.8 %collective-permute-start.2 = (bf16[3072,256]{1,0:T(8,128)(2,1)}, bf16[3072,256]{1,0:T(8,128)(2,1)}, u32[]{:S(2)}, u32[]{:S(2)}) collective-permute-start(bf16[3072,256]{1,0:T(8,128)(2,1)} %get-tuple-element.20.refs_0_), channel_id=1, source_target_pairs={{0,2},{2,0},{4,6},{6,4},{1,3},{3,1},{5,7},{7,5},{8,10},{10,8},{12,... | collective-permute-start | bytes 4718600 | tf_op jit(solution)/shard_map/ppermute | solution.py:126
  144.4 45.0 %copy-start = (bf16[3072,256]{1,0:T(8,128)(2,1)S(1)}, bf16[3072,256]{1,0:T(8,128)(2,1)}, u32[]{:S(2)}) copy-start(bf16[3072,256]{1,0:T(8,128)(2,1)} %get-tuple-element.20.refs_0_) | copy-start | bytes 4718596
  146.5 40.3 %all-to-all-start = ((bf16[32,16,1024]{2,1,0:T(8,128)(2,1)}), bf16[32,16,1024]{2,1,0:T(8,128)(2,1)S(1)}, u32[]{:S(2)}, u32[]{:S(2)}) async-start(bf16[32,16,1024]{2,1,0:T(8,128)(2,1)} %bitcast.54), calls=%async_computation | async-start | bytes 2097152 | tf_op jit(solution)/shard_map/all_to_all | solution.py:165
  158.2 37.2 %collective-permute-start.3 = (bf16[3072,256]{1,0:T(8,128)(2,1)}, bf16[3072,256]{1,0:T(8,128)(2,1)}, u32[]{:S(2)}, u32[]{:S(2)}) collective-permute-start(bf16[3072,256]{1,0:T(8,128)(2,1)} %collective-permute-done.1.refs_2_), channel_id=1, source_target_pairs={{0,2},{2,0},{4,6},{6,4},{1,3},{3,1},{5,7},{7,5},{8,10},{10,8},{12,... | collective-permute-start | bytes 4718600 | tf_op jit(solution)/shard_map/ppermute | solution.py:128
  186.8 2.7 %collective-permute-start = (bf16[512,1024]{1,0:T(8,128)(2,1)S(1)}, bf16[512,1024]{1,0:T(8,128)(2,1)S(1)}, u32[]{:S(2)}, u32[]{:S(2)}) collective-permute-start(bf16[512,1024]{1,0:T(8,128)(2,1)S(1)} %bitcast.50), channel_id=1, source_target_pairs={{0,1},{1,0},{2,3},{3,2},{4,5},{5,4},{6,7},{7,6},{8,9},{9,8},{10,11... | collective-permute-start | bytes 3145736 | tf_op jit(solution)/shard_map/ppermute | solution.py:168
  199.2 2.7 %collective-permute-start.4 = (bf16[512,1024]{1,0:T(8,128)(2,1)S(1)}, bf16[512,1024]{1,0:T(8,128)(2,1)S(1)}, u32[]{:S(2)}, u32[]{:S(2)}) collective-permute-start(bf16[512,1024]{1,0:T(8,128)(2,1)S(1)} %get-tuple-element.26), channel_id=1, source_target_pairs={{0,1},{1,0},{2,3},{3,2},{4,5},{5,4},{6,7},{7,6},{8,9},{9,8},{10,11... | collective-permute-start | bytes 3145736 | tf_op jit(solution)/shard_map/ppermute | solution.py:171
  203.3 9.3 %copy-start.1 = (f32[128,64]{0,1:T(8,128)S(1)}, f32[128,64]{0,1:T(8,128)}, u32[]{:S(2)}) copy-start(f32[128,64]{0,1:T(8,128)} %param.9) | copy-start | bytes 98308
  203.3 37.6 %all-to-all-start.1 = ((bf16[32,16,1024]{2,1,0:T(8,128)(2,1)}), bf16[32,16,1024]{2,1,0:T(8,128)(2,1)S(1)}, u32[]{:S(2)}, u32[]{:S(2)}) async-start(bf16[32,16,1024]{2,1,0:T(8,128)(2,1)} %bitcast.20), calls=%async_computation.1 | async-start | bytes 2097152 | tf_op jit(solution)/shard_map/all_to_all | solution.py:172
  241.4 7.7 %collective-permute-start.5 = (f32[128,256]{1,0:T(8,128)S(1)}, f32[128,256]{1,0:T(8,128)S(1)}, u32[]{:S(2)}, u32[]{:S(2)}) collective-permute-start(f32[128,256]{1,0:T(8,128)S(1)} %get-tuple-element.27), channel_id=1, source_target_pairs={{0,2},{2,4},{4,6},{6,0},{1,3},{3,5},{5,7},{7,1},{8,10},{10,12},{12... | collective-permute-start | bytes 393224 | tf_op jit(solution)/shard_map/ppermute | solution.py:189
  241.8 7.3 %collective-permute-start.6 = (f32[128,256]{1,0:T(8,128)S(1)}, f32[128,256]{1,0:T(8,128)S(1)}, u32[]{:S(2)}, u32[]{:S(2)}) collective-permute-start(f32[128,256]{1,0:T(8,128)S(1)} %get-tuple-element.29), channel_id=1, source_target_pairs={{0,4},{2,6},{4,0},{6,2},{1,5},{3,7},{5,1},{7,3},{8,12},{10,14},{12... | collective-permute-start | bytes 393224 | tf_op jit(solution)/shard_map/ppermute | solution.py:189
  244.1 5.9 %collective-permute-start.7 = (f32[128,256]{1,0:T(8,128)S(1)}, f32[128,256]{1,0:T(8,128)S(1)}, u32[]{:S(2)}, u32[]{:S(2)}) collective-permute-start(f32[128,256]{1,0:T(8,128)S(1)} %get-tuple-element.28), channel_id=1, source_target_pairs={{0,6},{2,0},{4,2},{6,4},{1,7},{3,1},{5,3},{7,5},{8,14},{10,8},{12,... | collective-permute-start | bytes 393224 | tf_op jit(solution)/shard_map/ppermute | solution.py:189

commit v4 on v3

v4 whole, which is shorter than its diff:
```python
import functools
import jax
import jax.numpy as jnp
from jax import lax
from jax.experimental import pallas as pl
from jax.experimental.pallas import tpu as pltpu
from jax.sharding import Mesh, PartitionSpec as P

epsilon = 1e-05
chip_cores = 2
block = 256
other_core = [(0, 1), (1, 0)]
near_chip = [(0, 1), (1, 0), (2, 3), (3, 2)]
cross_chip = [(0, 3), (3, 0), (1, 2), (2, 1)]


def pick_kernel(kind_ref, *refs):
    unit = refs[0].shape[2]
    for turn, packed in enumerate(refs[6:]):
        gate, up, down = refs[3 * turn : 3 * turn + 3]
        for j in range(packed.shape[0]):
            packed[j, :block, :unit] = gate[0, j * block : (j + 1) * block, :]
            packed[j, :block, unit:] = up[0, j * block : (j + 1) * block, :]
            packed[j, block:, :] = down[0, :, j * block : (j + 1) * block]


def pick_shards(kind, gate, up, down):
    depth, unit = gate.shape[1:]
    steps = 4
    each = depth // steps

    def specs(turn):
        def at(kind_ref):
            return kind_ref[0] if turn == 0 else 1 - kind_ref[0]

        tall = pl.BlockSpec((1, each, unit), lambda i, kind_ref: (at(kind_ref), i, 0))
        return [
            tall,
            tall,
            pl.BlockSpec((1, unit, each), lambda i, kind_ref: (at(kind_ref), 0, i)),
        ]

    packed = (depth // block, block + unit, block)
    out = pl.BlockSpec((each // block, *packed[1:]), lambda i, kind_ref: (i, 0, 0))
    return pl.pallas_call(
        pick_kernel,
        out_shape=(jax.ShapeDtypeStruct(packed, gate.dtype),) * 2,
        grid_spec=pltpu.PrefetchScalarGridSpec(
            num_scalar_prefetch=1, grid=(steps,), in_specs=specs(0) + specs(1), out_specs=(out, out)
        ),
        cost_estimate=pl.CostEstimate(flops=0, bytes_accessed=6 * 2**20, transcendentals=0),
    )(kind.reshape(1).astype(jnp.int32), gate, up, down, gate, up, down)


def ffn_kernel(count, place_ref, arrived, across, *refs):
    shards, added, (keep, give, hidden) = refs[:count], refs[count:-3], refs[-3:]
    row, core = place_ref[0], place_ref[1]
    f32 = jnp.float32
    rows, held = arrived.shape
    ring = held // block
    unit = block // 2

    def source(j, parity):
        return 2 * lax.rem(row - j + ring, ring) + parity

    def target(j, parity):
        return 2 * lax.rem(row + j, ring) + parity

    for k, shard in enumerate(shards):
        both = jnp.zeros((rows, block), f32)
        for j in range(ring):
            lanes = pl.ds(j * block, block)
            for part, parity in ((arrived, core), (across, 1 - core)):
                both += jnp.dot(
                    part[:, lanes], shard[source(j, parity), :block, :], preferred_element_type=f32
                )
        gate_val, up_val = both[:, :unit], both[:, unit:]
        silu = gate_val / (1.0 + jnp.exp(-gate_val))
        hidden[:, pl.ds(k * unit, unit)] = (silu * up_val).astype(hidden.dtype)
    for which, (parity, out) in enumerate(((core, keep), (1 - core, give))):
        for j in range(ring):
            lanes = pl.ds(j * block, block)
            total = added[which][:, lanes] if added else jnp.zeros((rows, block), f32)
            for k, shard in enumerate(shards):
                total += jnp.dot(
                    hidden[:, pl.ds(k * unit, unit)],
                    shard[target(j, parity), block:, :],
                    preferred_element_type=f32,
                )
            out[:, lanes] = total.astype(out.dtype)


def expert_rows(place, arrived, across, shards, added, give_type):
    rows, held = arrived.shape
    unit, width, count = block // 2, 2 * held, len(shards)
    whole = pl.BlockSpec(memory_space=pltpu.VMEM)
    return pl.pallas_call(
        functools.partial(ffn_kernel, count),
        out_shape=(
            jax.ShapeDtypeStruct((rows, held), jnp.float32),
            jax.ShapeDtypeStruct((rows, held), give_type),
        ),
        in_specs=[pl.BlockSpec(memory_space=pltpu.SMEM)] + [whole] * (2 + count + len(added)),
        out_specs=(whole, whole),
        scratch_shapes=[pltpu.VMEM((rows, count * unit), jnp.bfloat16)],
        compiler_params=pltpu.CompilerParams(vmem_limit_bytes=40 * 2**20),
        cost_estimate=pl.CostEstimate(
            flops=2 * rows * width * unit, bytes_accessed=2**20, transcendentals=0
        ),
    )(place, arrived, across, *shards, *added)


def on_device(tokens, norm_gain, router_logits, routes, gate_proj, up_proj, down_proj):
    bf16, f32 = jnp.bfloat16, jnp.float32
    ep_count = lax.axis_size("ep")
    row_count = lax.axis_size("x")
    group_size, width = tokens.shape
    local_experts = gate_proj.shape[0]
    top_count = routes.shape[1]
    expert_count = local_experts * ep_count
    capacity = 2 * group_size * top_count // expert_count
    share = capacity // (row_count // local_experts)
    core = lax.axis_index("core")
    row = lax.axis_index("x")
    kind = row // local_experts
    half = row % local_experts

    place = jnp.stack([row, core]).astype(jnp.int32)

    def ring_send(one, step):
        pairs = [(at, (at + step) % row_count) for at in range(row_count)]
        return lax.ppermute(one, "x", pairs)

    stacked = jnp.concatenate([tokens, jnp.broadcast_to(norm_gain[None, :], (16, width))], axis=0)
    parts = [stacked] + [ring_send(stacked, step) for step in range(1, row_count)]

    own, other = pick_shards(kind, gate_proj, up_proj, down_proj)
    parts, own, other = lax.optimization_barrier((parts, own, other))
    crossed = lax.ppermute(other, "x", cross_chip)
    near = lax.ppermute(own, "x", near_chip)
    crossed, near = lax.optimization_barrier((crossed, near))
    relayed = lax.ppermute(crossed, "x", near_chip)

    expert_iota = jnp.arange(expert_count, dtype=jnp.int32)
    hits = jnp.any(routes[:, :, None] == expert_iota[None, None, :], axis=1)
    earlier = jnp.tril(jnp.ones((group_size, group_size), bf16), -1)
    position = jnp.dot(earlier, hits.astype(bf16), preferred_element_type=f32)
    shifted = jnp.where(hits, router_logits, -jnp.inf)
    shifted = jnp.exp(shifted - jnp.max(shifted, axis=1, keepdims=True))
    gates = shifted / jnp.sum(shifted, axis=1, keepdims=True)

    def of_kind(table):
        return lax.dynamic_index_in_dim(
            table.reshape(group_size, ep_count, local_experts), kind, 2, keepdims=False
        )

    slot = jnp.where(of_kind(hits), of_kind(position), -1.0)
    gates = of_kind(gates)
    slot_iota = (jnp.arange(share, dtype=jnp.int32) + half * share).astype(f32)

    floated = [part[:group_size].astype(f32) for part in parts]
    squares = sum(jnp.sum(one * one, axis=1) for one in floated)[None, :]
    squares = squares + lax.ppermute(squares, "core", other_core)
    scale = lax.rsqrt(squares[0] / (width * row_count * chip_cores) + epsilon)[:, None]
    normed = jnp.concatenate(
        [
            (one * scale * part[group_size : group_size + 1].astype(f32)).astype(bf16)
            for one, part in zip(floated, parts)
        ],
        axis=1,
    )

    table = (slot.T[:, None, :] == slot_iota[None, :, None]).astype(bf16)
    outgoing = jnp.dot(
        table.reshape(ep_count * share, group_size), normed, preferred_element_type=f32
    ).astype(bf16)
    arrived = lax.all_to_all(
        outgoing.reshape(ep_count, share, -1), "ep", split_axis=0, concat_axis=0, tiled=True
    ).reshape(ep_count * share, -1)
    across = lax.ppermute(arrived, "core", other_core)
    added = expert_rows(place, arrived, across, (own, near, crossed), (), f32)
    keep, give = expert_rows(place, arrived, across, (relayed,), added, bf16)
    summed = keep + lax.ppermute(give, "core", other_core).astype(f32)
    returned = lax.all_to_all(
        summed.astype(bf16).reshape(ep_count, share, -1), "ep", split_axis=0, concat_axis=0, tiled=True
    ).reshape(ep_count * share, -1)

    weight = jnp.where(slot[:, :, None] == slot_iota[None, None, :], gates[:, :, None], 0.0)
    weight = weight.reshape(group_size, ep_count * share)
    high = lax.reduce_precision(weight, 8, 7)
    both = jnp.concatenate([high.astype(bf16), (weight - high).astype(bf16)], axis=0)
    mixed = jnp.dot(both, returned, preferred_element_type=f32)
    mixed = mixed[:group_size] + mixed[group_size:]

    result = mixed[:, :width]
    for step in range(1, row_count):
        result = result + ring_send(mixed[:, step * width : (step + 1) * width], step)
    return result.astype(bf16)


def solution(mesh):
    ep_count, tp_count = mesh.devices.shape
    fine = Mesh(
        mesh.devices.reshape(ep_count, tp_count // chip_cores, chip_cores), ("ep", "x", "core")
    )
    tp = ("x", "core")
    return jax.shard_map(
        on_device,
        mesh=fine,
        in_specs=(
            P("ep", tp),
            P(tp),
            P("ep", None),
            P("ep", None),
            P("ep", None, tp),
            P("ep", None, tp),
            P("ep", tp, None),
        ),
        out_specs=P("ep", tp),
        check_vma=False,
    )
```

time: 251 us -> 148 us (0.59)
  Pallas kernels: 106 us -> 13.7 us
  blocking collectives: 44.4 us -> 0 us
  waiting for transfers between devices: 66 us -> 88.6 us
  starting transfers between devices: 28.5 us -> 33.8 us
  local copies, waits for them, and re-layouts: 0.27 us -> 4.84 us
    pallas_call x1, Pallas kernels: 96.6 us -> 4.41 us  [pick_shards(): pl.pallas_call(pick_kernel, out_shape=(jax.ShapeDtypeStruct(packed, gate....]
    all_gather x1 -> x0, blocking collectives: 44.4 us -> none  [on_device(): whole = lax.all_gather(stacked, ('x', 'core'), axis=0, tiled=False)]
    all_to_all x1, waiting for transfers between devices: 28.5 us -> 3.29 us  [on_device(): lax.all_to_all(outgoing.reshape(ep_count, share, -1), 'ep', split_axis=0,...]
    ppermute x1, waiting for transfers between devices: 0.01 us -> 24 us  [on_device(): crossed = lax.ppermute(other, 'x', cross_chip)]
    ppermute x1, waiting for transfers between devices: 0.01 us -> 22 us  [on_device(): relayed = lax.ppermute(crossed, 'x', near_chip)]
    ppermute x3 -> x7, starting transfers between devices: 4.17 us -> 9.22 us  [the longest x6 9.12 us: ring_send(): return lax.ppermute(one, 'x', pairs)]
    unnamed x11 -> x8, local copies, waits for them, and re-layouts: 0.02 us -> 3.99 us
    all_to_all x1, starting transfers between devices: 9.21 us -> 12 us  [on_device(): lax.all_to_all(summed.astype(bf16).reshape(ep_count, share, -1), 'ep', sp...]
  transfers between devices with their start and end apart: 10 -> 14, of which waited for: 6 -> 9; matrix products, arithmetic and copies ran while one was open for 1% -> 2% of each run, Pallas kernels for 2% -> 7%
where the time goes in v4:
time: 148 us
  waiting for transfers between devices  88.6 us (60%)
  starting transfers between devices  33.8 us (23%)
  Pallas kernels  13.7 us (9%)
  local copies, waits for them, and re-layouts  4.84 us (3%)
  other arithmetic  4.46 us (3%)
  matrix products  2.08 us (1%)
    all_to_all x1, waiting for transfers between devices, on_device(): lax.all_to_all(summed.astype(bf16).reshape(ep_count, share, -1), 'ep', sp...  28.1 us
    ppermute x1, waiting for transfers between devices, on_device(): crossed = lax.ppermute(other, 'x', cross_chip)  24 us
    ppermute x1, waiting for transfers between devices, on_device(): relayed = lax.ppermute(crossed, 'x', near_chip)  22 us
    all_to_all x1, starting transfers between devices, on_device(): lax.all_to_all(summed.astype(bf16).reshape(ep_count, share, -1), 'ep', sp...  12 us
    all_to_all x1, starting transfers between devices, on_device(): lax.all_to_all(outgoing.reshape(ep_count, share, -1), 'ep', split_axis=0,...  11.7 us
    pallas_call x2, Pallas kernels, expert_rows(): pl.pallas_call(functools.partial(ffn_kernel, count), out_shape=(jax.Shape...  9.3 us
    ppermute x6, starting transfers between devices, ring_send(): return lax.ppermute(one, 'x', pairs)  9.12 us
    ppermute x6, waiting for transfers between devices, ring_send(): return lax.ppermute(one, 'x', pairs)  5.76 us
  transfers between devices with their start and end apart: 14, of which 9 were waited for; matrix products, arithmetic and copies ran while one was open for 2% of the time, Pallas kernels for 7%

profile of v4, /device:TPU:8, one launch (start us, length us, event | category | flops | bytes accessed | tf_op | source)
XLA Modules:
  0.0 147.8 jit_solution(11882801477718570922)
XLA Ops:
  0.0 0.7 broadcast_in_dim.56
  0.7 0.8 pad_maximum_fusion
  1.5 1.5 %collective-permute-start = (bf16[144,256]{1,0:T(8,128)(2,1)S(1)}, bf16[144,256]{1,0:T(8,128)(2,1)S(1)}, u32[]{:S(2)}, u32[]{:S(2)}) collective-permute-start(bf16[144,256]{1,0:T(8,128)(2,1)S(1)} %pad_maximum_fusion), channel_id=1, source_target_pairs={{0,2},{2,4},{4,6},{6,0},{1,3},{3,5},{5,7},{7,1},{8,10},{10,12},{12... | collective-permute-start | bytes 221192 | tf_op jit(solution)/shard_map/ppermute | solution.py:132
  3.0 2.7 %collective-permute-start.1 = (bf16[144,256]{1,0:T(8,128)(2,1)S(1)}, bf16[144,256]{1,0:T(8,128)(2,1)S(1)}, u32[]{:S(2)}, u32[]{:S(2)}) collective-permute-start(bf16[144,256]{1,0:T(8,128)(2,1)S(1)} %pad_maximum_fusion), channel_id=1, source_target_pairs={{0,4},{2,6},{4,0},{6,2},{1,5},{3,7},{5,1},{7,3},{8,12},{10,14},{12... | collective-permute-start | bytes 221192 | tf_op jit(solution)/shard_map/ppermute | solution.py:132
  5.7 1.4 collective-permute-start.2
  7.2 0.7 fusion.12
  8.0 0.2 fusion.30
  8.2 0.1 eq.60
  8.3 0.1 bitcast_compare_fusion
  8.5 4.4 %shard_map.73 = (bf16[8,384,256]{2,1,0:T(8,128)(2,1)}, bf16[8,384,256]{2,1,0:T(8,128)(2,1)}) custom-call(s32[1]{0:T(128)} %bitcast.11.kind_ref, bf16[2,2048,128]{2,1,0:T(8,128)(2,1)} %refs_3_.1, bf16[2,2048,128]{2,1,0:T(8,128)(2,1)} %refs_4_.1, bf16[2,128,2048]{2,1,0:T(8,128)(2,1)} %refs_5_.1, bf16[2,2048,128]{2,1,0:T(8,128)(2,1)} %refs_3_.1, ...), custom_call_target="tpu_custom_call" | custom-call | bytes 6291456 | tf_op jit(solution)/shard_map/pallas_call | solution.py:45
  12.9 0.0 collective-permute-done
  12.9 0.0 collective-permute-done.1
  12.9 0.0 collective-permute-done.2
  12.9 0.1 fusion.19
  13.0 0.1 fusion.13
  13.2 0.1 collective-permute-start.3
  13.3 0.1 collective-permute-start.5
  13.4 0.7 collective-permute-start.6
  14.1 0.3 collective-permute-done.3
  14.4 0.1 fusion.15
  14.5 1.4 convolution_convert_fusion
  16.0 11.7 %all-to-all-start = ((bf16[32,16,1024]{2,1,0:T(8,128)(2,1)}), bf16[32,16,1024]{2,1,0:T(8,128)(2,1)S(1)}, u32[]{:S(2)}, u32[]{:S(2)}) async-start(bf16[32,16,1024]{2,1,0:T(8,128)(2,1)} %bitcast.48), calls=%async_computation | async-start | bytes 2097152 | tf_op jit(solution)/shard_map/all_to_all | solution.py:177
  27.7 24.0 %collective-permute-done.5.refs_2_ = bf16[8,384,256]{2,1,0:T(8,128)(2,1)} collective-permute-done((bf16[8,384,256]{2,1,0:T(8,128)(2,1)}, bf16[8,384,256]{2,1,0:T(8,128)(2,1)}, u32[]{:S(2)}, u32[]{:S(2)}) %collective-permute-start.5) | collective-permute-done | bytes 1572896 | tf_op jit(solution)/shard_map/ppermute | solution.py:139
  51.6 0.0 collective-permute-done.6.refs_1_
  51.6 0.0 copy-start.1
  51.6 1.2 copy-done.1
  52.8 0.0 collective-permute-start.7
  52.8 3.3 %all-to-all-done = bf16[32,16,1024]{2,1,0:T(8,128)(2,1)S(1)} async-done(((bf16[32,16,1024]{2,1,0:T(8,128)(2,1)}), bf16[32,16,1024]{2,1,0:T(8,128)(2,1)S(1)}, u32[]{:S(2)}, u32[]{:S(2)}) %all-to-all-start) | async-done | bytes 1048608 | tf_op jit(solution)/shard_map/all_to_all | solution.py:177
  56.1 0.0 collective-permute-start.4
  56.1 0.1 pad_add_fusion.place_ref
  56.2 2.6 %collective-permute-done.4.across = bf16[512,1024]{1,0:T(8,128)(2,1)S(1)} collective-permute-done((bf16[512,1024]{1,0:T(8,128)(2,1)S(1)}, bf16[512,1024]{1,0:T(8,128)(2,1)S(1)}, u32[]{:S(2)}, u32[]{:S(2)}) %collective-permute-start.4) | collective-permute-done | bytes 1048608 | tf_op jit(solution)/shard_map/ppermute | solution.py:180
  58.8 0.0 copy-start
  58.8 1.4 copy-done
  60.2 0.0 copy-start.2
  60.2 1.4 copy-done.2
  61.6 5.5 %shard_map.74 = (f32[512,1024]{1,0:T(8,128)S(1)}, f32[512,1024]{1,0:T(8,128)S(1)}) custom-call(s32[2]{0:T(128)S(1)} %pad_add_fusion.place_ref, bf16[512,1024]{1,0:T(8,128)(2,1)S(1)} %bitcast.45, bf16[512,1024]{1,0:T(8,128)(2,1)S(1)} %collective-permute-done.4.across, bf16[8,384,256]{2,1,0:T(8,128)(2,1)S(1)} %copy-done, bf16[8,384,256]{2,1,0:T(8,128)(2,1)S(1)} %copy-done.2, ...), custom_call_target="tpu_custom_call" | custom-call | flops 268435456 | bytes 1048576 | tf_op jit(solution)/shard_map/pallas_call | solution.py:97
  67.1 22.0 %collective-permute-done.7.refs_0_ = bf16[8,384,256]{2,1,0:T(8,128)(2,1)} collective-permute-done((bf16[8,384,256]{2,1,0:T(8,128)(2,1)}, bf16[8,384,256]{2,1,0:T(8,128)(2,1)}, u32[]{:S(2)}, u32[]{:S(2)}) %collective-permute-start.7) | collective-permute-done | bytes 1572896 | tf_op jit(solution)/shard_map/ppermute | solution.py:142
  89.1 3.8 %shard_map.75 = (f32[512,1024]{1,0:T(8,128)S(1)}, bf16[512,1024]{1,0:T(8,128)(2,1)S(1)}) custom-call(s32[2]{0:T(128)S(1)} %pad_add_fusion.place_ref, bf16[512,1024]{1,0:T(8,128)(2,1)S(1)} %bitcast.46, bf16[512,1024]{1,0:T(8,128)(2,1)S(1)} %collective-permute-done.4.across, bf16[8,384,256]{2,1,0:T(8,128)(2,1)} %collective-permute-done.7.refs_0_, ...), custom_call_target="tpu_custom_call" | custom-call | flops 268435456 | bytes 1048576 | tf_op jit(solution)/shard_map/pallas_call | solution.py:97
  92.9 0.1 collective-permute-start.8
  93.0 2.6 %collective-permute-done.8 = bf16[512,1024]{1,0:T(8,128)(2,1)S(1)} collective-permute-done((bf16[512,1024]{1,0:T(8,128)(2,1)S(1)}, bf16[512,1024]{1,0:T(8,128)(2,1)S(1)}, u32[]{:S(2)}, u32[]{:S(2)}) %collective-permute-start.8) | collective-permute-done | bytes 1048608 | tf_op jit(solution)/shard_map/ppermute | solution.py:183
  95.6 1.3 add_convert_fusion
  96.9 0.0 copy-start.3
  96.9 12.0 %all-to-all-start.1 = ((bf16[32,16,1024]{2,1,0:T(8,128)(2,1)}), bf16[32,16,1024]{2,1,0:T(8,128)(2,1)S(1)}, u32[]{:S(2)}, u32[]{:S(2)}) async-start(bf16[32,16,1024]{2,1,0:T(8,128)(2,1)} %bitcast.20), calls=%async_computation.1 | async-start | bytes 2097152 | tf_op jit(solution)/shard_map/all_to_all | solution.py:184
  109.0 0.0 copy-done.3
  109.1 0.1 reduce-precision_convert_fusion
  109.2 28.1 %all-to-all-done.1 = bf16[32,16,1024]{2,1,0:T(8,128)(2,1)S(1)} async-done(((bf16[32,16,1024]{2,1,0:T(8,128)(2,1)}), bf16[32,16,1024]{2,1,0:T(8,128)(2,1)S(1)}, u32[]{:S(2)}, u32[]{:S(2)}) %all-to-all-start.1) | async-done | bytes 1048608 | tf_op jit(solution)/shard_map/all_to_all | solution.py:184
  137.3 0.5 fusion.1
  137.8 0.1 slice_add_fusion
  137.9 1.4 collective-permute-start.10
  139.3 1.6 %collective-permute-start.11 = (f32[128,256]{1,0:T(8,128)S(1)}, f32[128,256]{1,0:T(8,128)S(1)}, u32[]{:S(2)}, u32[]{:S(2)}) collective-permute-start(f32[128,256]{1,0:T(8,128)S(1)} %get-tuple-element.34), channel_id=1, source_target_pairs={{0,6},{2,0},{4,2},{6,4},{1,7},{3,1},{5,3},{7,5},{8,14},{10,8},{12,... | collective-permute-start | bytes 393224 | tf_op jit(solution)/shard_map/ppermute | solution.py:132
  140.9 0.4 collective-permute-start.9
  141.4 3.2 %collective-permute-done.10 = f32[128,256]{1,0:T(8,128)S(1)} collective-permute-done((f32[128,256]{1,0:T(8,128)S(1)}, f32[128,256]{1,0:T(8,128)S(1)}, u32[]{:S(2)}, u32[]{:S(2)}) %collective-permute-start.10) | collective-permute-done | bytes 131104 | tf_op jit(solution)/shard_map/ppermute | solution.py:132
  144.6 0.0 collective-permute-done.11
  144.6 2.6 %collective-permute-done.9 = f32[128,256]{1,0:T(8,128)S(1)} collective-permute-done((f32[128,256]{1,0:T(8,128)S(1)}, f32[128,256]{1,0:T(8,128)S(1)}, u32[]{:S(2)}, u32[]{:S(2)}) %collective-permute-start.9) | collective-permute-done | bytes 131104 | tf_op jit(solution)/shard_map/ppermute | solution.py:132
  147.1 0.7 fusion.27
  (16 shorter events, 0.2 us)
Async XLA Ops:
  1.5 11.4 %collective-permute-start = (bf16[144,256]{1,0:T(8,128)(2,1)S(1)}, bf16[144,256]{1,0:T(8,128)(2,1)S(1)}, u32[]{:S(2)}, u32[]{:S(2)}) collective-permute-start(bf16[144,256]{1,0:T(8,128)(2,1)S(1)} %pad_maximum_fusion), channel_id=1, source_target_pairs={{0,2},{2,4},{4,6},{6,0},{1,3},{3,5},{5,7},{7,1},{8,10},{10,12},{12... | collective-permute-start | bytes 221192 | tf_op jit(solution)/shard_map/ppermute | solution.py:132
  3.0 9.9 %collective-permute-start.1 = (bf16[144,256]{1,0:T(8,128)(2,1)S(1)}, bf16[144,256]{1,0:T(8,128)(2,1)S(1)}, u32[]{:S(2)}, u32[]{:S(2)}) collective-permute-start(bf16[144,256]{1,0:T(8,128)(2,1)S(1)} %pad_maximum_fusion), channel_id=1, source_target_pairs={{0,4},{2,6},{4,0},{6,2},{1,5},{3,7},{5,1},{7,3},{8,12},{10,14},{12... | collective-permute-start | bytes 221192 | tf_op jit(solution)/shard_map/ppermute | solution.py:132
  5.7 7.2 %collective-permute-start.2 = (bf16[144,256]{1,0:T(8,128)(2,1)S(1)}, bf16[144,256]{1,0:T(8,128)(2,1)S(1)}, u32[]{:S(2)}, u32[]{:S(2)}) collective-permute-start(bf16[144,256]{1,0:T(8,128)(2,1)S(1)} %pad_maximum_fusion), channel_id=1, source_target_pairs={{0,6},{2,0},{4,2},{6,4},{1,7},{3,1},{5,3},{7,5},{8,14},{10,8},{12,... | collective-permute-start | bytes 221192 | tf_op jit(solution)/shard_map/ppermute | solution.py:132
  13.2 1.2 collective-permute-start.3
  13.3 38.3 %collective-permute-start.5 = (bf16[8,384,256]{2,1,0:T(8,128)(2,1)}, bf16[8,384,256]{2,1,0:T(8,128)(2,1)}, u32[]{:S(2)}, u32[]{:S(2)}) collective-permute-start(bf16[8,384,256]{2,1,0:T(8,128)(2,1)} %get-tuple-element.25), channel_id=1, source_target_pairs={{0,6},{6,0},{2,4},{4,2},{1,7},{7,1},{3,5},{5,3},{8,14},{14,8},{10,... | collective-permute-start | bytes 4718600 | tf_op jit(solution)/shard_map/ppermute | solution.py:139
  13.4 38.2 %collective-permute-start.6 = (bf16[8,384,256]{2,1,0:T(8,128)(2,1)}, bf16[8,384,256]{2,1,0:T(8,128)(2,1)S(1)}, u32[]{:S(2)}, u32[]{:S(2)}) collective-permute-start(bf16[8,384,256]{2,1,0:T(8,128)(2,1)} %get-tuple-element.26.refs_0_), channel_id=1, source_target_pairs={{0,2},{2,0},{4,6},{6,4},{1,3},{3,1},{5,7},{7,5},{8,10},{10,8},{12,... | collective-permute-start | bytes 4718600 | tf_op jit(solution)/shard_map/ppermute | solution.py:140
  16.0 40.1 %all-to-all-start = ((bf16[32,16,1024]{2,1,0:T(8,128)(2,1)}), bf16[32,16,1024]{2,1,0:T(8,128)(2,1)S(1)}, u32[]{:S(2)}, u32[]{:S(2)}) async-start(bf16[32,16,1024]{2,1,0:T(8,128)(2,1)} %bitcast.48), calls=%async_computation | async-start | bytes 2097152 | tf_op jit(solution)/shard_map/all_to_all | solution.py:177
  51.6 1.2 copy-start.1
  52.8 36.3 %collective-permute-start.7 = (bf16[8,384,256]{2,1,0:T(8,128)(2,1)}, bf16[8,384,256]{2,1,0:T(8,128)(2,1)}, u32[]{:S(2)}, u32[]{:S(2)}) collective-permute-start(bf16[8,384,256]{2,1,0:T(8,128)(2,1)} %collective-permute-done.5.refs_2_), channel_id=1, source_target_pairs={{0,2},{2,0},{4,6},{6,4},{1,3},{3,1},{5,7},{7,5},{8,10},{10,8},{12,... | collective-permute-start | bytes 4718600 | tf_op jit(solution)/shard_map/ppermute | solution.py:142
  56.1 2.7 %collective-permute-start.4 = (bf16[512,1024]{1,0:T(8,128)(2,1)S(1)}, bf16[512,1024]{1,0:T(8,128)(2,1)S(1)}, u32[]{:S(2)}, u32[]{:S(2)}) collective-permute-start(bf16[512,1024]{1,0:T(8,128)(2,1)S(1)} %bitcast.44), channel_id=1, source_target_pairs={{0,1},{1,0},{2,3},{3,2},{4,5},{5,4},{6,7},{7,6},{8,9},{9,8},{10,11... | collective-permute-start | bytes 3145736 | tf_op jit(solution)/shard_map/ppermute | solution.py:180
  58.8 1.4 copy-start
  60.2 1.4 copy-start.2
  92.9 2.7 %collective-permute-start.8 = (bf16[512,1024]{1,0:T(8,128)(2,1)S(1)}, bf16[512,1024]{1,0:T(8,128)(2,1)S(1)}, u32[]{:S(2)}, u32[]{:S(2)}) collective-permute-start(bf16[512,1024]{1,0:T(8,128)(2,1)S(1)} %get-tuple-element.32), channel_id=1, source_target_pairs={{0,1},{1,0},{2,3},{3,2},{4,5},{5,4},{6,7},{7,6},{8,9},{9,8},{10,11... | collective-permute-start | bytes 3145736 | tf_op jit(solution)/shard_map/ppermute | solution.py:183
  96.9 12.0 %copy-start.3 = (f32[128,64]{0,1:T(8,128)S(1)}, f32[128,64]{0,1:T(8,128)}, u32[]{:S(2)}) copy-start(f32[128,64]{0,1:T(8,128)} %param.9) | copy-start | bytes 98308
  96.9 40.4 %all-to-all-start.1 = ((bf16[32,16,1024]{2,1,0:T(8,128)(2,1)}), bf16[32,16,1024]{2,1,0:T(8,128)(2,1)S(1)}, u32[]{:S(2)}, u32[]{:S(2)}) async-start(bf16[32,16,1024]{2,1,0:T(8,128)(2,1)} %bitcast.20), calls=%async_computation.1 | async-start | bytes 2097152 | tf_op jit(solution)/shard_map/all_to_all | solution.py:184
  137.9 6.7 %collective-permute-start.10 = (f32[128,256]{1,0:T(8,128)S(1)}, f32[128,256]{1,0:T(8,128)S(1)}, u32[]{:S(2)}, u32[]{:S(2)}) collective-permute-start(f32[128,256]{1,0:T(8,128)S(1)} %get-tuple-element.35), channel_id=1, source_target_pairs={{0,4},{2,6},{4,0},{6,2},{1,5},{3,7},{5,1},{7,3},{8,12},{10,14},{12... | collective-permute-start | bytes 393224 | tf_op jit(solution)/shard_map/ppermute | solution.py:132
  139.3 5.2 %collective-permute-start.11 = (f32[128,256]{1,0:T(8,128)S(1)}, f32[128,256]{1,0:T(8,128)S(1)}, u32[]{:S(2)}, u32[]{:S(2)}) collective-permute-start(f32[128,256]{1,0:T(8,128)S(1)} %get-tuple-element.34), channel_id=1, source_target_pairs={{0,6},{2,0},{4,2},{6,4},{1,7},{3,1},{5,3},{7,5},{8,14},{10,8},{12,... | collective-permute-start | bytes 393224 | tf_op jit(solution)/shard_map/ppermute | solution.py:132
  140.9 6.2 %collective-permute-start.9 = (f32[128,256]{1,0:T(8,128)S(1)}, f32[128,256]{1,0:T(8,128)S(1)}, u32[]{:S(2)}, u32[]{:S(2)}) collective-permute-start(f32[128,256]{1,0:T(8,128)S(1)} %get-tuple-element.33), channel_id=1, source_target_pairs={{0,2},{2,4},{4,6},{6,0},{1,3},{3,5},{5,7},{7,1},{8,10},{10,12},{12... | collective-permute-start | bytes 393224 | tf_op jit(solution)/shard_map/ppermute | solution.py:132

commit v5 on v4

--- a/solution.py
+++ b/solution.py
@@ -14,46 +14,49 @@
 cross_chip = [(0, 3), (3, 0), (1, 2), (2, 1)]
 
 
-def pick_kernel(kind_ref, *refs):
-    unit = refs[0].shape[2]
-    for turn, packed in enumerate(refs[6:]):
-        gate, up, down = refs[3 * turn : 3 * turn + 3]
+def pick_kernel(kind_ref, gate, up, down, own, other, sems):
+    unit = gate.shape[2]
+    copies = []
+    for turn, packed in enumerate((other, own)):
+        at = kind_ref[0] if packed is own else 1 - kind_ref[0]
         for j in range(packed.shape[0]):
-            packed[j, :block, :unit] = gate[0, j * block : (j + 1) * block, :]
-            packed[j, :block, unit:] = up[0, j * block : (j + 1) * block, :]
-            packed[j, block:, :] = down[0, :, j * block : (j + 1) * block]
+            wide = pl.ds(j * block, block)
+            for source, target in (
+                (gate.at[at, wide, :], packed.at[j, pl.ds(0, block), pl.ds(0, unit)]),
+                (up.at[at, wide, :], packed.at[j, pl.ds(0, block), pl.ds(unit, unit)]),
+                (down.at[at, :, wide], packed.at[j, pl.ds(block, unit), :]),
+            ):
+                copies.append(pltpu.make_async_copy(source, target, sems.at[len(copies)]))
+    for copy in copies:
+        copy.start()
+    for copy in copies:
+        copy.wait()
 
 
 def pick_shards(kind, gate, up, down):
     depth, unit = gate.shape[1:]
-    steps = 4
-    each = depth // steps
-
-    def specs(turn):
-        def at(kind_ref):
-            return kind_ref[0] if turn == 0 else 1 - kind_ref[0]
-
-        tall = pl.BlockSpec((1, each, unit), lambda i, kind_ref: (at(kind_ref), i, 0))
-        return [
-            tall,
-            tall,
-            pl.BlockSpec((1, unit, each), lambda i, kind_ref: (at(kind_ref), 0, i)),
-        ]
-
-    packed = (depth // block, block + unit, block)
-    out = pl.BlockSpec((each // block, *packed[1:]), lambda i, kind_ref: (i, 0, 0))
+    count = depth // block
+    packed = jax.ShapeDtypeStruct((count, block + unit, block), gate.dtype)
+    anywhere = pl.BlockSpec(memory_space=pl.ANY)
+    whole = pl.BlockSpec(memory_space=pltpu.VMEM)
     return pl.pallas_call(
         pick_kernel,
-        out_shape=(jax.ShapeDtypeStruct(packed, gate.dtype),) * 2,
-        grid_spec=pltpu.PrefetchScalarGridSpec(
-            num_scalar_prefetch=1, grid=(steps,), in_specs=specs(0) + specs(1), out_specs=(out, out)
-        ),
+        out_shape=(packed, packed),
+        in_specs=[pl.BlockSpec(memory_space=pltpu.SMEM)] + [anywhere] * 3,
+        out_specs=(whole, whole),
+        scratch_shapes=[pltpu.SemaphoreType.DMA((6 * count,))],
         cost_estimate=pl.CostEstimate(flops=0, bytes_accessed=6 * 2**20, transcendentals=0),
-    )(kind.reshape(1).astype(jnp.int32), gate, up, down, gate, up, down)
+    )(kind.reshape(1).astype(jnp.int32), gate, up, down)
 
 
 def ffn_kernel(count, place_ref, arrived, across, *refs):
-    shards, added, (keep, give, hidden) = refs[:count], refs[count:-3], refs[-3:]
+    lying, added, (keep, give, hidden, held_shards, sems) = refs[:count], refs[count:-5], refs[-5:]
+    copies = [
+        pltpu.make_async_copy(one, held_shards.at[k], sems.at[k]) for k, one in enumerate(lying)
+    ]
+    for copy in copies:
+        copy.start()
+    shards = [held_shards.at[k] for k in range(count)]
     row, core = place_ref[0], place_ref[1]
     f32 = jnp.float32
     rows, held = arrived.shape
@@ -67,6 +70,7 @@
         return 2 * lax.rem(row + j, ring) + parity
 
     for k, shard in enumerate(shards):
+        copies[k].wait()
         both = jnp.zeros((rows, block), f32)
         for j in range(ring):
             lanes = pl.ds(j * block, block)
@@ -100,9 +104,16 @@
             jax.ShapeDtypeStruct((rows, held), jnp.float32),
             jax.ShapeDtypeStruct((rows, held), give_type),
         ),
-        in_specs=[pl.BlockSpec(memory_space=pltpu.SMEM)] + [whole] * (2 + count + len(added)),
+        in_specs=[pl.BlockSpec(memory_space=pltpu.SMEM)]
+        + [whole] * 2
+        + [pl.BlockSpec(memory_space=pl.ANY)] * count
+        + [whole] * len(added),
         out_specs=(whole, whole),
-        scratch_shapes=[pltpu.VMEM((rows, count * unit), jnp.bfloat16)],
+        scratch_shapes=[
+            pltpu.VMEM((rows, count * unit), jnp.bfloat16),
+            pltpu.VMEM((count, *shards[0].shape), jnp.bfloat16),
+            pltpu.SemaphoreType.DMA((count,)),
+        ],
         compiler_params=pltpu.CompilerParams(vmem_limit_bytes=40 * 2**20),
         cost_estimate=pl.CostEstimate(
             flops=2 * rows * width * unit, bytes_accessed=2**20, transcendentals=0
@@ -131,15 +142,17 @@
         pairs = [(at, (at + step) % row_count) for at in range(row_count)]
         return lax.ppermute(one, "x", pairs)
 
-    stacked = jnp.concatenate([tokens, jnp.broadcast_to(norm_gain[None, :], (16, width))], axis=0)
+    padded = lax.pad(tokens, jnp.zeros((), bf16), [(0, 16, 0), (0, 0, 0)])
+    at_row = lax.broadcasted_iota(jnp.int32, padded.shape, 0)
+    stacked = jnp.where(at_row < group_size, padded, norm_gain[None, :])
     parts = [stacked] + [ring_send(stacked, step) for step in range(1, row_count)]
 
     own, other = pick_shards(kind, gate_proj, up_proj, down_proj)
     parts, own, other = lax.optimization_barrier((parts, own, other))
     crossed = lax.ppermute(other, "x", cross_chip)
     near = lax.ppermute(own, "x", near_chip)
-    crossed, near = lax.optimization_barrier((crossed, near))
-    relayed = lax.ppermute(crossed, "x", near_chip)
+    gated, _ = lax.optimization_barrier((crossed, near))
+    relayed = lax.ppermute(gated, "x", near_chip)
 
     expert_iota = jnp.arange(expert_count, dtype=jnp.int32)
     hits = jnp.any(routes[:, :, None] == expert_iota[None, None, :], axis=1)

time: 148 us -> 148 us (level)
  no operation moved by 1% of the time
where the time goes in v5:
time: 148 us; the launch traced here: 147 us
  waiting for transfers between devices  87.9 us (59%)
  starting transfers between devices  33.9 us (23%)
  Pallas kernels  14.5 us (10%)
  other arithmetic  4.55 us (3%)
  local copies, waits for them, and re-layouts  4.19 us (3%)
  matrix products  2.08 us (1%)
    all_to_all x1, waiting for transfers between devices, on_device(): lax.all_to_all(summed.astype(bf16).reshape(ep_count, share, -1), 'ep', sp...  28.1 us
    ppermute x1, waiting for transfers between devices, on_device(): crossed = lax.ppermute(other, 'x', cross_chip)  24 us
    ppermute x1, waiting for transfers between devices, on_device(): relayed = lax.ppermute(gated, 'x', near_chip)  21.3 us
    all_to_all x1, starting transfers between devices, on_device(): lax.all_to_all(summed.astype(bf16).reshape(ep_count, share, -1), 'ep', sp...  11.8 us
    all_to_all x1, starting transfers between devices, on_device(): lax.all_to_all(outgoing.reshape(ep_count, share, -1), 'ep', split_axis=0,...  11.7 us
    pallas_call x2, Pallas kernels, expert_rows(): pl.pallas_call(functools.partial(ffn_kernel, count), out_shape=(jax.Shape...  10.5 us
    ppermute x6, starting transfers between devices, ring_send(): return lax.ppermute(one, 'x', pairs)  9.2 us
    ppermute x6, waiting for transfers between devices, ring_send(): return lax.ppermute(one, 'x', pairs)  5.76 us
  transfers between devices with their start and end apart: 14, of which 9 were waited for; matrix products, arithmetic and copies ran while one was open for 2% of the time, Pallas kernels for 7%

profile of v5, /device:TPU:8, one launch (start us, length us, event | category | flops | bytes accessed | tf_op | source)
XLA Modules:
  0.0 147.4 jit_solution(2823252896684134986)
XLA Ops:
  0.0 0.9 pad_select_fusion
  0.9 1.6 %collective-permute-start = (bf16[144,256]{1,0:T(8,128)(2,1)S(1)}, bf16[144,256]{1,0:T(8,128)(2,1)S(1)}, u32[]{:S(2)}, u32[]{:S(2)}) collective-permute-start(bf16[144,256]{1,0:T(8,128)(2,1)S(1)} %pad_select_fusion), channel_id=1, source_target_pairs={{0,2},{2,4},{4,6},{6,0},{1,3},{3,5},{5,7},{7,1},{8,10},{10,12},{12... | collective-permute-start | bytes 221192 | tf_op jit(solution)/shard_map/ppermute | solution.py:143
  2.5 2.7 %collective-permute-start.1 = (bf16[144,256]{1,0:T(8,128)(2,1)S(1)}, bf16[144,256]{1,0:T(8,128)(2,1)S(1)}, u32[]{:S(2)}, u32[]{:S(2)}) collective-permute-start(bf16[144,256]{1,0:T(8,128)(2,1)S(1)} %pad_select_fusion), channel_id=1, source_target_pairs={{0,4},{2,6},{4,0},{6,2},{1,5},{3,7},{5,1},{7,3},{8,12},{10,14},{12... | collective-permute-start | bytes 221192 | tf_op jit(solution)/shard_map/ppermute | solution.py:143
  5.2 1.4 collective-permute-start.2
  6.7 0.7 fusion.12
  7.5 0.2 fusion.30
  7.8 0.1 eq.60
  7.8 0.1 bitcast_compare_fusion
  8.0 4.0 %shard_map.73 = (bf16[8,384,256]{2,1,0:T(8,128)(2,1)}, bf16[8,384,256]{2,1,0:T(8,128)(2,1)}) custom-call(s32[1]{0:T(128)} %bitcast.11.kind_ref, bf16[2,2048,128]{2,1,0:T(8,128)(2,1)} %gate.1, bf16[2,2048,128]{2,1,0:T(8,128)(2,1)} %up.1, bf16[2,128,2048]{2,1,0:T(8,128)(2,1)} %down.1), custom_call_target="tpu_custom_call" | custom-call | bytes 6291456 | tf_op jit(solution)/shard_map/pallas_call | solution.py:42
  11.9 0.0 collective-permute-done
  12.0 0.0 collective-permute-done.1
  12.0 0.0 collective-permute-done.2
  12.0 0.1 fusion.19
  12.1 0.1 fusion.13
  12.2 0.1 collective-permute-start.3
  12.4 0.3 collective-permute-start.5
  12.7 0.4 collective-permute-start.6
  13.1 0.3 collective-permute-done.3
  13.5 0.1 fusion.15
  13.6 1.4 convolution_convert_fusion
  15.0 11.7 %all-to-all-start = ((bf16[32,16,1024]{2,1,0:T(8,128)(2,1)}), bf16[32,16,1024]{2,1,0:T(8,128)(2,1)S(1)}, u32[]{:S(2)}, u32[]{:S(2)}) async-start(bf16[32,16,1024]{2,1,0:T(8,128)(2,1)} %bitcast.48), calls=%async_computation | async-start | bytes 2097152 | tf_op jit(solution)/shard_map/all_to_all | solution.py:190
  26.7 24.0 %collective-permute-done.5.refs_2_ = bf16[8,384,256]{2,1,0:T(8,128)(2,1)} collective-permute-done((bf16[8,384,256]{2,1,0:T(8,128)(2,1)}, bf16[8,384,256]{2,1,0:T(8,128)(2,1)}, u32[]{:S(2)}, u32[]{:S(2)}) %collective-permute-start.5) | collective-permute-done | bytes 1572896 | tf_op jit(solution)/shard_map/ppermute | solution.py:152
  50.7 0.0 collective-permute-done.6.refs_1_
  50.7 0.0 copy-start.1
  50.7 1.2 copy-done.1
  51.9 0.0 collective-permute-start.7
  51.9 3.3 %all-to-all-done = bf16[32,16,1024]{2,1,0:T(8,128)(2,1)S(1)} async-done(((bf16[32,16,1024]{2,1,0:T(8,128)(2,1)}), bf16[32,16,1024]{2,1,0:T(8,128)(2,1)S(1)}, u32[]{:S(2)}, u32[]{:S(2)}) %all-to-all-start) | async-done | bytes 1048608 | tf_op jit(solution)/shard_map/all_to_all | solution.py:190
  55.2 0.0 collective-permute-start.4
  55.2 0.1 pad_add_fusion.place_ref
  55.3 2.6 %collective-permute-done.4.across = bf16[512,1024]{1,0:T(8,128)(2,1)S(1)} collective-permute-done((bf16[512,1024]{1,0:T(8,128)(2,1)S(1)}, bf16[512,1024]{1,0:T(8,128)(2,1)S(1)}, u32[]{:S(2)}, u32[]{:S(2)}) %collective-permute-start.4) | collective-permute-done | bytes 1048608 | tf_op jit(solution)/shard_map/ppermute | solution.py:193
  57.8 0.0 copy-start
  57.8 1.4 copy-done
  59.2 0.0 copy-start.2
  59.2 1.4 copy-done.2
  60.7 6.2 %shard_map.74 = (f32[512,1024]{1,0:T(8,128)S(1)}, f32[512,1024]{1,0:T(8,128)S(1)}) custom-call(s32[2]{0:T(128)S(1)} %pad_add_fusion.place_ref, bf16[512,1024]{1,0:T(8,128)(2,1)S(1)} %bitcast.45, bf16[512,1024]{1,0:T(8,128)(2,1)S(1)} %collective-permute-done.4.across, bf16[8,384,256]{2,1,0:T(8,128)(2,1)S(1)} %copy-done, bf16[8,384,256]{2,1,0:T(8,128)(2,1)S(1)} %copy-done.2, ...), custom_call_target="tpu_custom_call" | custom-call | flops 268435456 | bytes 1048576 | tf_op jit(solution)/shard_map/pallas_call | solution.py:101
  66.9 21.3 %collective-permute-done.7.refs_0_ = bf16[8,384,256]{2,1,0:T(8,128)(2,1)} collective-permute-done((bf16[8,384,256]{2,1,0:T(8,128)(2,1)}, bf16[8,384,256]{2,1,0:T(8,128)(2,1)}, u32[]{:S(2)}, u32[]{:S(2)}) %collective-permute-start.7) | collective-permute-done | bytes 1572896 | tf_op jit(solution)/shard_map/ppermute | solution.py:155
  88.1 4.3 %shard_map.75 = (f32[512,1024]{1,0:T(8,128)S(1)}, bf16[512,1024]{1,0:T(8,128)(2,1)S(1)}) custom-call(s32[2]{0:T(128)S(1)} %pad_add_fusion.place_ref, bf16[512,1024]{1,0:T(8,128)(2,1)S(1)} %bitcast.46, bf16[512,1024]{1,0:T(8,128)(2,1)S(1)} %collective-permute-done.4.across, bf16[8,384,256]{2,1,0:T(8,128)(2,1)} %collective-permute-done.7.refs_0_, ...), custom_call_target="tpu_custom_call" | custom-call | flops 268435456 | bytes 1048576 | tf_op jit(solution)/shard_map/pallas_call | solution.py:101
  92.5 0.3 collective-permute-start.8
  92.8 2.6 %collective-permute-done.8 = bf16[512,1024]{1,0:T(8,128)(2,1)S(1)} collective-permute-done((bf16[512,1024]{1,0:T(8,128)(2,1)S(1)}, bf16[512,1024]{1,0:T(8,128)(2,1)S(1)}, u32[]{:S(2)}, u32[]{:S(2)}) %collective-permute-start.8) | collective-permute-done | bytes 1048608 | tf_op jit(solution)/shard_map/ppermute | solution.py:196
  95.4 1.3 add_convert_fusion
  96.7 0.0 copy-start.3
  96.7 11.8 %all-to-all-start.1 = ((bf16[32,16,1024]{2,1,0:T(8,128)(2,1)}), bf16[32,16,1024]{2,1,0:T(8,128)(2,1)S(1)}, u32[]{:S(2)}, u32[]{:S(2)}) async-start(bf16[32,16,1024]{2,1,0:T(8,128)(2,1)} %bitcast.20), calls=%async_computation.1 | async-start | bytes 2097152 | tf_op jit(solution)/shard_map/all_to_all | solution.py:197
  108.6 0.0 copy-done.3
  108.7 0.1 reduce-precision_convert_fusion
  108.8 28.1 %all-to-all-done.1 = bf16[32,16,1024]{2,1,0:T(8,128)(2,1)S(1)} async-done(((bf16[32,16,1024]{2,1,0:T(8,128)(2,1)}), bf16[32,16,1024]{2,1,0:T(8,128)(2,1)S(1)}, u32[]{:S(2)}, u32[]{:S(2)}) %all-to-all-start.1) | async-done | bytes 1048608 | tf_op jit(solution)/shard_map/all_to_all | solution.py:197
  136.9 0.5 fusion.1
  137.4 0.1 slice_add_fusion
  137.5 1.4 collective-permute-start.10
  138.9 1.6 %collective-permute-start.11 = (f32[128,256]{1,0:T(8,128)S(1)}, f32[128,256]{1,0:T(8,128)S(1)}, u32[]{:S(2)}, u32[]{:S(2)}) collective-permute-start(f32[128,256]{1,0:T(8,128)S(1)} %get-tuple-element.32), channel_id=1, source_target_pairs={{0,6},{2,0},{4,2},{6,4},{1,7},{3,1},{5,3},{7,5},{8,14},{10,8},{12,... | collective-permute-start | bytes 393224 | tf_op jit(solution)/shard_map/ppermute | solution.py:143
  140.5 0.4 collective-permute-start.9
  141.0 3.2 %collective-permute-done.10 = f32[128,256]{1,0:T(8,128)S(1)} collective-permute-done((f32[128,256]{1,0:T(8,128)S(1)}, f32[128,256]{1,0:T(8,128)S(1)}, u32[]{:S(2)}, u32[]{:S(2)}) %collective-permute-start.10) | collective-permute-done | bytes 131104 | tf_op jit(solution)/shard_map/ppermute | solution.py:143
  144.2 0.0 collective-permute-done.11
  144.2 2.6 %collective-permute-done.9 = f32[128,256]{1,0:T(8,128)S(1)} collective-permute-done((f32[128,256]{1,0:T(8,128)S(1)}, f32[128,256]{1,0:T(8,128)S(1)}, u32[]{:S(2)}, u32[]{:S(2)}) %collective-permute-start.9) | collective-permute-done | bytes 131104 | tf_op jit(solution)/shard_map/ppermute | solution.py:143
  146.7 0.7 fusion.27
  (17 shorter events, 0.3 us)
Async XLA Ops:
  0.9 11.0 %collective-permute-start = (bf16[144,256]{1,0:T(8,128)(2,1)S(1)}, bf16[144,256]{1,0:T(8,128)(2,1)S(1)}, u32[]{:S(2)}, u32[]{:S(2)}) collective-permute-start(bf16[144,256]{1,0:T(8,128)(2,1)S(1)} %pad_select_fusion), channel_id=1, source_target_pairs={{0,2},{2,4},{4,6},{6,0},{1,3},{3,5},{5,7},{7,1},{8,10},{10,12},{12... | collective-permute-start | bytes 221192 | tf_op jit(solution)/shard_map/ppermute | solution.py:143
  2.5 9.5 %collective-permute-start.1 = (bf16[144,256]{1,0:T(8,128)(2,1)S(1)}, bf16[144,256]{1,0:T(8,128)(2,1)S(1)}, u32[]{:S(2)}, u32[]{:S(2)}) collective-permute-start(bf16[144,256]{1,0:T(8,128)(2,1)S(1)} %pad_select_fusion), channel_id=1, source_target_pairs={{0,4},{2,6},{4,0},{6,2},{1,5},{3,7},{5,1},{7,3},{8,12},{10,14},{12... | collective-permute-start | bytes 221192 | tf_op jit(solution)/shard_map/ppermute | solution.py:143
  5.2 6.7 %collective-permute-start.2 = (bf16[144,256]{1,0:T(8,128)(2,1)S(1)}, bf16[144,256]{1,0:T(8,128)(2,1)S(1)}, u32[]{:S(2)}, u32[]{:S(2)}) collective-permute-start(bf16[144,256]{1,0:T(8,128)(2,1)S(1)} %pad_select_fusion), channel_id=1, source_target_pairs={{0,6},{2,0},{4,2},{6,4},{1,7},{3,1},{5,3},{7,5},{8,14},{10,8},{12,... | collective-permute-start | bytes 221192 | tf_op jit(solution)/shard_map/ppermute | solution.py:143
  12.2 1.2 collective-permute-start.3
  12.4 38.3 %collective-permute-start.5 = (bf16[8,384,256]{2,1,0:T(8,128)(2,1)}, bf16[8,384,256]{2,1,0:T(8,128)(2,1)}, u32[]{:S(2)}, u32[]{:S(2)}) collective-permute-start(bf16[8,384,256]{2,1,0:T(8,128)(2,1)} %get-tuple-element.24), channel_id=1, source_target_pairs={{0,6},{6,0},{2,4},{4,2},{1,7},{7,1},{3,5},{5,3},{8,14},{14,8},{10,... | collective-permute-start | bytes 4718600 | tf_op jit(solution)/shard_map/ppermute | solution.py:152
  12.7 38.0 %collective-permute-start.6 = (bf16[8,384,256]{2,1,0:T(8,128)(2,1)}, bf16[8,384,256]{2,1,0:T(8,128)(2,1)S(1)}, u32[]{:S(2)}, u32[]{:S(2)}) collective-permute-start(bf16[8,384,256]{2,1,0:T(8,128)(2,1)} %get-tuple-element.25.refs_0_), channel_id=1, source_target_pairs={{0,2},{2,0},{4,6},{6,4},{1,3},{3,1},{5,7},{7,5},{8,10},{10,8},{12,... | collective-permute-start | bytes 4718600 | tf_op jit(solution)/shard_map/ppermute | solution.py:153
  15.0 40.1 %all-to-all-start = ((bf16[32,16,1024]{2,1,0:T(8,128)(2,1)}), bf16[32,16,1024]{2,1,0:T(8,128)(2,1)S(1)}, u32[]{:S(2)}, u32[]{:S(2)}) async-start(bf16[32,16,1024]{2,1,0:T(8,128)(2,1)} %bitcast.48), calls=%async_computation | async-start | bytes 2097152 | tf_op jit(solution)/shard_map/all_to_all | solution.py:190
  50.7 1.2 copy-start.1
  51.9 36.3 %collective-permute-start.7 = (bf16[8,384,256]{2,1,0:T(8,128)(2,1)}, bf16[8,384,256]{2,1,0:T(8,128)(2,1)}, u32[]{:S(2)}, u32[]{:S(2)}) collective-permute-start(bf16[8,384,256]{2,1,0:T(8,128)(2,1)} %collective-permute-done.5.refs_2_), channel_id=1, source_target_pairs={{0,2},{2,0},{4,6},{6,4},{1,3},{3,1},{5,7},{7,5},{8,10},{10,8},{12,... | collective-permute-start | bytes 4718600 | tf_op jit(solution)/shard_map/ppermute | solution.py:155
  55.2 2.7 %collective-permute-start.4 = (bf16[512,1024]{1,0:T(8,128)(2,1)S(1)}, bf16[512,1024]{1,0:T(8,128)(2,1)S(1)}, u32[]{:S(2)}, u32[]{:S(2)}) collective-permute-start(bf16[512,1024]{1,0:T(8,128)(2,1)S(1)} %bitcast.44), channel_id=1, source_target_pairs={{0,1},{1,0},{2,3},{3,2},{4,5},{5,4},{6,7},{7,6},{8,9},{9,8},{10,11... | collective-permute-start | bytes 3145736 | tf_op jit(solution)/shard_map/ppermute | solution.py:193
  57.8 1.4 copy-start
  59.2 1.4 copy-start.2
  92.5 2.9 %collective-permute-start.8 = (bf16[512,1024]{1,0:T(8,128)(2,1)S(1)}, bf16[512,1024]{1,0:T(8,128)(2,1)S(1)}, u32[]{:S(2)}, u32[]{:S(2)}) collective-permute-start(bf16[512,1024]{1,0:T(8,128)(2,1)S(1)} %get-tuple-element.30), channel_id=1, source_target_pairs={{0,1},{1,0},{2,3},{3,2},{4,5},{5,4},{6,7},{7,6},{8,9},{9,8},{10,11... | collective-permute-start | bytes 3145736 | tf_op jit(solution)/shard_map/ppermute | solution.py:196
  96.7 11.8 %copy-start.3 = (f32[128,64]{0,1:T(8,128)S(1)}, f32[128,64]{0,1:T(8,128)}, u32[]{:S(2)}) copy-start(f32[128,64]{0,1:T(8,128)} %param.9) | copy-start | bytes 98308
  96.7 40.2 %all-to-all-start.1 = ((bf16[32,16,1024]{2,1,0:T(8,128)(2,1)}), bf16[32,16,1024]{2,1,0:T(8,128)(2,1)S(1)}, u32[]{:S(2)}, u32[]{:S(2)}) async-start(bf16[32,16,1024]{2,1,0:T(8,128)(2,1)} %bitcast.20), calls=%async_computation.1 | async-start | bytes 2097152 | tf_op jit(solution)/shard_map/all_to_all | solution.py:197
  137.5 6.7 %collective-permute-start.10 = (f32[128,256]{1,0:T(8,128)S(1)}, f32[128,256]{1,0:T(8,128)S(1)}, u32[]{:S(2)}, u32[]{:S(2)}) collective-permute-start(f32[128,256]{1,0:T(8,128)S(1)} %get-tuple-element.33), channel_id=1, source_target_pairs={{0,4},{2,6},{4,0},{6,2},{1,5},{3,7},{5,1},{7,3},{8,12},{10,14},{12... | collective-permute-start | bytes 393224 | tf_op jit(solution)/shard_map/ppermute | solution.py:143
  138.9 5.2 %collective-permute-start.11 = (f32[128,256]{1,0:T(8,128)S(1)}, f32[128,256]{1,0:T(8,128)S(1)}, u32[]{:S(2)}, u32[]{:S(2)}) collective-permute-start(f32[128,256]{1,0:T(8,128)S(1)} %get-tuple-element.32), channel_id=1, source_target_pairs={{0,6},{2,0},{4,2},{6,4},{1,7},{3,1},{5,3},{7,5},{8,14},{10,8},{12,... | collective-permute-start | bytes 393224 | tf_op jit(solution)/shard_map/ppermute | solution.py:143
  140.5 6.2 %collective-permute-start.9 = (f32[128,256]{1,0:T(8,128)S(1)}, f32[128,256]{1,0:T(8,128)S(1)}, u32[]{:S(2)}, u32[]{:S(2)}) collective-permute-start(f32[128,256]{1,0:T(8,128)S(1)} %get-tuple-element.31), channel_id=1, source_target_pairs={{0,2},{2,4},{4,6},{6,0},{1,3},{3,5},{5,7},{7,1},{8,10},{10,12},{12... | collective-permute-start | bytes 393224 | tf_op jit(solution)/shard_map/ppermute | solution.py:143

commit v6 on v5

v6 whole, which is shorter than its diff:
```python
import functools
import jax
import jax.numpy as jnp
from jax import lax
from jax.experimental import pallas as pl
from jax.experimental.pallas import tpu as pltpu
from jax.sharding import Mesh, PartitionSpec as P

epsilon = 1e-05
chip_cores = 2
block = 256
other_core = [(0, 1), (1, 0)]
detoured = 2


def row_pairs(partner, lent=False):
    pairs = []
    for parity in range(2):
        turn = 1 - parity if lent else parity
        for part in range(4):
            source, target = (part + turn) % 4, (partner(part) + turn) % 4
            pairs.append((4 * parity + source, 4 * parity + target))
    return pairs


near_chip = row_pairs(lambda part: part ^ 1)
near_lent = row_pairs(lambda part: part ^ 1, True)
cross_chip = row_pairs(lambda part: 3 - part)
other_row = [(at, (at + 4) % 8) for at in range(8)]


def pick_kernel(kind_ref, gate, up, down, *refs):
    pieces, sems = refs[:-1], refs[-1]
    unit = gate.shape[2]
    copies = []
    first = 0
    for turn, packed in enumerate(pieces):
        first = 0 if turn in (0, 2) else first
        at = 1 - kind_ref[0] if turn < 2 else kind_ref[0]
        for j in range(packed.shape[0]):
            wide = pl.ds((first + j) * block, block)
            for source, target in (
                (gate.at[at, wide, :], packed.at[j, pl.ds(0, block), pl.ds(0, unit)]),
                (up.at[at, wide, :], packed.at[j, pl.ds(0, block), pl.ds(unit, unit)]),
                (down.at[at, :, wide], packed.at[j, pl.ds(block, unit), :]),
            ):
                copies.append(pltpu.make_async_copy(source, target, sems.at[len(copies)]))
        first += packed.shape[0]
    for copy in copies:
        copy.start()
    for copy in copies:
        copy.wait()


def pick_shards(kind, gate, up, down):
    depth, unit = gate.shape[1:]
    count = depth // block
    anywhere = pl.BlockSpec(memory_space=pl.ANY)
    whole = pl.BlockSpec(memory_space=pltpu.VMEM)
    other = [count - detoured, detoured]
    own = [count - detoured, detoured]
    picked = pl.pallas_call(
        pick_kernel,
        out_shape=tuple(
            jax.ShapeDtypeStruct((size, block + unit, block), gate.dtype) for size in other + own
        ),
        in_specs=[pl.BlockSpec(memory_space=pltpu.SMEM)] + [anywhere] * 3,
        out_specs=(whole,) * 4,
        scratch_shapes=[pltpu.SemaphoreType.DMA((6 * count,))],
        cost_estimate=pl.CostEstimate(flops=0, bytes_accessed=6 * 2**20, transcendentals=0),
    )(kind.reshape(1).astype(jnp.int32), gate, up, down)
    return picked[:2], picked[2:]


def ffn_kernel(count, place_ref, arrived, across, *refs):
    lying, added, (keep, give, hidden, held_shards, sems) = refs[:count], refs[count:-5], refs[-5:]
    total_blocks = held_shards.shape[1]
    copies, first = [], 0
    for n, piece in enumerate(lying):
        into = held_shards.at[first // total_blocks, pl.ds(first % total_blocks, piece.shape[0])]
        copies.append((first // total_blocks, pltpu.make_async_copy(piece, into, sems.at[n])))
        first += piece.shape[0]
    for _, copy in copies:
        copy.start()
    shards = [held_shards.at[k] for k in range(held_shards.shape[0])]
    row, core = place_ref[0], place_ref[1]
    f32 = jnp.float32
    rows, held = arrived.shape
    ring = held // block
    unit = block // 2

    def source(j, parity):
        return 2 * lax.rem(row - j + ring, ring) + parity

    def target(j, parity):
        return 2 * lax.rem(row + j, ring) + parity

    for k, shard in enumerate(shards):
        for shard_of, copy in copies:
            if shard_of == k:
                copy.wait()
        both = jnp.zeros((rows, block), f32)
        for j in range(ring):
            lanes = pl.ds(j * block, block)
            for part, parity in ((arrived, core), (across, 1 - core)):
                both += jnp.dot(
                    part[:, lanes], shard[source(j, parity), :block, :], preferred_element_type=f32
                )
        gate_val, up_val = both[:, :unit], both[:, unit:]
        silu = gate_val / (1.0 + jnp.exp(-gate_val))
        hidden[:, pl.ds(k * unit, unit)] = (silu * up_val).astype(hidden.dtype)
    for which, (parity, out) in enumerate(((core, keep), (1 - core, give))):
        for j in range(ring):
            lanes = pl.ds(j * block, block)
            total = added[which][:, lanes] if added else jnp.zeros((rows, block), f32)
            down = jnp.concatenate([shard[target(j, parity), block:, :] for shard in shards], axis=0)
            total += jnp.dot(hidden[...], down, preferred_element_type=f32)
            out[:, lanes] = total.astype(out.dtype)


def expert_rows(place, arrived, across, pieces, added, give_type):
    rows, held = arrived.shape
    unit, width, count = block // 2, 2 * held, len(pieces)
    blocks = width // block
    shards = sum(piece.shape[0] for piece in pieces) // blocks
    whole = pl.BlockSpec(memory_space=pltpu.VMEM)
    return pl.pallas_call(
        functools.partial(ffn_kernel, count),
        out_shape=(
            jax.ShapeDtypeStruct((rows, held), jnp.float32),
            jax.ShapeDtypeStruct((rows, held), give_type),
        ),
        in_specs=[pl.BlockSpec(memory_space=pltpu.SMEM)]
        + [whole] * 2
        + [pl.BlockSpec(memory_space=pl.ANY)] * count
        + [whole] * len(added),
        out_specs=(whole, whole),
        scratch_shapes=[
            pltpu.VMEM((rows, shards * unit), jnp.bfloat16),
            pltpu.VMEM((shards, blocks, *pieces[0].shape[1:]), jnp.bfloat16),
            pltpu.SemaphoreType.DMA((count,)),
        ],
        compiler_params=pltpu.CompilerParams(vmem_limit_bytes=40 * 2**20),
        cost_estimate=pl.CostEstimate(
            flops=2 * rows * width * unit, bytes_accessed=2**20, transcendentals=0
        ),
    )(place, arrived, across, *pieces, *added)


def on_device(tokens, norm_gain, router_logits, routes, gate_proj, up_proj, down_proj):
    bf16, f32 = jnp.bfloat16, jnp.float32
    ep = ("line", "pair")
    ep_count = lax.axis_size(ep)
    row_count = lax.axis_size("x")
    group_size, width = tokens.shape
    local_experts = gate_proj.shape[0]
    top_count = routes.shape[1]
    expert_count = local_experts * ep_count
    capacity = 2 * group_size * top_count // expert_count
    share = capacity // (row_count // local_experts)
    core = lax.axis_index("core")
    row = lax.axis_index("x")
    split = row_count // local_experts
    part = (row - lax.axis_index("pair")) % row_count
    peers = (row - jnp.arange(ep_count, dtype=jnp.int32) % 2) % row_count

    place = jnp.stack([row, core]).astype(jnp.int32)

    def ring_send(one, step):
        pairs = [(at, (at + step) % row_count) for at in range(row_count)]
        return lax.ppermute(one, "x", pairs)

    padded = lax.pad(tokens, jnp.zeros((), bf16), [(0, 16, 0), (0, 0, 0)])
    at_row = lax.broadcasted_iota(jnp.int32, padded.shape, 0)
    stacked = jnp.where(at_row < group_size, padded, norm_gain[None, :])
    parts = [stacked] + [ring_send(stacked, step) for step in range(1, row_count)]

    other, own = pick_shards(part // split, gate_proj, up_proj, down_proj)
    parts, own, other = lax.optimization_barrier((parts, own, other))

    def send(one, pairs):
        return lax.ppermute(one, ("pair", "x"), pairs)

    def after(one, *others):
        return lax.optimization_barrier((one, *others))[0]

    crossed = [send(other[0], cross_chip)]
    near = send(own[0], near_chip)
    crossed.append(send(after(other[1], crossed[0]), cross_chip))
    relayed = [send(after(crossed[0], near), near_chip)]
    relayed.append(send(after(crossed[1], relayed[0]), near_chip))
    passed = send(after(send(own[1], other_row), crossed[1]), near_lent)
    lent = send(passed, other_row)

    expert_iota = jnp.arange(expert_count, dtype=jnp.int32)
    hits = jnp.any(routes[:, :, None] == expert_iota[None, None, :], axis=1)
    earlier = jnp.tril(jnp.ones((group_size, group_size), bf16), -1)
    position = jnp.dot(earlier, hits.astype(bf16), preferred_element_type=f32)
    shifted = jnp.where(hits, router_logits, -jnp.inf)
    shifted = jnp.exp(shifted - jnp.max(shifted, axis=1, keepdims=True))
    gates = shifted / jnp.sum(shifted, axis=1, keepdims=True)

    def of_kind(table):
        table = table.reshape(group_size, ep_count, local_experts)
        return jnp.where((peers // split == 0)[None, :], table[:, :, 0], table[:, :, 1])

    slot = jnp.where(of_kind(hits), of_kind(position), -1.0)
    slot = slot - (peers % split * share).astype(f32)[None, :]
    gates = of_kind(gates)
    slot_iota = jnp.arange(share, dtype=jnp.int32).astype(f32)

    floated = [part[:group_size].astype(f32) for part in parts]
    squares = sum(jnp.sum(one * one, axis=1) for one in floated)[None, :]
    squares = squares + lax.ppermute(squares, "core", other_core)
    scale = lax.rsqrt(squares[0] / (width * row_count * chip_cores) + epsilon)[:, None]
    normed = jnp.concatenate(
        [
            (one * scale * part[group_size : group_size + 1].astype(f32)).astype(bf16)
            for one, part in zip(floated, parts)
        ],
        axis=1,
    )

    table = (slot.T[:, None, :] == slot_iota[None, :, None]).astype(bf16)
    outgoing = jnp.dot(
        table.reshape(ep_count * share, group_size), normed, preferred_element_type=f32
    ).astype(bf16)
    arrived = lax.all_to_all(
        outgoing.reshape(ep_count, share, -1), ep, split_axis=0, concat_axis=0, tiled=True
    ).reshape(ep_count * share, -1)
    arrived = after(arrived, relayed[0], passed)
    across = lax.ppermute(arrived, "core", other_core)
    added = expert_rows(place, arrived, across, (*own, *crossed), (), f32)
    keep, give = expert_rows(place, arrived, across, (near, lent, *relayed), added, bf16)
    summed = keep + lax.ppermute(give, "core", other_core).astype(f32)
    returned = lax.all_to_all(
        summed.astype(bf16).reshape(ep_count, share, -1), ep, split_axis=0, concat_axis=0, tiled=True
    ).reshape(ep_count * share, -1)

    weight = jnp.where(slot[:, :, None] == slot_iota[None, None, :], gates[:, :, None], 0.0)
    weight = weight.reshape(group_size, ep_count * share)
    high = lax.reduce_precision(weight, 8, 7)
    both = jnp.concatenate([high.astype(bf16), (weight - high).astype(bf16)], axis=0)
    mixed = jnp.dot(both, returned, preferred_element_type=f32)
    mixed = mixed[:group_size] + mixed[group_size:]

    result = mixed[:, :width]
    for step in range(1, row_count):
        sent = mixed[:, step * width : (step + 1) * width].astype(bf16)
        result = result + ring_send(sent, step).astype(f32)
    return result.astype(bf16)


def solution(mesh):
    ep_count, tp_count = mesh.devices.shape
    fine = Mesh(
        mesh.devices.reshape(ep_count // 2, 2, tp_count // chip_cores, chip_cores),
        ("line", "pair", "x", "core"),
    )
    ep, tp = ("line", "pair"), ("x", "core")
    return jax.shard_map(
        on_device,
        mesh=fine,
        in_specs=(
            P(ep, tp),
            P(tp),
            P(ep, None),
            P(ep, None),
            P(ep, None, tp),
            P(ep, None, tp),
            P(ep, tp, None),
        ),
        out_specs=P(ep, tp),
        check_vma=False,
    )
```

time: 148 us -> 145 us (0.980)
  waiting for transfers between devices: 87.9 us -> 82.2 us
  starting transfers between devices: 33.9 us -> 37 us
  other arithmetic: 4.55 us -> 7.1 us
  local copies, waits for them, and re-layouts: 4.19 us -> 2.47 us
    ppermute x3 -> x8, starting transfers between devices: 0.78 us -> 4.64 us  [send(): return lax.ppermute(one, ('pair', 'x'), pairs)]
    all_to_all x2, waiting for transfers between devices: 31.4 us -> 28.2 us  [the longest x1 28.2 us: on_device(): lax.all_to_all(summed.astype(bf16).reshape(ep_count, share, -1), ep, spli...]
    ppermute x6, waiting for transfers between devices: 5.76 us -> 3.8 us  [ring_send(): return lax.ppermute(one, 'x', pairs)]
    unnamed x8 -> x6, local copies, waits for them, and re-layouts: 3.99 us -> 2.27 us
    ppermute x3 -> x8, waiting for transfers between devices: 45.2 us -> 45.6 us  [send(): return lax.ppermute(one, ('pair', 'x'), pairs)]
  transfers between devices with their start and end apart: 14 -> 19, of which waited for: 9 -> 12; matrix products, arithmetic and copies ran while one was open for 2% -> 4% of each run, Pallas kernels for 7% -> 6%
where the time goes in v6:
time: 145 us; the launch traced here: 144 us
  waiting for transfers between devices  82.2 us (57%)
  starting transfers between devices  37 us (26%)
  Pallas kernels  13.1 us (9%)
  other arithmetic  7.1 us (5%)
  local copies, waits for them, and re-layouts  2.47 us (2%)
  matrix products  2.08 us (1%)
    ppermute x8, waiting for transfers between devices, send(): return lax.ppermute(one, ('pair', 'x'), pairs)  45.6 us
    all_to_all x1, waiting for transfers between devices, on_device(): lax.all_to_all(summed.astype(bf16).reshape(ep_count, share, -1), ep, spli...  28.2 us
    all_to_all x1, starting transfers between devices, on_device(): lax.all_to_all(outgoing.reshape(ep_count, share, -1), ep, split_axis=0, c...  11.6 us
    all_to_all x1, starting transfers between devices, on_device(): lax.all_to_all(summed.astype(bf16).reshape(ep_count, share, -1), ep, spli...  11.5 us
    pallas_call x2, Pallas kernels, expert_rows(): pl.pallas_call(functools.partial(ffn_kernel, count), out_shape=(jax.Shape...  9.1 us
    ppermute x6, starting transfers between devices, ring_send(): return lax.ppermute(one, 'x', pairs)  9.05 us
    ppermute x8, starting transfers between devices, send(): return lax.ppermute(one, ('pair', 'x'), pairs)  4.64 us
    pallas_call x1, Pallas kernels, pick_shards(): pl.pallas_call(pick_kernel, out_shape=tuple((jax.ShapeDtypeStruct((size,...  3.97 us
  transfers between devices with their start and end apart: 19, of which 12 were waited for; matrix products, arithmetic and copies ran while one was open for 4% of the time, Pallas kernels for 6%

profile of v6, /device:TPU:8, one launch (start us, length us, event | category | flops | bytes accessed | tf_op | source)
XLA Modules:
  0.0 144.2 jit_solution(12393449109871533987)
XLA Ops:
  0.0 0.9 pad_select_fusion
  0.9 1.6 %collective-permute-start = (bf16[144,256]{1,0:T(8,128)(2,1)S(1)}, bf16[144,256]{1,0:T(8,128)(2,1)S(1)}, u32[]{:S(2)}, u32[]{:S(2)}) collective-permute-start(bf16[144,256]{1,0:T(8,128)(2,1)S(1)} %pad_select_fusion), channel_id=1, source_target_pairs={{0,2},{2,4},{4,6},{6,0},{1,3},{3,5},{5,7},{7,1},{8,10},{10,12},{12... | collective-permute-start | bytes 221192 | tf_op jit(solution)/shard_map/ppermute | solution.py:171
  2.5 2.7 %collective-permute-start.1 = (bf16[144,256]{1,0:T(8,128)(2,1)S(1)}, bf16[144,256]{1,0:T(8,128)(2,1)S(1)}, u32[]{:S(2)}, u32[]{:S(2)}) collective-permute-start(bf16[144,256]{1,0:T(8,128)(2,1)S(1)} %pad_select_fusion), channel_id=1, source_target_pairs={{0,4},{2,6},{4,0},{6,2},{1,5},{3,7},{5,1},{7,3},{8,12},{10,14},{12... | collective-permute-start | bytes 221192 | tf_op jit(solution)/shard_map/ppermute | solution.py:171
  5.2 1.4 collective-permute-start.2
  6.7 0.7 fusion.12
  7.5 0.8 fusion.39
  8.3 0.8 fusion.35
  9.1 0.8 fusion.34
  10.0 0.2 fusion.30
  10.2 0.1 subtract_bitcast_fusion
  10.3 0.1 fusion.38
  10.4 0.1 eq.78
  10.4 0.1 bitcast_compare_fusion
  10.6 4.0 %shard_map.73 = (bf16[6,384,256]{2,1,0:T(8,128)(2,1)}, bf16[2,384,256]{2,1,0:T(8,128)(2,1)}, bf16[6,384,256]{2,1,0:T(8,128)(2,1)}, bf16[2,384,256]{2,1,0:T(8,128)(2,1)}) custom-call(s32[1]{0:T(128)} %bitcast.15.kind_ref, bf16[2,2048,128]{2,1,0:T(8,128)(2,1)} %gate.1, bf16[2,2048,128]{2,1,0:T(8,128)(2,1)} %up.1, bf16[2,128,2048]{2,1,0:T(8,128)(2,1)} %down.1), custom_call_target="tpu_custom_call" | custom-call | bytes 6291456 | tf_op jit(solution)/shard_map/pallas_call | solution.py:62
  14.6 0.0 collective-permute-done
  14.6 0.0 collective-permute-done.1
  14.6 0.0 collective-permute-done.2
  14.6 0.1 fusion.19
  14.7 0.0 copy-start.1
  14.7 0.1 fusion.13
  14.9 0.1 collective-permute-start.3
  15.0 0.7 collective-permute-start.4
  15.7 0.5 collective-permute-start.5
  16.1 0.0 collective-permute-done.3
  16.1 0.1 fusion.15
  16.3 1.4 convolution_convert_fusion
  17.7 11.6 %all-to-all-start = ((bf16[32,16,1024]{2,1,0:T(8,128)(2,1)}), bf16[32,16,1024]{2,1,0:T(8,128)(2,1)S(1)}, u32[]{:S(2)}, u32[]{:S(2)}) async-start(bf16[32,16,1024]{2,1,0:T(8,128)(2,1)} %bitcast.65), calls=%async_computation | async-start | bytes 2097152 | tf_op jit(solution)/shard_map/all_to_all | solution.py:228
  29.4 14.3 %collective-permute-done.4.refs_2_ = bf16[6,384,256]{2,1,0:T(8,128)(2,1)} collective-permute-done((bf16[6,384,256]{2,1,0:T(8,128)(2,1)}, bf16[6,384,256]{2,1,0:T(8,128)(2,1)}, u32[]{:S(2)}, u32[]{:S(2)}) %collective-permute-start.4) | collective-permute-done | bytes 1179680 | tf_op jit(solution)/shard_map/ppermute | solution.py:182
  43.7 1.4 collective-permute-done.5.refs_0_
  45.1 0.5 collective-permute-start.6
  45.6 0.4 collective-permute-start.7
  45.9 1.4 collective-permute-start.8
  47.4 11.5 %collective-permute-done.7 = bf16[2,384,256]{2,1,0:T(8,128)(2,1)S(1)} collective-permute-done((bf16[2,384,256]{2,1,0:T(8,128)(2,1)S(1)}, bf16[2,384,256]{2,1,0:T(8,128)(2,1)S(1)}, u32[]{:S(2)}, u32[]{:S(2)}) %collective-permute-start.7) | collective-permute-done | bytes 393248 | tf_op jit(solution)/shard_map/ppermute | solution.py:182
  58.9 0.0 collective-permute-done.8.refs_3_
  58.9 0.5 collective-permute-start.9
  59.4 9.4 %collective-permute-done.9 = bf16[2,384,256]{2,1,0:T(8,128)(2,1)} collective-permute-done((bf16[2,384,256]{2,1,0:T(8,128)(2,1)S(1)}, bf16[2,384,256]{2,1,0:T(8,128)(2,1)}, u32[]{:S(2)}, u32[]{:S(2)}) %collective-permute-start.9) | collective-permute-done | bytes 393248 | tf_op jit(solution)/shard_map/ppermute | solution.py:182
  68.8 0.0 all-to-all-done
  68.8 5.0 %collective-permute-done.6.refs_2_ = bf16[6,384,256]{2,1,0:T(8,128)(2,1)} collective-permute-done((bf16[6,384,256]{2,1,0:T(8,128)(2,1)}, bf16[6,384,256]{2,1,0:T(8,128)(2,1)}, u32[]{:S(2)}, u32[]{:S(2)}) %collective-permute-start.6) | collective-permute-done | bytes 1179680 | tf_op jit(solution)/shard_map/ppermute | solution.py:182
  73.8 0.0 collective-permute-start.10
  73.8 0.0 collective-permute-start.11
  73.8 0.7 collective-permute-start.12
  74.5 0.1 pad_add_fusion.place_ref
  74.6 1.9 %collective-permute-done.10.across = bf16[512,1024]{1,0:T(8,128)(2,1)S(1)} collective-permute-done((bf16[512,1024]{1,0:T(8,128)(2,1)S(1)}, bf16[512,1024]{1,0:T(8,128)(2,1)S(1)}, u32[]{:S(2)}, u32[]{:S(2)}) %collective-permute-start.10) | collective-permute-done | bytes 1048608 | tf_op jit(solution)/shard_map/ppermute | solution.py:232
  76.5 1.3 copy-done
  77.7 1.0 copy-done.2
  78.7 4.2 %shard_map.74 = (f32[512,1024]{1,0:T(8,128)S(1)}, f32[512,1024]{1,0:T(8,128)S(1)}) custom-call(s32[2]{0:T(128)S(1)} %pad_add_fusion.place_ref, bf16[512,1024]{1,0:T(8,128)(2,1)S(1)} %bitcast.63, bf16[512,1024]{1,0:T(8,128)(2,1)S(1)} %collective-permute-done.10.across, bf16[6,384,256]{2,1,0:T(8,128)(2,1)S(1)} %copy-done, bf16[2,384,256]{2,1,0:T(8,128)(2,1)S(1)} %copy-done.2, ...), custom_call_target="tpu_custom_call" | custom-call | flops 268435456 | bytes 1048576 | tf_op jit(solution)/shard_map/pallas_call | solution.py:127
  82.9 2.7 %collective-permute-done.11.refs_1_ = bf16[2,384,256]{2,1,0:T(8,128)(2,1)} collective-permute-done((bf16[2,384,256]{2,1,0:T(8,128)(2,1)}, bf16[2,384,256]{2,1,0:T(8,128)(2,1)}, u32[]{:S(2)}, u32[]{:S(2)}) %collective-permute-start.11) | collective-permute-done | bytes 393248 | tf_op jit(solution)/shard_map/ppermute | solution.py:182
  85.7 1.2 collective-permute-done.12.refs_3_
  86.9 4.9 %shard_map.75 = (f32[512,1024]{1,0:T(8,128)S(1)}, bf16[512,1024]{1,0:T(8,128)(2,1)S(1)}) custom-call(s32[2]{0:T(128)S(1)} %pad_add_fusion.place_ref, bf16[512,1024]{1,0:T(8,128)(2,1)S(1)} %bitcast.64, bf16[512,1024]{1,0:T(8,128)(2,1)S(1)} %collective-permute-done.10.across, bf16[6,384,256]{2,1,0:T(8,128)(2,1)S(1)} %collective-permute-done.5.refs_0_, ...), custom_call_target="tpu_custom_call" | custom-call | flops 268435456 | bytes 1048576 | tf_op jit(solution)/shard_map/pallas_call | solution.py:127
  91.8 0.1 collective-permute-start.13
  91.9 2.6 %collective-permute-done.13 = bf16[512,1024]{1,0:T(8,128)(2,1)S(1)} collective-permute-done((bf16[512,1024]{1,0:T(8,128)(2,1)S(1)}, bf16[512,1024]{1,0:T(8,128)(2,1)S(1)}, u32[]{:S(2)}, u32[]{:S(2)}) %collective-permute-start.13) | collective-permute-done | bytes 1048608 | tf_op jit(solution)/shard_map/ppermute | solution.py:235
  94.6 1.4 add_convert_fusion
  95.9 11.5 %all-to-all-start.1 = ((bf16[32,16,1024]{2,1,0:T(8,128)(2,1)}), bf16[32,16,1024]{2,1,0:T(8,128)(2,1)S(1)}, u32[]{:S(2)}, u32[]{:S(2)}) async-start(bf16[32,16,1024]{2,1,0:T(8,128)(2,1)} %bitcast.24), calls=%async_computation.1 | async-start | bytes 2097152 | tf_op jit(solution)/shard_map/all_to_all | solution.py:236
  107.5 0.1 reduce-precision_convert_fusion
  107.6 28.2 %all-to-all-done.1 = bf16[32,16,1024]{2,1,0:T(8,128)(2,1)S(1)} async-done(((bf16[32,16,1024]{2,1,0:T(8,128)(2,1)}), bf16[32,16,1024]{2,1,0:T(8,128)(2,1)S(1)}, u32[]{:S(2)}, u32[]{:S(2)}) %all-to-all-start.1) | async-done | bytes 1048608 | tf_op jit(solution)/shard_map/all_to_all | solution.py:236
  135.8 0.5 fusion.1
  136.3 0.1 fusion.51
  136.4 0.3 collective-permute-start.14
  136.7 1.9 %collective-permute-start.15 = (bf16[128,256]{1,0:T(8,128)(2,1)S(1)}, bf16[128,256]{1,0:T(8,128)(2,1)S(1)}, u32[]{:S(2)}, u32[]{:S(2)}) collective-permute-start(bf16[128,256]{1,0:T(8,128)(2,1)S(1)} %get-tuple-element.54), channel_id=1, source_target_pairs={{0,4},{2,6},{4,0},{6,2},{1,5},{3,7},{5,1},{7,3},{8,12},{10,14},{12... | collective-permute-start | bytes 196616 | tf_op jit(solution)/shard_map/ppermute | solution.py:171
  138.6 1.1 collective-permute-start.16
  139.7 2.9 %collective-permute-done.14 = bf16[128,256]{1,0:T(8,128)(2,1)S(1)} collective-permute-done((bf16[128,256]{1,0:T(8,128)(2,1)S(1)}, bf16[128,256]{1,0:T(8,128)(2,1)S(1)}, u32[]{:S(2)}, u32[]{:S(2)}) %collective-permute-start.14) | collective-permute-done | bytes 65568 | tf_op jit(solution)/shard_map/ppermute | solution.py:171
  142.7 0.0 collective-permute-done.15
  142.7 0.9 collective-permute-done.16
  143.5 0.7 fusion.27
  (18 shorter events, 0.2 us)
Async XLA Ops:
  0.9 13.6 %collective-permute-start = (bf16[144,256]{1,0:T(8,128)(2,1)S(1)}, bf16[144,256]{1,0:T(8,128)(2,1)S(1)}, u32[]{:S(2)}, u32[]{:S(2)}) collective-permute-start(bf16[144,256]{1,0:T(8,128)(2,1)S(1)} %pad_select_fusion), channel_id=1, source_target_pairs={{0,2},{2,4},{4,6},{6,0},{1,3},{3,5},{5,7},{7,1},{8,10},{10,12},{12... | collective-permute-start | bytes 221192 | tf_op jit(solution)/shard_map/ppermute | solution.py:171
  2.5 12.1 %collective-permute-start.1 = (bf16[144,256]{1,0:T(8,128)(2,1)S(1)}, bf16[144,256]{1,0:T(8,128)(2,1)S(1)}, u32[]{:S(2)}, u32[]{:S(2)}) collective-permute-start(bf16[144,256]{1,0:T(8,128)(2,1)S(1)} %pad_select_fusion), channel_id=1, source_target_pairs={{0,4},{2,6},{4,0},{6,2},{1,5},{3,7},{5,1},{7,3},{8,12},{10,14},{12... | collective-permute-start | bytes 221192 | tf_op jit(solution)/shard_map/ppermute | solution.py:171
  5.2 9.3 %collective-permute-start.2 = (bf16[144,256]{1,0:T(8,128)(2,1)S(1)}, bf16[144,256]{1,0:T(8,128)(2,1)S(1)}, u32[]{:S(2)}, u32[]{:S(2)}) collective-permute-start(bf16[144,256]{1,0:T(8,128)(2,1)S(1)} %pad_select_fusion), channel_id=1, source_target_pairs={{0,6},{2,0},{4,2},{6,4},{1,7},{3,1},{5,3},{7,5},{8,14},{10,8},{12,... | collective-permute-start | bytes 221192 | tf_op jit(solution)/shard_map/ppermute | solution.py:171
  14.7 30.9 %copy-start.1 = (bf16[2,384,256]{2,1,0:T(8,128)(2,1)S(1)}, bf16[2,384,256]{2,1,0:T(8,128)(2,1)}, u32[]{:S(2)}) copy-start(bf16[2,384,256]{2,1,0:T(8,128)(2,1)} %get-tuple-element.37.refs_1_) | copy-start | bytes 1179652
  14.9 1.3 collective-permute-start.3
  15.0 28.7 %collective-permute-start.4 = (bf16[6,384,256]{2,1,0:T(8,128)(2,1)}, bf16[6,384,256]{2,1,0:T(8,128)(2,1)}, u32[]{:S(2)}, u32[]{:S(2)}) collective-permute-start(bf16[6,384,256]{2,1,0:T(8,128)(2,1)} %get-tuple-element.34), channel_id=1, source_target_pairs={{0,6},{2,4},{4,2},{6,0},{10,8},{12,14},{14,12},{8,10},{1,7},{3,5},... | collective-permute-start | bytes 3538952 | tf_op jit(solution)/shard_map/ppermute | solution.py:182
  15.7 29.4 %collective-permute-start.5 = (bf16[6,384,256]{2,1,0:T(8,128)(2,1)}, bf16[6,384,256]{2,1,0:T(8,128)(2,1)S(1)}, u32[]{:S(2)}, u32[]{:S(2)}) collective-permute-start(bf16[6,384,256]{2,1,0:T(8,128)(2,1)} %get-tuple-element.35.refs_0_), channel_id=1, source_target_pairs={{0,2},{2,0},{4,6},{6,4},{10,12},{12,10},{14,8},{8,14},{1,3},{3,1},... | collective-permute-start | bytes 3538952 | tf_op jit(solution)/shard_map/ppermute | solution.py:182
  17.7 51.1 %all-to-all-start = ((bf16[32,16,1024]{2,1,0:T(8,128)(2,1)}), bf16[32,16,1024]{2,1,0:T(8,128)(2,1)S(1)}, u32[]{:S(2)}, u32[]{:S(2)}) async-start(bf16[32,16,1024]{2,1,0:T(8,128)(2,1)} %bitcast.65), calls=%async_computation | async-start | bytes 2097152 | tf_op jit(solution)/shard_map/all_to_all | solution.py:228
  45.1 28.7 %collective-permute-start.6 = (bf16[6,384,256]{2,1,0:T(8,128)(2,1)}, bf16[6,384,256]{2,1,0:T(8,128)(2,1)}, u32[]{:S(2)}, u32[]{:S(2)}) collective-permute-start(bf16[6,384,256]{2,1,0:T(8,128)(2,1)} %collective-permute-done.4.refs_2_), channel_id=1, source_target_pairs={{0,2},{2,0},{4,6},{6,4},{10,12},{12,10},{14,8},{8,14},{1,3},{3,1},... | collective-permute-start | bytes 3538952 | tf_op jit(solution)/shard_map/ppermute | solution.py:182
  45.6 13.3 %collective-permute-start.7 = (bf16[2,384,256]{2,1,0:T(8,128)(2,1)S(1)}, bf16[2,384,256]{2,1,0:T(8,128)(2,1)S(1)}, u32[]{:S(2)}, u32[]{:S(2)}) collective-permute-start(bf16[2,384,256]{2,1,0:T(8,128)(2,1)S(1)} %copy-done.1), channel_id=1, source_target_pairs={{0,8},{2,10},{4,12},{6,14},{8,0},{10,2},{12,4},{14,6},{1,9},{3,11}... | collective-permute-start | bytes 1179656 | tf_op jit(solution)/shard_map/ppermute | solution.py:182
  45.9 12.9 %collective-permute-start.8 = (bf16[2,384,256]{2,1,0:T(8,128)(2,1)}, bf16[2,384,256]{2,1,0:T(8,128)(2,1)}, u32[]{:S(2)}, u32[]{:S(2)}) collective-permute-start(bf16[2,384,256]{2,1,0:T(8,128)(2,1)} %get-tuple-element.39), channel_id=1, source_target_pairs={{0,6},{2,4},{4,2},{6,0},{10,8},{12,14},{14,12},{8,10},{1,7},{3,5},... | collective-permute-start | bytes 1179656 | tf_op jit(solution)/shard_map/ppermute | solution.py:182
  58.9 10.0 %collective-permute-start.9 = (bf16[2,384,256]{2,1,0:T(8,128)(2,1)S(1)}, bf16[2,384,256]{2,1,0:T(8,128)(2,1)}, u32[]{:S(2)}, u32[]{:S(2)}) collective-permute-start(bf16[2,384,256]{2,1,0:T(8,128)(2,1)S(1)} %collective-permute-done.7), channel_id=1, source_target_pairs={{2,4},{4,2},{6,0},{0,6},{8,10},{10,8},{12,14},{14,12},{3,5},{5,3},... | collective-permute-start | bytes 1179656 | tf_op jit(solution)/shard_map/ppermute | solution.py:182
  73.8 2.7 %collective-permute-start.10 = (bf16[512,1024]{1,0:T(8,128)(2,1)S(1)}, bf16[512,1024]{1,0:T(8,128)(2,1)S(1)}, u32[]{:S(2)}, u32[]{:S(2)}) collective-permute-start(bf16[512,1024]{1,0:T(8,128)(2,1)S(1)} %bitcast.62), channel_id=1, source_target_pairs={{0,1},{1,0},{2,3},{3,2},{4,5},{5,4},{6,7},{7,6},{8,9},{9,8},{10,11... | collective-permute-start | bytes 3145736 | tf_op jit(solution)/shard_map/ppermute | solution.py:232
  73.8 11.8 %collective-permute-start.11 = (bf16[2,384,256]{2,1,0:T(8,128)(2,1)}, bf16[2,384,256]{2,1,0:T(8,128)(2,1)}, u32[]{:S(2)}, u32[]{:S(2)}) collective-permute-start(bf16[2,384,256]{2,1,0:T(8,128)(2,1)} %collective-permute-done.9), channel_id=1, source_target_pairs={{0,8},{2,10},{4,12},{6,14},{8,0},{10,2},{12,4},{14,6},{1,9},{3,11}... | collective-permute-start | bytes 1179656 | tf_op jit(solution)/shard_map/ppermute | solution.py:182
  73.8 13.1 %collective-permute-start.12 = (bf16[2,384,256]{2,1,0:T(8,128)(2,1)}, bf16[2,384,256]{2,1,0:T(8,128)(2,1)}, u32[]{:S(2)}, u32[]{:S(2)}) collective-permute-start(bf16[2,384,256]{2,1,0:T(8,128)(2,1)} %collective-permute-done.8.refs_3_), channel_id=1, source_target_pairs={{0,2},{2,0},{4,6},{6,4},{10,12},{12,10},{14,8},{8,14},{1,3},{3,1},... | collective-permute-start | bytes 1179656 | tf_op jit(solution)/shard_map/ppermute | solution.py:182
  76.5 1.3 copy-start
  77.7 1.0 copy-start.2
  91.8 2.7 %collective-permute-start.13 = (bf16[512,1024]{1,0:T(8,128)(2,1)S(1)}, bf16[512,1024]{1,0:T(8,128)(2,1)S(1)}, u32[]{:S(2)}, u32[]{:S(2)}) collective-permute-start(bf16[512,1024]{1,0:T(8,128)(2,1)S(1)} %get-tuple-element.46), channel_id=1, source_target_pairs={{0,1},{1,0},{2,3},{3,2},{4,5},{5,4},{6,7},{7,6},{8,9},{9,8},{10,11... | collective-permute-start | bytes 3145736 | tf_op jit(solution)/shard_map/ppermute | solution.py:235
  95.9 39.9 %all-to-all-start.1 = ((bf16[32,16,1024]{2,1,0:T(8,128)(2,1)}), bf16[32,16,1024]{2,1,0:T(8,128)(2,1)S(1)}, u32[]{:S(2)}, u32[]{:S(2)}) async-start(bf16[32,16,1024]{2,1,0:T(8,128)(2,1)} %bitcast.24), calls=%async_computation.1 | async-start | bytes 2097152 | tf_op jit(solution)/shard_map/all_to_all | solution.py:236
  136.4 6.3 %collective-permute-start.14 = (bf16[128,256]{1,0:T(8,128)(2,1)S(1)}, bf16[128,256]{1,0:T(8,128)(2,1)S(1)}, u32[]{:S(2)}, u32[]{:S(2)}) collective-permute-start(bf16[128,256]{1,0:T(8,128)(2,1)S(1)} %get-tuple-element.52), channel_id=1, source_target_pairs={{0,2},{2,4},{4,6},{6,0},{1,3},{3,5},{5,7},{7,1},{8,10},{10,12},{12... | collective-permute-start | bytes 196616 | tf_op jit(solution)/shard_map/ppermute | solution.py:171
  136.7 5.9 %collective-permute-start.15 = (bf16[128,256]{1,0:T(8,128)(2,1)S(1)}, bf16[128,256]{1,0:T(8,128)(2,1)S(1)}, u32[]{:S(2)}, u32[]{:S(2)}) collective-permute-start(bf16[128,256]{1,0:T(8,128)(2,1)S(1)} %get-tuple-element.54), channel_id=1, source_target_pairs={{0,4},{2,6},{4,0},{6,2},{1,5},{3,7},{5,1},{7,3},{8,12},{10,14},{12... | collective-permute-start | bytes 196616 | tf_op jit(solution)/shard_map/ppermute | solution.py:171
  138.6 4.9 %collective-permute-start.16 = (bf16[128,256]{1,0:T(8,128)(2,1)S(1)}, bf16[128,256]{1,0:T(8,128)(2,1)S(1)}, u32[]{:S(2)}, u32[]{:S(2)}) collective-permute-start(bf16[128,256]{1,0:T(8,128)(2,1)S(1)} %get-tuple-element.53), channel_id=1, source_target_pairs={{0,6},{2,0},{4,2},{6,4},{1,7},{3,1},{5,3},{7,5},{8,14},{10,8},{12,... | collective-permute-start | bytes 196616 | tf_op jit(solution)/shard_map/ppermute | solution.py:171

commit v7 on v6

--- a/solution.py
+++ b/solution.py
@@ -72,73 +72,80 @@
     return picked[:2], picked[2:]
 
 
-def ffn_kernel(count, place_ref, arrived, across, *refs):
-    lying, added, (keep, give, hidden, held_shards, sems) = refs[:count], refs[count:-5], refs[-5:]
-    total_blocks = held_shards.shape[1]
-    copies, first = [], 0
-    for n, piece in enumerate(lying):
-        into = held_shards.at[first // total_blocks, pl.ds(first % total_blocks, piece.shape[0])]
-        copies.append((first // total_blocks, pltpu.make_async_copy(piece, into, sems.at[n])))
-        first += piece.shape[0]
-    for _, copy in copies:
-        copy.start()
-    shards = [held_shards.at[k] for k in range(held_shards.shape[0])]
+def ffn_kernel(sizes, place_ref, arrived, across, *refs):
+    pieces, added = refs[: len(sizes)], refs[len(sizes) : -6]
+    keep, give, joined, downs, hidden, sems = refs[-6:]
     row, core = place_ref[0], place_ref[1]
     f32 = jnp.float32
-    rows, held = arrived.shape
+    held = arrived.shape[1]
     ring = held // block
     unit = block // 2
 
-    def source(j, parity):
-        return 2 * lax.rem(row - j + ring, ring) + parity
-
-    def target(j, parity):
-        return 2 * lax.rem(row + j, ring) + parity
-
-    for k, shard in enumerate(shards):
-        for shard_of, copy in copies:
-            if shard_of == k:
+    copies, first = [], 0
+    for piece, size in zip(pieces, sizes):
+        for j in range(size):
+            k, i = divmod(first + j, 2 * ring)
+            mine = lax.rem(i % 2 + core, 2)
+            source = mine * ring + lax.rem(row - i // 2 + ring, ring)
+            target = lax.rem(i // 2 - row + ring, ring)
+            gate_up = joined.at[k, source]
+            lanes = pl.ds(pl.multiple_of(target * block, block), block)
+            down = downs.at[mine, pl.ds(k * unit, unit), lanes]
+            for turn, (part, into) in enumerate(
+                ((piece.at[j, pl.ds(0, block)], gate_up), (piece.at[j, pl.ds(block, unit)], down))
+            ):
+                sem = sems.at[2 * (first + j) + turn]
+                copies.append((k, turn, pltpu.make_async_copy(part, into, sem)))
+        first += size
+    for turn in range(2):
+        for _, when, copy in copies:
+            if when == turn:
+                copy.start()
+
+    for k in range(joined.shape[0]):
+        for shard_of, turn, copy in copies:
+            if shard_of == k and turn == 0:
                 copy.wait()
-        both = jnp.zeros((rows, block), f32)
-        for j in range(ring):
-            lanes = pl.ds(j * block, block)
-            for part, parity in ((arrived, core), (across, 1 - core)):
-                both += jnp.dot(
-                    part[:, lanes], shard[source(j, parity), :block, :], preferred_element_type=f32
-                )
+        mine = joined[k, :ring].reshape(held, block)
+        theirs = joined[k, ring:].reshape(held, block)
+        both = jnp.dot(arrived[...], mine, preferred_element_type=f32)
+        both += jnp.dot(across[...], theirs, preferred_element_type=f32)
         gate_val, up_val = both[:, :unit], both[:, unit:]
         silu = gate_val / (1.0 + jnp.exp(-gate_val))
         hidden[:, pl.ds(k * unit, unit)] = (silu * up_val).astype(hidden.dtype)
-    for which, (parity, out) in enumerate(((core, keep), (1 - core, give))):
-        for j in range(ring):
-            lanes = pl.ds(j * block, block)
-            total = added[which][:, lanes] if added else jnp.zeros((rows, block), f32)
-            down = jnp.concatenate([shard[target(j, parity), block:, :] for shard in shards], axis=0)
-            total += jnp.dot(hidden[...], down, preferred_element_type=f32)
-            out[:, lanes] = total.astype(out.dtype)
+    for _, turn, copy in copies:
+        if turn == 1:
+            copy.wait()
+    for which, out in enumerate((keep, give)):
+        total = jnp.dot(hidden[...], downs[which], preferred_element_type=f32)
+        if added:
+            total += added[which][...]
+        out[...] = total.astype(out.dtype)
 
 
 def expert_rows(place, arrived, across, pieces, added, give_type):
     rows, held = arrived.shape
-    unit, width, count = block // 2, 2 * held, len(pieces)
+    unit, width = block // 2, 2 * held
+    sizes = tuple(piece.shape[0] for piece in pieces)
     blocks = width // block
-    shards = sum(piece.shape[0] for piece in pieces) // blocks
+    shards = sum(sizes) // blocks
     whole = pl.BlockSpec(memory_space=pltpu.VMEM)
     return pl.pallas_call(
-        functools.partial(ffn_kernel, count),
+        functools.partial(ffn_kernel, sizes),
         out_shape=(
             jax.ShapeDtypeStruct((rows, held), jnp.float32),
             jax.ShapeDtypeStruct((rows, held), give_type),
         ),
         in_specs=[pl.BlockSpec(memory_space=pltpu.SMEM)]
         + [whole] * 2
-        + [pl.BlockSpec(memory_space=pl.ANY)] * count
+        + [pl.BlockSpec(memory_space=pl.ANY)] * len(sizes)
         + [whole] * len(added),
         out_specs=(whole, whole),
         scratch_shapes=[
+            pltpu.VMEM((shards, blocks, block, block), jnp.bfloat16),
+            pltpu.VMEM((2, shards * unit, held), jnp.bfloat16),
             pltpu.VMEM((rows, shards * unit), jnp.bfloat16),
-            pltpu.VMEM((shards, blocks, *pieces[0].shape[1:]), jnp.bfloat16),
-            pltpu.SemaphoreType.DMA((count,)),
+            pltpu.SemaphoreType.DMA((2 * shards * blocks,)),
         ],
         compiler_params=pltpu.CompilerParams(vmem_limit_bytes=40 * 2**20),
         cost_estimate=pl.CostEstimate(
@@ -192,13 +199,12 @@
     passed = send(after(send(own[1], other_row), crossed[1]), near_lent)
     lent = send(passed, other_row)
 
+    routes = after(routes, own[0])
+
     expert_iota = jnp.arange(expert_count, dtype=jnp.int32)
     hits = jnp.any(routes[:, :, None] == expert_iota[None, None, :], axis=1)
     earlier = jnp.tril(jnp.ones((group_size, group_size), bf16), -1)
     position = jnp.dot(earlier, hits.astype(bf16), preferred_element_type=f32)
-    shifted = jnp.where(hits, router_logits, -jnp.inf)
-    shifted = jnp.exp(shifted - jnp.max(shifted, axis=1, keepdims=True))
-    gates = shifted / jnp.sum(shifted, axis=1, keepdims=True)
 
     def of_kind(table):
         table = table.reshape(group_size, ep_count, local_experts)
@@ -206,7 +212,6 @@
 
     slot = jnp.where(of_kind(hits), of_kind(position), -1.0)
     slot = slot - (peers % split * share).astype(f32)[None, :]
-    gates = of_kind(gates)
     slot_iota = jnp.arange(share, dtype=jnp.int32).astype(f32)
 
     floated = [part[:group_size].astype(f32) for part in parts]
@@ -237,6 +242,9 @@
         summed.astype(bf16).reshape(ep_count, share, -1), ep, split_axis=0, concat_axis=0, tiled=True
     ).reshape(ep_count * share, -1)
 
+    shifted = jnp.where(hits, after(router_logits, arrived), -jnp.inf)
+    shifted = jnp.exp(shifted - jnp.max(shifted, axis=1, keepdims=True))
+    gates = of_kind(shifted / jnp.sum(shifted, axis=1, keepdims=True))
     weight = jnp.where(slot[:, :, None] == slot_iota[None, None, :], gates[:, :, None], 0.0)
     weight = weight.reshape(group_size, ep_count * share)
     high = lax.reduce_precision(weight, 8, 7)

time: 145 us -> 144 us (level)
  other arithmetic: 7.1 us -> 4.21 us
  Pallas kernels: 13.1 us -> 15.6 us
  waiting for transfers between devices: 82.2 us -> 79.9 us
  starting transfers between devices: 37 us -> 39 us
    ppermute x8, waiting for transfers between devices: 45.6 us -> 42.7 us  [send(): return lax.ppermute(one, ('pair', 'x'), pairs)]
    pallas_call x2, Pallas kernels: 9.1 us -> 11.6 us  [expert_rows(): pl.pallas_call(functools.partial(ffn_kernel, sizes), out_shape=(jax.Shape...]
    ppermute x8, starting transfers between devices: 4.64 us -> 6.87 us  [send(): return lax.ppermute(one, ('pair', 'x'), pairs)]
    ppermute x6, waiting for transfers between devices: 3.8 us -> 5.37 us  [ring_send(): return lax.ppermute(one, 'x', pairs)]
  transfers between devices with their start and end apart: 19 -> 19, of which waited for: 12 -> 13; matrix products, arithmetic and copies ran while one was open for 4% -> 2% of each run, Pallas kernels for 6% -> 7%
where the time goes in v7:
time: 144 us; the launch traced here: 143 us
  waiting for transfers between devices  79.9 us (55%)
  starting transfers between devices  39 us (27%)
  Pallas kernels  15.6 us (11%)
  other arithmetic  4.21 us (3%)
  local copies, waits for them, and re-layouts  2.48 us (2%)
  matrix products  2.07 us (1%)
    ppermute x8, waiting for transfers between devices, send(): return lax.ppermute(one, ('pair', 'x'), pairs)  42.7 us
    all_to_all x1, waiting for transfers between devices, on_device(): lax.all_to_all(summed.astype(bf16).reshape(ep_count, share, -1), ep, spli...  28 us
    all_to_all x1, starting transfers between devices, on_device(): lax.all_to_all(summed.astype(bf16).reshape(ep_count, share, -1), ep, spli...  11.7 us
    pallas_call x2, Pallas kernels, expert_rows(): pl.pallas_call(functools.partial(ffn_kernel, sizes), out_shape=(jax.Shape...  11.6 us
    all_to_all x1, starting transfers between devices, on_device(): lax.all_to_all(outgoing.reshape(ep_count, share, -1), ep, split_axis=0, c...  11.5 us
    ppermute x6, starting transfers between devices, ring_send(): return lax.ppermute(one, 'x', pairs)  8.73 us
    ppermute x8, starting transfers between devices, send(): return lax.ppermute(one, ('pair', 'x'), pairs)  6.87 us
    ppermute x6, waiting for transfers between devices, ring_send(): return lax.ppermute(one, 'x', pairs)  5.37 us
  transfers between devices with their start and end apart: 19, of which 13 were waited for; matrix products, arithmetic and copies ran while one was open for 2% of the time, Pallas kernels for 7%

profile of v7, /device:TPU:8, one launch (start us, length us, event | category | flops | bytes accessed | tf_op | source)
XLA Modules:
  0.0 143.5 jit_solution(4261862379836827418)
XLA Ops:
  0.0 0.0 copy-start.4
  0.0 0.9 pad_select_fusion
  0.9 1.6 %collective-permute-start = (bf16[144,256]{1,0:T(8,128)(2,1)S(1)}, bf16[144,256]{1,0:T(8,128)(2,1)S(1)}, u32[]{:S(2)}, u32[]{:S(2)}) collective-permute-start(bf16[144,256]{1,0:T(8,128)(2,1)S(1)} %pad_select_fusion), channel_id=1, source_target_pairs={{0,2},{2,4},{4,6},{6,0},{1,3},{3,5},{5,7},{7,1},{8,10},{10,12},{12... | collective-permute-start | bytes 221192 | tf_op jit(solution)/shard_map/ppermute | solution.py:178
  2.5 2.7 %collective-permute-start.1 = (bf16[144,256]{1,0:T(8,128)(2,1)S(1)}, bf16[144,256]{1,0:T(8,128)(2,1)S(1)}, u32[]{:S(2)}, u32[]{:S(2)}) collective-permute-start(bf16[144,256]{1,0:T(8,128)(2,1)S(1)} %pad_select_fusion), channel_id=1, source_target_pairs={{0,4},{2,6},{4,0},{6,2},{1,5},{3,7},{5,1},{7,3},{8,12},{10,14},{12... | collective-permute-start | bytes 221192 | tf_op jit(solution)/shard_map/ppermute | solution.py:178
  5.2 1.4 collective-permute-start.2
  6.7 0.1 eq.78
  6.8 4.0 %shard_map.73 = (bf16[6,384,256]{2,1,0:T(8,128)(2,1)}, bf16[2,384,256]{2,1,0:T(8,128)(2,1)}, bf16[6,384,256]{2,1,0:T(8,128)(2,1)}, bf16[2,384,256]{2,1,0:T(8,128)(2,1)}) custom-call(s32[1]{0:T(128)} %bitcast.kind_ref, bf16[2,2048,128]{2,1,0:T(8,128)(2,1)} %gate.1, bf16[2,2048,128]{2,1,0:T(8,128)(2,1)} %up.1, bf16[2,128,2048]{2,1,0:T(8,128)(2,1)} %down.1), custom_call_target="tpu_custom_call" | custom-call | bytes 6291456 | tf_op jit(solution)/shard_map/pallas_call | solution.py:62
  10.8 0.0 collective-permute-done
  10.8 0.0 collective-permute-done.1
  10.8 0.0 collective-permute-done.2
  10.8 0.1 fusion.13
  10.9 0.1 fusion.19
  11.1 1.5 %collective-permute-start.5 = (bf16[6,384,256]{2,1,0:T(8,128)(2,1)}, bf16[6,384,256]{2,1,0:T(8,128)(2,1)S(1)}, u32[]{:S(2)}, u32[]{:S(2)}) collective-permute-start(bf16[6,384,256]{2,1,0:T(8,128)(2,1)} %get-tuple-element.32.refs_0_), channel_id=1, source_target_pairs={{0,2},{2,0},{4,6},{6,4},{10,12},{12,10},{14,8},{8,14},{1,3},{3,1},... | collective-permute-start | bytes 3538952 | tf_op jit(solution)/shard_map/ppermute | solution.py:189
  12.6 0.0 copy-done.4
  12.7 0.1 collective-permute-start.3
  12.8 0.1 collective-permute-start.4
  12.9 0.2 fusion.30
  13.1 0.1 subtract_bitcast_fusion
  13.2 0.1 fusion.38
  13.3 0.1 bitcast_compare_fusion
  13.5 0.5 collective-permute-done.3
  13.9 0.1 fusion.15
  14.1 1.4 convolution_convert_fusion
  15.5 11.5 %all-to-all-start = ((bf16[32,16,1024]{2,1,0:T(8,128)(2,1)}), bf16[32,16,1024]{2,1,0:T(8,128)(2,1)S(1)}, u32[]{:S(2)}, u32[]{:S(2)}) async-start(bf16[32,16,1024]{2,1,0:T(8,128)(2,1)} %bitcast.65), calls=%async_computation | async-start | bytes 2097152 | tf_op jit(solution)/shard_map/all_to_all | solution.py:233
  27.0 14.5 %collective-permute-done.4.refs_2_ = bf16[6,384,256]{2,1,0:T(8,128)(2,1)} collective-permute-done((bf16[6,384,256]{2,1,0:T(8,128)(2,1)}, bf16[6,384,256]{2,1,0:T(8,128)(2,1)}, u32[]{:S(2)}, u32[]{:S(2)}) %collective-permute-start.4) | collective-permute-done | bytes 1179680 | tf_op jit(solution)/shard_map/ppermute | solution.py:189
  41.5 0.0 collective-permute-done.5.refs_0_
  41.5 1.8 %collective-permute-start.6 = (bf16[6,384,256]{2,1,0:T(8,128)(2,1)}, bf16[6,384,256]{2,1,0:T(8,128)(2,1)}, u32[]{:S(2)}, u32[]{:S(2)}) collective-permute-start(bf16[6,384,256]{2,1,0:T(8,128)(2,1)} %collective-permute-done.4.refs_2_), channel_id=1, source_target_pairs={{0,2},{2,0},{4,6},{6,4},{10,12},{12,10},{14,8},{8,14},{1,3},{3,1},... | collective-permute-start | bytes 3538952 | tf_op jit(solution)/shard_map/ppermute | solution.py:189
  43.4 0.0 copy-done.1
  43.4 0.0 collective-permute-start.7
  43.4 1.0 collective-permute-start.8
  44.4 12.5 %collective-permute-done.7 = bf16[2,384,256]{2,1,0:T(8,128)(2,1)S(1)} collective-permute-done((bf16[2,384,256]{2,1,0:T(8,128)(2,1)S(1)}, bf16[2,384,256]{2,1,0:T(8,128)(2,1)S(1)}, u32[]{:S(2)}, u32[]{:S(2)}) %collective-permute-start.7) | collective-permute-done | bytes 393248 | tf_op jit(solution)/shard_map/ppermute | solution.py:189
  56.9 0.0 collective-permute-done.8.refs_3_
  56.9 0.6 collective-permute-start.9
  57.5 9.7 %collective-permute-done.9 = bf16[2,384,256]{2,1,0:T(8,128)(2,1)} collective-permute-done((bf16[2,384,256]{2,1,0:T(8,128)(2,1)S(1)}, bf16[2,384,256]{2,1,0:T(8,128)(2,1)}, u32[]{:S(2)}, u32[]{:S(2)}) %collective-permute-start.9) | collective-permute-done | bytes 393248 | tf_op jit(solution)/shard_map/ppermute | solution.py:189
  67.2 0.0 all-to-all-done
  67.2 3.4 %collective-permute-done.6.refs_2_ = bf16[6,384,256]{2,1,0:T(8,128)(2,1)} collective-permute-done((bf16[6,384,256]{2,1,0:T(8,128)(2,1)}, bf16[6,384,256]{2,1,0:T(8,128)(2,1)}, u32[]{:S(2)}, u32[]{:S(2)}) %collective-permute-start.6) | collective-permute-done | bytes 1179680 | tf_op jit(solution)/shard_map/ppermute | solution.py:189
  70.6 0.0 collective-permute-start.10
  70.6 0.0 collective-permute-start.11
  70.6 1.8 %collective-permute-start.12 = (bf16[2,384,256]{2,1,0:T(8,128)(2,1)}, bf16[2,384,256]{2,1,0:T(8,128)(2,1)}, u32[]{:S(2)}, u32[]{:S(2)}) collective-permute-start(bf16[2,384,256]{2,1,0:T(8,128)(2,1)} %collective-permute-done.8.refs_3_), channel_id=1, source_target_pairs={{0,2},{2,0},{4,6},{6,4},{10,12},{12,10},{14,8},{8,14},{1,3},{3,1},... | collective-permute-start | bytes 1179656 | tf_op jit(solution)/shard_map/ppermute | solution.py:189
  72.4 0.1 pad_add_fusion.place_ref
  72.5 0.8 collective-permute-done.10.across
  73.2 1.3 copy-done
  74.5 1.0 copy-done.2
  75.5 5.5 %shard_map.74 = (f32[512,1024]{1,0:T(8,128)S(1)}, f32[512,1024]{1,0:T(8,128)S(1)}) custom-call(s32[2]{0:T(128)S(1)} %pad_add_fusion.place_ref, bf16[512,1024]{1,0:T(8,128)(2,1)S(1)} %bitcast.63, bf16[512,1024]{1,0:T(8,128)(2,1)S(1)} %collective-permute-done.10.across, bf16[6,384,256]{2,1,0:T(8,128)(2,1)S(1)} %copy-done, bf16[2,384,256]{2,1,0:T(8,128)(2,1)S(1)} %copy-done.2, ...), custom_call_target="tpu_custom_call" | custom-call | flops 268435456 | bytes 1048576 | tf_op jit(solution)/shard_map/pallas_call | solution.py:133
  81.1 1.4 collective-permute-done.11.refs_1_
  82.4 1.2 collective-permute-done.12.refs_3_
  83.6 6.1 %shard_map.75 = (f32[512,1024]{1,0:T(8,128)S(1)}, bf16[512,1024]{1,0:T(8,128)(2,1)S(1)}) custom-call(s32[2]{0:T(128)S(1)} %pad_add_fusion.place_ref, bf16[512,1024]{1,0:T(8,128)(2,1)S(1)} %bitcast.64, bf16[512,1024]{1,0:T(8,128)(2,1)S(1)} %collective-permute-done.10.across, bf16[6,384,256]{2,1,0:T(8,128)(2,1)S(1)} %collective-permute-done.5.refs_0_, ...), custom_call_target="tpu_custom_call" | custom-call | flops 268435456 | bytes 1048576 | tf_op jit(solution)/shard_map/pallas_call | solution.py:133
  89.7 0.1 collective-permute-start.13
  89.8 2.6 %collective-permute-done.13 = bf16[512,1024]{1,0:T(8,128)(2,1)S(1)} collective-permute-done((bf16[512,1024]{1,0:T(8,128)(2,1)S(1)}, bf16[512,1024]{1,0:T(8,128)(2,1)S(1)}, u32[]{:S(2)}, u32[]{:S(2)}) %collective-permute-start.13) | collective-permute-done | bytes 1048608 | tf_op jit(solution)/shard_map/ppermute | solution.py:240
  92.5 1.4 add_convert_fusion
  93.9 11.7 %all-to-all-start.1 = ((bf16[32,16,1024]{2,1,0:T(8,128)(2,1)}), bf16[32,16,1024]{2,1,0:T(8,128)(2,1)S(1)}, u32[]{:S(2)}, u32[]{:S(2)}) async-start(bf16[32,16,1024]{2,1,0:T(8,128)(2,1)} %bitcast.24), calls=%async_computation.1 | async-start | bytes 2097152 | tf_op jit(solution)/shard_map/all_to_all | solution.py:241
  105.5 0.0 copy-done.3
  105.7 0.1 select_bitcast_fusion
  105.7 0.1 reduce-precision_convert_fusion
  105.9 28.0 %all-to-all-done.1 = bf16[32,16,1024]{2,1,0:T(8,128)(2,1)S(1)} async-done(((bf16[32,16,1024]{2,1,0:T(8,128)(2,1)}), bf16[32,16,1024]{2,1,0:T(8,128)(2,1)S(1)}, u32[]{:S(2)}, u32[]{:S(2)}) %all-to-all-start.1) | async-done | bytes 1048608 | tf_op jit(solution)/shard_map/all_to_all | solution.py:241
  133.9 0.5 fusion.8
  134.4 0.1 fusion.51
  134.5 1.9 %collective-permute-start.16 = (bf16[128,256]{1,0:T(8,128)(2,1)S(1)}, bf16[128,256]{1,0:T(8,128)(2,1)S(1)}, u32[]{:S(2)}, u32[]{:S(2)}) collective-permute-start(bf16[128,256]{1,0:T(8,128)(2,1)S(1)} %get-tuple-element.57), channel_id=1, source_target_pairs={{0,6},{2,0},{4,2},{6,4},{1,7},{3,1},{5,3},{7,5},{8,14},{10,8},{12,... | collective-permute-start | bytes 196616 | tf_op jit(solution)/shard_map/ppermute | solution.py:178
  136.4 0.5 collective-permute-start.15
  136.9 0.6 collective-permute-start.14
  137.5 1.3 collective-permute-done.16
  138.8 3.4 %collective-permute-done.15 = bf16[128,256]{1,0:T(8,128)(2,1)S(1)} collective-permute-done((bf16[128,256]{1,0:T(8,128)(2,1)S(1)}, bf16[128,256]{1,0:T(8,128)(2,1)S(1)}, u32[]{:S(2)}, u32[]{:S(2)}) %collective-permute-start.15) | collective-permute-done | bytes 65568 | tf_op jit(solution)/shard_map/ppermute | solution.py:178
  142.2 0.7 collective-permute-done.14
  142.8 0.7 fusion.27
  (23 shorter events, 0.3 us)
Async XLA Ops:
  0.0 12.6 %copy-start.4 = (s32[128,8]{0,1:T(8,128)S(1)}, s32[128,8]{0,1:T(8,128)}, u32[]{:S(2)}) copy-start(s32[128,8]{0,1:T(8,128)} %param.10) | copy-start | bytes 12292
  0.9 9.8 %collective-permute-start = (bf16[144,256]{1,0:T(8,128)(2,1)S(1)}, bf16[144,256]{1,0:T(8,128)(2,1)S(1)}, u32[]{:S(2)}, u32[]{:S(2)}) collective-permute-start(bf16[144,256]{1,0:T(8,128)(2,1)S(1)} %pad_select_fusion), channel_id=1, source_target_pairs={{0,2},{2,4},{4,6},{6,0},{1,3},{3,5},{5,7},{7,1},{8,10},{10,12},{12... | collective-permute-start | bytes 221192 | tf_op jit(solution)/shard_map/ppermute | solution.py:178
  2.5 8.3 %collective-permute-start.1 = (bf16[144,256]{1,0:T(8,128)(2,1)S(1)}, bf16[144,256]{1,0:T(8,128)(2,1)S(1)}, u32[]{:S(2)}, u32[]{:S(2)}) collective-permute-start(bf16[144,256]{1,0:T(8,128)(2,1)S(1)} %pad_select_fusion), channel_id=1, source_target_pairs={{0,4},{2,6},{4,0},{6,2},{1,5},{3,7},{5,1},{7,3},{8,12},{10,14},{12... | collective-permute-start | bytes 221192 | tf_op jit(solution)/shard_map/ppermute | solution.py:178
  5.2 5.6 %collective-permute-start.2 = (bf16[144,256]{1,0:T(8,128)(2,1)S(1)}, bf16[144,256]{1,0:T(8,128)(2,1)S(1)}, u32[]{:S(2)}, u32[]{:S(2)}) collective-permute-start(bf16[144,256]{1,0:T(8,128)(2,1)S(1)} %pad_select_fusion), channel_id=1, source_target_pairs={{0,6},{2,0},{4,2},{6,4},{1,7},{3,1},{5,3},{7,5},{8,14},{10,8},{12,... | collective-permute-start | bytes 221192 | tf_op jit(solution)/shard_map/ppermute | solution.py:178
  11.1 30.5 %collective-permute-start.5 = (bf16[6,384,256]{2,1,0:T(8,128)(2,1)}, bf16[6,384,256]{2,1,0:T(8,128)(2,1)S(1)}, u32[]{:S(2)}, u32[]{:S(2)}) collective-permute-start(bf16[6,384,256]{2,1,0:T(8,128)(2,1)} %get-tuple-element.32.refs_0_), channel_id=1, source_target_pairs={{0,2},{2,0},{4,6},{6,4},{10,12},{12,10},{14,8},{8,14},{1,3},{3,1},... | collective-permute-start | bytes 3538952 | tf_op jit(solution)/shard_map/ppermute | solution.py:189
  12.7 1.2 collective-permute-start.3
  12.8 28.7 %collective-permute-start.4 = (bf16[6,384,256]{2,1,0:T(8,128)(2,1)}, bf16[6,384,256]{2,1,0:T(8,128)(2,1)}, u32[]{:S(2)}, u32[]{:S(2)}) collective-permute-start(bf16[6,384,256]{2,1,0:T(8,128)(2,1)} %get-tuple-element.38), channel_id=1, source_target_pairs={{0,6},{2,4},{4,2},{6,0},{10,8},{12,14},{14,12},{8,10},{1,7},{3,5},... | collective-permute-start | bytes 3538952 | tf_op jit(solution)/shard_map/ppermute | solution.py:189
  13.2 30.1 %copy-start.1 = (bf16[2,384,256]{2,1,0:T(8,128)(2,1)S(1)}, bf16[2,384,256]{2,1,0:T(8,128)(2,1)}, u32[]{:S(2)}) copy-start(bf16[2,384,256]{2,1,0:T(8,128)(2,1)} %get-tuple-element.40.refs_1_) | copy-start | bytes 1179652
  15.5 51.7 %all-to-all-start = ((bf16[32,16,1024]{2,1,0:T(8,128)(2,1)}), bf16[32,16,1024]{2,1,0:T(8,128)(2,1)S(1)}, u32[]{:S(2)}, u32[]{:S(2)}) async-start(bf16[32,16,1024]{2,1,0:T(8,128)(2,1)} %bitcast.65), calls=%async_computation | async-start | bytes 2097152 | tf_op jit(solution)/shard_map/all_to_all | solution.py:233
  41.5 29.0 %collective-permute-start.6 = (bf16[6,384,256]{2,1,0:T(8,128)(2,1)}, bf16[6,384,256]{2,1,0:T(8,128)(2,1)}, u32[]{:S(2)}, u32[]{:S(2)}) collective-permute-start(bf16[6,384,256]{2,1,0:T(8,128)(2,1)} %collective-permute-done.4.refs_2_), channel_id=1, source_target_pairs={{0,2},{2,0},{4,6},{6,4},{10,12},{12,10},{14,8},{8,14},{1,3},{3,1},... | collective-permute-start | bytes 3538952 | tf_op jit(solution)/shard_map/ppermute | solution.py:189
  43.4 13.5 %collective-permute-start.7 = (bf16[2,384,256]{2,1,0:T(8,128)(2,1)S(1)}, bf16[2,384,256]{2,1,0:T(8,128)(2,1)S(1)}, u32[]{:S(2)}, u32[]{:S(2)}) collective-permute-start(bf16[2,384,256]{2,1,0:T(8,128)(2,1)S(1)} %copy-done.1), channel_id=1, source_target_pairs={{0,8},{2,10},{4,12},{6,14},{8,0},{10,2},{12,4},{14,6},{1,9},{3,11}... | collective-permute-start | bytes 1179656 | tf_op jit(solution)/shard_map/ppermute | solution.py:189
  43.4 13.5 %collective-permute-start.8 = (bf16[2,384,256]{2,1,0:T(8,128)(2,1)}, bf16[2,384,256]{2,1,0:T(8,128)(2,1)}, u32[]{:S(2)}, u32[]{:S(2)}) collective-permute-start(bf16[2,384,256]{2,1,0:T(8,128)(2,1)} %get-tuple-element.42), channel_id=1, source_target_pairs={{0,6},{2,4},{4,2},{6,0},{10,8},{12,14},{14,12},{8,10},{1,7},{3,5},... | collective-permute-start | bytes 1179656 | tf_op jit(solution)/shard_map/ppermute | solution.py:189
  56.9 10.3 %collective-permute-start.9 = (bf16[2,384,256]{2,1,0:T(8,128)(2,1)S(1)}, bf16[2,384,256]{2,1,0:T(8,128)(2,1)}, u32[]{:S(2)}, u32[]{:S(2)}) collective-permute-start(bf16[2,384,256]{2,1,0:T(8,128)(2,1)S(1)} %collective-permute-done.7), channel_id=1, source_target_pairs={{2,4},{4,2},{6,0},{0,6},{8,10},{10,8},{12,14},{14,12},{3,5},{5,3},... | collective-permute-start | bytes 1179656 | tf_op jit(solution)/shard_map/ppermute | solution.py:189
  70.6 2.7 %collective-permute-start.10 = (bf16[512,1024]{1,0:T(8,128)(2,1)S(1)}, bf16[512,1024]{1,0:T(8,128)(2,1)S(1)}, u32[]{:S(2)}, u32[]{:S(2)}) collective-permute-start(bf16[512,1024]{1,0:T(8,128)(2,1)S(1)} %bitcast.62), channel_id=1, source_target_pairs={{0,1},{1,0},{2,3},{3,2},{4,5},{5,4},{6,7},{7,6},{8,9},{9,8},{10,11... | collective-permute-start | bytes 3145736 | tf_op jit(solution)/shard_map/ppermute | solution.py:237
  70.6 11.8 %collective-permute-start.11 = (bf16[2,384,256]{2,1,0:T(8,128)(2,1)}, bf16[2,384,256]{2,1,0:T(8,128)(2,1)}, u32[]{:S(2)}, u32[]{:S(2)}) collective-permute-start(bf16[2,384,256]{2,1,0:T(8,128)(2,1)} %collective-permute-done.9), channel_id=1, source_target_pairs={{0,8},{2,10},{4,12},{6,14},{8,0},{10,2},{12,4},{14,6},{1,9},{3,11}... | collective-permute-start | bytes 1179656 | tf_op jit(solution)/shard_map/ppermute | solution.py:189
  70.6 13.1 %collective-permute-start.12 = (bf16[2,384,256]{2,1,0:T(8,128)(2,1)}, bf16[2,384,256]{2,1,0:T(8,128)(2,1)}, u32[]{:S(2)}, u32[]{:S(2)}) collective-permute-start(bf16[2,384,256]{2,1,0:T(8,128)(2,1)} %collective-permute-done.8.refs_3_), channel_id=1, source_target_pairs={{0,2},{2,0},{4,6},{6,4},{10,12},{12,10},{14,8},{8,14},{1,3},{3,1},... | collective-permute-start | bytes 1179656 | tf_op jit(solution)/shard_map/ppermute | solution.py:189
  73.2 1.3 copy-start
  74.5 1.0 copy-start.2
  89.7 2.7 %collective-permute-start.13 = (bf16[512,1024]{1,0:T(8,128)(2,1)S(1)}, bf16[512,1024]{1,0:T(8,128)(2,1)S(1)}, u32[]{:S(2)}, u32[]{:S(2)}) collective-permute-start(bf16[512,1024]{1,0:T(8,128)(2,1)S(1)} %get-tuple-element.50), channel_id=1, source_target_pairs={{0,1},{1,0},{2,3},{3,2},{4,5},{5,4},{6,7},{7,6},{8,9},{9,8},{10,11... | collective-permute-start | bytes 3145736 | tf_op jit(solution)/shard_map/ppermute | solution.py:240
  93.9 11.7 %copy-start.3 = (f32[128,64]{0,1:T(8,128)S(1)}, f32[128,64]{0,1:T(8,128)}, u32[]{:S(2)}) copy-start(f32[128,64]{0,1:T(8,128)} %param.9) | copy-start | bytes 98308
  93.9 40.0 %all-to-all-start.1 = ((bf16[32,16,1024]{2,1,0:T(8,128)(2,1)}), bf16[32,16,1024]{2,1,0:T(8,128)(2,1)S(1)}, u32[]{:S(2)}, u32[]{:S(2)}) async-start(bf16[32,16,1024]{2,1,0:T(8,128)(2,1)} %bitcast.24), calls=%async_computation.1 | async-start | bytes 2097152 | tf_op jit(solution)/shard_map/all_to_all | solution.py:241
  134.5 4.3 %collective-permute-start.16 = (bf16[128,256]{1,0:T(8,128)(2,1)S(1)}, bf16[128,256]{1,0:T(8,128)(2,1)S(1)}, u32[]{:S(2)}, u32[]{:S(2)}) collective-permute-start(bf16[128,256]{1,0:T(8,128)(2,1)S(1)} %get-tuple-element.57), channel_id=1, source_target_pairs={{0,6},{2,0},{4,2},{6,4},{1,7},{3,1},{5,3},{7,5},{8,14},{10,8},{12,... | collective-permute-start | bytes 196616 | tf_op jit(solution)/shard_map/ppermute | solution.py:178
  136.4 5.8 %collective-permute-start.15 = (bf16[128,256]{1,0:T(8,128)(2,1)S(1)}, bf16[128,256]{1,0:T(8,128)(2,1)S(1)}, u32[]{:S(2)}, u32[]{:S(2)}) collective-permute-start(bf16[128,256]{1,0:T(8,128)(2,1)S(1)} %get-tuple-element.58), channel_id=1, source_target_pairs={{0,4},{2,6},{4,0},{6,2},{1,5},{3,7},{5,1},{7,3},{8,12},{10,14},{12... | collective-permute-start | bytes 196616 | tf_op jit(solution)/shard_map/ppermute | solution.py:178
  136.9 6.0 %collective-permute-start.14 = (bf16[128,256]{1,0:T(8,128)(2,1)S(1)}, bf16[128,256]{1,0:T(8,128)(2,1)S(1)}, u32[]{:S(2)}, u32[]{:S(2)}) collective-permute-start(bf16[128,256]{1,0:T(8,128)(2,1)S(1)} %get-tuple-element.56), channel_id=1, source_target_pairs={{0,2},{2,4},{4,6},{6,0},{1,3},{3,5},{5,7},{7,1},{8,10},{10,12},{12... | collective-permute-start | bytes 196616 | tf_op jit(solution)/shard_map/ppermute | solution.py:178

commit v8 on v6

--- a/solution.py
+++ b/solution.py
@@ -73,7 +73,7 @@
 
 
 def ffn_kernel(count, place_ref, arrived, across, *refs):
-    lying, added, (keep, give, hidden, held_shards, sems) = refs[:count], refs[count:-5], refs[-5:]
+    lying, (keep, give, hidden, held_shards, sems) = refs[:count], refs[count:]
     total_blocks = held_shards.shape[1]
     copies, first = [], 0
     for n, piece in enumerate(lying):
@@ -109,16 +109,15 @@
         gate_val, up_val = both[:, :unit], both[:, unit:]
         silu = gate_val / (1.0 + jnp.exp(-gate_val))
         hidden[:, pl.ds(k * unit, unit)] = (silu * up_val).astype(hidden.dtype)
-    for which, (parity, out) in enumerate(((core, keep), (1 - core, give))):
+    for parity, out in ((core, keep), (1 - core, give)):
         for j in range(ring):
             lanes = pl.ds(j * block, block)
-            total = added[which][:, lanes] if added else jnp.zeros((rows, block), f32)
             down = jnp.concatenate([shard[target(j, parity), block:, :] for shard in shards], axis=0)
-            total += jnp.dot(hidden[...], down, preferred_element_type=f32)
+            total = jnp.dot(hidden[...], down, preferred_element_type=f32)
             out[:, lanes] = total.astype(out.dtype)
 
 
-def expert_rows(place, arrived, across, pieces, added, give_type):
+def expert_rows(place, arrived, across, pieces):
     rows, held = arrived.shape
     unit, width, count = block // 2, 2 * held, len(pieces)
     blocks = width // block
@@ -128,12 +127,11 @@
         functools.partial(ffn_kernel, count),
         out_shape=(
             jax.ShapeDtypeStruct((rows, held), jnp.float32),
-            jax.ShapeDtypeStruct((rows, held), give_type),
+            jax.ShapeDtypeStruct((rows, held), jnp.bfloat16),
         ),
         in_specs=[pl.BlockSpec(memory_space=pltpu.SMEM)]
         + [whole] * 2
-        + [pl.BlockSpec(memory_space=pl.ANY)] * count
-        + [whole] * len(added),
+        + [pl.BlockSpec(memory_space=pl.ANY)] * count,
         out_specs=(whole, whole),
         scratch_shapes=[
             pltpu.VMEM((rows, shards * unit), jnp.bfloat16),
@@ -144,7 +142,7 @@
         cost_estimate=pl.CostEstimate(
             flops=2 * rows * width * unit, bytes_accessed=2**20, transcendentals=0
         ),
-    )(place, arrived, across, *pieces, *added)
+    )(place, arrived, across, *pieces)
 
 
 def on_device(tokens, norm_gain, router_logits, routes, gate_proj, up_proj, down_proj):
@@ -186,19 +184,18 @@
 
     crossed = [send(other[0], cross_chip)]
     near = send(own[0], near_chip)
-    crossed.append(send(after(other[1], crossed[0]), cross_chip))
-    relayed = [send(after(crossed[0], near), near_chip)]
-    relayed.append(send(after(crossed[1], relayed[0]), near_chip))
-    passed = send(after(send(own[1], other_row), crossed[1]), near_lent)
+    passed = after(send(own[1], other_row), crossed[0], near)
+    passed = send(passed, near_lent)
+    crossed.append(send(after(other[1], passed), cross_chip))
     lent = send(passed, other_row)
+    relayed = [send(after(crossed[0], near), near_chip), send(crossed[1], near_chip)]
+
+    routes = after(routes, own[0])
 
     expert_iota = jnp.arange(expert_count, dtype=jnp.int32)
     hits = jnp.any(routes[:, :, None] == expert_iota[None, None, :], axis=1)
     earlier = jnp.tril(jnp.ones((group_size, group_size), bf16), -1)
     position = jnp.dot(earlier, hits.astype(bf16), preferred_element_type=f32)
-    shifted = jnp.where(hits, router_logits, -jnp.inf)
-    shifted = jnp.exp(shifted - jnp.max(shifted, axis=1, keepdims=True))
-    gates = shifted / jnp.sum(shifted, axis=1, keepdims=True)
 
     def of_kind(table):
         table = table.reshape(group_size, ep_count, local_experts)
@@ -206,7 +203,6 @@
 
     slot = jnp.where(of_kind(hits), of_kind(position), -1.0)
     slot = slot - (peers % split * share).astype(f32)[None, :]
-    gates = of_kind(gates)
     slot_iota = jnp.arange(share, dtype=jnp.int32).astype(f32)
 
     floated = [part[:group_size].astype(f32) for part in parts]
@@ -228,15 +224,18 @@
     arrived = lax.all_to_all(
         outgoing.reshape(ep_count, share, -1), ep, split_axis=0, concat_axis=0, tiled=True
     ).reshape(ep_count * share, -1)
-    arrived = after(arrived, relayed[0], passed)
+    arrived = after(arrived, *relayed, lent)
     across = lax.ppermute(arrived, "core", other_core)
-    added = expert_rows(place, arrived, across, (*own, *crossed), (), f32)
-    keep, give = expert_rows(place, arrived, across, (near, lent, *relayed), added, bf16)
+    pieces = (*own, near, lent, *crossed, *relayed)
+    keep, give = expert_rows(place, arrived, across, pieces)
     summed = keep + lax.ppermute(give, "core", other_core).astype(f32)
     returned = lax.all_to_all(
         summed.astype(bf16).reshape(ep_count, share, -1), ep, split_axis=0, concat_axis=0, tiled=True
     ).reshape(ep_count * share, -1)
 
+    shifted = jnp.where(hits, after(router_logits, arrived), -jnp.inf)
+    shifted = jnp.exp(shifted - jnp.max(shifted, axis=1, keepdims=True))
+    gates = of_kind(shifted / jnp.sum(shifted, axis=1, keepdims=True))
     weight = jnp.where(slot[:, :, None] == slot_iota[None, None, :], gates[:, :, None], 0.0)
     weight = weight.reshape(group_size, ep_count * share)
     high = lax.reduce_precision(weight, 8, 7)

time: 145 us -> 150 us (1.034)
  starting transfers between devices: 37 us -> 45.6 us
  other arithmetic: 7.1 us -> 4.2 us
    ppermute x8, starting transfers between devices: 4.64 us -> 12.3 us  [send(): return lax.ppermute(one, ('pair', 'x'), pairs)]
    ppermute x8, waiting for transfers between devices: 45.6 us -> 43.2 us  [send(): return lax.ppermute(one, ('pair', 'x'), pairs)]
    ppermute x6, waiting for transfers between devices: 3.8 us -> 5.33 us  [ring_send(): return lax.ppermute(one, 'x', pairs)]
    pallas_call x2 -> x1, Pallas kernels: 9.1 us -> 8.29 us  [expert_rows(): pl.pallas_call(functools.partial(ffn_kernel, count), out_shape=(jax.Shape...]
  transfers between devices with their start and end apart: 19 -> 19, of which waited for: 12 -> 12; matrix products, arithmetic and copies ran while one was open for 4% -> 2% of each run, Pallas kernels for 6% -> 3%
where the time goes in v8:
time: 150 us
  waiting for transfers between devices  82.2 us (55%)
  starting transfers between devices  45.6 us (30%)
  Pallas kernels  12.3 us (8%)
  other arithmetic  4.2 us (3%)
  local copies, waits for them, and re-layouts  2.94 us (2%)
  matrix products  2.07 us (1%)
    ppermute x8, waiting for transfers between devices, send(): return lax.ppermute(one, ('pair', 'x'), pairs)  43.2 us
    all_to_all x1, waiting for transfers between devices, on_device(): lax.all_to_all(summed.astype(bf16).reshape(ep_count, share, -1), ep, spli...  28 us
    all_to_all x1, starting transfers between devices, on_device(): lax.all_to_all(summed.astype(bf16).reshape(ep_count, share, -1), ep, spli...  12.8 us
    ppermute x8, starting transfers between devices, send(): return lax.ppermute(one, ('pair', 'x'), pairs)  12.3 us
    all_to_all x1, starting transfers between devices, on_device(): lax.all_to_all(outgoing.reshape(ep_count, share, -1), ep, split_axis=0, c...  11.5 us
    ppermute x6, starting transfers between devices, ring_send(): return lax.ppermute(one, 'x', pairs)  8.68 us
    pallas_call x1, Pallas kernels, expert_rows(): pl.pallas_call(functools.partial(ffn_kernel, count), out_shape=(jax.Shape...  8.29 us
    ppermute x6, waiting for transfers between devices, ring_send(): return lax.ppermute(one, 'x', pairs)  5.33 us
  transfers between devices with their start and end apart: 19, of which 12 were waited for; matrix products, arithmetic and copies ran while one was open for 2% of the time, Pallas kernels for 3%

profile of v8, /device:TPU:8, one launch (start us, length us, event | category | flops | bytes accessed | tf_op | source)
XLA Modules:
  0.0 149.6 jit_solution(11131753340528573176)
XLA Ops:
  0.0 0.0 copy-start.5
  0.0 0.9 pad_select_fusion
  0.9 1.6 %collective-permute-start = (bf16[144,256]{1,0:T(8,128)(2,1)S(1)}, bf16[144,256]{1,0:T(8,128)(2,1)S(1)}, u32[]{:S(2)}, u32[]{:S(2)}) collective-permute-start(bf16[144,256]{1,0:T(8,128)(2,1)S(1)} %pad_select_fusion), channel_id=1, source_target_pairs={{0,2},{2,4},{4,6},{6,0},{1,3},{3,5},{5,7},{7,1},{8,10},{10,12},{12... | collective-permute-start | bytes 221192 | tf_op jit(solution)/shard_map/ppermute | solution.py:169
  2.5 2.7 %collective-permute-start.1 = (bf16[144,256]{1,0:T(8,128)(2,1)S(1)}, bf16[144,256]{1,0:T(8,128)(2,1)S(1)}, u32[]{:S(2)}, u32[]{:S(2)}) collective-permute-start(bf16[144,256]{1,0:T(8,128)(2,1)S(1)} %pad_select_fusion), channel_id=1, source_target_pairs={{0,4},{2,6},{4,0},{6,2},{1,5},{3,7},{5,1},{7,3},{8,12},{10,14},{12... | collective-permute-start | bytes 221192 | tf_op jit(solution)/shard_map/ppermute | solution.py:169
  5.2 1.4 collective-permute-start.2
  6.7 0.1 eq.78
  6.8 4.0 %shard_map.73 = (bf16[6,384,256]{2,1,0:T(8,128)(2,1)}, bf16[2,384,256]{2,1,0:T(8,128)(2,1)}, bf16[6,384,256]{2,1,0:T(8,128)(2,1)}, bf16[2,384,256]{2,1,0:T(8,128)(2,1)}) custom-call(s32[1]{0:T(128)} %bitcast.kind_ref, bf16[2,2048,128]{2,1,0:T(8,128)(2,1)} %gate.1, bf16[2,2048,128]{2,1,0:T(8,128)(2,1)} %up.1, bf16[2,128,2048]{2,1,0:T(8,128)(2,1)} %down.1), custom_call_target="tpu_custom_call" | custom-call | bytes 6291456 | tf_op jit(solution)/shard_map/pallas_call | solution.py:62
  10.8 0.0 collective-permute-done
  10.8 0.0 collective-permute-done.1
  10.9 0.0 collective-permute-done.2
  10.9 0.1 fusion.13
  11.0 0.1 fusion.19
  11.1 1.5 collective-permute-start.5
  12.6 0.0 copy-done.5
  12.7 0.1 collective-permute-start.3
  12.8 0.1 collective-permute-start.4
  12.9 0.2 fusion.30
  13.1 0.1 subtract_bitcast_fusion
  13.2 0.1 fusion.38
  13.3 0.1 bitcast_compare_fusion
  13.5 0.5 collective-permute-done.3
  13.9 0.1 fusion.15
  14.1 1.4 convolution_convert_fusion
  15.5 11.5 %all-to-all-start = ((bf16[32,16,1024]{2,1,0:T(8,128)(2,1)}), bf16[32,16,1024]{2,1,0:T(8,128)(2,1)S(1)}, u32[]{:S(2)}, u32[]{:S(2)}) async-start(bf16[32,16,1024]{2,1,0:T(8,128)(2,1)} %bitcast.64), calls=%async_computation | async-start | bytes 2097152 | tf_op jit(solution)/shard_map/all_to_all | solution.py:224
  27.1 0.3 collective-permute-start.7
  27.4 16.8 %collective-permute-done.7 = bf16[2,384,256]{2,1,0:T(8,128)(2,1)S(1)} collective-permute-done((bf16[2,384,256]{2,1,0:T(8,128)(2,1)}, bf16[2,384,256]{2,1,0:T(8,128)(2,1)S(1)}, u32[]{:S(2)}, u32[]{:S(2)}) %collective-permute-start.7) | collective-permute-done | bytes 393248 | tf_op jit(solution)/shard_map/ppermute | solution.py:180
  44.2 0.0 collective-permute-done.4.refs_4_
  44.2 0.0 collective-permute-done.5.refs_2_
  44.2 1.8 %collective-permute-start.8 = (bf16[2,384,256]{2,1,0:T(8,128)(2,1)S(1)}, bf16[2,384,256]{2,1,0:T(8,128)(2,1)S(1)}, u32[]{:S(2)}, u32[]{:S(2)}) collective-permute-start(bf16[2,384,256]{2,1,0:T(8,128)(2,1)S(1)} %collective-permute-done.7), channel_id=1, source_target_pairs={{2,4},{4,2},{6,0},{0,6},{8,10},{10,8},{12,14},{14,12},{3,5},{5,3},... | collective-permute-start | bytes 1179656 | tf_op jit(solution)/shard_map/ppermute | solution.py:180
  46.0 1.9 %collective-permute-start.6 = (bf16[6,384,256]{2,1,0:T(8,128)(2,1)}, bf16[6,384,256]{2,1,0:T(8,128)(2,1)}, u32[]{:S(2)}, u32[]{:S(2)}) collective-permute-start(bf16[6,384,256]{2,1,0:T(8,128)(2,1)} %collective-permute-done.4.refs_4_), channel_id=1, source_target_pairs={{0,2},{2,0},{4,6},{6,4},{10,12},{12,10},{14,8},{8,14},{1,3},{3,1},... | collective-permute-start | bytes 3538952 | tf_op jit(solution)/shard_map/ppermute | solution.py:180
  47.9 5.8 %collective-permute-done.8 = bf16[2,384,256]{2,1,0:T(8,128)(2,1)S(1)} collective-permute-done((bf16[2,384,256]{2,1,0:T(8,128)(2,1)S(1)}, bf16[2,384,256]{2,1,0:T(8,128)(2,1)S(1)}, u32[]{:S(2)}, u32[]{:S(2)}) %collective-permute-start.8) | collective-permute-done | bytes 393248 | tf_op jit(solution)/shard_map/ppermute | solution.py:180
  53.6 1.5 %collective-permute-start.9 = (bf16[2,384,256]{2,1,0:T(8,128)(2,1)}, bf16[2,384,256]{2,1,0:T(8,128)(2,1)}, u32[]{:S(2)}, u32[]{:S(2)}) collective-permute-start(bf16[2,384,256]{2,1,0:T(8,128)(2,1)} %get-tuple-element.40), channel_id=1, source_target_pairs={{0,6},{2,4},{4,2},{6,0},{10,8},{12,14},{14,12},{8,10},{1,7},{3,5},... | collective-permute-start | bytes 1179656 | tf_op jit(solution)/shard_map/ppermute | solution.py:180
  55.1 3.5 %collective-permute-start.11 = (bf16[2,384,256]{2,1,0:T(8,128)(2,1)S(1)}, bf16[2,384,256]{2,1,0:T(8,128)(2,1)S(1)}, u32[]{:S(2)}, u32[]{:S(2)}) collective-permute-start(bf16[2,384,256]{2,1,0:T(8,128)(2,1)S(1)} %collective-permute-done.8), channel_id=1, source_target_pairs={{0,8},{2,10},{4,12},{6,14},{8,0},{10,2},{12,4},{14,6},{1,9},{3,11}... | collective-permute-start | bytes 1179656 | tf_op jit(solution)/shard_map/ppermute | solution.py:180
  58.7 3.9 %collective-permute-done.9.refs_5_ = bf16[2,384,256]{2,1,0:T(8,128)(2,1)} collective-permute-done((bf16[2,384,256]{2,1,0:T(8,128)(2,1)}, bf16[2,384,256]{2,1,0:T(8,128)(2,1)}, u32[]{:S(2)}, u32[]{:S(2)}) %collective-permute-start.9) | collective-permute-done | bytes 393248 | tf_op jit(solution)/shard_map/ppermute | solution.py:180
  62.6 1.7 %collective-permute-start.10 = (bf16[2,384,256]{2,1,0:T(8,128)(2,1)}, bf16[2,384,256]{2,1,0:T(8,128)(2,1)}, u32[]{:S(2)}, u32[]{:S(2)}) collective-permute-start(bf16[2,384,256]{2,1,0:T(8,128)(2,1)} %collective-permute-done.9.refs_5_), channel_id=1, source_target_pairs={{0,2},{2,0},{4,6},{6,4},{10,12},{12,10},{14,8},{8,14},{1,3},{3,1},... | collective-permute-start | bytes 1179656 | tf_op jit(solution)/shard_map/ppermute | solution.py:180
  64.3 0.5 collective-permute-done.11.refs_3_
  64.8 0.7 copy-done.2
  65.6 0.0 all-to-all-done
  65.6 16.1 %collective-permute-done.10.refs_7_ = bf16[2,384,256]{2,1,0:T(8,128)(2,1)} collective-permute-done((bf16[2,384,256]{2,1,0:T(8,128)(2,1)}, bf16[2,384,256]{2,1,0:T(8,128)(2,1)}, u32[]{:S(2)}, u32[]{:S(2)}) %collective-permute-start.10) | collective-permute-done | bytes 393248 | tf_op jit(solution)/shard_map/ppermute | solution.py:180
  81.7 0.0 collective-permute-done.6.refs_6_
  81.7 0.0 collective-permute-start.12
  81.7 0.1 pad_add_fusion.place_ref
  81.8 2.7 %collective-permute-done.12.across = bf16[512,1024]{1,0:T(8,128)(2,1)} collective-permute-done((bf16[512,1024]{1,0:T(8,128)(2,1)S(1)}, bf16[512,1024]{1,0:T(8,128)(2,1)}, u32[]{:S(2)}, u32[]{:S(2)}) %collective-permute-start.12) | collective-permute-done | bytes 1048608 | tf_op jit(solution)/shard_map/ppermute | solution.py:228
  84.5 0.0 copy-done
  84.5 1.0 copy-done.1
  85.5 1.0 copy-done.3
  86.5 8.3 %shard_map.74 = (f32[512,1024]{1,0:T(8,128)S(1)}, bf16[512,1024]{1,0:T(8,128)(2,1)S(1)}) custom-call(s32[2]{0:T(128)S(1)} %pad_add_fusion.place_ref, bf16[512,1024]{1,0:T(8,128)(2,1)S(1)} %bitcast.63, bf16[512,1024]{1,0:T(8,128)(2,1)} %collective-permute-done.12.across, bf16[6,384,256]{2,1,0:T(8,128)(2,1)S(1)} %copy-done, ...), custom_call_target="tpu_custom_call" | custom-call | flops 268435456 | bytes 1048576 | tf_op jit(solution)/shard_map/pallas_call | solution.py:126
  94.8 0.2 collective-permute-start.13
  95.0 2.5 %collective-permute-done.13 = bf16[512,1024]{1,0:T(8,128)(2,1)S(1)} collective-permute-done((bf16[512,1024]{1,0:T(8,128)(2,1)S(1)}, bf16[512,1024]{1,0:T(8,128)(2,1)S(1)}, u32[]{:S(2)}, u32[]{:S(2)}) %collective-permute-start.13) | collective-permute-done | bytes 1048608 | tf_op jit(solution)/shard_map/ppermute | solution.py:231
  97.5 1.4 add_convert_fusion
  98.9 12.8 %all-to-all-start.1 = ((bf16[32,16,1024]{2,1,0:T(8,128)(2,1)}), bf16[32,16,1024]{2,1,0:T(8,128)(2,1)S(1)}, u32[]{:S(2)}, u32[]{:S(2)}) async-start(bf16[32,16,1024]{2,1,0:T(8,128)(2,1)} %bitcast.24), calls=%async_computation.1 | async-start | bytes 2097152 | tf_op jit(solution)/shard_map/all_to_all | solution.py:232
  111.7 0.0 copy-done.4
  111.8 0.1 select_bitcast_fusion
  111.9 0.1 reduce-precision_convert_fusion
  112.0 28.0 %all-to-all-done.1 = bf16[32,16,1024]{2,1,0:T(8,128)(2,1)S(1)} async-done(((bf16[32,16,1024]{2,1,0:T(8,128)(2,1)}), bf16[32,16,1024]{2,1,0:T(8,128)(2,1)S(1)}, u32[]{:S(2)}, u32[]{:S(2)}) %all-to-all-start.1) | async-done | bytes 1048608 | tf_op jit(solution)/shard_map/all_to_all | solution.py:232
  140.1 0.5 fusion.8
  140.5 0.1 fusion.51
  140.6 1.2 collective-permute-start.16
  141.9 1.6 %collective-permute-start.15 = (bf16[128,256]{1,0:T(8,128)(2,1)S(1)}, bf16[128,256]{1,0:T(8,128)(2,1)S(1)}, u32[]{:S(2)}, u32[]{:S(2)}) collective-permute-start(bf16[128,256]{1,0:T(8,128)(2,1)S(1)} %get-tuple-element.52), channel_id=1, source_target_pairs={{0,4},{2,6},{4,0},{6,2},{1,5},{3,7},{5,1},{7,3},{8,12},{10,14},{12... | collective-permute-start | bytes 196616 | tf_op jit(solution)/shard_map/ppermute | solution.py:169
  143.4 0.2 collective-permute-start.14
  143.6 1.4 collective-permute-done.16
  145.0 2.7 %collective-permute-done.15 = bf16[128,256]{1,0:T(8,128)(2,1)S(1)} collective-permute-done((bf16[128,256]{1,0:T(8,128)(2,1)S(1)}, bf16[128,256]{1,0:T(8,128)(2,1)S(1)}, u32[]{:S(2)}, u32[]{:S(2)}) %collective-permute-start.15) | collective-permute-done | bytes 65568 | tf_op jit(solution)/shard_map/ppermute | solution.py:169
  147.6 1.3 collective-permute-done.14
  148.9 0.7 fusion.27
  (24 shorter events, 0.3 us)
Async XLA Ops:
  0.0 12.6 %copy-start.5 = (s32[128,8]{0,1:T(8,128)S(1)}, s32[128,8]{0,1:T(8,128)}, u32[]{:S(2)}) copy-start(s32[128,8]{0,1:T(8,128)} %param.10) | copy-start | bytes 12292
  0.9 9.9 %collective-permute-start = (bf16[144,256]{1,0:T(8,128)(2,1)S(1)}, bf16[144,256]{1,0:T(8,128)(2,1)S(1)}, u32[]{:S(2)}, u32[]{:S(2)}) collective-permute-start(bf16[144,256]{1,0:T(8,128)(2,1)S(1)} %pad_select_fusion), channel_id=1, source_target_pairs={{0,2},{2,4},{4,6},{6,0},{1,3},{3,5},{5,7},{7,1},{8,10},{10,12},{12... | collective-permute-start | bytes 221192 | tf_op jit(solution)/shard_map/ppermute | solution.py:169
  2.5 8.3 %collective-permute-start.1 = (bf16[144,256]{1,0:T(8,128)(2,1)S(1)}, bf16[144,256]{1,0:T(8,128)(2,1)S(1)}, u32[]{:S(2)}, u32[]{:S(2)}) collective-permute-start(bf16[144,256]{1,0:T(8,128)(2,1)S(1)} %pad_select_fusion), channel_id=1, source_target_pairs={{0,4},{2,6},{4,0},{6,2},{1,5},{3,7},{5,1},{7,3},{8,12},{10,14},{12... | collective-permute-start | bytes 221192 | tf_op jit(solution)/shard_map/ppermute | solution.py:169
  5.2 5.6 %collective-permute-start.2 = (bf16[144,256]{1,0:T(8,128)(2,1)S(1)}, bf16[144,256]{1,0:T(8,128)(2,1)S(1)}, u32[]{:S(2)}, u32[]{:S(2)}) collective-permute-start(bf16[144,256]{1,0:T(8,128)(2,1)S(1)} %pad_select_fusion), channel_id=1, source_target_pairs={{0,6},{2,0},{4,2},{6,4},{1,7},{3,1},{5,3},{7,5},{8,14},{10,8},{12,... | collective-permute-start | bytes 221192 | tf_op jit(solution)/shard_map/ppermute | solution.py:169
  11.1 33.1 %collective-permute-start.5 = (bf16[6,384,256]{2,1,0:T(8,128)(2,1)}, bf16[6,384,256]{2,1,0:T(8,128)(2,1)S(1)}, u32[]{:S(2)}, u32[]{:S(2)}) collective-permute-start(bf16[6,384,256]{2,1,0:T(8,128)(2,1)} %get-tuple-element.29.refs_0_), channel_id=1, source_target_pairs={{0,2},{2,0},{4,6},{6,4},{10,12},{12,10},{14,8},{8,14},{1,3},{3,1},... | collective-permute-start | bytes 3538952 | tf_op jit(solution)/shard_map/ppermute | solution.py:180
  12.7 1.2 collective-permute-start.3
  12.8 31.3 %collective-permute-start.4 = (bf16[6,384,256]{2,1,0:T(8,128)(2,1)}, bf16[6,384,256]{2,1,0:T(8,128)(2,1)}, u32[]{:S(2)}, u32[]{:S(2)}) collective-permute-start(bf16[6,384,256]{2,1,0:T(8,128)(2,1)} %get-tuple-element.35), channel_id=1, source_target_pairs={{0,6},{2,4},{4,2},{6,0},{10,8},{12,14},{14,12},{8,10},{1,7},{3,5},... | collective-permute-start | bytes 3538952 | tf_op jit(solution)/shard_map/ppermute | solution.py:180
  13.2 71.2 %copy-start = (bf16[6,384,256]{2,1,0:T(8,128)(2,1)S(1)}, bf16[6,384,256]{2,1,0:T(8,128)(2,1)}, u32[]{:S(2)}) copy-start(bf16[6,384,256]{2,1,0:T(8,128)(2,1)} %get-tuple-element.29.refs_0_) | copy-start | bytes 3538948
  15.5 50.1 %all-to-all-start = ((bf16[32,16,1024]{2,1,0:T(8,128)(2,1)}), bf16[32,16,1024]{2,1,0:T(8,128)(2,1)S(1)}, u32[]{:S(2)}, u32[]{:S(2)}) async-start(bf16[32,16,1024]{2,1,0:T(8,128)(2,1)} %bitcast.64), calls=%async_computation | async-start | bytes 2097152 | tf_op jit(solution)/shard_map/all_to_all | solution.py:224
  27.1 17.1 %collective-permute-start.7 = (bf16[2,384,256]{2,1,0:T(8,128)(2,1)}, bf16[2,384,256]{2,1,0:T(8,128)(2,1)S(1)}, u32[]{:S(2)}, u32[]{:S(2)}) collective-permute-start(bf16[2,384,256]{2,1,0:T(8,128)(2,1)} %get-tuple-element.38.refs_1_), channel_id=1, source_target_pairs={{0,8},{2,10},{4,12},{6,14},{8,0},{10,2},{12,4},{14,6},{1,9},{3,11}... | collective-permute-start | bytes 1179656 | tf_op jit(solution)/shard_map/ppermute | solution.py:180
  44.2 9.5 %collective-permute-start.8 = (bf16[2,384,256]{2,1,0:T(8,128)(2,1)S(1)}, bf16[2,384,256]{2,1,0:T(8,128)(2,1)S(1)}, u32[]{:S(2)}, u32[]{:S(2)}) collective-permute-start(bf16[2,384,256]{2,1,0:T(8,128)(2,1)S(1)} %collective-permute-done.7), channel_id=1, source_target_pairs={{2,4},{4,2},{6,0},{0,6},{8,10},{10,8},{12,14},{14,12},{3,5},{5,3},... | collective-permute-start | bytes 1179656 | tf_op jit(solution)/shard_map/ppermute | solution.py:180
  46.0 35.7 %collective-permute-start.6 = (bf16[6,384,256]{2,1,0:T(8,128)(2,1)}, bf16[6,384,256]{2,1,0:T(8,128)(2,1)}, u32[]{:S(2)}, u32[]{:S(2)}) collective-permute-start(bf16[6,384,256]{2,1,0:T(8,128)(2,1)} %collective-permute-done.4.refs_4_), channel_id=1, source_target_pairs={{0,2},{2,0},{4,6},{6,4},{10,12},{12,10},{14,8},{8,14},{1,3},{3,1},... | collective-permute-start | bytes 3538952 | tf_op jit(solution)/shard_map/ppermute | solution.py:180
  53.6 9.0 %collective-permute-start.9 = (bf16[2,384,256]{2,1,0:T(8,128)(2,1)}, bf16[2,384,256]{2,1,0:T(8,128)(2,1)}, u32[]{:S(2)}, u32[]{:S(2)}) collective-permute-start(bf16[2,384,256]{2,1,0:T(8,128)(2,1)} %get-tuple-element.40), channel_id=1, source_target_pairs={{0,6},{2,4},{4,2},{6,0},{10,8},{12,14},{14,12},{8,10},{1,7},{3,5},... | collective-permute-start | bytes 1179656 | tf_op jit(solution)/shard_map/ppermute | solution.py:180
  55.1 9.7 %collective-permute-start.11 = (bf16[2,384,256]{2,1,0:T(8,128)(2,1)S(1)}, bf16[2,384,256]{2,1,0:T(8,128)(2,1)S(1)}, u32[]{:S(2)}, u32[]{:S(2)}) collective-permute-start(bf16[2,384,256]{2,1,0:T(8,128)(2,1)S(1)} %collective-permute-done.8), channel_id=1, source_target_pairs={{0,8},{2,10},{4,12},{6,14},{8,0},{10,2},{12,4},{14,6},{1,9},{3,11}... | collective-permute-start | bytes 1179656 | tf_op jit(solution)/shard_map/ppermute | solution.py:180
  62.6 19.1 %collective-permute-start.10 = (bf16[2,384,256]{2,1,0:T(8,128)(2,1)}, bf16[2,384,256]{2,1,0:T(8,128)(2,1)}, u32[]{:S(2)}, u32[]{:S(2)}) collective-permute-start(bf16[2,384,256]{2,1,0:T(8,128)(2,1)} %collective-permute-done.9.refs_5_), channel_id=1, source_target_pairs={{0,2},{2,0},{4,6},{6,4},{10,12},{12,10},{14,8},{8,14},{1,3},{3,1},... | collective-permute-start | bytes 1179656 | tf_op jit(solution)/shard_map/ppermute | solution.py:180
  64.8 0.7 copy-start.2
  81.7 2.8 %collective-permute-start.12 = (bf16[512,1024]{1,0:T(8,128)(2,1)S(1)}, bf16[512,1024]{1,0:T(8,128)(2,1)}, u32[]{:S(2)}, u32[]{:S(2)}) collective-permute-start(bf16[512,1024]{1,0:T(8,128)(2,1)S(1)} %bitcast.62), channel_id=1, source_target_pairs={{0,1},{1,0},{2,3},{3,2},{4,5},{5,4},{6,7},{7,6},{8,9},{9,8},{10,11... | collective-permute-start | bytes 3145736 | tf_op jit(solution)/shard_map/ppermute | solution.py:228
  84.5 1.0 copy-start.1
  85.5 1.0 copy-start.3
  94.8 2.7 %collective-permute-start.13 = (bf16[512,1024]{1,0:T(8,128)(2,1)S(1)}, bf16[512,1024]{1,0:T(8,128)(2,1)S(1)}, u32[]{:S(2)}, u32[]{:S(2)}) collective-permute-start(bf16[512,1024]{1,0:T(8,128)(2,1)S(1)} %get-tuple-element.44), channel_id=1, source_target_pairs={{0,1},{1,0},{2,3},{3,2},{4,5},{5,4},{6,7},{7,6},{8,9},{9,8},{10,11... | collective-permute-start | bytes 3145736 | tf_op jit(solution)/shard_map/ppermute | solution.py:231
  98.9 12.8 %copy-start.4 = (f32[128,64]{0,1:T(8,128)S(1)}, f32[128,64]{0,1:T(8,128)}, u32[]{:S(2)}) copy-start(f32[128,64]{0,1:T(8,128)} %param.9) | copy-start | bytes 98308
  98.9 41.2 %all-to-all-start.1 = ((bf16[32,16,1024]{2,1,0:T(8,128)(2,1)}), bf16[32,16,1024]{2,1,0:T(8,128)(2,1)S(1)}, u32[]{:S(2)}, u32[]{:S(2)}) async-start(bf16[32,16,1024]{2,1,0:T(8,128)(2,1)} %bitcast.24), calls=%async_computation.1 | async-start | bytes 2097152 | tf_op jit(solution)/shard_map/all_to_all | solution.py:232
  140.6 4.3 %collective-permute-start.16 = (bf16[128,256]{1,0:T(8,128)(2,1)S(1)}, bf16[128,256]{1,0:T(8,128)(2,1)S(1)}, u32[]{:S(2)}, u32[]{:S(2)}) collective-permute-start(bf16[128,256]{1,0:T(8,128)(2,1)S(1)} %get-tuple-element.51), channel_id=1, source_target_pairs={{0,6},{2,0},{4,2},{6,4},{1,7},{3,1},{5,3},{7,5},{8,14},{10,8},{12,... | collective-permute-start | bytes 196616 | tf_op jit(solution)/shard_map/ppermute | solution.py:169
  141.9 5.8 %collective-permute-start.15 = (bf16[128,256]{1,0:T(8,128)(2,1)S(1)}, bf16[128,256]{1,0:T(8,128)(2,1)S(1)}, u32[]{:S(2)}, u32[]{:S(2)}) collective-permute-start(bf16[128,256]{1,0:T(8,128)(2,1)S(1)} %get-tuple-element.52), channel_id=1, source_target_pairs={{0,4},{2,6},{4,0},{6,2},{1,5},{3,7},{5,1},{7,3},{8,12},{10,14},{12... | collective-permute-start | bytes 196616 | tf_op jit(solution)/shard_map/ppermute | solution.py:169
  143.4 5.5 %collective-permute-start.14 = (bf16[128,256]{1,0:T(8,128)(2,1)S(1)}, bf16[128,256]{1,0:T(8,128)(2,1)S(1)}, u32[]{:S(2)}, u32[]{:S(2)}) collective-permute-start(bf16[128,256]{1,0:T(8,128)(2,1)S(1)} %get-tuple-element.50), channel_id=1, source_target_pairs={{0,2},{2,4},{4,6},{6,0},{1,3},{3,5},{5,7},{7,1},{8,10},{10,12},{12... | collective-permute-start | bytes 196616 | tf_op jit(solution)/shard_map/ppermute | solution.py:169

commit v9 on v8

--- a/solution.py
+++ b/solution.py
@@ -73,7 +73,7 @@
 
 
 def ffn_kernel(count, place_ref, arrived, across, *refs):
-    lying, (keep, give, hidden, held_shards, sems) = refs[:count], refs[count:]
+    lying, added, (keep, give, hidden, held_shards, sems) = refs[:count], refs[count:-5], refs[-5:]
     total_blocks = held_shards.shape[1]
     copies, first = [], 0
     for n, piece in enumerate(lying):
@@ -109,15 +109,16 @@
         gate_val, up_val = both[:, :unit], both[:, unit:]
         silu = gate_val / (1.0 + jnp.exp(-gate_val))
         hidden[:, pl.ds(k * unit, unit)] = (silu * up_val).astype(hidden.dtype)
-    for parity, out in ((core, keep), (1 - core, give)):
+    for which, (parity, out) in enumerate(((core, keep), (1 - core, give))):
         for j in range(ring):
             lanes = pl.ds(j * block, block)
+            total = added[which][:, lanes] if added else jnp.zeros((rows, block), f32)
             down = jnp.concatenate([shard[target(j, parity), block:, :] for shard in shards], axis=0)
-            total = jnp.dot(hidden[...], down, preferred_element_type=f32)
+            total += jnp.dot(hidden[...], down, preferred_element_type=f32)
             out[:, lanes] = total.astype(out.dtype)
 
 
-def expert_rows(place, arrived, across, pieces):
+def expert_rows(place, arrived, across, pieces, added, give_type):
     rows, held = arrived.shape
     unit, width, count = block // 2, 2 * held, len(pieces)
     blocks = width // block
@@ -127,11 +128,12 @@
         functools.partial(ffn_kernel, count),
         out_shape=(
             jax.ShapeDtypeStruct((rows, held), jnp.float32),
-            jax.ShapeDtypeStruct((rows, held), jnp.bfloat16),
+            jax.ShapeDtypeStruct((rows, held), give_type),
         ),
         in_specs=[pl.BlockSpec(memory_space=pltpu.SMEM)]
         + [whole] * 2
-        + [pl.BlockSpec(memory_space=pl.ANY)] * count,
+        + [pl.BlockSpec(memory_space=pl.ANY)] * count
+        + [whole] * len(added),
         out_specs=(whole, whole),
         scratch_shapes=[
             pltpu.VMEM((rows, shards * unit), jnp.bfloat16),
@@ -142,7 +144,7 @@
         cost_estimate=pl.CostEstimate(
             flops=2 * rows * width * unit, bytes_accessed=2**20, transcendentals=0
         ),
-    )(place, arrived, across, *pieces)
+    )(place, arrived, across, *pieces, *added)
 
 
 def on_device(tokens, norm_gain, router_logits, routes, gate_proj, up_proj, down_proj):
@@ -224,10 +226,10 @@
     arrived = lax.all_to_all(
         outgoing.reshape(ep_count, share, -1), ep, split_axis=0, concat_axis=0, tiled=True
     ).reshape(ep_count * share, -1)
-    arrived = after(arrived, *relayed, lent)
+    arrived = after(arrived, relayed[0], lent, crossed[1])
     across = lax.ppermute(arrived, "core", other_core)
-    pieces = (*own, near, lent, *crossed, *relayed)
-    keep, give = expert_rows(place, arrived, across, pieces)
+    added = expert_rows(place, arrived, across, (*own, near, lent, *crossed), (), f32)
+    keep, give = expert_rows(place, arrived, across, relayed, added, bf16)
     summed = keep + lax.ppermute(give, "core", other_core).astype(f32)
     returned = lax.all_to_all(
         summed.astype(bf16).reshape(ep_count, share, -1), ep, split_axis=0, concat_axis=0, tiled=True

time: 150 us -> 138 us (0.920)
  waiting for transfers between devices: 82.2 us -> 70.2 us
  Pallas kernels: 12.3 us -> 14.8 us
  starting transfers between devices: 45.6 us -> 43.1 us
    ppermute x8, waiting for transfers between devices: 43.2 us -> 33.6 us  [send(): return lax.ppermute(one, ('pair', 'x'), pairs)]
    ppermute x8, starting transfers between devices: 12.3 us -> 9.53 us  [send(): return lax.ppermute(one, ('pair', 'x'), pairs)]
    pallas_call x1 -> x2, Pallas kernels: 8.29 us -> 10.8 us  [expert_rows(): pl.pallas_call(functools.partial(ffn_kernel, count), out_shape=(jax.Shape...]
    ppermute x6, waiting for transfers between devices: 5.33 us -> 3.39 us  [ring_send(): return lax.ppermute(one, 'x', pairs)]
  transfers between devices with their start and end apart: 19 -> 19, of which waited for: 12 -> 15; matrix products, arithmetic and copies ran while one was open for 2% -> 2% of each run, Pallas kernels for 3% -> 8%
where the time goes in v9:
time: 138 us
  waiting for transfers between devices  70.2 us (51%)
  starting transfers between devices  43.1 us (31%)
  Pallas kernels  14.8 us (11%)
  other arithmetic  4.18 us (3%)
  local copies, waits for them, and re-layouts  2.96 us (2%)
  matrix products  2.08 us (2%)
    ppermute x8, waiting for transfers between devices, send(): return lax.ppermute(one, ('pair', 'x'), pairs)  33.6 us
    all_to_all x1, waiting for transfers between devices, on_device(): lax.all_to_all(summed.astype(bf16).reshape(ep_count, share, -1), ep, spli...  28 us
    all_to_all x1, starting transfers between devices, on_device(): lax.all_to_all(summed.astype(bf16).reshape(ep_count, share, -1), ep, spli...  11.8 us
    all_to_all x1, starting transfers between devices, on_device(): lax.all_to_all(outgoing.reshape(ep_count, share, -1), ep, split_axis=0, c...  11.7 us
    pallas_call x2, Pallas kernels, expert_rows(): pl.pallas_call(functools.partial(ffn_kernel, count), out_shape=(jax.Shape...  10.8 us
    ppermute x6, starting transfers between devices, ring_send(): return lax.ppermute(one, 'x', pairs)  9.94 us
    ppermute x8, starting transfers between devices, send(): return lax.ppermute(one, ('pair', 'x'), pairs)  9.53 us
    pallas_call x1, Pallas kernels, pick_shards(): pl.pallas_call(pick_kernel, out_shape=tuple((jax.ShapeDtypeStruct((size,...  4 us
  transfers between devices with their start and end apart: 19, of which 15 were waited for; matrix products, arithmetic and copies ran while one was open for 2% of the time, Pallas kernels for 8%

profile of v9, /device:TPU:8, one launch (start us, length us, event | category | flops | bytes accessed | tf_op | source)
XLA Modules:
  0.0 137.6 jit_solution(8454776523703830905)
XLA Ops:
  0.0 0.9 pad_select_fusion
  0.9 1.6 %collective-permute-start = (bf16[144,256]{1,0:T(8,128)(2,1)S(1)}, bf16[144,256]{1,0:T(8,128)(2,1)S(1)}, u32[]{:S(2)}, u32[]{:S(2)}) collective-permute-start(bf16[144,256]{1,0:T(8,128)(2,1)S(1)} %pad_select_fusion), channel_id=1, source_target_pairs={{0,2},{2,4},{4,6},{6,0},{1,3},{3,5},{5,7},{7,1},{8,10},{10,12},{12... | collective-permute-start | bytes 221192 | tf_op jit(solution)/shard_map/ppermute | solution.py:171
  2.5 2.7 %collective-permute-start.1 = (bf16[144,256]{1,0:T(8,128)(2,1)S(1)}, bf16[144,256]{1,0:T(8,128)(2,1)S(1)}, u32[]{:S(2)}, u32[]{:S(2)}) collective-permute-start(bf16[144,256]{1,0:T(8,128)(2,1)S(1)} %pad_select_fusion), channel_id=1, source_target_pairs={{0,4},{2,6},{4,0},{6,2},{1,5},{3,7},{5,1},{7,3},{8,12},{10,14},{12... | collective-permute-start | bytes 221192 | tf_op jit(solution)/shard_map/ppermute | solution.py:171
  5.2 1.4 %collective-permute-start.2 = (bf16[144,256]{1,0:T(8,128)(2,1)S(1)}, bf16[144,256]{1,0:T(8,128)(2,1)S(1)}, u32[]{:S(2)}, u32[]{:S(2)}) collective-permute-start(bf16[144,256]{1,0:T(8,128)(2,1)S(1)} %pad_select_fusion), channel_id=1, source_target_pairs={{0,6},{2,0},{4,2},{6,4},{1,7},{3,1},{5,3},{7,5},{8,14},{10,8},{12,... | collective-permute-start | bytes 221192 | tf_op jit(solution)/shard_map/ppermute | solution.py:171
  6.7 0.1 eq.78
  6.8 4.0 %shard_map.73 = (bf16[6,384,256]{2,1,0:T(8,128)(2,1)}, bf16[2,384,256]{2,1,0:T(8,128)(2,1)}, bf16[6,384,256]{2,1,0:T(8,128)(2,1)}, bf16[2,384,256]{2,1,0:T(8,128)(2,1)}) custom-call(s32[1]{0:T(128)} %bitcast.kind_ref, bf16[2,2048,128]{2,1,0:T(8,128)(2,1)} %gate.1, bf16[2,2048,128]{2,1,0:T(8,128)(2,1)} %up.1, bf16[2,128,2048]{2,1,0:T(8,128)(2,1)} %down.1), custom_call_target="tpu_custom_call" | custom-call | bytes 6291456 | tf_op jit(solution)/shard_map/pallas_call | solution.py:62
  10.9 0.0 collective-permute-done
  10.9 0.0 collective-permute-done.1
  10.9 0.0 collective-permute-done.2
  10.9 0.1 fusion.19
  11.0 0.1 fusion.13
  11.1 0.7 collective-permute-start.4
  11.8 0.9 collective-permute-start.5
  12.7 0.0 collective-permute-start.3
  12.7 0.0 copy-done.6
  12.8 0.2 fusion.30
  13.0 0.1 subtract_bitcast_fusion
  13.1 0.1 fusion.38
  13.2 0.1 bitcast_compare_fusion
  13.4 0.4 collective-permute-done.3
  13.8 0.1 fusion.15
  14.0 1.4 %convolution_convert_fusion = bf16[512,1024]{1,0:T(8,128)(2,1)} fusion(pred[512,128]{1,0:T(32,128)(4,1)S(1)} %bitcast_compare_fusion, bf16[128,256]{1,0:T(8,128)(2,1)S(1)} %get-tuple-element.66, bf16[128,256]{1,0:T(8,128)(2,1)S(1)} %get-tuple-element.65, bf16[128,256]{1,0:T(8,128)(2,1)S(1)} %get-tuple-element.64, bf16[128,256]{1,0:T(8,128)(2,1)S(1)} %get-tuple-element.63), kind=kOutput, calls=%fused_computation.1 | convolution fusion | flops 135790592 | bytes 1376256 | tf_op jit(solution)/shard_map/dot_general | solution.py:223
  15.4 11.7 %all-to-all-start = ((bf16[32,16,1024]{2,1,0:T(8,128)(2,1)}), bf16[32,16,1024]{2,1,0:T(8,128)(2,1)S(1)}, u32[]{:S(2)}, u32[]{:S(2)}) async-start(bf16[32,16,1024]{2,1,0:T(8,128)(2,1)} %bitcast.65), calls=%async_computation | async-start | bytes 2097152 | tf_op jit(solution)/shard_map/all_to_all | solution.py:226
  27.1 0.0 copy-done.1
  27.1 0.3 collective-permute-start.7
  27.4 11.0 %collective-permute-done.4.refs_4_ = bf16[6,384,256]{2,1,0:T(8,128)(2,1)} collective-permute-done((bf16[6,384,256]{2,1,0:T(8,128)(2,1)}, bf16[6,384,256]{2,1,0:T(8,128)(2,1)}, u32[]{:S(2)}, u32[]{:S(2)}) %collective-permute-start.4) | collective-permute-done | bytes 1179680 | tf_op jit(solution)/shard_map/ppermute | solution.py:182
  38.4 1.5 %collective-permute-done.5.refs_2_ = bf16[6,384,256]{2,1,0:T(8,128)(2,1)} collective-permute-done((bf16[6,384,256]{2,1,0:T(8,128)(2,1)}, bf16[6,384,256]{2,1,0:T(8,128)(2,1)}, u32[]{:S(2)}, u32[]{:S(2)}) %collective-permute-start.5) | collective-permute-done | bytes 1179680 | tf_op jit(solution)/shard_map/ppermute | solution.py:182
  39.9 0.6 collective-permute-start.6
  40.6 3.7 %collective-permute-done.7 = bf16[2,384,256]{2,1,0:T(8,128)(2,1)S(1)} collective-permute-done((bf16[2,384,256]{2,1,0:T(8,128)(2,1)S(1)}, bf16[2,384,256]{2,1,0:T(8,128)(2,1)S(1)}, u32[]{:S(2)}, u32[]{:S(2)}) %collective-permute-start.7) | collective-permute-done | bytes 393248 | tf_op jit(solution)/shard_map/ppermute | solution.py:182
  44.2 1.9 %collective-permute-start.8 = (bf16[2,384,256]{2,1,0:T(8,128)(2,1)S(1)}, bf16[2,384,256]{2,1,0:T(8,128)(2,1)S(1)}, u32[]{:S(2)}, u32[]{:S(2)}) collective-permute-start(bf16[2,384,256]{2,1,0:T(8,128)(2,1)S(1)} %collective-permute-done.7), channel_id=1, source_target_pairs={{2,4},{4,2},{6,0},{0,6},{8,10},{10,8},{12,14},{14,12},{3,5},{5,3},... | collective-permute-start | bytes 1179656 | tf_op jit(solution)/shard_map/ppermute | solution.py:182
  46.2 8.0 %collective-permute-done.8 = bf16[2,384,256]{2,1,0:T(8,128)(2,1)S(1)} collective-permute-done((bf16[2,384,256]{2,1,0:T(8,128)(2,1)S(1)}, bf16[2,384,256]{2,1,0:T(8,128)(2,1)S(1)}, u32[]{:S(2)}, u32[]{:S(2)}) %collective-permute-start.8) | collective-permute-done | bytes 393248 | tf_op jit(solution)/shard_map/ppermute | solution.py:182
  54.2 1.7 %collective-permute-start.10 = (bf16[2,384,256]{2,1,0:T(8,128)(2,1)}, bf16[2,384,256]{2,1,0:T(8,128)(2,1)}, u32[]{:S(2)}, u32[]{:S(2)}) collective-permute-start(bf16[2,384,256]{2,1,0:T(8,128)(2,1)} %get-tuple-element.42), channel_id=1, source_target_pairs={{0,6},{2,4},{4,2},{6,0},{10,8},{12,14},{14,12},{8,10},{1,7},{3,5},... | collective-permute-start | bytes 1179656 | tf_op jit(solution)/shard_map/ppermute | solution.py:182
  55.9 3.0 %collective-permute-start.9 = (bf16[2,384,256]{2,1,0:T(8,128)(2,1)S(1)}, bf16[2,384,256]{2,1,0:T(8,128)(2,1)S(1)}, u32[]{:S(2)}, u32[]{:S(2)}) collective-permute-start(bf16[2,384,256]{2,1,0:T(8,128)(2,1)S(1)} %collective-permute-done.8), channel_id=1, source_target_pairs={{0,8},{2,10},{4,12},{6,14},{8,0},{10,2},{12,4},{14,6},{1,9},{3,11}... | collective-permute-start | bytes 1179656 | tf_op jit(solution)/shard_map/ppermute | solution.py:182
  58.9 4.7 %collective-permute-done.10.refs_5_ = bf16[2,384,256]{2,1,0:T(8,128)(2,1)} collective-permute-done((bf16[2,384,256]{2,1,0:T(8,128)(2,1)}, bf16[2,384,256]{2,1,0:T(8,128)(2,1)}, u32[]{:S(2)}, u32[]{:S(2)}) %collective-permute-start.10) | collective-permute-done | bytes 393248 | tf_op jit(solution)/shard_map/ppermute | solution.py:182
  63.6 1.5 %collective-permute-done.9.refs_3_ = bf16[2,384,256]{2,1,0:T(8,128)(2,1)S(1)} collective-permute-done((bf16[2,384,256]{2,1,0:T(8,128)(2,1)S(1)}, bf16[2,384,256]{2,1,0:T(8,128)(2,1)S(1)}, u32[]{:S(2)}, u32[]{:S(2)}) %collective-permute-start.9) | collective-permute-done | bytes 393248 | tf_op jit(solution)/shard_map/ppermute | solution.py:182
  65.1 0.8 copy-done.3
  65.9 0.0 all-to-all-done
  65.9 1.2 collective-permute-done.6.refs_0_
  67.1 0.0 collective-permute-start.11
  67.1 0.4 collective-permute-start.12
  67.5 0.1 pad_add_fusion.place_ref
  67.6 2.2 %collective-permute-done.11.across = bf16[512,1024]{1,0:T(8,128)(2,1)S(1)} collective-permute-done((bf16[512,1024]{1,0:T(8,128)(2,1)S(1)}, bf16[512,1024]{1,0:T(8,128)(2,1)S(1)}, u32[]{:S(2)}, u32[]{:S(2)}) %collective-permute-start.11) | collective-permute-done | bytes 1048608 | tf_op jit(solution)/shard_map/ppermute | solution.py:230
  69.8 0.0 copy-done
  69.8 1.0 copy-done.2
  70.8 1.0 copy-done.4
  71.8 6.5 %shard_map.74 = (f32[512,1024]{1,0:T(8,128)S(1)}, f32[512,1024]{1,0:T(8,128)S(1)}) custom-call(s32[2]{0:T(128)S(1)} %pad_add_fusion.place_ref, bf16[512,1024]{1,0:T(8,128)(2,1)S(1)} %bitcast.63, bf16[512,1024]{1,0:T(8,128)(2,1)S(1)} %collective-permute-done.11.across, bf16[6,384,256]{2,1,0:T(8,128)(2,1)S(1)} %copy-done, bf16[2,384,256]{2,1,0:T(8,128)(2,1)S(1)} %copy-done.2, ...), custom_call_target="tpu_custom_call" | custom-call | flops 268435456 | bytes 1048576 | tf_op jit(solution)/shard_map/pallas_call | solution.py:127
  78.3 1.9 %collective-permute-done.12.refs_1_ = bf16[2,384,256]{2,1,0:T(8,128)(2,1)} collective-permute-done((bf16[2,384,256]{2,1,0:T(8,128)(2,1)}, bf16[2,384,256]{2,1,0:T(8,128)(2,1)}, u32[]{:S(2)}, u32[]{:S(2)}) %collective-permute-start.12) | collective-permute-done | bytes 393248 | tf_op jit(solution)/shard_map/ppermute | solution.py:182
  80.2 4.3 %shard_map.75 = (f32[512,1024]{1,0:T(8,128)S(1)}, bf16[512,1024]{1,0:T(8,128)(2,1)S(1)}) custom-call(s32[2]{0:T(128)S(1)} %pad_add_fusion.place_ref, bf16[512,1024]{1,0:T(8,128)(2,1)S(1)} %bitcast.64, bf16[512,1024]{1,0:T(8,128)(2,1)S(1)} %collective-permute-done.11.across, bf16[6,384,256]{2,1,0:T(8,128)(2,1)} %collective-permute-done.6.refs_0_, ...), custom_call_target="tpu_custom_call" | custom-call | flops 268435456 | bytes 1048576 | tf_op jit(solution)/shard_map/pallas_call | solution.py:127
  84.5 0.1 collective-permute-start.13
  84.6 2.6 %collective-permute-done.13 = bf16[512,1024]{1,0:T(8,128)(2,1)S(1)} collective-permute-done((bf16[512,1024]{1,0:T(8,128)(2,1)S(1)}, bf16[512,1024]{1,0:T(8,128)(2,1)S(1)}, u32[]{:S(2)}, u32[]{:S(2)}) %collective-permute-start.13) | collective-permute-done | bytes 1048608 | tf_op jit(solution)/shard_map/ppermute | solution.py:233
  87.2 1.4 add_convert_fusion
  88.6 11.8 %all-to-all-start.1 = ((bf16[32,16,1024]{2,1,0:T(8,128)(2,1)}), bf16[32,16,1024]{2,1,0:T(8,128)(2,1)S(1)}, u32[]{:S(2)}, u32[]{:S(2)}) async-start(bf16[32,16,1024]{2,1,0:T(8,128)(2,1)} %bitcast.24), calls=%async_computation.1 | async-start | bytes 2097152 | tf_op jit(solution)/shard_map/all_to_all | solution.py:234
  100.5 0.1 select_bitcast_fusion
  100.6 0.1 reduce-precision_convert_fusion
  100.7 28.0 %all-to-all-done.1 = bf16[32,16,1024]{2,1,0:T(8,128)(2,1)S(1)} async-done(((bf16[32,16,1024]{2,1,0:T(8,128)(2,1)}), bf16[32,16,1024]{2,1,0:T(8,128)(2,1)S(1)}, u32[]{:S(2)}, u32[]{:S(2)}) %all-to-all-start.1) | async-done | bytes 1048608 | tf_op jit(solution)/shard_map/all_to_all | solution.py:234
  128.8 0.5 fusion.8
  129.2 0.1 fusion.51
  129.3 0.3 collective-permute-start.14
  129.7 3.0 %collective-permute-start.15 = (bf16[128,256]{1,0:T(8,128)(2,1)S(1)}, bf16[128,256]{1,0:T(8,128)(2,1)S(1)}, u32[]{:S(2)}, u32[]{:S(2)}) collective-permute-start(bf16[128,256]{1,0:T(8,128)(2,1)S(1)} %get-tuple-element.56), channel_id=1, source_target_pairs={{0,4},{2,6},{4,0},{6,2},{1,5},{3,7},{5,1},{7,3},{8,12},{10,14},{12... | collective-permute-start | bytes 196616 | tf_op jit(solution)/shard_map/ppermute | solution.py:171
  132.7 0.9 collective-permute-start.16
  133.5 1.3 collective-permute-done.14
  134.9 0.7 collective-permute-done.15
  135.6 1.3 collective-permute-done.16
  136.9 0.7 fusion.27
  (27 shorter events, 0.3 us)
Async XLA Ops:
  0.0 12.7 %copy-start.6 = (s32[128,8]{0,1:T(8,128)S(1)}, s32[128,8]{0,1:T(8,128)}, u32[]{:S(2)}) copy-start(s32[128,8]{0,1:T(8,128)} %param.10) | copy-start | bytes 12292
  0.9 9.9 %collective-permute-start = (bf16[144,256]{1,0:T(8,128)(2,1)S(1)}, bf16[144,256]{1,0:T(8,128)(2,1)S(1)}, u32[]{:S(2)}, u32[]{:S(2)}) collective-permute-start(bf16[144,256]{1,0:T(8,128)(2,1)S(1)} %pad_select_fusion), channel_id=1, source_target_pairs={{0,2},{2,4},{4,6},{6,0},{1,3},{3,5},{5,7},{7,1},{8,10},{10,12},{12... | collective-permute-start | bytes 221192 | tf_op jit(solution)/shard_map/ppermute | solution.py:171
  2.5 8.3 %collective-permute-start.1 = (bf16[144,256]{1,0:T(8,128)(2,1)S(1)}, bf16[144,256]{1,0:T(8,128)(2,1)S(1)}, u32[]{:S(2)}, u32[]{:S(2)}) collective-permute-start(bf16[144,256]{1,0:T(8,128)(2,1)S(1)} %pad_select_fusion), channel_id=1, source_target_pairs={{0,4},{2,6},{4,0},{6,2},{1,5},{3,7},{5,1},{7,3},{8,12},{10,14},{12... | collective-permute-start | bytes 221192 | tf_op jit(solution)/shard_map/ppermute | solution.py:171
  5.2 5.6 %collective-permute-start.2 = (bf16[144,256]{1,0:T(8,128)(2,1)S(1)}, bf16[144,256]{1,0:T(8,128)(2,1)S(1)}, u32[]{:S(2)}, u32[]{:S(2)}) collective-permute-start(bf16[144,256]{1,0:T(8,128)(2,1)S(1)} %pad_select_fusion), channel_id=1, source_target_pairs={{0,6},{2,0},{4,2},{6,4},{1,7},{3,1},{5,3},{7,5},{8,14},{10,8},{12,... | collective-permute-start | bytes 221192 | tf_op jit(solution)/shard_map/ppermute | solution.py:171
  11.1 27.3 %collective-permute-start.4 = (bf16[6,384,256]{2,1,0:T(8,128)(2,1)}, bf16[6,384,256]{2,1,0:T(8,128)(2,1)}, u32[]{:S(2)}, u32[]{:S(2)}) collective-permute-start(bf16[6,384,256]{2,1,0:T(8,128)(2,1)} %get-tuple-element.37), channel_id=1, source_target_pairs={{0,6},{2,4},{4,2},{6,0},{10,8},{12,14},{14,12},{8,10},{1,7},{3,5},... | collective-permute-start | bytes 3538952 | tf_op jit(solution)/shard_map/ppermute | solution.py:182
  11.8 28.1 %collective-permute-start.5 = (bf16[6,384,256]{2,1,0:T(8,128)(2,1)}, bf16[6,384,256]{2,1,0:T(8,128)(2,1)}, u32[]{:S(2)}, u32[]{:S(2)}) collective-permute-start(bf16[6,384,256]{2,1,0:T(8,128)(2,1)} %get-tuple-element.31.refs_0_), channel_id=1, source_target_pairs={{0,2},{2,0},{4,6},{6,4},{10,12},{12,10},{14,8},{8,14},{1,3},{3,1},... | collective-permute-start | bytes 3538952 | tf_op jit(solution)/shard_map/ppermute | solution.py:182
  12.7 1.1 collective-permute-start.3
  13.1 14.0 %copy-start.1 = (bf16[2,384,256]{2,1,0:T(8,128)(2,1)S(1)}, bf16[2,384,256]{2,1,0:T(8,128)(2,1)}, u32[]{:S(2)}) copy-start(bf16[2,384,256]{2,1,0:T(8,128)(2,1)} %get-tuple-element.39.refs_1_) | copy-start | bytes 1179652
  13.1 56.7 %copy-start = (bf16[6,384,256]{2,1,0:T(8,128)(2,1)S(1)}, bf16[6,384,256]{2,1,0:T(8,128)(2,1)}, u32[]{:S(2)}) copy-start(bf16[6,384,256]{2,1,0:T(8,128)(2,1)} %get-tuple-element.31.refs_0_) | copy-start | bytes 3538948
  15.4 50.5 %all-to-all-start = ((bf16[32,16,1024]{2,1,0:T(8,128)(2,1)}), bf16[32,16,1024]{2,1,0:T(8,128)(2,1)S(1)}, u32[]{:S(2)}, u32[]{:S(2)}) async-start(bf16[32,16,1024]{2,1,0:T(8,128)(2,1)} %bitcast.65), calls=%async_computation | async-start | bytes 2097152 | tf_op jit(solution)/shard_map/all_to_all | solution.py:226
  27.1 17.1 %collective-permute-start.7 = (bf16[2,384,256]{2,1,0:T(8,128)(2,1)S(1)}, bf16[2,384,256]{2,1,0:T(8,128)(2,1)S(1)}, u32[]{:S(2)}, u32[]{:S(2)}) collective-permute-start(bf16[2,384,256]{2,1,0:T(8,128)(2,1)S(1)} %copy-done.1), channel_id=1, source_target_pairs={{0,8},{2,10},{4,12},{6,14},{8,0},{10,2},{12,4},{14,6},{1,9},{3,11}... | collective-permute-start | bytes 1179656 | tf_op jit(solution)/shard_map/ppermute | solution.py:182
  39.9 27.2 %collective-permute-start.6 = (bf16[6,384,256]{2,1,0:T(8,128)(2,1)}, bf16[6,384,256]{2,1,0:T(8,128)(2,1)}, u32[]{:S(2)}, u32[]{:S(2)}) collective-permute-start(bf16[6,384,256]{2,1,0:T(8,128)(2,1)} %collective-permute-done.4.refs_4_), channel_id=1, source_target_pairs={{0,2},{2,0},{4,6},{6,4},{10,12},{12,10},{14,8},{8,14},{1,3},{3,1},... | collective-permute-start | bytes 3538952 | tf_op jit(solution)/shard_map/ppermute | solution.py:182
  44.2 9.9 %collective-permute-start.8 = (bf16[2,384,256]{2,1,0:T(8,128)(2,1)S(1)}, bf16[2,384,256]{2,1,0:T(8,128)(2,1)S(1)}, u32[]{:S(2)}, u32[]{:S(2)}) collective-permute-start(bf16[2,384,256]{2,1,0:T(8,128)(2,1)S(1)} %collective-permute-done.7), channel_id=1, source_target_pairs={{2,4},{4,2},{6,0},{0,6},{8,10},{10,8},{12,14},{14,12},{3,5},{5,3},... | collective-permute-start | bytes 1179656 | tf_op jit(solution)/shard_map/ppermute | solution.py:182
  54.2 9.4 %collective-permute-start.10 = (bf16[2,384,256]{2,1,0:T(8,128)(2,1)}, bf16[2,384,256]{2,1,0:T(8,128)(2,1)}, u32[]{:S(2)}, u32[]{:S(2)}) collective-permute-start(bf16[2,384,256]{2,1,0:T(8,128)(2,1)} %get-tuple-element.42), channel_id=1, source_target_pairs={{0,6},{2,4},{4,2},{6,0},{10,8},{12,14},{14,12},{8,10},{1,7},{3,5},... | collective-permute-start | bytes 1179656 | tf_op jit(solution)/shard_map/ppermute | solution.py:182
  55.9 9.2 %collective-permute-start.9 = (bf16[2,384,256]{2,1,0:T(8,128)(2,1)S(1)}, bf16[2,384,256]{2,1,0:T(8,128)(2,1)S(1)}, u32[]{:S(2)}, u32[]{:S(2)}) collective-permute-start(bf16[2,384,256]{2,1,0:T(8,128)(2,1)S(1)} %collective-permute-done.8), channel_id=1, source_target_pairs={{0,8},{2,10},{4,12},{6,14},{8,0},{10,2},{12,4},{14,6},{1,9},{3,11}... | collective-permute-start | bytes 1179656 | tf_op jit(solution)/shard_map/ppermute | solution.py:182
  65.1 0.8 copy-start.3
  67.1 2.7 %collective-permute-start.11 = (bf16[512,1024]{1,0:T(8,128)(2,1)S(1)}, bf16[512,1024]{1,0:T(8,128)(2,1)S(1)}, u32[]{:S(2)}, u32[]{:S(2)}) collective-permute-start(bf16[512,1024]{1,0:T(8,128)(2,1)S(1)} %bitcast.62), channel_id=1, source_target_pairs={{0,1},{1,0},{2,3},{3,2},{4,5},{5,4},{6,7},{7,6},{8,9},{9,8},{10,11... | collective-permute-start | bytes 3145736 | tf_op jit(solution)/shard_map/ppermute | solution.py:230
  67.1 13.1 %collective-permute-start.12 = (bf16[2,384,256]{2,1,0:T(8,128)(2,1)}, bf16[2,384,256]{2,1,0:T(8,128)(2,1)}, u32[]{:S(2)}, u32[]{:S(2)}) collective-permute-start(bf16[2,384,256]{2,1,0:T(8,128)(2,1)} %collective-permute-done.10.refs_5_), channel_id=1, source_target_pairs={{0,2},{2,0},{4,6},{6,4},{10,12},{12,10},{14,8},{8,14},{1,3},{3,1},... | collective-permute-start | bytes 1179656 | tf_op jit(solution)/shard_map/ppermute | solution.py:182
  69.8 1.0 copy-start.2
  70.8 1.0 copy-start.4
  84.5 2.7 %collective-permute-start.13 = (bf16[512,1024]{1,0:T(8,128)(2,1)S(1)}, bf16[512,1024]{1,0:T(8,128)(2,1)S(1)}, u32[]{:S(2)}, u32[]{:S(2)}) collective-permute-start(bf16[512,1024]{1,0:T(8,128)(2,1)S(1)} %get-tuple-element.48), channel_id=1, source_target_pairs={{0,1},{1,0},{2,3},{3,2},{4,5},{5,4},{6,7},{7,6},{8,9},{9,8},{10,11... | collective-permute-start | bytes 3145736 | tf_op jit(solution)/shard_map/ppermute | solution.py:233
  88.6 11.8 %copy-start.5 = (f32[128,64]{0,1:T(8,128)S(1)}, f32[128,64]{0,1:T(8,128)}, u32[]{:S(2)}) copy-start(f32[128,64]{0,1:T(8,128)} %param.9) | copy-start | bytes 98308
  88.6 40.2 %all-to-all-start.1 = ((bf16[32,16,1024]{2,1,0:T(8,128)(2,1)}), bf16[32,16,1024]{2,1,0:T(8,128)(2,1)S(1)}, u32[]{:S(2)}, u32[]{:S(2)}) async-start(bf16[32,16,1024]{2,1,0:T(8,128)(2,1)} %bitcast.24), calls=%async_computation.1 | async-start | bytes 2097152 | tf_op jit(solution)/shard_map/all_to_all | solution.py:234
  129.3 5.6 %collective-permute-start.14 = (bf16[128,256]{1,0:T(8,128)(2,1)S(1)}, bf16[128,256]{1,0:T(8,128)(2,1)S(1)}, u32[]{:S(2)}, u32[]{:S(2)}) collective-permute-start(bf16[128,256]{1,0:T(8,128)(2,1)S(1)} %get-tuple-element.54), channel_id=1, source_target_pairs={{0,2},{2,4},{4,6},{6,0},{1,3},{3,5},{5,7},{7,1},{8,10},{10,12},{12... | collective-permute-start | bytes 196616 | tf_op jit(solution)/shard_map/ppermute | solution.py:171
  129.7 5.9 %collective-permute-start.15 = (bf16[128,256]{1,0:T(8,128)(2,1)S(1)}, bf16[128,256]{1,0:T(8,128)(2,1)S(1)}, u32[]{:S(2)}, u32[]{:S(2)}) collective-permute-start(bf16[128,256]{1,0:T(8,128)(2,1)S(1)} %get-tuple-element.56), channel_id=1, source_target_pairs={{0,4},{2,6},{4,0},{6,2},{1,5},{3,7},{5,1},{7,3},{8,12},{10,14},{12... | collective-permute-start | bytes 196616 | tf_op jit(solution)/shard_map/ppermute | solution.py:171
  132.7 4.3 %collective-permute-start.16 = (bf16[128,256]{1,0:T(8,128)(2,1)S(1)}, bf16[128,256]{1,0:T(8,128)(2,1)S(1)}, u32[]{:S(2)}, u32[]{:S(2)}) collective-permute-start(bf16[128,256]{1,0:T(8,128)(2,1)S(1)} %get-tuple-element.55), channel_id=1, source_target_pairs={{0,6},{2,0},{4,2},{6,4},{1,7},{3,1},{5,3},{7,5},{8,14},{10,8},{12,... | collective-permute-start | bytes 196616 | tf_op jit(solution)/shard_map/ppermute | solution.py:171

commit v10 on v9

--- a/solution.py
+++ b/solution.py
@@ -72,8 +72,8 @@
     return picked[:2], picked[2:]
 
 
-def ffn_kernel(count, place_ref, arrived, across, *refs):
-    lying, added, (keep, give, hidden, held_shards, sems) = refs[:count], refs[count:-5], refs[-5:]
+def ffn_kernel(count, last, place_ref, arrived, across, *refs):
+    lying, (early, give, hidden, held_shards, sems) = refs[:count], refs[count:]
     total_blocks = held_shards.shape[1]
     copies, first = [], 0
     for n, piece in enumerate(lying):
@@ -109,34 +109,84 @@
         gate_val, up_val = both[:, :unit], both[:, unit:]
         silu = gate_val / (1.0 + jnp.exp(-gate_val))
         hidden[:, pl.ds(k * unit, unit)] = (silu * up_val).astype(hidden.dtype)
-    for which, (parity, out) in enumerate(((core, keep), (1 - core, give))):
+    for parity, out in ((1 - core, give),) if last else ((core, early), (1 - core, give)):
         for j in range(ring):
             lanes = pl.ds(j * block, block)
-            total = added[which][:, lanes] if added else jnp.zeros((rows, block), f32)
             down = jnp.concatenate([shard[target(j, parity), block:, :] for shard in shards], axis=0)
-            total += jnp.dot(hidden[...], down, preferred_element_type=f32)
+            total = jnp.dot(hidden[...], down, preferred_element_type=f32)
+            if last:
+                total += early[:, lanes]
             out[:, lanes] = total.astype(out.dtype)
 
 
-def expert_rows(place, arrived, across, pieces, added, give_type):
+def lie(pieces):
+    return [pltpu.with_memory_space_constraint(piece, pltpu.HBM) for piece in pieces]
+
+
+def sums_kernel(count, place_ref, hidden, *refs):
+    lying, (added, keep, downs, sems) = refs[:count], refs[count:]
+    copies, first = [], 0
+    for n, piece in enumerate(lying):
+        source = piece.at[:, pl.ds(block, downs.shape[1]), :]
+        into = downs.at[pl.ds(first, piece.shape[0])]
+        copies.append(pltpu.make_async_copy(source, into, sems.at[n]))
+        first += piece.shape[0]
+    for copy in copies:
+        copy.start()
+    for copy in copies:
+        copy.wait()
+    row, core = place_ref[0], place_ref[1]
+    ring = keep.shape[1] // block
+    for j in range(ring):
+        lanes = pl.ds(j * block, block)
+        down = downs[2 * lax.rem(row + j, ring) + core]
+        keep[:, lanes] = added[:, lanes] + jnp.dot(
+            hidden[...], down, preferred_element_type=jnp.float32
+        )
+
+
+def kept_sums(place, hidden, pieces, added):
+    count = len(pieces)
+    blocks = sum(piece.shape[0] for piece in pieces)
+    whole = pl.BlockSpec(memory_space=pltpu.VMEM)
+    return pl.pallas_call(
+        functools.partial(sums_kernel, count),
+        out_shape=jax.ShapeDtypeStruct(added.shape, added.dtype),
+        in_specs=[pl.BlockSpec(memory_space=pltpu.SMEM), whole]
+        + [pl.BlockSpec(memory_space=pl.ANY)] * count
+        + [whole],
+        out_specs=whole,
+        scratch_shapes=[
+            pltpu.VMEM((blocks, block // 2, block), jnp.bfloat16),
+            pltpu.SemaphoreType.DMA((count,)),
+        ],
+        compiler_params=pltpu.CompilerParams(vmem_limit_bytes=40 * 2**20),
+        cost_estimate=pl.CostEstimate(
+            flops=2 * hidden.size * added.shape[1], bytes_accessed=2**20, transcendentals=0
+        ),
+    )(place, hidden, *lie(pieces), added)
+
+
+def expert_rows(place, arrived, across, pieces, early=None):
     rows, held = arrived.shape
     unit, width, count = block // 2, 2 * held, len(pieces)
     blocks = width // block
     shards = sum(piece.shape[0] for piece in pieces) // blocks
+    last = early is not None
+    sums = jax.ShapeDtypeStruct((rows, held), jnp.float32)
+    leaving = jax.ShapeDtypeStruct((rows, held), jnp.bfloat16)
+    hidden = jax.ShapeDtypeStruct((rows, shards * unit), jnp.bfloat16)
     whole = pl.BlockSpec(memory_space=pltpu.VMEM)
     return pl.pallas_call(
-        functools.partial(ffn_kernel, count),
-        out_shape=(
-            jax.ShapeDtypeStruct((rows, held), jnp.float32),
-            jax.ShapeDtypeStruct((rows, held), give_type),
-        ),
+        functools.partial(ffn_kernel, count, last),
+        out_shape=(leaving, hidden) if last else (sums, sums),
         in_specs=[pl.BlockSpec(memory_space=pltpu.SMEM)]
         + [whole] * 2
         + [pl.BlockSpec(memory_space=pl.ANY)] * count
-        + [whole] * len(added),
+        + [whole] * last,
         out_specs=(whole, whole),
-        scratch_shapes=[
-            pltpu.VMEM((rows, shards * unit), jnp.bfloat16),
+        scratch_shapes=([] if last else [pltpu.VMEM(hidden.shape, hidden.dtype)])
+        + [
             pltpu.VMEM((shards, blocks, *pieces[0].shape[1:]), jnp.bfloat16),
             pltpu.SemaphoreType.DMA((count,)),
         ],
@@ -144,7 +194,7 @@
         cost_estimate=pl.CostEstimate(
             flops=2 * rows * width * unit, bytes_accessed=2**20, transcendentals=0
         ),
-    )(place, arrived, across, *pieces, *added)
+    )(place, arrived, across, *lie(pieces), *([early] if last else []))
 
 
 def on_device(tokens, norm_gain, router_logits, routes, gate_proj, up_proj, down_proj):
@@ -186,8 +236,8 @@
 
     crossed = [send(other[0], cross_chip)]
     near = send(own[0], near_chip)
-    passed = after(send(own[1], other_row), crossed[0], near)
-    passed = send(passed, near_lent)
+    hopped = send(own[1], other_row)
+    passed = send(after(hopped, crossed[0], near), near_lent)
     crossed.append(send(after(other[1], passed), cross_chip))
     lent = send(passed, other_row)
     relayed = [send(after(crossed[0], near), near_chip), send(crossed[1], near_chip)]
@@ -223,13 +273,15 @@
     outgoing = jnp.dot(
         table.reshape(ep_count * share, group_size), normed, preferred_element_type=f32
     ).astype(bf16)
+    outgoing = after(outgoing, hopped)
     arrived = lax.all_to_all(
         outgoing.reshape(ep_count, share, -1), ep, split_axis=0, concat_axis=0, tiled=True
     ).reshape(ep_count * share, -1)
     arrived = after(arrived, relayed[0], lent, crossed[1])
     across = lax.ppermute(arrived, "core", other_core)
-    added = expert_rows(place, arrived, across, (*own, near, lent, *crossed), (), f32)
-    keep, give = expert_rows(place, arrived, across, relayed, added, bf16)
+    kept, leaving = expert_rows(place, arrived, across, (*own, near, lent, *crossed))
+    give, hidden = expert_rows(place, arrived, across, relayed, leaving)
+    keep = kept_sums(place, hidden, relayed, kept)
     summed = keep + lax.ppermute(give, "core", other_core).astype(f32)
     returned = lax.all_to_all(
         summed.astype(bf16).reshape(ep_count, share, -1), ep, split_axis=0, concat_axis=0, tiled=True

time: 138 us -> 136 us (0.986)
  starting transfers between devices: 43.1 us -> 39 us
  waiting for transfers between devices: 70.2 us -> 72.7 us
  local copies, waits for them, and re-layouts: 2.96 us -> 0.98 us
  Pallas kernels: 14.8 us -> 16.7 us
    ppermute x8, waiting for transfers between devices: 33.6 us -> 37.9 us  [send(): return lax.ppermute(one, ('pair', 'x'), pairs)]
    ppermute x8, starting transfers between devices: 9.53 us -> 6.54 us  [send(): return lax.ppermute(one, ('pair', 'x'), pairs)]
    ppermute x1, waiting for transfers between devices: 2.65 us -> 0.62 us  [on_device(): summed = keep + lax.ppermute(give, 'core', other_core).astype(f32)]
    unnamed x14 -> x12, local copies, waits for them, and re-layouts: 2.76 us -> 0.78 us
    pallas_call x2 -> x3, Pallas kernels: 10.8 us -> 12.7 us  [the longest x2 10.7 us: expert_rows(): pl.pallas_call(functools.partial(ffn_kernel, count, last), out_shape=(lea...]
  transfers between devices with their start and end apart: 19 -> 19, of which waited for: 15 -> 14; matrix products, arithmetic and copies ran while one was open for 2% -> 2% of each run, Pallas kernels for 8% -> 10%
where the time goes in v10:
time: 136 us
  waiting for transfers between devices  72.7 us (53%)
  starting transfers between devices  39 us (29%)
  Pallas kernels  16.7 us (12%)
  other arithmetic  4.17 us (3%)
  matrix products  2.08 us (2%)
    ppermute x8, waiting for transfers between devices, send(): return lax.ppermute(one, ('pair', 'x'), pairs)  37.9 us
    all_to_all x1, waiting for transfers between devices, on_device(): lax.all_to_all(summed.astype(bf16).reshape(ep_count, share, -1), ep, spli...  28 us
    all_to_all x1, starting transfers between devices, on_device(): lax.all_to_all(summed.astype(bf16).reshape(ep_count, share, -1), ep, spli...  11.6 us
    all_to_all x1, starting transfers between devices, on_device(): lax.all_to_all(outgoing.reshape(ep_count, share, -1), ep, split_axis=0, c...  11.6 us
    pallas_call x2, Pallas kernels, expert_rows(): pl.pallas_call(functools.partial(ffn_kernel, count, last), out_shape=(lea...  10.7 us
    ppermute x6, starting transfers between devices, ring_send(): return lax.ppermute(one, 'x', pairs)  9.04 us
    ppermute x8, starting transfers between devices, send(): return lax.ppermute(one, ('pair', 'x'), pairs)  6.54 us
    pallas_call x1, Pallas kernels, pick_shards(): pl.pallas_call(pick_kernel, out_shape=tuple((jax.ShapeDtypeStruct((size,...  3.99 us
  transfers between devices with their start and end apart: 19, of which 14 were waited for; matrix products, arithmetic and copies ran while one was open for 2% of the time, Pallas kernels for 10%

profile of v10, /device:TPU:8, one launch (start us, length us, event | category | flops | bytes accessed | tf_op | source)
XLA Modules:
  0.0 135.9 jit_solution(7977863933510832718)
XLA Ops:
  0.0 0.9 pad_select_fusion
  0.9 1.6 %collective-permute-start = (bf16[144,256]{1,0:T(8,128)(2,1)S(1)}, bf16[144,256]{1,0:T(8,128)(2,1)S(1)}, u32[]{:S(2)}, u32[]{:S(2)}) collective-permute-start(bf16[144,256]{1,0:T(8,128)(2,1)S(1)} %pad_select_fusion), channel_id=1, source_target_pairs={{0,2},{2,4},{4,6},{6,0},{1,3},{3,5},{5,7},{7,1},{8,10},{10,12},{12... | collective-permute-start | bytes 221192 | tf_op jit(solution)/shard_map/ppermute | solution.py:221
  2.5 2.7 %collective-permute-start.1 = (bf16[144,256]{1,0:T(8,128)(2,1)S(1)}, bf16[144,256]{1,0:T(8,128)(2,1)S(1)}, u32[]{:S(2)}, u32[]{:S(2)}) collective-permute-start(bf16[144,256]{1,0:T(8,128)(2,1)S(1)} %pad_select_fusion), channel_id=1, source_target_pairs={{0,4},{2,6},{4,0},{6,2},{1,5},{3,7},{5,1},{7,3},{8,12},{10,14},{12... | collective-permute-start | bytes 221192 | tf_op jit(solution)/shard_map/ppermute | solution.py:221
  5.2 1.4 %collective-permute-start.2 = (bf16[144,256]{1,0:T(8,128)(2,1)S(1)}, bf16[144,256]{1,0:T(8,128)(2,1)S(1)}, u32[]{:S(2)}, u32[]{:S(2)}) collective-permute-start(bf16[144,256]{1,0:T(8,128)(2,1)S(1)} %pad_select_fusion), channel_id=1, source_target_pairs={{0,6},{2,0},{4,2},{6,4},{1,7},{3,1},{5,3},{7,5},{8,14},{10,8},{12,... | collective-permute-start | bytes 221192 | tf_op jit(solution)/shard_map/ppermute | solution.py:221
  6.7 0.1 eq.78
  6.8 4.0 %shard_map.73 = (bf16[6,384,256]{2,1,0:T(8,128)(2,1)}, bf16[2,384,256]{2,1,0:T(8,128)(2,1)}, bf16[6,384,256]{2,1,0:T(8,128)(2,1)}, bf16[2,384,256]{2,1,0:T(8,128)(2,1)}) custom-call(s32[1]{0:T(128)} %bitcast.kind_ref, bf16[2,2048,128]{2,1,0:T(8,128)(2,1)} %gate.1, bf16[2,2048,128]{2,1,0:T(8,128)(2,1)} %up.1, bf16[2,128,2048]{2,1,0:T(8,128)(2,1)} %down.1), custom_call_target="tpu_custom_call" | custom-call | bytes 6291456 | tf_op jit(solution)/shard_map/pallas_call | solution.py:62
  10.8 0.0 collective-permute-done
  10.9 0.0 collective-permute-done.1
  10.9 0.0 collective-permute-done.2
  10.9 0.1 fusion.19
  11.0 0.1 fusion.13
  11.1 0.7 collective-permute-start.5
  11.8 0.9 collective-permute-start.6
  12.7 1.2 collective-permute-start.4
  13.9 0.0 collective-permute-start.3
  13.9 0.0 copy-done.5
  14.0 0.2 fusion.30
  14.2 0.1 subtract_bitcast_fusion
  14.3 0.1 fusion.38
  14.4 0.1 bitcast_compare_fusion
  14.6 0.5 collective-permute-done.3
  15.0 0.1 fusion.15
  15.2 1.4 %convolution_convert_fusion = bf16[512,1024]{1,0:T(8,128)(2,1)} fusion(pred[512,128]{1,0:T(32,128)(4,1)S(1)} %bitcast_compare_fusion, bf16[128,256]{1,0:T(8,128)(2,1)S(1)} %get-tuple-element.68, bf16[128,256]{1,0:T(8,128)(2,1)S(1)} %get-tuple-element.67, bf16[128,256]{1,0:T(8,128)(2,1)S(1)} %get-tuple-element.66, bf16[128,256]{1,0:T(8,128)(2,1)S(1)} %get-tuple-element.65), kind=kOutput, calls=%fused_computation.1 | convolution fusion | flops 135790592 | bytes 1376256 | tf_op jit(solution)/shard_map/dot_general | solution.py:273
  16.6 5.6 %collective-permute-done.4 = bf16[2,384,256]{2,1,0:T(8,128)(2,1)} collective-permute-done((bf16[2,384,256]{2,1,0:T(8,128)(2,1)}, bf16[2,384,256]{2,1,0:T(8,128)(2,1)}, u32[]{:S(2)}, u32[]{:S(2)}) %collective-permute-start.4) | collective-permute-done | bytes 393248 | tf_op jit(solution)/shard_map/ppermute | solution.py:232
  22.2 11.6 %all-to-all-start = ((bf16[32,16,1024]{2,1,0:T(8,128)(2,1)}), bf16[32,16,1024]{2,1,0:T(8,128)(2,1)S(1)}, u32[]{:S(2)}, u32[]{:S(2)}) async-start(bf16[32,16,1024]{2,1,0:T(8,128)(2,1)} %bitcast.17), calls=%async_computation | async-start | bytes 2097152 | tf_op jit(solution)/shard_map/all_to_all | solution.py:277
  33.8 4.5 %collective-permute-done.5.refs_4_ = bf16[6,384,256]{2,1,0:T(8,128)(2,1)S(1)} collective-permute-done((bf16[6,384,256]{2,1,0:T(8,128)(2,1)}, bf16[6,384,256]{2,1,0:T(8,128)(2,1)S(1)}, u32[]{:S(2)}, u32[]{:S(2)}) %collective-permute-start.5) | collective-permute-done | bytes 1179680 | tf_op jit(solution)/shard_map/ppermute | solution.py:232
  38.3 1.6 %collective-permute-done.6.refs_2_ = bf16[6,384,256]{2,1,0:T(8,128)(2,1)} collective-permute-done((bf16[6,384,256]{2,1,0:T(8,128)(2,1)}, bf16[6,384,256]{2,1,0:T(8,128)(2,1)}, u32[]{:S(2)}, u32[]{:S(2)}) %collective-permute-start.6) | collective-permute-done | bytes 1179680 | tf_op jit(solution)/shard_map/ppermute | solution.py:232
  39.9 0.6 collective-permute-start.7
  40.6 0.0 collective-permute-start.8
  40.6 9.3 %collective-permute-done.8 = bf16[2,384,256]{2,1,0:T(8,128)(2,1)S(1)} collective-permute-done((bf16[2,384,256]{2,1,0:T(8,128)(2,1)}, bf16[2,384,256]{2,1,0:T(8,128)(2,1)S(1)}, u32[]{:S(2)}, u32[]{:S(2)}) %collective-permute-start.8) | collective-permute-done | bytes 393248 | tf_op jit(solution)/shard_map/ppermute | solution.py:232
  49.8 0.0 collective-permute-start.10
  49.9 2.5 %collective-permute-start.9 = (bf16[2,384,256]{2,1,0:T(8,128)(2,1)S(1)}, bf16[2,384,256]{2,1,0:T(8,128)(2,1)S(1)}, u32[]{:S(2)}, u32[]{:S(2)}) collective-permute-start(bf16[2,384,256]{2,1,0:T(8,128)(2,1)S(1)} %collective-permute-done.8), channel_id=1, source_target_pairs={{0,8},{2,10},{4,12},{6,14},{8,0},{10,2},{12,4},{14,6},{1,9},{3,11}... | collective-permute-start | bytes 1179656 | tf_op jit(solution)/shard_map/ppermute | solution.py:232
  52.3 5.5 %collective-permute-done.10.refs_5_ = bf16[2,384,256]{2,1,0:T(8,128)(2,1)S(1)} collective-permute-done((bf16[2,384,256]{2,1,0:T(8,128)(2,1)}, bf16[2,384,256]{2,1,0:T(8,128)(2,1)S(1)}, u32[]{:S(2)}, u32[]{:S(2)}) %collective-permute-start.10) | collective-permute-done | bytes 393248 | tf_op jit(solution)/shard_map/ppermute | solution.py:232
  57.8 2.7 %collective-permute-done.9.refs_3_ = bf16[2,384,256]{2,1,0:T(8,128)(2,1)S(1)} collective-permute-done((bf16[2,384,256]{2,1,0:T(8,128)(2,1)S(1)}, bf16[2,384,256]{2,1,0:T(8,128)(2,1)S(1)}, u32[]{:S(2)}, u32[]{:S(2)}) %collective-permute-start.9) | collective-permute-done | bytes 393248 | tf_op jit(solution)/shard_map/ppermute | solution.py:232
  60.5 0.0 copy-done.2
  60.5 0.8 copy-done.3
  61.3 5.5 %collective-permute-done.7.refs_0_ = bf16[6,384,256]{2,1,0:T(8,128)(2,1)S(1)} collective-permute-done((bf16[6,384,256]{2,1,0:T(8,128)(2,1)S(1)}, bf16[6,384,256]{2,1,0:T(8,128)(2,1)S(1)}, u32[]{:S(2)}, u32[]{:S(2)}) %collective-permute-start.7) | collective-permute-done | bytes 1179680 | tf_op jit(solution)/shard_map/ppermute | solution.py:232
  66.8 0.0 all-to-all-done
  66.8 0.0 copy-done.1
  66.8 0.1 collective-permute-start.11
  66.9 0.7 collective-permute-start.12
  67.6 0.1 pad_add_fusion.place_ref
  67.7 1.9 %collective-permute-done.11.across = bf16[512,1024]{1,0:T(8,128)(2,1)S(1)} collective-permute-done((bf16[512,1024]{1,0:T(8,128)(2,1)S(1)}, bf16[512,1024]{1,0:T(8,128)(2,1)S(1)}, u32[]{:S(2)}, u32[]{:S(2)}) %collective-permute-start.11) | collective-permute-done | bytes 1048608 | tf_op jit(solution)/shard_map/ppermute | solution.py:281
  69.6 7.2 %shard_map.74 = (f32[512,1024]{1,0:T(8,128)S(1)}, f32[512,1024]{1,0:T(8,128)S(1)}) custom-call(s32[2]{0:T(128)S(1)} %pad_add_fusion.place_ref, bf16[512,1024]{1,0:T(8,128)(2,1)S(1)} %bitcast.63, bf16[512,1024]{1,0:T(8,128)(2,1)S(1)} %collective-permute-done.11.across, bf16[6,384,256]{2,1,0:T(8,128)(2,1)} %get-tuple-element.32.refs_0_, ...), custom_call_target="tpu_custom_call" | custom-call | flops 268435456 | bytes 1048576 | tf_op jit(solution)/shard_map/pallas_call | solution.py:180
  76.8 0.0 copy-done
  76.8 3.1 %collective-permute-done.12.refs_1_ = bf16[2,384,256]{2,1,0:T(8,128)(2,1)} collective-permute-done((bf16[2,384,256]{2,1,0:T(8,128)(2,1)}, bf16[2,384,256]{2,1,0:T(8,128)(2,1)}, u32[]{:S(2)}, u32[]{:S(2)}) %collective-permute-start.12) | collective-permute-done | bytes 393248 | tf_op jit(solution)/shard_map/ppermute | solution.py:232
  80.0 3.5 %shard_map.75 = (bf16[512,1024]{1,0:T(8,128)(2,1)S(1)}, bf16[512,128]{1,0:T(8,128)(2,1)S(1)}) custom-call(s32[2]{0:T(128)S(1)} %pad_add_fusion.place_ref, bf16[512,1024]{1,0:T(8,128)(2,1)S(1)} %bitcast.64, bf16[512,1024]{1,0:T(8,128)(2,1)S(1)} %collective-permute-done.11.across, bf16[6,384,256]{2,1,0:T(8,128)(2,1)} %copy-done, ...), custom_call_target="tpu_custom_call" | custom-call | flops 268435456 | bytes 1048576 | tf_op jit(solution)/shard_map/pallas_call | solution.py:180
  83.5 0.1 collective-permute-start.13
  83.6 2.0 %shard_map.76 = f32[512,1024]{1,0:T(8,128)S(1)} custom-call(s32[2]{0:T(128)S(1)} %pad_add_fusion.place_ref, bf16[512,128]{1,0:T(8,128)(2,1)S(1)} %get-tuple-element.48.hidden, bf16[6,384,256]{2,1,0:T(8,128)(2,1)} %copy-done, bf16[2,384,256]{2,1,0:T(8,128)(2,1)} %collective-permute-done.12.refs_1_, f32[512,1024]{1,0:T(8,128)S(1)} %get-tuple-element.49.refs_2_), custom_call_target="tpu_custom_call" | custom-call | flops 134217728 | bytes 1048576 | tf_op jit(solution)/shard_map/pallas_call | solution.py:152
  85.6 0.6 collective-permute-done.13
  86.2 1.3 add_convert_fusion
  87.5 11.6 %all-to-all-start.1 = ((bf16[32,16,1024]{2,1,0:T(8,128)(2,1)}), bf16[32,16,1024]{2,1,0:T(8,128)(2,1)S(1)}, u32[]{:S(2)}, u32[]{:S(2)}) async-start(bf16[32,16,1024]{2,1,0:T(8,128)(2,1)} %bitcast.24), calls=%async_computation.1 | async-start | bytes 2097152 | tf_op jit(solution)/shard_map/all_to_all | solution.py:286
  99.3 0.1 select_bitcast_fusion
  99.4 0.1 reduce-precision_convert_fusion
  99.6 28.0 %all-to-all-done.1 = bf16[32,16,1024]{2,1,0:T(8,128)(2,1)S(1)} async-done(((bf16[32,16,1024]{2,1,0:T(8,128)(2,1)}), bf16[32,16,1024]{2,1,0:T(8,128)(2,1)S(1)}, u32[]{:S(2)}, u32[]{:S(2)}) %all-to-all-start.1) | async-done | bytes 1048608 | tf_op jit(solution)/shard_map/all_to_all | solution.py:286
  127.6 0.5 fusion.8
  128.0 0.1 fusion.51
  128.1 0.1 collective-permute-start.14
  128.2 1.9 %collective-permute-start.15 = (bf16[128,256]{1,0:T(8,128)(2,1)S(1)}, bf16[128,256]{1,0:T(8,128)(2,1)S(1)}, u32[]{:S(2)}, u32[]{:S(2)}) collective-permute-start(bf16[128,256]{1,0:T(8,128)(2,1)S(1)} %get-tuple-element.58), channel_id=1, source_target_pairs={{0,4},{2,6},{4,0},{6,2},{1,5},{3,7},{5,1},{7,3},{8,12},{10,14},{12... | collective-permute-start | bytes 196616 | tf_op jit(solution)/shard_map/ppermute | solution.py:221
  130.1 1.4 %collective-permute-start.16 = (bf16[128,256]{1,0:T(8,128)(2,1)S(1)}, bf16[128,256]{1,0:T(8,128)(2,1)S(1)}, u32[]{:S(2)}, u32[]{:S(2)}) collective-permute-start(bf16[128,256]{1,0:T(8,128)(2,1)S(1)} %get-tuple-element.57), channel_id=1, source_target_pairs={{0,6},{2,0},{4,2},{6,4},{1,7},{3,1},{5,3},{7,5},{8,14},{10,8},{12,... | collective-permute-start | bytes 196616 | tf_op jit(solution)/shard_map/ppermute | solution.py:221
  131.5 2.9 %collective-permute-done.14 = bf16[128,256]{1,0:T(8,128)(2,1)S(1)} collective-permute-done((bf16[128,256]{1,0:T(8,128)(2,1)S(1)}, bf16[128,256]{1,0:T(8,128)(2,1)S(1)}, u32[]{:S(2)}, u32[]{:S(2)}) %collective-permute-start.14) | collective-permute-done | bytes 65568 | tf_op jit(solution)/shard_map/ppermute | solution.py:221
  134.4 0.0 collective-permute-done.15
  134.4 0.9 collective-permute-done.16
  135.3 0.7 fusion.27
  (26 shorter events, 0.3 us)
Async XLA Ops:
  0.0 13.9 %copy-start.5 = (s32[128,8]{0,1:T(8,128)S(1)}, s32[128,8]{0,1:T(8,128)}, u32[]{:S(2)}) copy-start(s32[128,8]{0,1:T(8,128)} %param.10) | copy-start | bytes 12292
  0.9 9.9 %collective-permute-start = (bf16[144,256]{1,0:T(8,128)(2,1)S(1)}, bf16[144,256]{1,0:T(8,128)(2,1)S(1)}, u32[]{:S(2)}, u32[]{:S(2)}) collective-permute-start(bf16[144,256]{1,0:T(8,128)(2,1)S(1)} %pad_select_fusion), channel_id=1, source_target_pairs={{0,2},{2,4},{4,6},{6,0},{1,3},{3,5},{5,7},{7,1},{8,10},{10,12},{12... | collective-permute-start | bytes 221192 | tf_op jit(solution)/shard_map/ppermute | solution.py:221
  2.5 8.3 %collective-permute-start.1 = (bf16[144,256]{1,0:T(8,128)(2,1)S(1)}, bf16[144,256]{1,0:T(8,128)(2,1)S(1)}, u32[]{:S(2)}, u32[]{:S(2)}) collective-permute-start(bf16[144,256]{1,0:T(8,128)(2,1)S(1)} %pad_select_fusion), channel_id=1, source_target_pairs={{0,4},{2,6},{4,0},{6,2},{1,5},{3,7},{5,1},{7,3},{8,12},{10,14},{12... | collective-permute-start | bytes 221192 | tf_op jit(solution)/shard_map/ppermute | solution.py:221
  5.2 5.6 %collective-permute-start.2 = (bf16[144,256]{1,0:T(8,128)(2,1)S(1)}, bf16[144,256]{1,0:T(8,128)(2,1)S(1)}, u32[]{:S(2)}, u32[]{:S(2)}) collective-permute-start(bf16[144,256]{1,0:T(8,128)(2,1)S(1)} %pad_select_fusion), channel_id=1, source_target_pairs={{0,6},{2,0},{4,2},{6,4},{1,7},{3,1},{5,3},{7,5},{8,14},{10,8},{12,... | collective-permute-start | bytes 221192 | tf_op jit(solution)/shard_map/ppermute | solution.py:221
  11.1 27.2 %collective-permute-start.5 = (bf16[6,384,256]{2,1,0:T(8,128)(2,1)}, bf16[6,384,256]{2,1,0:T(8,128)(2,1)S(1)}, u32[]{:S(2)}, u32[]{:S(2)}) collective-permute-start(bf16[6,384,256]{2,1,0:T(8,128)(2,1)} %get-tuple-element.40), channel_id=1, source_target_pairs={{0,6},{2,4},{4,2},{6,0},{10,8},{12,14},{14,12},{8,10},{1,7},{3,5},... | collective-permute-start | bytes 3538952 | tf_op jit(solution)/shard_map/ppermute | solution.py:232
  11.8 28.1 %collective-permute-start.6 = (bf16[6,384,256]{2,1,0:T(8,128)(2,1)}, bf16[6,384,256]{2,1,0:T(8,128)(2,1)}, u32[]{:S(2)}, u32[]{:S(2)}) collective-permute-start(bf16[6,384,256]{2,1,0:T(8,128)(2,1)} %get-tuple-element.32.refs_0_), channel_id=1, source_target_pairs={{0,2},{2,0},{4,6},{6,4},{10,12},{12,10},{14,8},{8,14},{1,3},{3,1},... | collective-permute-start | bytes 3538952 | tf_op jit(solution)/shard_map/ppermute | solution.py:232
  12.7 9.5 %collective-permute-start.4 = (bf16[2,384,256]{2,1,0:T(8,128)(2,1)}, bf16[2,384,256]{2,1,0:T(8,128)(2,1)}, u32[]{:S(2)}, u32[]{:S(2)}) collective-permute-start(bf16[2,384,256]{2,1,0:T(8,128)(2,1)} %get-tuple-element.38.refs_1_), channel_id=1, source_target_pairs={{0,8},{2,10},{4,12},{6,14},{8,0},{10,2},{12,4},{14,6},{1,9},{3,11}... | collective-permute-start | bytes 1179656 | tf_op jit(solution)/shard_map/ppermute | solution.py:232
  13.9 1.1 collective-permute-start.3
  22.2 44.6 %all-to-all-start = ((bf16[32,16,1024]{2,1,0:T(8,128)(2,1)}), bf16[32,16,1024]{2,1,0:T(8,128)(2,1)S(1)}, u32[]{:S(2)}, u32[]{:S(2)}) async-start(bf16[32,16,1024]{2,1,0:T(8,128)(2,1)} %bitcast.17), calls=%async_computation | async-start | bytes 2097152 | tf_op jit(solution)/shard_map/all_to_all | solution.py:277
  38.3 28.5 %copy-start.1 = (bf16[6,384,256]{2,1,0:T(8,128)(2,1)}, bf16[6,384,256]{2,1,0:T(8,128)(2,1)S(1)}, u32[]{:S(2)}) copy-start(bf16[6,384,256]{2,1,0:T(8,128)(2,1)S(1)} %collective-permute-done.5.refs_4_) | copy-start | bytes 3538948
  39.9 26.9 %collective-permute-start.7 = (bf16[6,384,256]{2,1,0:T(8,128)(2,1)S(1)}, bf16[6,384,256]{2,1,0:T(8,128)(2,1)S(1)}, u32[]{:S(2)}, u32[]{:S(2)}) collective-permute-start(bf16[6,384,256]{2,1,0:T(8,128)(2,1)S(1)} %collective-permute-done.5.refs_4_), channel_id=1, source_target_pairs={{0,2},{2,0},{4,6},{6,4},{10,12},{12,10},{14,8},{8,14},{1,3},{3,1},... | collective-permute-start | bytes 3538952 | tf_op jit(solution)/shard_map/ppermute | solution.py:232
  40.6 9.3 %collective-permute-start.8 = (bf16[2,384,256]{2,1,0:T(8,128)(2,1)}, bf16[2,384,256]{2,1,0:T(8,128)(2,1)S(1)}, u32[]{:S(2)}, u32[]{:S(2)}) collective-permute-start(bf16[2,384,256]{2,1,0:T(8,128)(2,1)} %collective-permute-done.4), channel_id=1, source_target_pairs={{2,4},{4,2},{6,0},{0,6},{8,10},{10,8},{12,14},{14,12},{3,5},{5,3},... | collective-permute-start | bytes 1179656 | tf_op jit(solution)/shard_map/ppermute | solution.py:232
  49.8 8.0 %collective-permute-start.10 = (bf16[2,384,256]{2,1,0:T(8,128)(2,1)}, bf16[2,384,256]{2,1,0:T(8,128)(2,1)S(1)}, u32[]{:S(2)}, u32[]{:S(2)}) collective-permute-start(bf16[2,384,256]{2,1,0:T(8,128)(2,1)} %get-tuple-element.44), channel_id=1, source_target_pairs={{0,6},{2,4},{4,2},{6,0},{10,8},{12,14},{14,12},{8,10},{1,7},{3,5},... | collective-permute-start | bytes 1179656 | tf_op jit(solution)/shard_map/ppermute | solution.py:232
  49.9 10.7 %collective-permute-start.9 = (bf16[2,384,256]{2,1,0:T(8,128)(2,1)S(1)}, bf16[2,384,256]{2,1,0:T(8,128)(2,1)S(1)}, u32[]{:S(2)}, u32[]{:S(2)}) collective-permute-start(bf16[2,384,256]{2,1,0:T(8,128)(2,1)S(1)} %collective-permute-done.8), channel_id=1, source_target_pairs={{0,8},{2,10},{4,12},{6,14},{8,0},{10,2},{12,4},{14,6},{1,9},{3,11}... | collective-permute-start | bytes 1179656 | tf_op jit(solution)/shard_map/ppermute | solution.py:232
  57.8 2.7 %copy-start.2 = (bf16[2,384,256]{2,1,0:T(8,128)(2,1)}, bf16[2,384,256]{2,1,0:T(8,128)(2,1)S(1)}, u32[]{:S(2)}) copy-start(bf16[2,384,256]{2,1,0:T(8,128)(2,1)S(1)} %collective-permute-done.10.refs_5_) | copy-start | bytes 1179652
  60.5 0.8 copy-start.3
  66.8 10.0 %copy-start = (bf16[6,384,256]{2,1,0:T(8,128)(2,1)}, bf16[6,384,256]{2,1,0:T(8,128)(2,1)S(1)}, u32[]{:S(2)}) copy-start(bf16[6,384,256]{2,1,0:T(8,128)(2,1)S(1)} %collective-permute-done.7.refs_0_) | copy-start | bytes 3538948
  66.8 2.7 %collective-permute-start.11 = (bf16[512,1024]{1,0:T(8,128)(2,1)S(1)}, bf16[512,1024]{1,0:T(8,128)(2,1)S(1)}, u32[]{:S(2)}, u32[]{:S(2)}) collective-permute-start(bf16[512,1024]{1,0:T(8,128)(2,1)S(1)} %bitcast.62), channel_id=1, source_target_pairs={{0,1},{1,0},{2,3},{3,2},{4,5},{5,4},{6,7},{7,6},{8,9},{9,8},{10,11... | collective-permute-start | bytes 3145736 | tf_op jit(solution)/shard_map/ppermute | solution.py:281
  66.9 13.0 %collective-permute-start.12 = (bf16[2,384,256]{2,1,0:T(8,128)(2,1)}, bf16[2,384,256]{2,1,0:T(8,128)(2,1)}, u32[]{:S(2)}, u32[]{:S(2)}) collective-permute-start(bf16[2,384,256]{2,1,0:T(8,128)(2,1)} %copy-done.2), channel_id=1, source_target_pairs={{0,2},{2,0},{4,6},{6,4},{10,12},{12,10},{14,8},{8,14},{1,3},{3,1},... | collective-permute-start | bytes 1179656 | tf_op jit(solution)/shard_map/ppermute | solution.py:232
  83.5 2.7 %collective-permute-start.13 = (bf16[512,1024]{1,0:T(8,128)(2,1)S(1)}, bf16[512,1024]{1,0:T(8,128)(2,1)S(1)}, u32[]{:S(2)}, u32[]{:S(2)}) collective-permute-start(bf16[512,1024]{1,0:T(8,128)(2,1)S(1)} %get-tuple-element.50), channel_id=1, source_target_pairs={{0,1},{1,0},{2,3},{3,2},{4,5},{5,4},{6,7},{7,6},{8,9},{9,8},{10,11... | collective-permute-start | bytes 3145736 | tf_op jit(solution)/shard_map/ppermute | solution.py:285
  87.5 11.7 %copy-start.4 = (f32[128,64]{0,1:T(8,128)S(1)}, f32[128,64]{0,1:T(8,128)}, u32[]{:S(2)}) copy-start(f32[128,64]{0,1:T(8,128)} %param.9) | copy-start | bytes 98308
  87.5 40.0 %all-to-all-start.1 = ((bf16[32,16,1024]{2,1,0:T(8,128)(2,1)}), bf16[32,16,1024]{2,1,0:T(8,128)(2,1)S(1)}, u32[]{:S(2)}, u32[]{:S(2)}) async-start(bf16[32,16,1024]{2,1,0:T(8,128)(2,1)} %bitcast.24), calls=%async_computation.1 | async-start | bytes 2097152 | tf_op jit(solution)/shard_map/all_to_all | solution.py:286
  128.1 6.3 %collective-permute-start.14 = (bf16[128,256]{1,0:T(8,128)(2,1)S(1)}, bf16[128,256]{1,0:T(8,128)(2,1)S(1)}, u32[]{:S(2)}, u32[]{:S(2)}) collective-permute-start(bf16[128,256]{1,0:T(8,128)(2,1)S(1)} %get-tuple-element.56), channel_id=1, source_target_pairs={{0,2},{2,4},{4,6},{6,0},{1,3},{3,5},{5,7},{7,1},{8,10},{10,12},{12... | collective-permute-start | bytes 196616 | tf_op jit(solution)/shard_map/ppermute | solution.py:221
  128.2 6.2 %collective-permute-start.15 = (bf16[128,256]{1,0:T(8,128)(2,1)S(1)}, bf16[128,256]{1,0:T(8,128)(2,1)S(1)}, u32[]{:S(2)}, u32[]{:S(2)}) collective-permute-start(bf16[128,256]{1,0:T(8,128)(2,1)S(1)} %get-tuple-element.58), channel_id=1, source_target_pairs={{0,4},{2,6},{4,0},{6,2},{1,5},{3,7},{5,1},{7,3},{8,12},{10,14},{12... | collective-permute-start | bytes 196616 | tf_op jit(solution)/shard_map/ppermute | solution.py:221
  130.1 5.2 %collective-permute-start.16 = (bf16[128,256]{1,0:T(8,128)(2,1)S(1)}, bf16[128,256]{1,0:T(8,128)(2,1)S(1)}, u32[]{:S(2)}, u32[]{:S(2)}) collective-permute-start(bf16[128,256]{1,0:T(8,128)(2,1)S(1)} %get-tuple-element.57), channel_id=1, source_target_pairs={{0,6},{2,0},{4,2},{6,4},{1,7},{3,1},{5,3},{7,5},{8,14},{10,8},{12,... | collective-permute-start | bytes 196616 | tf_op jit(solution)/shard_map/ppermute | solution.py:221

commit v11 on v10

--- a/solution.py
+++ b/solution.py
@@ -30,45 +30,58 @@
 
 
 def pick_kernel(kind_ref, gate, up, down, *refs):
-    pieces, sems = refs[:-1], refs[-1]
-    unit = gate.shape[2]
-    copies = []
-    first = 0
-    for turn, packed in enumerate(pieces):
+    pieces, scratch, (sems, out_sems) = refs[:4], refs[4:8], refs[8:]
+    unit = gate.shape[3]
+    loads, used, first = [], 0, 0
+    for turn, packed in enumerate(scratch):
         first = 0 if turn in (0, 2) else first
         at = 1 - kind_ref[0] if turn < 2 else kind_ref[0]
-        for j in range(packed.shape[0]):
+        size = packed.shape[0]
+        pairs = [
+            (gate.at[at, pl.ds(first, size)], packed.at[:, pl.ds(0, block), pl.ds(0, unit)]),
+            (up.at[at, pl.ds(first, size)], packed.at[:, pl.ds(0, block), pl.ds(unit, unit)]),
+        ]
+        for j in range(size):
             wide = pl.ds((first + j) * block, block)
-            for source, target in (
-                (gate.at[at, wide, :], packed.at[j, pl.ds(0, block), pl.ds(0, unit)]),
-                (up.at[at, wide, :], packed.at[j, pl.ds(0, block), pl.ds(unit, unit)]),
-                (down.at[at, :, wide], packed.at[j, pl.ds(block, unit), :]),
-            ):
-                copies.append(pltpu.make_async_copy(source, target, sems.at[len(copies)]))
-        first += packed.shape[0]
-    for copy in copies:
-        copy.start()
-    for copy in copies:
-        copy.wait()
+            pairs.append((down.at[at, :, wide], packed.at[j, pl.ds(block, unit), :]))
+        first += size
+        loads.append([])
+        for source, target in pairs:
+            loads[-1].append(pltpu.make_async_copy(source, target, sems.at[used]))
+            used += 1
+    order = (0, 2, 1, 3)
+    for turn in order:
+        for copy in loads[turn]:
+            copy.start()
+    stores = [pltpu.make_async_copy(scratch[n], pieces[n], out_sems.at[n]) for n in range(4)]
+    for turn in order:
+        for copy in loads[turn]:
+            copy.wait()
+        stores[turn].start()
+    for turn in order:
+        stores[turn].wait()
 
 
 def pick_shards(kind, gate, up, down):
-    depth, unit = gate.shape[1:]
+    experts, depth, unit = gate.shape
     count = depth // block
+    sizes = (count - detoured, detoured) * 2
+    shapes = [(size, block + unit, block) for size in sizes]
     anywhere = pl.BlockSpec(memory_space=pl.ANY)
-    whole = pl.BlockSpec(memory_space=pltpu.VMEM)
-    other = [count - detoured, detoured]
-    own = [count - detoured, detoured]
     picked = pl.pallas_call(
         pick_kernel,
-        out_shape=tuple(
-            jax.ShapeDtypeStruct((size, block + unit, block), gate.dtype) for size in other + own
-        ),
+        out_shape=tuple(jax.ShapeDtypeStruct(shape, gate.dtype) for shape in shapes),
         in_specs=[pl.BlockSpec(memory_space=pltpu.SMEM)] + [anywhere] * 3,
-        out_specs=(whole,) * 4,
-        scratch_shapes=[pltpu.SemaphoreType.DMA((6 * count,))],
+        out_specs=(pl.BlockSpec(memory_space=pltpu.HBM),) * 4,
+        scratch_shapes=[pltpu.VMEM(shape, gate.dtype) for shape in shapes]
+        + [pltpu.SemaphoreType.DMA((8 + 2 * count,)), pltpu.SemaphoreType.DMA((4,))],
         cost_estimate=pl.CostEstimate(flops=0, bytes_accessed=6 * 2**20, transcendentals=0),
-    )(kind.reshape(1).astype(jnp.int32), gate, up, down)
+    )(
+        kind.reshape(1).astype(jnp.int32),
+        gate.reshape(experts, count, block, unit),
+        up.reshape(experts, count, block, unit),
+        down,
+    )
     return picked[:2], picked[2:]
 
 

time: 136 us -> 136 us (level)
  transfers between devices with their start and end apart: 19 -> 19, of which waited for: 14 -> 14; matrix products, arithmetic and copies ran while one was open for 2% -> 2% of each run, Pallas kernels for 10% -> 9%
where the time goes in v11:
time: 136 us; the launch traced here: 135 us
  waiting for transfers between devices  71.7 us (53%)
  starting transfers between devices  40 us (29%)
  Pallas kernels  15.9 us (12%)
  other arithmetic  4.17 us (3%)
  matrix products  2.08 us (2%)
    ppermute x8, waiting for transfers between devices, send(): return lax.ppermute(one, ('pair', 'x'), pairs)  37.7 us
    all_to_all x1, waiting for transfers between devices, on_device(): lax.all_to_all(summed.astype(bf16).reshape(ep_count, share, -1), ep, spli...  28 us
    all_to_all x1, starting transfers between devices, on_device(): lax.all_to_all(summed.astype(bf16).reshape(ep_count, share, -1), ep, spli...  11.6 us
    all_to_all x1, starting transfers between devices, on_device(): lax.all_to_all(outgoing.reshape(ep_count, share, -1), ep, split_axis=0, c...  11.6 us
    pallas_call x2, Pallas kernels, expert_rows(): pl.pallas_call(functools.partial(ffn_kernel, count, last), out_shape=(lea...  10.7 us
    ppermute x6, starting transfers between devices, ring_send(): return lax.ppermute(one, 'x', pairs)  9.04 us
    ppermute x8, starting transfers between devices, send(): return lax.ppermute(one, ('pair', 'x'), pairs)  7.53 us
    ppermute x6, waiting for transfers between devices, ring_send(): return lax.ppermute(one, 'x', pairs)  3.8 us
  transfers between devices with their start and end apart: 19, of which 14 were waited for; matrix products, arithmetic and copies ran while one was open for 2% of the time, Pallas kernels for 9%

profile of v11, /device:TPU:8, one launch (start us, length us, event | category | flops | bytes accessed | tf_op | source)
XLA Modules:
  0.0 135.1 jit_solution(18089161585686364596)
XLA Ops:
  0.0 0.9 pad_select_fusion
  0.9 1.6 %collective-permute-start = (bf16[144,256]{1,0:T(8,128)(2,1)S(1)}, bf16[144,256]{1,0:T(8,128)(2,1)S(1)}, u32[]{:S(2)}, u32[]{:S(2)}) collective-permute-start(bf16[144,256]{1,0:T(8,128)(2,1)S(1)} %pad_select_fusion), channel_id=1, source_target_pairs={{0,2},{2,4},{4,6},{6,0},{1,3},{3,5},{5,7},{7,1},{8,10},{10,12},{12... | collective-permute-start | bytes 221192 | tf_op jit(solution)/shard_map/ppermute | solution.py:234
  2.5 2.7 %collective-permute-start.1 = (bf16[144,256]{1,0:T(8,128)(2,1)S(1)}, bf16[144,256]{1,0:T(8,128)(2,1)S(1)}, u32[]{:S(2)}, u32[]{:S(2)}) collective-permute-start(bf16[144,256]{1,0:T(8,128)(2,1)S(1)} %pad_select_fusion), channel_id=1, source_target_pairs={{0,4},{2,6},{4,0},{6,2},{1,5},{3,7},{5,1},{7,3},{8,12},{10,14},{12... | collective-permute-start | bytes 221192 | tf_op jit(solution)/shard_map/ppermute | solution.py:234
  5.2 1.4 %collective-permute-start.2 = (bf16[144,256]{1,0:T(8,128)(2,1)S(1)}, bf16[144,256]{1,0:T(8,128)(2,1)S(1)}, u32[]{:S(2)}, u32[]{:S(2)}) collective-permute-start(bf16[144,256]{1,0:T(8,128)(2,1)S(1)} %pad_select_fusion), channel_id=1, source_target_pairs={{0,6},{2,0},{4,2},{6,4},{1,7},{3,1},{5,3},{7,5},{8,14},{10,8},{12,... | collective-permute-start | bytes 221192 | tf_op jit(solution)/shard_map/ppermute | solution.py:234
  6.7 0.1 eq.78
  6.8 3.1 %shard_map.73 = (bf16[6,384,256]{2,1,0:T(8,128)(2,1)}, bf16[2,384,256]{2,1,0:T(8,128)(2,1)}, bf16[6,384,256]{2,1,0:T(8,128)(2,1)}, bf16[2,384,256]{2,1,0:T(8,128)(2,1)}) custom-call(s32[1]{0:T(128)} %bitcast.kind_ref, bf16[2,8,256,128]{3,2,1,0:T(8,128)(2,1)} %bitcast.68, bf16[2,8,256,128]{3,2,1,0:T(8,128)(2,1)} %bitcast.69, bf16[2,128,2048]{2,1,0:T(8,128)(2,1)} %down.1), custom_call_target="tpu_custom_call" | custom-call | bytes 6291456 | tf_op jit(solution)/shard_map/pallas_call | solution.py:71
  10.0 0.0 collective-permute-done
  10.0 0.0 collective-permute-done.1
  10.0 0.0 collective-permute-done.2
  10.0 0.1 fusion.19
  10.2 0.1 fusion.13
  10.3 0.7 collective-permute-start.5
  11.0 1.7 %collective-permute-start.6 = (bf16[6,384,256]{2,1,0:T(8,128)(2,1)}, bf16[6,384,256]{2,1,0:T(8,128)(2,1)}, u32[]{:S(2)}, u32[]{:S(2)}) collective-permute-start(bf16[6,384,256]{2,1,0:T(8,128)(2,1)} %get-tuple-element.32.refs_0_), channel_id=1, source_target_pairs={{0,2},{2,0},{4,6},{6,4},{10,12},{12,10},{14,8},{8,14},{1,3},{3,1},... | collective-permute-start | bytes 3538952 | tf_op jit(solution)/shard_map/ppermute | solution.py:245
  12.7 0.8 collective-permute-start.4
  13.4 0.0 collective-permute-start.3
  13.4 0.0 copy-done.5
  13.6 0.2 fusion.30
  13.8 0.1 subtract_bitcast_fusion
  13.9 0.1 fusion.38
  14.0 0.1 bitcast_compare_fusion
  14.1 0.5 collective-permute-done.3
  14.6 0.1 fusion.15
  14.7 1.4 %convolution_convert_fusion = bf16[512,1024]{1,0:T(8,128)(2,1)} fusion(pred[512,128]{1,0:T(32,128)(4,1)S(1)} %bitcast_compare_fusion, bf16[128,256]{1,0:T(8,128)(2,1)S(1)} %get-tuple-element.68, bf16[128,256]{1,0:T(8,128)(2,1)S(1)} %get-tuple-element.67, bf16[128,256]{1,0:T(8,128)(2,1)S(1)} %get-tuple-element.66, bf16[128,256]{1,0:T(8,128)(2,1)S(1)} %get-tuple-element.65), kind=kOutput, calls=%fused_computation.1 | convolution fusion | flops 135790592 | bytes 1376256 | tf_op jit(solution)/shard_map/dot_general | solution.py:286
  16.1 6.1 %collective-permute-done.4 = bf16[2,384,256]{2,1,0:T(8,128)(2,1)} collective-permute-done((bf16[2,384,256]{2,1,0:T(8,128)(2,1)}, bf16[2,384,256]{2,1,0:T(8,128)(2,1)}, u32[]{:S(2)}, u32[]{:S(2)}) %collective-permute-start.4) | collective-permute-done | bytes 393248 | tf_op jit(solution)/shard_map/ppermute | solution.py:245
  22.2 11.6 %all-to-all-start = ((bf16[32,16,1024]{2,1,0:T(8,128)(2,1)}), bf16[32,16,1024]{2,1,0:T(8,128)(2,1)S(1)}, u32[]{:S(2)}, u32[]{:S(2)}) async-start(bf16[32,16,1024]{2,1,0:T(8,128)(2,1)} %bitcast.19), calls=%async_computation | async-start | bytes 2097152 | tf_op jit(solution)/shard_map/all_to_all | solution.py:290
  33.8 3.6 %collective-permute-done.5.refs_4_ = bf16[6,384,256]{2,1,0:T(8,128)(2,1)S(1)} collective-permute-done((bf16[6,384,256]{2,1,0:T(8,128)(2,1)}, bf16[6,384,256]{2,1,0:T(8,128)(2,1)S(1)}, u32[]{:S(2)}, u32[]{:S(2)}) %collective-permute-start.5) | collective-permute-done | bytes 1179680 | tf_op jit(solution)/shard_map/ppermute | solution.py:245
  37.5 1.6 %collective-permute-done.6.refs_2_ = bf16[6,384,256]{2,1,0:T(8,128)(2,1)} collective-permute-done((bf16[6,384,256]{2,1,0:T(8,128)(2,1)}, bf16[6,384,256]{2,1,0:T(8,128)(2,1)}, u32[]{:S(2)}, u32[]{:S(2)}) %collective-permute-start.6) | collective-permute-done | bytes 1179680 | tf_op jit(solution)/shard_map/ppermute | solution.py:245
  39.1 1.5 %collective-permute-start.7 = (bf16[6,384,256]{2,1,0:T(8,128)(2,1)S(1)}, bf16[6,384,256]{2,1,0:T(8,128)(2,1)S(1)}, u32[]{:S(2)}, u32[]{:S(2)}) collective-permute-start(bf16[6,384,256]{2,1,0:T(8,128)(2,1)S(1)} %collective-permute-done.5.refs_4_), channel_id=1, source_target_pairs={{0,2},{2,0},{4,6},{6,4},{10,12},{12,10},{14,8},{8,14},{1,3},{3,1},... | collective-permute-start | bytes 3538952 | tf_op jit(solution)/shard_map/ppermute | solution.py:245
  40.6 0.0 collective-permute-start.8
  40.6 9.3 %collective-permute-done.8 = bf16[2,384,256]{2,1,0:T(8,128)(2,1)S(1)} collective-permute-done((bf16[2,384,256]{2,1,0:T(8,128)(2,1)}, bf16[2,384,256]{2,1,0:T(8,128)(2,1)S(1)}, u32[]{:S(2)}, u32[]{:S(2)}) %collective-permute-start.8) | collective-permute-done | bytes 393248 | tf_op jit(solution)/shard_map/ppermute | solution.py:245
  49.8 0.0 collective-permute-start.10
  49.9 1.3 collective-permute-start.9
  51.2 6.6 %collective-permute-done.10.refs_5_ = bf16[2,384,256]{2,1,0:T(8,128)(2,1)S(1)} collective-permute-done((bf16[2,384,256]{2,1,0:T(8,128)(2,1)}, bf16[2,384,256]{2,1,0:T(8,128)(2,1)S(1)}, u32[]{:S(2)}, u32[]{:S(2)}) %collective-permute-start.10) | collective-permute-done | bytes 393248 | tf_op jit(solution)/shard_map/ppermute | solution.py:245
  57.8 1.9 %collective-permute-done.9.refs_3_ = bf16[2,384,256]{2,1,0:T(8,128)(2,1)S(1)} collective-permute-done((bf16[2,384,256]{2,1,0:T(8,128)(2,1)S(1)}, bf16[2,384,256]{2,1,0:T(8,128)(2,1)S(1)}, u32[]{:S(2)}, u32[]{:S(2)}) %collective-permute-start.9) | collective-permute-done | bytes 393248 | tf_op jit(solution)/shard_map/ppermute | solution.py:245
  59.7 0.0 copy-done.2
  59.7 0.8 copy-done.3
  60.5 5.5 %collective-permute-done.7.refs_0_ = bf16[6,384,256]{2,1,0:T(8,128)(2,1)S(1)} collective-permute-done((bf16[6,384,256]{2,1,0:T(8,128)(2,1)S(1)}, bf16[6,384,256]{2,1,0:T(8,128)(2,1)S(1)}, u32[]{:S(2)}, u32[]{:S(2)}) %collective-permute-start.7) | collective-permute-done | bytes 1179680 | tf_op jit(solution)/shard_map/ppermute | solution.py:245
  66.0 0.0 all-to-all-done
  66.0 0.0 copy-done.1
  66.0 0.1 collective-permute-start.11
  66.1 1.5 %collective-permute-start.12 = (bf16[2,384,256]{2,1,0:T(8,128)(2,1)}, bf16[2,384,256]{2,1,0:T(8,128)(2,1)}, u32[]{:S(2)}, u32[]{:S(2)}) collective-permute-start(bf16[2,384,256]{2,1,0:T(8,128)(2,1)} %copy-done.2), channel_id=1, source_target_pairs={{0,2},{2,0},{4,6},{6,4},{10,12},{12,10},{14,8},{8,14},{1,3},{3,1},... | collective-permute-start | bytes 1179656 | tf_op jit(solution)/shard_map/ppermute | solution.py:245
  67.6 0.1 pad_add_fusion.place_ref
  67.7 1.0 collective-permute-done.11.across
  68.7 7.2 %shard_map.74 = (f32[512,1024]{1,0:T(8,128)S(1)}, f32[512,1024]{1,0:T(8,128)S(1)}) custom-call(s32[2]{0:T(128)S(1)} %pad_add_fusion.place_ref, bf16[512,1024]{1,0:T(8,128)(2,1)S(1)} %bitcast.65, bf16[512,1024]{1,0:T(8,128)(2,1)S(1)} %collective-permute-done.11.across, bf16[6,384,256]{2,1,0:T(8,128)(2,1)} %get-tuple-element.32.refs_0_, ...), custom_call_target="tpu_custom_call" | custom-call | flops 268435456 | bytes 1048576 | tf_op jit(solution)/shard_map/pallas_call | solution.py:193
  76.0 3.1 %collective-permute-done.12.refs_1_ = bf16[2,384,256]{2,1,0:T(8,128)(2,1)} collective-permute-done((bf16[2,384,256]{2,1,0:T(8,128)(2,1)}, bf16[2,384,256]{2,1,0:T(8,128)(2,1)}, u32[]{:S(2)}, u32[]{:S(2)}) %collective-permute-start.12) | collective-permute-done | bytes 393248 | tf_op jit(solution)/shard_map/ppermute | solution.py:245
  79.1 3.5 %shard_map.75 = (bf16[512,1024]{1,0:T(8,128)(2,1)S(1)}, bf16[512,128]{1,0:T(8,128)(2,1)S(1)}) custom-call(s32[2]{0:T(128)S(1)} %pad_add_fusion.place_ref, bf16[512,1024]{1,0:T(8,128)(2,1)S(1)} %bitcast.66, bf16[512,1024]{1,0:T(8,128)(2,1)S(1)} %collective-permute-done.11.across, bf16[6,384,256]{2,1,0:T(8,128)(2,1)} %copy-done, ...), custom_call_target="tpu_custom_call" | custom-call | flops 268435456 | bytes 1048576 | tf_op jit(solution)/shard_map/pallas_call | solution.py:193
  82.6 0.1 collective-permute-start.13
  82.7 2.0 %shard_map.76 = f32[512,1024]{1,0:T(8,128)S(1)} custom-call(s32[2]{0:T(128)S(1)} %pad_add_fusion.place_ref, bf16[512,128]{1,0:T(8,128)(2,1)S(1)} %get-tuple-element.48.hidden, bf16[6,384,256]{2,1,0:T(8,128)(2,1)} %copy-done, bf16[2,384,256]{2,1,0:T(8,128)(2,1)} %collective-permute-done.12.refs_1_, f32[512,1024]{1,0:T(8,128)S(1)} %get-tuple-element.49.refs_2_), custom_call_target="tpu_custom_call" | custom-call | flops 134217728 | bytes 1048576 | tf_op jit(solution)/shard_map/pallas_call | solution.py:165
  84.7 0.6 collective-permute-done.13
  85.4 1.3 add_convert_fusion
  86.7 11.6 %all-to-all-start.1 = ((bf16[32,16,1024]{2,1,0:T(8,128)(2,1)}), bf16[32,16,1024]{2,1,0:T(8,128)(2,1)S(1)}, u32[]{:S(2)}, u32[]{:S(2)}) async-start(bf16[32,16,1024]{2,1,0:T(8,128)(2,1)} %bitcast.26), calls=%async_computation.1 | async-start | bytes 2097152 | tf_op jit(solution)/shard_map/all_to_all | solution.py:299
  98.3 0.0 copy-done.4
  98.5 0.1 select_bitcast_fusion
  98.6 0.1 reduce-precision_convert_fusion
  98.7 28.0 %all-to-all-done.1 = bf16[32,16,1024]{2,1,0:T(8,128)(2,1)S(1)} async-done(((bf16[32,16,1024]{2,1,0:T(8,128)(2,1)}), bf16[32,16,1024]{2,1,0:T(8,128)(2,1)S(1)}, u32[]{:S(2)}, u32[]{:S(2)}) %all-to-all-start.1) | async-done | bytes 1048608 | tf_op jit(solution)/shard_map/all_to_all | solution.py:299
  126.7 0.5 fusion.8
  127.2 0.1 fusion.51
  127.3 0.1 collective-permute-start.14
  127.4 2.7 %collective-permute-start.15 = (bf16[128,256]{1,0:T(8,128)(2,1)S(1)}, bf16[128,256]{1,0:T(8,128)(2,1)S(1)}, u32[]{:S(2)}, u32[]{:S(2)}) collective-permute-start(bf16[128,256]{1,0:T(8,128)(2,1)S(1)} %get-tuple-element.58), channel_id=1, source_target_pairs={{0,4},{2,6},{4,0},{6,2},{1,5},{3,7},{5,1},{7,3},{8,12},{10,14},{12... | collective-permute-start | bytes 196616 | tf_op jit(solution)/shard_map/ppermute | solution.py:234
  130.1 0.5 collective-permute-start.16
  130.6 2.9 %collective-permute-done.14 = bf16[128,256]{1,0:T(8,128)(2,1)S(1)} collective-permute-done((bf16[128,256]{1,0:T(8,128)(2,1)S(1)}, bf16[128,256]{1,0:T(8,128)(2,1)S(1)}, u32[]{:S(2)}, u32[]{:S(2)}) %collective-permute-start.14) | collective-permute-done | bytes 65568 | tf_op jit(solution)/shard_map/ppermute | solution.py:234
  133.5 0.0 collective-permute-done.15
  133.5 0.9 collective-permute-done.16
  134.4 0.7 fusion.27
  (26 shorter events, 0.3 us)
Async XLA Ops:
  0.0 13.4 %copy-start.5 = (s32[128,8]{0,1:T(8,128)S(1)}, s32[128,8]{0,1:T(8,128)}, u32[]{:S(2)}) copy-start(s32[128,8]{0,1:T(8,128)} %param.10) | copy-start | bytes 12292
  0.9 9.0 %collective-permute-start = (bf16[144,256]{1,0:T(8,128)(2,1)S(1)}, bf16[144,256]{1,0:T(8,128)(2,1)S(1)}, u32[]{:S(2)}, u32[]{:S(2)}) collective-permute-start(bf16[144,256]{1,0:T(8,128)(2,1)S(1)} %pad_select_fusion), channel_id=1, source_target_pairs={{0,2},{2,4},{4,6},{6,0},{1,3},{3,5},{5,7},{7,1},{8,10},{10,12},{12... | collective-permute-start | bytes 221192 | tf_op jit(solution)/shard_map/ppermute | solution.py:234
  2.5 7.5 %collective-permute-start.1 = (bf16[144,256]{1,0:T(8,128)(2,1)S(1)}, bf16[144,256]{1,0:T(8,128)(2,1)S(1)}, u32[]{:S(2)}, u32[]{:S(2)}) collective-permute-start(bf16[144,256]{1,0:T(8,128)(2,1)S(1)} %pad_select_fusion), channel_id=1, source_target_pairs={{0,4},{2,6},{4,0},{6,2},{1,5},{3,7},{5,1},{7,3},{8,12},{10,14},{12... | collective-permute-start | bytes 221192 | tf_op jit(solution)/shard_map/ppermute | solution.py:234
  5.2 4.8 %collective-permute-start.2 = (bf16[144,256]{1,0:T(8,128)(2,1)S(1)}, bf16[144,256]{1,0:T(8,128)(2,1)S(1)}, u32[]{:S(2)}, u32[]{:S(2)}) collective-permute-start(bf16[144,256]{1,0:T(8,128)(2,1)S(1)} %pad_select_fusion), channel_id=1, source_target_pairs={{0,6},{2,0},{4,2},{6,4},{1,7},{3,1},{5,3},{7,5},{8,14},{10,8},{12,... | collective-permute-start | bytes 221192 | tf_op jit(solution)/shard_map/ppermute | solution.py:234
  10.3 27.2 %collective-permute-start.5 = (bf16[6,384,256]{2,1,0:T(8,128)(2,1)}, bf16[6,384,256]{2,1,0:T(8,128)(2,1)S(1)}, u32[]{:S(2)}, u32[]{:S(2)}) collective-permute-start(bf16[6,384,256]{2,1,0:T(8,128)(2,1)} %get-tuple-element.40), channel_id=1, source_target_pairs={{0,6},{2,4},{4,2},{6,0},{10,8},{12,14},{14,12},{8,10},{1,7},{3,5},... | collective-permute-start | bytes 3538952 | tf_op jit(solution)/shard_map/ppermute | solution.py:245
  11.0 28.1 %collective-permute-start.6 = (bf16[6,384,256]{2,1,0:T(8,128)(2,1)}, bf16[6,384,256]{2,1,0:T(8,128)(2,1)}, u32[]{:S(2)}, u32[]{:S(2)}) collective-permute-start(bf16[6,384,256]{2,1,0:T(8,128)(2,1)} %get-tuple-element.32.refs_0_), channel_id=1, source_target_pairs={{0,2},{2,0},{4,6},{6,4},{10,12},{12,10},{14,8},{8,14},{1,3},{3,1},... | collective-permute-start | bytes 3538952 | tf_op jit(solution)/shard_map/ppermute | solution.py:245
  12.7 9.5 %collective-permute-start.4 = (bf16[2,384,256]{2,1,0:T(8,128)(2,1)}, bf16[2,384,256]{2,1,0:T(8,128)(2,1)}, u32[]{:S(2)}, u32[]{:S(2)}) collective-permute-start(bf16[2,384,256]{2,1,0:T(8,128)(2,1)} %get-tuple-element.38.refs_1_), channel_id=1, source_target_pairs={{0,8},{2,10},{4,12},{6,14},{8,0},{10,2},{12,4},{14,6},{1,9},{3,11}... | collective-permute-start | bytes 1179656 | tf_op jit(solution)/shard_map/ppermute | solution.py:245
  13.4 1.1 collective-permute-start.3
  22.2 43.7 %all-to-all-start = ((bf16[32,16,1024]{2,1,0:T(8,128)(2,1)}), bf16[32,16,1024]{2,1,0:T(8,128)(2,1)S(1)}, u32[]{:S(2)}, u32[]{:S(2)}) async-start(bf16[32,16,1024]{2,1,0:T(8,128)(2,1)} %bitcast.19), calls=%async_computation | async-start | bytes 2097152 | tf_op jit(solution)/shard_map/all_to_all | solution.py:290
  37.5 28.5 %copy-start.1 = (bf16[6,384,256]{2,1,0:T(8,128)(2,1)}, bf16[6,384,256]{2,1,0:T(8,128)(2,1)S(1)}, u32[]{:S(2)}) copy-start(bf16[6,384,256]{2,1,0:T(8,128)(2,1)S(1)} %collective-permute-done.5.refs_4_) | copy-start | bytes 3538948
  39.1 26.9 %collective-permute-start.7 = (bf16[6,384,256]{2,1,0:T(8,128)(2,1)S(1)}, bf16[6,384,256]{2,1,0:T(8,128)(2,1)S(1)}, u32[]{:S(2)}, u32[]{:S(2)}) collective-permute-start(bf16[6,384,256]{2,1,0:T(8,128)(2,1)S(1)} %collective-permute-done.5.refs_4_), channel_id=1, source_target_pairs={{0,2},{2,0},{4,6},{6,4},{10,12},{12,10},{14,8},{8,14},{1,3},{3,1},... | collective-permute-start | bytes 3538952 | tf_op jit(solution)/shard_map/ppermute | solution.py:245
  40.6 9.3 %collective-permute-start.8 = (bf16[2,384,256]{2,1,0:T(8,128)(2,1)}, bf16[2,384,256]{2,1,0:T(8,128)(2,1)S(1)}, u32[]{:S(2)}, u32[]{:S(2)}) collective-permute-start(bf16[2,384,256]{2,1,0:T(8,128)(2,1)} %collective-permute-done.4), channel_id=1, source_target_pairs={{2,4},{4,2},{6,0},{0,6},{8,10},{10,8},{12,14},{14,12},{3,5},{5,3},... | collective-permute-start | bytes 1179656 | tf_op jit(solution)/shard_map/ppermute | solution.py:245
  49.8 8.0 %collective-permute-start.10 = (bf16[2,384,256]{2,1,0:T(8,128)(2,1)}, bf16[2,384,256]{2,1,0:T(8,128)(2,1)S(1)}, u32[]{:S(2)}, u32[]{:S(2)}) collective-permute-start(bf16[2,384,256]{2,1,0:T(8,128)(2,1)} %get-tuple-element.44), channel_id=1, source_target_pairs={{0,6},{2,4},{4,2},{6,0},{10,8},{12,14},{14,12},{8,10},{1,7},{3,5},... | collective-permute-start | bytes 1179656 | tf_op jit(solution)/shard_map/ppermute | solution.py:245
  49.9 9.9 %collective-permute-start.9 = (bf16[2,384,256]{2,1,0:T(8,128)(2,1)S(1)}, bf16[2,384,256]{2,1,0:T(8,128)(2,1)S(1)}, u32[]{:S(2)}, u32[]{:S(2)}) collective-permute-start(bf16[2,384,256]{2,1,0:T(8,128)(2,1)S(1)} %collective-permute-done.8), channel_id=1, source_target_pairs={{0,8},{2,10},{4,12},{6,14},{8,0},{10,2},{12,4},{14,6},{1,9},{3,11}... | collective-permute-start | bytes 1179656 | tf_op jit(solution)/shard_map/ppermute | solution.py:245
  57.8 1.9 %copy-start.2 = (bf16[2,384,256]{2,1,0:T(8,128)(2,1)}, bf16[2,384,256]{2,1,0:T(8,128)(2,1)S(1)}, u32[]{:S(2)}) copy-start(bf16[2,384,256]{2,1,0:T(8,128)(2,1)S(1)} %collective-permute-done.10.refs_5_) | copy-start | bytes 1179652
  59.7 0.8 copy-start.3
  66.0 10.0 %copy-start = (bf16[6,384,256]{2,1,0:T(8,128)(2,1)}, bf16[6,384,256]{2,1,0:T(8,128)(2,1)S(1)}, u32[]{:S(2)}) copy-start(bf16[6,384,256]{2,1,0:T(8,128)(2,1)S(1)} %collective-permute-done.7.refs_0_) | copy-start | bytes 3538948
  66.0 2.7 %collective-permute-start.11 = (bf16[512,1024]{1,0:T(8,128)(2,1)S(1)}, bf16[512,1024]{1,0:T(8,128)(2,1)S(1)}, u32[]{:S(2)}, u32[]{:S(2)}) collective-permute-start(bf16[512,1024]{1,0:T(8,128)(2,1)S(1)} %bitcast.64), channel_id=1, source_target_pairs={{0,1},{1,0},{2,3},{3,2},{4,5},{5,4},{6,7},{7,6},{8,9},{9,8},{10,11... | collective-permute-start | bytes 3145736 | tf_op jit(solution)/shard_map/ppermute | solution.py:294
  66.1 13.0 %collective-permute-start.12 = (bf16[2,384,256]{2,1,0:T(8,128)(2,1)}, bf16[2,384,256]{2,1,0:T(8,128)(2,1)}, u32[]{:S(2)}, u32[]{:S(2)}) collective-permute-start(bf16[2,384,256]{2,1,0:T(8,128)(2,1)} %copy-done.2), channel_id=1, source_target_pairs={{0,2},{2,0},{4,6},{6,4},{10,12},{12,10},{14,8},{8,14},{1,3},{3,1},... | collective-permute-start | bytes 1179656 | tf_op jit(solution)/shard_map/ppermute | solution.py:245
  82.6 2.7 %collective-permute-start.13 = (bf16[512,1024]{1,0:T(8,128)(2,1)S(1)}, bf16[512,1024]{1,0:T(8,128)(2,1)S(1)}, u32[]{:S(2)}, u32[]{:S(2)}) collective-permute-start(bf16[512,1024]{1,0:T(8,128)(2,1)S(1)} %get-tuple-element.50), channel_id=1, source_target_pairs={{0,1},{1,0},{2,3},{3,2},{4,5},{5,4},{6,7},{7,6},{8,9},{9,8},{10,11... | collective-permute-start | bytes 3145736 | tf_op jit(solution)/shard_map/ppermute | solution.py:298
  86.7 11.7 %copy-start.4 = (f32[128,64]{0,1:T(8,128)S(1)}, f32[128,64]{0,1:T(8,128)}, u32[]{:S(2)}) copy-start(f32[128,64]{0,1:T(8,128)} %param.9) | copy-start | bytes 98308
  86.7 40.0 %all-to-all-start.1 = ((bf16[32,16,1024]{2,1,0:T(8,128)(2,1)}), bf16[32,16,1024]{2,1,0:T(8,128)(2,1)S(1)}, u32[]{:S(2)}, u32[]{:S(2)}) async-start(bf16[32,16,1024]{2,1,0:T(8,128)(2,1)} %bitcast.26), calls=%async_computation.1 | async-start | bytes 2097152 | tf_op jit(solution)/shard_map/all_to_all | solution.py:299
  127.3 6.3 %collective-permute-start.14 = (bf16[128,256]{1,0:T(8,128)(2,1)S(1)}, bf16[128,256]{1,0:T(8,128)(2,1)S(1)}, u32[]{:S(2)}, u32[]{:S(2)}) collective-permute-start(bf16[128,256]{1,0:T(8,128)(2,1)S(1)} %get-tuple-element.56), channel_id=1, source_target_pairs={{0,2},{2,4},{4,6},{6,0},{1,3},{3,5},{5,7},{7,1},{8,10},{10,12},{12... | collective-permute-start | bytes 196616 | tf_op jit(solution)/shard_map/ppermute | solution.py:234
  127.4 6.2 %collective-permute-start.15 = (bf16[128,256]{1,0:T(8,128)(2,1)S(1)}, bf16[128,256]{1,0:T(8,128)(2,1)S(1)}, u32[]{:S(2)}, u32[]{:S(2)}) collective-permute-start(bf16[128,256]{1,0:T(8,128)(2,1)S(1)} %get-tuple-element.58), channel_id=1, source_target_pairs={{0,4},{2,6},{4,0},{6,2},{1,5},{3,7},{5,1},{7,3},{8,12},{10,14},{12... | collective-permute-start | bytes 196616 | tf_op jit(solution)/shard_map/ppermute | solution.py:234
  130.1 4.3 %collective-permute-start.16 = (bf16[128,256]{1,0:T(8,128)(2,1)S(1)}, bf16[128,256]{1,0:T(8,128)(2,1)S(1)}, u32[]{:S(2)}, u32[]{:S(2)}) collective-permute-start(bf16[128,256]{1,0:T(8,128)(2,1)S(1)} %get-tuple-element.57), channel_id=1, source_target_pairs={{0,6},{2,0},{4,2},{6,4},{1,7},{3,1},{5,3},{7,5},{8,14},{10,8},{12,... | collective-permute-start | bytes 196616 | tf_op jit(solution)/shard_map/ppermute | solution.py:234

commit v12 on v11

--- a/solution.py
+++ b/solution.py
@@ -233,12 +233,14 @@
         pairs = [(at, (at + step) % row_count) for at in range(row_count)]
         return lax.ppermute(one, "x", pairs)
 
+    other, own = pick_shards(part // split, gate_proj, up_proj, down_proj)
+    tokens, other, own = lax.optimization_barrier((tokens, other, own))
+
     padded = lax.pad(tokens, jnp.zeros((), bf16), [(0, 16, 0), (0, 0, 0)])
     at_row = lax.broadcasted_iota(jnp.int32, padded.shape, 0)
     stacked = jnp.where(at_row < group_size, padded, norm_gain[None, :])
     parts = [stacked] + [ring_send(stacked, step) for step in range(1, row_count)]
 
-    other, own = pick_shards(part // split, gate_proj, up_proj, down_proj)
     parts, own, other = lax.optimization_barrier((parts, own, other))
 
     def send(one, pairs):

time: 136 us -> 138 us (1.015)
  starting transfers between devices: 40 us -> 42.3 us
    ppermute x6, waiting for transfers between devices: 3.8 us -> 7.03 us  [ring_send(): return lax.ppermute(one, 'x', pairs)]
    ppermute x8, waiting for transfers between devices: 37.7 us -> 35.7 us  [send(): return lax.ppermute(one, ('pair', 'x'), pairs)]
  transfers between devices with their start and end apart: 19 -> 19, of which waited for: 14 -> 17; matrix products, arithmetic and copies ran while one was open for 2% -> 2% of each run, Pallas kernels for 9% -> 7%
where the time goes in v12:
time: 138 us; the launch traced here: 137 us
  waiting for transfers between devices  71.8 us (52%)
  starting transfers between devices  42.3 us (31%)
  Pallas kernels  15.9 us (12%)
  other arithmetic  3.38 us (2%)
  matrix products  2.07 us (1%)
  local copies, waits for them, and re-layouts  1.73 us (1%)
    ppermute x8, waiting for transfers between devices, send(): return lax.ppermute(one, ('pair', 'x'), pairs)  35.7 us
    all_to_all x1, waiting for transfers between devices, on_device(): lax.all_to_all(summed.astype(bf16).reshape(ep_count, share, -1), ep, spli...  28 us
    all_to_all x1, starting transfers between devices, on_device(): lax.all_to_all(summed.astype(bf16).reshape(ep_count, share, -1), ep, spli...  11.7 us
    all_to_all x1, starting transfers between devices, on_device(): lax.all_to_all(outgoing.reshape(ep_count, share, -1), ep, split_axis=0, c...  11.6 us
    pallas_call x2, Pallas kernels, expert_rows(): pl.pallas_call(functools.partial(ffn_kernel, count, last), out_shape=(lea...  10.7 us
    ppermute x6, starting transfers between devices, ring_send(): return lax.ppermute(one, 'x', pairs)  9.94 us
    ppermute x8, starting transfers between devices, send(): return lax.ppermute(one, ('pair', 'x'), pairs)  8.89 us
    ppermute x6, waiting for transfers between devices, ring_send(): return lax.ppermute(one, 'x', pairs)  7.03 us
  transfers between devices with their start and end apart: 19, of which 17 were waited for; matrix products, arithmetic and copies ran while one was open for 2% of the time, Pallas kernels for 7%

profile of v12, /device:TPU:8, one launch (start us, length us, event | category | flops | bytes accessed | tf_op | source)
XLA Modules:
  0.0 137.4 jit_solution(13306680189090515275)
XLA Ops:
  0.1 3.1 %shard_map.73 = (bf16[6,384,256]{2,1,0:T(8,128)(2,1)}, bf16[2,384,256]{2,1,0:T(8,128)(2,1)}, bf16[6,384,256]{2,1,0:T(8,128)(2,1)}, bf16[2,384,256]{2,1,0:T(8,128)(2,1)}) custom-call(s32[1]{0:T(128)} %bitcast.kind_ref, bf16[2,8,256,128]{3,2,1,0:T(8,128)(2,1)} %bitcast.68, bf16[2,8,256,128]{3,2,1,0:T(8,128)(2,1)} %bitcast.69, bf16[2,128,2048]{2,1,0:T(8,128)(2,1)} %down.1), custom_call_target="tpu_custom_call" | custom-call | bytes 6291456 | tf_op jit(solution)/shard_map/pallas_call | solution.py:71
  3.2 0.0 copy-done.5
  3.2 0.1 pad_select_fusion
  3.3 1.6 %collective-permute-start = (bf16[144,256]{1,0:T(8,128)(2,1)S(1)}, bf16[144,256]{1,0:T(8,128)(2,1)S(1)}, u32[]{:S(2)}, u32[]{:S(2)}) collective-permute-start(bf16[144,256]{1,0:T(8,128)(2,1)S(1)} %pad_select_fusion), channel_id=1, source_target_pairs={{0,2},{2,4},{4,6},{6,0},{1,3},{3,5},{5,7},{7,1},{8,10},{10,12},{12... | collective-permute-start | bytes 221192 | tf_op jit(solution)/shard_map/ppermute | solution.py:234
  4.9 2.7 %collective-permute-start.1 = (bf16[144,256]{1,0:T(8,128)(2,1)S(1)}, bf16[144,256]{1,0:T(8,128)(2,1)S(1)}, u32[]{:S(2)}, u32[]{:S(2)}) collective-permute-start(bf16[144,256]{1,0:T(8,128)(2,1)S(1)} %pad_select_fusion), channel_id=1, source_target_pairs={{0,4},{2,6},{4,0},{6,2},{1,5},{3,7},{5,1},{7,3},{8,12},{10,14},{12... | collective-permute-start | bytes 221192 | tf_op jit(solution)/shard_map/ppermute | solution.py:234
  7.6 1.4 %collective-permute-start.2 = (bf16[144,256]{1,0:T(8,128)(2,1)S(1)}, bf16[144,256]{1,0:T(8,128)(2,1)S(1)}, u32[]{:S(2)}, u32[]{:S(2)}) collective-permute-start(bf16[144,256]{1,0:T(8,128)(2,1)S(1)} %pad_select_fusion), channel_id=1, source_target_pairs={{0,6},{2,0},{4,2},{6,4},{1,7},{3,1},{5,3},{7,5},{8,14},{10,8},{12,... | collective-permute-start | bytes 221192 | tf_op jit(solution)/shard_map/ppermute | solution.py:234
  9.1 0.1 eq.78
  9.2 0.3 collective-permute-done
  9.5 1.7 %collective-permute-done.1 = bf16[144,256]{1,0:T(8,128)(2,1)S(1)} collective-permute-done((bf16[144,256]{1,0:T(8,128)(2,1)S(1)}, bf16[144,256]{1,0:T(8,128)(2,1)S(1)}, u32[]{:S(2)}, u32[]{:S(2)}) %collective-permute-start.1) | collective-permute-done | bytes 73760 | tf_op jit(solution)/shard_map/ppermute | solution.py:234
  11.2 0.8 collective-permute-done.2
  12.0 0.1 fusion.19
  12.1 0.1 fusion.13
  12.2 0.7 collective-permute-start.5
  13.0 2.1 %collective-permute-start.6 = (bf16[6,384,256]{2,1,0:T(8,128)(2,1)}, bf16[6,384,256]{2,1,0:T(8,128)(2,1)}, u32[]{:S(2)}, u32[]{:S(2)}) collective-permute-start(bf16[6,384,256]{2,1,0:T(8,128)(2,1)} %get-tuple-element.42.refs_0_), channel_id=1, source_target_pairs={{0,2},{2,0},{4,6},{6,4},{10,12},{12,10},{14,8},{8,14},{1,3},{3,1},... | collective-permute-start | bytes 3538952 | tf_op jit(solution)/shard_map/ppermute | solution.py:247
  15.1 0.7 collective-permute-start.4
  15.8 0.0 collective-permute-start.3
  15.8 0.0 copy-done.6
  15.9 0.2 fusion.30
  16.1 0.1 subtract_bitcast_fusion
  16.2 0.1 fusion.38
  16.3 0.1 bitcast_compare_fusion
  16.5 0.5 collective-permute-done.3
  16.9 0.1 fusion.15
  17.1 1.4 %convolution_convert_fusion = bf16[512,1024]{1,0:T(8,128)(2,1)} fusion(pred[512,128]{1,0:T(32,128)(4,1)S(1)} %bitcast_compare_fusion, bf16[128,256]{1,0:T(8,128)(2,1)S(1)} %get-tuple-element.78, bf16[128,256]{1,0:T(8,128)(2,1)S(1)} %get-tuple-element.77, bf16[128,256]{1,0:T(8,128)(2,1)S(1)} %get-tuple-element.76, bf16[128,256]{1,0:T(8,128)(2,1)S(1)} %get-tuple-element.75), kind=kOutput, calls=%fused_computation.1 | convolution fusion | flops 135790592 | bytes 1376256 | tf_op jit(solution)/shard_map/dot_general | solution.py:288
  18.5 6.0 %collective-permute-done.4 = bf16[2,384,256]{2,1,0:T(8,128)(2,1)S(1)} collective-permute-done((bf16[2,384,256]{2,1,0:T(8,128)(2,1)}, bf16[2,384,256]{2,1,0:T(8,128)(2,1)S(1)}, u32[]{:S(2)}, u32[]{:S(2)}) %collective-permute-start.4) | collective-permute-done | bytes 393248 | tf_op jit(solution)/shard_map/ppermute | solution.py:247
  24.5 0.7 copy-done.8
  25.2 11.6 %all-to-all-start = ((bf16[32,16,1024]{2,1,0:T(8,128)(2,1)}), bf16[32,16,1024]{2,1,0:T(8,128)(2,1)S(1)}, u32[]{:S(2)}, u32[]{:S(2)}) async-start(bf16[32,16,1024]{2,1,0:T(8,128)(2,1)} %bitcast.19), calls=%async_computation | async-start | bytes 2097152 | tf_op jit(solution)/shard_map/all_to_all | solution.py:292
  36.8 2.3 %collective-permute-done.5.refs_4_ = bf16[6,384,256]{2,1,0:T(8,128)(2,1)S(1)} collective-permute-done((bf16[6,384,256]{2,1,0:T(8,128)(2,1)}, bf16[6,384,256]{2,1,0:T(8,128)(2,1)S(1)}, u32[]{:S(2)}, u32[]{:S(2)}) %collective-permute-start.5) | collective-permute-done | bytes 1179680 | tf_op jit(solution)/shard_map/ppermute | solution.py:247
  39.1 1.4 %collective-permute-done.6.refs_2_ = bf16[6,384,256]{2,1,0:T(8,128)(2,1)} collective-permute-done((bf16[6,384,256]{2,1,0:T(8,128)(2,1)}, bf16[6,384,256]{2,1,0:T(8,128)(2,1)}, u32[]{:S(2)}, u32[]{:S(2)}) %collective-permute-start.6) | collective-permute-done | bytes 1179680 | tf_op jit(solution)/shard_map/ppermute | solution.py:247
  40.6 2.4 %collective-permute-start.7 = (bf16[6,384,256]{2,1,0:T(8,128)(2,1)S(1)}, bf16[6,384,256]{2,1,0:T(8,128)(2,1)S(1)}, u32[]{:S(2)}, u32[]{:S(2)}) collective-permute-start(bf16[6,384,256]{2,1,0:T(8,128)(2,1)S(1)} %collective-permute-done.5.refs_4_), channel_id=1, source_target_pairs={{0,2},{2,0},{4,6},{6,4},{10,12},{12,10},{14,8},{8,14},{1,3},{3,1},... | collective-permute-start | bytes 3538952 | tf_op jit(solution)/shard_map/ppermute | solution.py:247
  42.9 0.0 collective-permute-start.8
  42.9 9.3 %collective-permute-done.8 = bf16[2,384,256]{2,1,0:T(8,128)(2,1)S(1)} collective-permute-done((bf16[2,384,256]{2,1,0:T(8,128)(2,1)}, bf16[2,384,256]{2,1,0:T(8,128)(2,1)S(1)}, u32[]{:S(2)}, u32[]{:S(2)}) %collective-permute-start.8) | collective-permute-done | bytes 393248 | tf_op jit(solution)/shard_map/ppermute | solution.py:247
  52.2 0.0 collective-permute-start.10
  52.2 0.0 collective-permute-start.9
  52.2 8.0 %collective-permute-done.10.refs_5_ = bf16[2,384,256]{2,1,0:T(8,128)(2,1)S(1)} collective-permute-done((bf16[2,384,256]{2,1,0:T(8,128)(2,1)}, bf16[2,384,256]{2,1,0:T(8,128)(2,1)S(1)}, u32[]{:S(2)}, u32[]{:S(2)}) %collective-permute-start.10) | collective-permute-done | bytes 393248 | tf_op jit(solution)/shard_map/ppermute | solution.py:247
  60.2 2.4 %collective-permute-done.9.refs_3_ = bf16[2,384,256]{2,1,0:T(8,128)(2,1)S(1)} collective-permute-done((bf16[2,384,256]{2,1,0:T(8,128)(2,1)S(1)}, bf16[2,384,256]{2,1,0:T(8,128)(2,1)S(1)}, u32[]{:S(2)}, u32[]{:S(2)}) %collective-permute-start.9) | collective-permute-done | bytes 393248 | tf_op jit(solution)/shard_map/ppermute | solution.py:247
  62.6 0.8 copy-done.3
  63.4 3.6 %collective-permute-done.7.refs_0_ = bf16[6,384,256]{2,1,0:T(8,128)(2,1)S(1)} collective-permute-done((bf16[6,384,256]{2,1,0:T(8,128)(2,1)S(1)}, bf16[6,384,256]{2,1,0:T(8,128)(2,1)S(1)}, u32[]{:S(2)}, u32[]{:S(2)}) %collective-permute-start.7) | collective-permute-done | bytes 1179680 | tf_op jit(solution)/shard_map/ppermute | solution.py:247
  66.9 0.0 all-to-all-done
  66.9 0.1 collective-permute-start.11
  67.0 2.9 %collective-permute-start.12 = (bf16[2,384,256]{2,1,0:T(8,128)(2,1)}, bf16[2,384,256]{2,1,0:T(8,128)(2,1)}, u32[]{:S(2)}, u32[]{:S(2)}) collective-permute-start(bf16[2,384,256]{2,1,0:T(8,128)(2,1)} %copy-done.2), channel_id=1, source_target_pairs={{0,2},{2,0},{4,6},{6,4},{10,12},{12,10},{14,8},{8,14},{1,3},{3,1},... | collective-permute-start | bytes 1179656 | tf_op jit(solution)/shard_map/ppermute | solution.py:247
  70.0 0.1 pad_add_fusion.place_ref
  70.0 0.0 collective-permute-done.11.across
  70.0 7.3 %shard_map.74 = (f32[512,1024]{1,0:T(8,128)S(1)}, f32[512,1024]{1,0:T(8,128)S(1)}) custom-call(s32[2]{0:T(128)S(1)} %pad_add_fusion.place_ref, bf16[512,1024]{1,0:T(8,128)(2,1)S(1)} %bitcast.65, bf16[512,1024]{1,0:T(8,128)(2,1)S(1)} %collective-permute-done.11.across, bf16[6,384,256]{2,1,0:T(8,128)(2,1)} %get-tuple-element.42.refs_0_, ...), custom_call_target="tpu_custom_call" | custom-call | flops 268435456 | bytes 1048576 | tf_op jit(solution)/shard_map/pallas_call | solution.py:193
  77.3 2.7 %collective-permute-done.12.refs_1_ = bf16[2,384,256]{2,1,0:T(8,128)(2,1)} collective-permute-done((bf16[2,384,256]{2,1,0:T(8,128)(2,1)}, bf16[2,384,256]{2,1,0:T(8,128)(2,1)}, u32[]{:S(2)}, u32[]{:S(2)}) %collective-permute-start.12) | collective-permute-done | bytes 393248 | tf_op jit(solution)/shard_map/ppermute | solution.py:247
  80.1 3.5 %shard_map.75 = (bf16[512,1024]{1,0:T(8,128)(2,1)S(1)}, bf16[512,128]{1,0:T(8,128)(2,1)S(1)}) custom-call(s32[2]{0:T(128)S(1)} %pad_add_fusion.place_ref, bf16[512,1024]{1,0:T(8,128)(2,1)S(1)} %bitcast.66, bf16[512,1024]{1,0:T(8,128)(2,1)S(1)} %collective-permute-done.11.across, bf16[6,384,256]{2,1,0:T(8,128)(2,1)} %copy-done, ...), custom_call_target="tpu_custom_call" | custom-call | flops 268435456 | bytes 1048576 | tf_op jit(solution)/shard_map/pallas_call | solution.py:193
  83.6 0.1 collective-permute-start.13
  83.7 2.0 %shard_map.76 = f32[512,1024]{1,0:T(8,128)S(1)} custom-call(s32[2]{0:T(128)S(1)} %pad_add_fusion.place_ref, bf16[512,128]{1,0:T(8,128)(2,1)S(1)} %get-tuple-element.58.hidden, bf16[6,384,256]{2,1,0:T(8,128)(2,1)} %copy-done, bf16[2,384,256]{2,1,0:T(8,128)(2,1)} %collective-permute-done.12.refs_1_, f32[512,1024]{1,0:T(8,128)S(1)} %get-tuple-element.59.refs_2_), custom_call_target="tpu_custom_call" | custom-call | flops 134217728 | bytes 1048576 | tf_op jit(solution)/shard_map/pallas_call | solution.py:165
  85.7 0.6 collective-permute-done.13
  86.3 1.4 %add_convert_fusion = bf16[512,1024]{1,0:T(8,128)(2,1)} fusion(f32[512,1024]{1,0:T(8,128)S(1)} %shard_map.76, bf16[512,1024]{1,0:T(8,128)(2,1)S(1)} %collective-permute-done.13), kind=kLoop, calls=%fused_computation | loop fusion | flops 1572864 | bytes 4194304 | tf_op jit(solution)/shard_map/convert_element_type | solution.py:302
  87.7 11.7 %all-to-all-start.1 = ((bf16[32,16,1024]{2,1,0:T(8,128)(2,1)}), bf16[32,16,1024]{2,1,0:T(8,128)(2,1)S(1)}, u32[]{:S(2)}, u32[]{:S(2)}) async-start(bf16[32,16,1024]{2,1,0:T(8,128)(2,1)} %bitcast.26), calls=%async_computation.1 | async-start | bytes 2097152 | tf_op jit(solution)/shard_map/all_to_all | solution.py:301
  99.4 0.0 copy-done.4
  99.5 0.1 select_bitcast_fusion
  99.6 0.1 reduce-precision_convert_fusion
  99.7 28.0 %all-to-all-done.1 = bf16[32,16,1024]{2,1,0:T(8,128)(2,1)S(1)} async-done(((bf16[32,16,1024]{2,1,0:T(8,128)(2,1)}), bf16[32,16,1024]{2,1,0:T(8,128)(2,1)S(1)}, u32[]{:S(2)}, u32[]{:S(2)}) %all-to-all-start.1) | async-done | bytes 1048608 | tf_op jit(solution)/shard_map/all_to_all | solution.py:301
  127.7 0.5 fusion.8
  128.2 0.1 fusion.51
  128.3 0.1 collective-permute-start.14
  128.4 4.1 %collective-permute-start.15 = (bf16[128,256]{1,0:T(8,128)(2,1)S(1)}, bf16[128,256]{1,0:T(8,128)(2,1)S(1)}, u32[]{:S(2)}, u32[]{:S(2)}) collective-permute-start(bf16[128,256]{1,0:T(8,128)(2,1)S(1)} %get-tuple-element.68), channel_id=1, source_target_pairs={{0,4},{2,6},{4,0},{6,2},{1,5},{3,7},{5,1},{7,3},{8,12},{10,14},{12... | collective-permute-start | bytes 196616 | tf_op jit(solution)/shard_map/ppermute | solution.py:234
  132.5 0.0 collective-permute-start.16
  132.5 1.3 collective-permute-done.14
  133.9 1.6 %collective-permute-done.15 = bf16[128,256]{1,0:T(8,128)(2,1)S(1)} collective-permute-done((bf16[128,256]{1,0:T(8,128)(2,1)S(1)}, bf16[128,256]{1,0:T(8,128)(2,1)S(1)}, u32[]{:S(2)}, u32[]{:S(2)}) %collective-permute-start.15) | collective-permute-done | bytes 65568 | tf_op jit(solution)/shard_map/ppermute | solution.py:234
  135.5 1.3 collective-permute-done.16
  136.8 0.7 fusion.27
  (32 shorter events, 0.3 us)
Async XLA Ops:
  0.0 3.2 %copy-start.5 = (bf16[128,256]{1,0:T(8,128)(2,1)S(1)}, bf16[128,256]{1,0:T(8,128)(2,1)}, u32[]{:S(2)}) copy-start(bf16[128,256]{1,0:T(8,128)(2,1)} %param.7) | copy-start | bytes 196612
  0.0 3.2 %copy-start.7 = (bf16[256]{0:T(256)(128)(2,1)S(1)}, bf16[256]{0:T(256)(128)(2,1)}, u32[]{:S(2)}) copy-start(bf16[256]{0:T(256)(128)(2,1)} %param.8) | copy-start | bytes 1540
  0.0 15.8 %copy-start.6 = (s32[128,8]{0,1:T(8,128)S(1)}, s32[128,8]{0,1:T(8,128)}, u32[]{:S(2)}) copy-start(s32[128,8]{0,1:T(8,128)} %param.10) | copy-start | bytes 12292
  3.3 6.1 %collective-permute-start = (bf16[144,256]{1,0:T(8,128)(2,1)S(1)}, bf16[144,256]{1,0:T(8,128)(2,1)S(1)}, u32[]{:S(2)}, u32[]{:S(2)}) collective-permute-start(bf16[144,256]{1,0:T(8,128)(2,1)S(1)} %pad_select_fusion), channel_id=1, source_target_pairs={{0,2},{2,4},{4,6},{6,0},{1,3},{3,5},{5,7},{7,1},{8,10},{10,12},{12... | collective-permute-start | bytes 221192 | tf_op jit(solution)/shard_map/ppermute | solution.py:234
  4.9 6.3 %collective-permute-start.1 = (bf16[144,256]{1,0:T(8,128)(2,1)S(1)}, bf16[144,256]{1,0:T(8,128)(2,1)S(1)}, u32[]{:S(2)}, u32[]{:S(2)}) collective-permute-start(bf16[144,256]{1,0:T(8,128)(2,1)S(1)} %pad_select_fusion), channel_id=1, source_target_pairs={{0,4},{2,6},{4,0},{6,2},{1,5},{3,7},{5,1},{7,3},{8,12},{10,14},{12... | collective-permute-start | bytes 221192 | tf_op jit(solution)/shard_map/ppermute | solution.py:234
  7.6 4.4 %collective-permute-start.2 = (bf16[144,256]{1,0:T(8,128)(2,1)S(1)}, bf16[144,256]{1,0:T(8,128)(2,1)S(1)}, u32[]{:S(2)}, u32[]{:S(2)}) collective-permute-start(bf16[144,256]{1,0:T(8,128)(2,1)S(1)} %pad_select_fusion), channel_id=1, source_target_pairs={{0,6},{2,0},{4,2},{6,4},{1,7},{3,1},{5,3},{7,5},{8,14},{10,8},{12,... | collective-permute-start | bytes 221192 | tf_op jit(solution)/shard_map/ppermute | solution.py:234
  12.2 26.9 %collective-permute-start.5 = (bf16[6,384,256]{2,1,0:T(8,128)(2,1)}, bf16[6,384,256]{2,1,0:T(8,128)(2,1)S(1)}, u32[]{:S(2)}, u32[]{:S(2)}) collective-permute-start(bf16[6,384,256]{2,1,0:T(8,128)(2,1)} %get-tuple-element.50), channel_id=1, source_target_pairs={{0,6},{2,4},{4,2},{6,0},{10,8},{12,14},{14,12},{8,10},{1,7},{3,5},... | collective-permute-start | bytes 3538952 | tf_op jit(solution)/shard_map/ppermute | solution.py:247
  13.0 27.6 %collective-permute-start.6 = (bf16[6,384,256]{2,1,0:T(8,128)(2,1)}, bf16[6,384,256]{2,1,0:T(8,128)(2,1)}, u32[]{:S(2)}, u32[]{:S(2)}) collective-permute-start(bf16[6,384,256]{2,1,0:T(8,128)(2,1)} %get-tuple-element.42.refs_0_), channel_id=1, source_target_pairs={{0,2},{2,0},{4,6},{6,4},{10,12},{12,10},{14,8},{8,14},{1,3},{3,1},... | collective-permute-start | bytes 3538952 | tf_op jit(solution)/shard_map/ppermute | solution.py:247
  15.1 9.4 %collective-permute-start.4 = (bf16[2,384,256]{2,1,0:T(8,128)(2,1)}, bf16[2,384,256]{2,1,0:T(8,128)(2,1)S(1)}, u32[]{:S(2)}, u32[]{:S(2)}) collective-permute-start(bf16[2,384,256]{2,1,0:T(8,128)(2,1)} %get-tuple-element.48.refs_1_), channel_id=1, source_target_pairs={{0,8},{2,10},{4,12},{6,14},{8,0},{10,2},{12,4},{14,6},{1,9},{3,11}... | collective-permute-start | bytes 1179656 | tf_op jit(solution)/shard_map/ppermute | solution.py:247
  15.8 1.1 collective-permute-start.3
  24.5 0.7 copy-start.8
  25.2 41.7 %all-to-all-start = ((bf16[32,16,1024]{2,1,0:T(8,128)(2,1)}), bf16[32,16,1024]{2,1,0:T(8,128)(2,1)S(1)}, u32[]{:S(2)}, u32[]{:S(2)}) async-start(bf16[32,16,1024]{2,1,0:T(8,128)(2,1)} %bitcast.19), calls=%async_computation | async-start | bytes 2097152 | tf_op jit(solution)/shard_map/all_to_all | solution.py:292
  39.1 27.8 %copy-start.1 = (bf16[6,384,256]{2,1,0:T(8,128)(2,1)}, bf16[6,384,256]{2,1,0:T(8,128)(2,1)S(1)}, u32[]{:S(2)}) copy-start(bf16[6,384,256]{2,1,0:T(8,128)(2,1)S(1)} %collective-permute-done.5.refs_4_) | copy-start | bytes 3538948
  40.6 26.3 %collective-permute-start.7 = (bf16[6,384,256]{2,1,0:T(8,128)(2,1)S(1)}, bf16[6,384,256]{2,1,0:T(8,128)(2,1)S(1)}, u32[]{:S(2)}, u32[]{:S(2)}) collective-permute-start(bf16[6,384,256]{2,1,0:T(8,128)(2,1)S(1)} %collective-permute-done.5.refs_4_), channel_id=1, source_target_pairs={{0,2},{2,0},{4,6},{6,4},{10,12},{12,10},{14,8},{8,14},{1,3},{3,1},... | collective-permute-start | bytes 3538952 | tf_op jit(solution)/shard_map/ppermute | solution.py:247
  42.9 9.3 %collective-permute-start.8 = (bf16[2,384,256]{2,1,0:T(8,128)(2,1)}, bf16[2,384,256]{2,1,0:T(8,128)(2,1)S(1)}, u32[]{:S(2)}, u32[]{:S(2)}) collective-permute-start(bf16[2,384,256]{2,1,0:T(8,128)(2,1)} %copy-done.8), channel_id=1, source_target_pairs={{2,4},{4,2},{6,0},{0,6},{8,10},{10,8},{12,14},{14,12},{3,5},{5,3},... | collective-permute-start | bytes 1179656 | tf_op jit(solution)/shard_map/ppermute | solution.py:247
  52.2 8.0 %collective-permute-start.10 = (bf16[2,384,256]{2,1,0:T(8,128)(2,1)}, bf16[2,384,256]{2,1,0:T(8,128)(2,1)S(1)}, u32[]{:S(2)}, u32[]{:S(2)}) collective-permute-start(bf16[2,384,256]{2,1,0:T(8,128)(2,1)} %get-tuple-element.54), channel_id=1, source_target_pairs={{0,6},{2,4},{4,2},{6,0},{10,8},{12,14},{14,12},{8,10},{1,7},{3,5},... | collective-permute-start | bytes 1179656 | tf_op jit(solution)/shard_map/ppermute | solution.py:247
  52.2 10.4 %collective-permute-start.9 = (bf16[2,384,256]{2,1,0:T(8,128)(2,1)S(1)}, bf16[2,384,256]{2,1,0:T(8,128)(2,1)S(1)}, u32[]{:S(2)}, u32[]{:S(2)}) collective-permute-start(bf16[2,384,256]{2,1,0:T(8,128)(2,1)S(1)} %collective-permute-done.8), channel_id=1, source_target_pairs={{0,8},{2,10},{4,12},{6,14},{8,0},{10,2},{12,4},{14,6},{1,9},{3,11}... | collective-permute-start | bytes 1179656 | tf_op jit(solution)/shard_map/ppermute | solution.py:247
  60.2 2.4 %copy-start.2 = (bf16[2,384,256]{2,1,0:T(8,128)(2,1)}, bf16[2,384,256]{2,1,0:T(8,128)(2,1)S(1)}, u32[]{:S(2)}) copy-start(bf16[2,384,256]{2,1,0:T(8,128)(2,1)S(1)} %collective-permute-done.10.refs_5_) | copy-start | bytes 1179652
  62.6 0.8 copy-start.3
  66.9 10.4 %copy-start = (bf16[6,384,256]{2,1,0:T(8,128)(2,1)}, bf16[6,384,256]{2,1,0:T(8,128)(2,1)S(1)}, u32[]{:S(2)}) copy-start(bf16[6,384,256]{2,1,0:T(8,128)(2,1)S(1)} %collective-permute-done.7.refs_0_) | copy-start | bytes 3538948
  66.9 3.1 %collective-permute-start.11 = (bf16[512,1024]{1,0:T(8,128)(2,1)S(1)}, bf16[512,1024]{1,0:T(8,128)(2,1)S(1)}, u32[]{:S(2)}, u32[]{:S(2)}) collective-permute-start(bf16[512,1024]{1,0:T(8,128)(2,1)S(1)} %bitcast.64), channel_id=1, source_target_pairs={{0,1},{1,0},{2,3},{3,2},{4,5},{5,4},{6,7},{7,6},{8,9},{9,8},{10,11... | collective-permute-start | bytes 3145736 | tf_op jit(solution)/shard_map/ppermute | solution.py:296
  67.0 13.0 %collective-permute-start.12 = (bf16[2,384,256]{2,1,0:T(8,128)(2,1)}, bf16[2,384,256]{2,1,0:T(8,128)(2,1)}, u32[]{:S(2)}, u32[]{:S(2)}) collective-permute-start(bf16[2,384,256]{2,1,0:T(8,128)(2,1)} %copy-done.2), channel_id=1, source_target_pairs={{0,2},{2,0},{4,6},{6,4},{10,12},{12,10},{14,8},{8,14},{1,3},{3,1},... | collective-permute-start | bytes 1179656 | tf_op jit(solution)/shard_map/ppermute | solution.py:247
  83.6 2.7 %collective-permute-start.13 = (bf16[512,1024]{1,0:T(8,128)(2,1)S(1)}, bf16[512,1024]{1,0:T(8,128)(2,1)S(1)}, u32[]{:S(2)}, u32[]{:S(2)}) collective-permute-start(bf16[512,1024]{1,0:T(8,128)(2,1)S(1)} %get-tuple-element.60), channel_id=1, source_target_pairs={{0,1},{1,0},{2,3},{3,2},{4,5},{5,4},{6,7},{7,6},{8,9},{9,8},{10,11... | collective-permute-start | bytes 3145736 | tf_op jit(solution)/shard_map/ppermute | solution.py:300
  87.7 11.7 %copy-start.4 = (f32[128,64]{0,1:T(8,128)S(1)}, f32[128,64]{0,1:T(8,128)}, u32[]{:S(2)}) copy-start(f32[128,64]{0,1:T(8,128)} %param.9) | copy-start | bytes 98308
  87.7 40.0 %all-to-all-start.1 = ((bf16[32,16,1024]{2,1,0:T(8,128)(2,1)}), bf16[32,16,1024]{2,1,0:T(8,128)(2,1)S(1)}, u32[]{:S(2)}, u32[]{:S(2)}) async-start(bf16[32,16,1024]{2,1,0:T(8,128)(2,1)} %bitcast.26), calls=%async_computation.1 | async-start | bytes 2097152 | tf_op jit(solution)/shard_map/all_to_all | solution.py:301
  128.3 5.6 %collective-permute-start.14 = (bf16[128,256]{1,0:T(8,128)(2,1)S(1)}, bf16[128,256]{1,0:T(8,128)(2,1)S(1)}, u32[]{:S(2)}, u32[]{:S(2)}) collective-permute-start(bf16[128,256]{1,0:T(8,128)(2,1)S(1)} %get-tuple-element.66), channel_id=1, source_target_pairs={{0,2},{2,4},{4,6},{6,0},{1,3},{3,5},{5,7},{7,1},{8,10},{10,12},{12... | collective-permute-start | bytes 196616 | tf_op jit(solution)/shard_map/ppermute | solution.py:234
  128.4 7.1 %collective-permute-start.15 = (bf16[128,256]{1,0:T(8,128)(2,1)S(1)}, bf16[128,256]{1,0:T(8,128)(2,1)S(1)}, u32[]{:S(2)}, u32[]{:S(2)}) collective-permute-start(bf16[128,256]{1,0:T(8,128)(2,1)S(1)} %get-tuple-element.68), channel_id=1, source_target_pairs={{0,4},{2,6},{4,0},{6,2},{1,5},{3,7},{5,1},{7,3},{8,12},{10,14},{12... | collective-permute-start | bytes 196616 | tf_op jit(solution)/shard_map/ppermute | solution.py:234
  132.5 4.3 %collective-permute-start.16 = (bf16[128,256]{1,0:T(8,128)(2,1)S(1)}, bf16[128,256]{1,0:T(8,128)(2,1)S(1)}, u32[]{:S(2)}, u32[]{:S(2)}) collective-permute-start(bf16[128,256]{1,0:T(8,128)(2,1)S(1)} %get-tuple-element.67), channel_id=1, source_target_pairs={{0,6},{2,0},{4,2},{6,4},{1,7},{3,1},{5,3},{7,5},{8,14},{10,8},{12,... | collective-permute-start | bytes 196616 | tf_op jit(solution)/shard_map/ppermute | solution.py:234

commit v13 on v11

--- a/solution.py
+++ b/solution.py
@@ -207,7 +207,7 @@
         cost_estimate=pl.CostEstimate(
             flops=2 * rows * width * unit, bytes_accessed=2**20, transcendentals=0
         ),
-    )(place, arrived, across, *lie(pieces), *([early] if last else []))
+    )(place, arrived, across, *(list(pieces[:1]) + lie(pieces[1:]) if last else lie(pieces)), *([early] if last else []))
 
 
 def on_device(tokens, norm_gain, router_logits, routes, gate_proj, up_proj, down_proj):

time: 136 us -> 135 us (level)
  no operation moved by 1% of the time
where the time goes in v13:
time: 135 us
  waiting for transfers between devices  71.7 us (53%)
  starting transfers between devices  40 us (30%)
  Pallas kernels  15.8 us (12%)
  other arithmetic  4.17 us (3%)
  matrix products  2.08 us (2%)
    ppermute x8, waiting for transfers between devices, send(): return lax.ppermute(one, ('pair', 'x'), pairs)  37.7 us
    all_to_all x1, waiting for transfers between devices, on_device(): lax.all_to_all(summed.astype(bf16).reshape(ep_count, share, -1), ep, spli...  28 us
    all_to_all x1, starting transfers between devices, on_device(): lax.all_to_all(summed.astype(bf16).reshape(ep_count, share, -1), ep, spli...  11.7 us
    all_to_all x1, starting transfers between devices, on_device(): lax.all_to_all(outgoing.reshape(ep_count, share, -1), ep, split_axis=0, c...  11.6 us
    pallas_call x2, Pallas kernels, expert_rows(): pl.pallas_call(functools.partial(ffn_kernel, count, last), out_shape=(lea...  10.6 us
    ppermute x6, starting transfers between devices, ring_send(): return lax.ppermute(one, 'x', pairs)  9.04 us
    ppermute x8, starting transfers between devices, send(): return lax.ppermute(one, ('pair', 'x'), pairs)  7.53 us
    ppermute x6, waiting for transfers between devices, ring_send(): return lax.ppermute(one, 'x', pairs)  3.8 us
  transfers between devices with their start and end apart: 19, of which 14 were waited for; matrix products, arithmetic and copies ran while one was open for 2% of the time, Pallas kernels for 9%

profile of v13, /device:TPU:8, one launch (start us, length us, event | category | flops | bytes accessed | tf_op | source)
XLA Modules:
  0.0 135.0 jit_solution(11606737537792857828)
XLA Ops:
  0.0 0.9 pad_select_fusion
  0.9 1.6 %collective-permute-start = (bf16[144,256]{1,0:T(8,128)(2,1)S(1)}, bf16[144,256]{1,0:T(8,128)(2,1)S(1)}, u32[]{:S(2)}, u32[]{:S(2)}) collective-permute-start(bf16[144,256]{1,0:T(8,128)(2,1)S(1)} %pad_select_fusion), channel_id=1, source_target_pairs={{0,2},{2,4},{4,6},{6,0},{1,3},{3,5},{5,7},{7,1},{8,10},{10,12},{12... | collective-permute-start | bytes 221192 | tf_op jit(solution)/shard_map/ppermute | solution.py:234
  2.5 2.7 %collective-permute-start.1 = (bf16[144,256]{1,0:T(8,128)(2,1)S(1)}, bf16[144,256]{1,0:T(8,128)(2,1)S(1)}, u32[]{:S(2)}, u32[]{:S(2)}) collective-permute-start(bf16[144,256]{1,0:T(8,128)(2,1)S(1)} %pad_select_fusion), channel_id=1, source_target_pairs={{0,4},{2,6},{4,0},{6,2},{1,5},{3,7},{5,1},{7,3},{8,12},{10,14},{12... | collective-permute-start | bytes 221192 | tf_op jit(solution)/shard_map/ppermute | solution.py:234
  5.2 1.4 %collective-permute-start.2 = (bf16[144,256]{1,0:T(8,128)(2,1)S(1)}, bf16[144,256]{1,0:T(8,128)(2,1)S(1)}, u32[]{:S(2)}, u32[]{:S(2)}) collective-permute-start(bf16[144,256]{1,0:T(8,128)(2,1)S(1)} %pad_select_fusion), channel_id=1, source_target_pairs={{0,6},{2,0},{4,2},{6,4},{1,7},{3,1},{5,3},{7,5},{8,14},{10,8},{12,... | collective-permute-start | bytes 221192 | tf_op jit(solution)/shard_map/ppermute | solution.py:234
  6.7 0.1 eq.78
  6.8 3.1 %shard_map.73 = (bf16[6,384,256]{2,1,0:T(8,128)(2,1)}, bf16[2,384,256]{2,1,0:T(8,128)(2,1)}, bf16[6,384,256]{2,1,0:T(8,128)(2,1)}, bf16[2,384,256]{2,1,0:T(8,128)(2,1)}) custom-call(s32[1]{0:T(128)} %bitcast.kind_ref, bf16[2,8,256,128]{3,2,1,0:T(8,128)(2,1)} %bitcast.68, bf16[2,8,256,128]{3,2,1,0:T(8,128)(2,1)} %bitcast.69, bf16[2,128,2048]{2,1,0:T(8,128)(2,1)} %down.1), custom_call_target="tpu_custom_call" | custom-call | bytes 6291456 | tf_op jit(solution)/shard_map/pallas_call | solution.py:71
  10.0 0.0 collective-permute-done
  10.0 0.0 collective-permute-done.1
  10.0 0.0 collective-permute-done.2
  10.0 0.1 fusion.19
  10.2 0.1 fusion.13
  10.3 0.7 collective-permute-start.5
  11.0 1.7 %collective-permute-start.6 = (bf16[6,384,256]{2,1,0:T(8,128)(2,1)}, bf16[6,384,256]{2,1,0:T(8,128)(2,1)}, u32[]{:S(2)}, u32[]{:S(2)}) collective-permute-start(bf16[6,384,256]{2,1,0:T(8,128)(2,1)} %get-tuple-element.32.refs_0_), channel_id=1, source_target_pairs={{0,2},{2,0},{4,6},{6,4},{10,12},{12,10},{14,8},{8,14},{1,3},{3,1},... | collective-permute-start | bytes 3538952 | tf_op jit(solution)/shard_map/ppermute | solution.py:245
  12.7 0.8 collective-permute-start.4
  13.4 0.0 collective-permute-start.3
  13.4 0.0 copy-done.5
  13.6 0.2 fusion.30
  13.8 0.1 subtract_bitcast_fusion
  13.9 0.1 fusion.38
  14.0 0.1 bitcast_compare_fusion
  14.1 0.5 collective-permute-done.3
  14.6 0.1 fusion.15
  14.7 1.4 %convolution_convert_fusion = bf16[512,1024]{1,0:T(8,128)(2,1)} fusion(pred[512,128]{1,0:T(32,128)(4,1)S(1)} %bitcast_compare_fusion, bf16[128,256]{1,0:T(8,128)(2,1)S(1)} %get-tuple-element.68, bf16[128,256]{1,0:T(8,128)(2,1)S(1)} %get-tuple-element.67, bf16[128,256]{1,0:T(8,128)(2,1)S(1)} %get-tuple-element.66, bf16[128,256]{1,0:T(8,128)(2,1)S(1)} %get-tuple-element.65), kind=kOutput, calls=%fused_computation.1 | convolution fusion | flops 135790592 | bytes 1376256 | tf_op jit(solution)/shard_map/dot_general | solution.py:286
  16.1 6.1 %collective-permute-done.4 = bf16[2,384,256]{2,1,0:T(8,128)(2,1)} collective-permute-done((bf16[2,384,256]{2,1,0:T(8,128)(2,1)}, bf16[2,384,256]{2,1,0:T(8,128)(2,1)}, u32[]{:S(2)}, u32[]{:S(2)}) %collective-permute-start.4) | collective-permute-done | bytes 393248 | tf_op jit(solution)/shard_map/ppermute | solution.py:245
  22.2 11.6 %all-to-all-start = ((bf16[32,16,1024]{2,1,0:T(8,128)(2,1)}), bf16[32,16,1024]{2,1,0:T(8,128)(2,1)S(1)}, u32[]{:S(2)}, u32[]{:S(2)}) async-start(bf16[32,16,1024]{2,1,0:T(8,128)(2,1)} %bitcast.19), calls=%async_computation | async-start | bytes 2097152 | tf_op jit(solution)/shard_map/all_to_all | solution.py:290
  33.8 3.6 %collective-permute-done.5.refs_4_ = bf16[6,384,256]{2,1,0:T(8,128)(2,1)S(1)} collective-permute-done((bf16[6,384,256]{2,1,0:T(8,128)(2,1)}, bf16[6,384,256]{2,1,0:T(8,128)(2,1)S(1)}, u32[]{:S(2)}, u32[]{:S(2)}) %collective-permute-start.5) | collective-permute-done | bytes 1179680 | tf_op jit(solution)/shard_map/ppermute | solution.py:245
  37.5 1.6 %collective-permute-done.6.refs_2_ = bf16[6,384,256]{2,1,0:T(8,128)(2,1)} collective-permute-done((bf16[6,384,256]{2,1,0:T(8,128)(2,1)}, bf16[6,384,256]{2,1,0:T(8,128)(2,1)}, u32[]{:S(2)}, u32[]{:S(2)}) %collective-permute-start.6) | collective-permute-done | bytes 1179680 | tf_op jit(solution)/shard_map/ppermute | solution.py:245
  39.1 1.5 %collective-permute-start.7 = (bf16[6,384,256]{2,1,0:T(8,128)(2,1)S(1)}, bf16[6,384,256]{2,1,0:T(8,128)(2,1)S(1)}, u32[]{:S(2)}, u32[]{:S(2)}) collective-permute-start(bf16[6,384,256]{2,1,0:T(8,128)(2,1)S(1)} %collective-permute-done.5.refs_4_), channel_id=1, source_target_pairs={{0,2},{2,0},{4,6},{6,4},{10,12},{12,10},{14,8},{8,14},{1,3},{3,1},... | collective-permute-start | bytes 3538952 | tf_op jit(solution)/shard_map/ppermute | solution.py:245
  40.6 0.0 collective-permute-start.8
  40.6 9.3 %collective-permute-done.8 = bf16[2,384,256]{2,1,0:T(8,128)(2,1)S(1)} collective-permute-done((bf16[2,384,256]{2,1,0:T(8,128)(2,1)}, bf16[2,384,256]{2,1,0:T(8,128)(2,1)S(1)}, u32[]{:S(2)}, u32[]{:S(2)}) %collective-permute-start.8) | collective-permute-done | bytes 393248 | tf_op jit(solution)/shard_map/ppermute | solution.py:245
  49.8 0.0 collective-permute-start.10
  49.9 1.3 collective-permute-start.9
  51.2 6.6 %collective-permute-done.10.refs_5_ = bf16[2,384,256]{2,1,0:T(8,128)(2,1)S(1)} collective-permute-done((bf16[2,384,256]{2,1,0:T(8,128)(2,1)}, bf16[2,384,256]{2,1,0:T(8,128)(2,1)S(1)}, u32[]{:S(2)}, u32[]{:S(2)}) %collective-permute-start.10) | collective-permute-done | bytes 393248 | tf_op jit(solution)/shard_map/ppermute | solution.py:245
  57.8 1.9 %collective-permute-done.9.refs_3_ = bf16[2,384,256]{2,1,0:T(8,128)(2,1)S(1)} collective-permute-done((bf16[2,384,256]{2,1,0:T(8,128)(2,1)S(1)}, bf16[2,384,256]{2,1,0:T(8,128)(2,1)S(1)}, u32[]{:S(2)}, u32[]{:S(2)}) %collective-permute-start.9) | collective-permute-done | bytes 393248 | tf_op jit(solution)/shard_map/ppermute | solution.py:245
  59.7 0.0 copy-done.2
  59.7 0.8 copy-done.3
  60.5 5.5 %collective-permute-done.7.refs_0_ = bf16[6,384,256]{2,1,0:T(8,128)(2,1)S(1)} collective-permute-done((bf16[6,384,256]{2,1,0:T(8,128)(2,1)S(1)}, bf16[6,384,256]{2,1,0:T(8,128)(2,1)S(1)}, u32[]{:S(2)}, u32[]{:S(2)}) %collective-permute-start.7) | collective-permute-done | bytes 1179680 | tf_op jit(solution)/shard_map/ppermute | solution.py:245
  66.0 0.0 all-to-all-done
  66.0 0.0 copy-done.1
  66.0 0.1 collective-permute-start.11
  66.1 1.5 %collective-permute-start.12 = (bf16[2,384,256]{2,1,0:T(8,128)(2,1)}, bf16[2,384,256]{2,1,0:T(8,128)(2,1)}, u32[]{:S(2)}, u32[]{:S(2)}) collective-permute-start(bf16[2,384,256]{2,1,0:T(8,128)(2,1)} %copy-done.2), channel_id=1, source_target_pairs={{0,2},{2,0},{4,6},{6,4},{10,12},{12,10},{14,8},{8,14},{1,3},{3,1},... | collective-permute-start | bytes 1179656 | tf_op jit(solution)/shard_map/ppermute | solution.py:245
  67.6 0.1 pad_add_fusion.place_ref
  67.7 1.0 collective-permute-done.11.across
  68.7 7.2 %shard_map.74 = (f32[512,1024]{1,0:T(8,128)S(1)}, f32[512,1024]{1,0:T(8,128)S(1)}) custom-call(s32[2]{0:T(128)S(1)} %pad_add_fusion.place_ref, bf16[512,1024]{1,0:T(8,128)(2,1)S(1)} %bitcast.65, bf16[512,1024]{1,0:T(8,128)(2,1)S(1)} %collective-permute-done.11.across, bf16[6,384,256]{2,1,0:T(8,128)(2,1)} %get-tuple-element.32.refs_0_, ...), custom_call_target="tpu_custom_call" | custom-call | flops 268435456 | bytes 1048576 | tf_op jit(solution)/shard_map/pallas_call | solution.py:193
  75.9 3.2 %collective-permute-done.12.refs_1_ = bf16[2,384,256]{2,1,0:T(8,128)(2,1)} collective-permute-done((bf16[2,384,256]{2,1,0:T(8,128)(2,1)}, bf16[2,384,256]{2,1,0:T(8,128)(2,1)}, u32[]{:S(2)}, u32[]{:S(2)}) %collective-permute-start.12) | collective-permute-done | bytes 393248 | tf_op jit(solution)/shard_map/ppermute | solution.py:245
  79.1 0.0 copy-done
  79.1 3.4 %shard_map.75 = (bf16[512,1024]{1,0:T(8,128)(2,1)S(1)}, bf16[512,128]{1,0:T(8,128)(2,1)S(1)}) custom-call(s32[2]{0:T(128)S(1)} %pad_add_fusion.place_ref, bf16[512,1024]{1,0:T(8,128)(2,1)S(1)} %bitcast.66, bf16[512,1024]{1,0:T(8,128)(2,1)S(1)} %collective-permute-done.11.across, bf16[6,384,256]{2,1,0:T(8,128)(2,1)S(1)} %collective-permute-done.7.refs_0_, ...), custom_call_target="tpu_custom_call" | custom-call | flops 268435456 | bytes 1048576 | tf_op jit(solution)/shard_map/pallas_call | solution.py:193
  82.5 0.1 collective-permute-start.13
  82.6 2.0 %shard_map.76 = f32[512,1024]{1,0:T(8,128)S(1)} custom-call(s32[2]{0:T(128)S(1)} %pad_add_fusion.place_ref, bf16[512,128]{1,0:T(8,128)(2,1)S(1)} %get-tuple-element.48.hidden, bf16[6,384,256]{2,1,0:T(8,128)(2,1)} %copy-done, bf16[2,384,256]{2,1,0:T(8,128)(2,1)} %collective-permute-done.12.refs_1_, f32[512,1024]{1,0:T(8,128)S(1)} %get-tuple-element.49.refs_2_), custom_call_target="tpu_custom_call" | custom-call | flops 134217728 | bytes 1048576 | tf_op jit(solution)/shard_map/pallas_call | solution.py:165
  84.6 0.6 collective-permute-done.13
  85.2 1.3 add_convert_fusion
  86.6 11.7 %all-to-all-start.1 = ((bf16[32,16,1024]{2,1,0:T(8,128)(2,1)}), bf16[32,16,1024]{2,1,0:T(8,128)(2,1)S(1)}, u32[]{:S(2)}, u32[]{:S(2)}) async-start(bf16[32,16,1024]{2,1,0:T(8,128)(2,1)} %bitcast.26), calls=%async_computation.1 | async-start | bytes 2097152 | tf_op jit(solution)/shard_map/all_to_all | solution.py:299
  98.4 0.1 select_bitcast_fusion
  98.4 0.1 reduce-precision_convert_fusion
  98.6 28.0 %all-to-all-done.1 = bf16[32,16,1024]{2,1,0:T(8,128)(2,1)S(1)} async-done(((bf16[32,16,1024]{2,1,0:T(8,128)(2,1)}), bf16[32,16,1024]{2,1,0:T(8,128)(2,1)S(1)}, u32[]{:S(2)}, u32[]{:S(2)}) %all-to-all-start.1) | async-done | bytes 1048608 | tf_op jit(solution)/shard_map/all_to_all | solution.py:299
  126.6 0.5 fusion.8
  127.1 0.1 fusion.51
  127.2 0.1 collective-permute-start.14
  127.3 2.7 %collective-permute-start.15 = (bf16[128,256]{1,0:T(8,128)(2,1)S(1)}, bf16[128,256]{1,0:T(8,128)(2,1)S(1)}, u32[]{:S(2)}, u32[]{:S(2)}) collective-permute-start(bf16[128,256]{1,0:T(8,128)(2,1)S(1)} %get-tuple-element.58), channel_id=1, source_target_pairs={{0,4},{2,6},{4,0},{6,2},{1,5},{3,7},{5,1},{7,3},{8,12},{10,14},{12... | collective-permute-start | bytes 196616 | tf_op jit(solution)/shard_map/ppermute | solution.py:234
  130.0 0.5 collective-permute-start.16
  130.5 2.9 %collective-permute-done.14 = bf16[128,256]{1,0:T(8,128)(2,1)S(1)} collective-permute-done((bf16[128,256]{1,0:T(8,128)(2,1)S(1)}, bf16[128,256]{1,0:T(8,128)(2,1)S(1)}, u32[]{:S(2)}, u32[]{:S(2)}) %collective-permute-start.14) | collective-permute-done | bytes 65568 | tf_op jit(solution)/shard_map/ppermute | solution.py:234
  133.4 0.0 collective-permute-done.15
  133.4 0.9 collective-permute-done.16
  134.3 0.7 fusion.27
  (26 shorter events, 0.3 us)
Async XLA Ops:
  0.0 13.4 %copy-start.5 = (s32[128,8]{0,1:T(8,128)S(1)}, s32[128,8]{0,1:T(8,128)}, u32[]{:S(2)}) copy-start(s32[128,8]{0,1:T(8,128)} %param.10) | copy-start | bytes 12292
  0.9 9.0 %collective-permute-start = (bf16[144,256]{1,0:T(8,128)(2,1)S(1)}, bf16[144,256]{1,0:T(8,128)(2,1)S(1)}, u32[]{:S(2)}, u32[]{:S(2)}) collective-permute-start(bf16[144,256]{1,0:T(8,128)(2,1)S(1)} %pad_select_fusion), channel_id=1, source_target_pairs={{0,2},{2,4},{4,6},{6,0},{1,3},{3,5},{5,7},{7,1},{8,10},{10,12},{12... | collective-permute-start | bytes 221192 | tf_op jit(solution)/shard_map/ppermute | solution.py:234
  2.5 7.5 %collective-permute-start.1 = (bf16[144,256]{1,0:T(8,128)(2,1)S(1)}, bf16[144,256]{1,0:T(8,128)(2,1)S(1)}, u32[]{:S(2)}, u32[]{:S(2)}) collective-permute-start(bf16[144,256]{1,0:T(8,128)(2,1)S(1)} %pad_select_fusion), channel_id=1, source_target_pairs={{0,4},{2,6},{4,0},{6,2},{1,5},{3,7},{5,1},{7,3},{8,12},{10,14},{12... | collective-permute-start | bytes 221192 | tf_op jit(solution)/shard_map/ppermute | solution.py:234
  5.2 4.8 %collective-permute-start.2 = (bf16[144,256]{1,0:T(8,128)(2,1)S(1)}, bf16[144,256]{1,0:T(8,128)(2,1)S(1)}, u32[]{:S(2)}, u32[]{:S(2)}) collective-permute-start(bf16[144,256]{1,0:T(8,128)(2,1)S(1)} %pad_select_fusion), channel_id=1, source_target_pairs={{0,6},{2,0},{4,2},{6,4},{1,7},{3,1},{5,3},{7,5},{8,14},{10,8},{12,... | collective-permute-start | bytes 221192 | tf_op jit(solution)/shard_map/ppermute | solution.py:234
  10.3 27.2 %collective-permute-start.5 = (bf16[6,384,256]{2,1,0:T(8,128)(2,1)}, bf16[6,384,256]{2,1,0:T(8,128)(2,1)S(1)}, u32[]{:S(2)}, u32[]{:S(2)}) collective-permute-start(bf16[6,384,256]{2,1,0:T(8,128)(2,1)} %get-tuple-element.40), channel_id=1, source_target_pairs={{0,6},{2,4},{4,2},{6,0},{10,8},{12,14},{14,12},{8,10},{1,7},{3,5},... | collective-permute-start | bytes 3538952 | tf_op jit(solution)/shard_map/ppermute | solution.py:245
  11.0 28.1 %collective-permute-start.6 = (bf16[6,384,256]{2,1,0:T(8,128)(2,1)}, bf16[6,384,256]{2,1,0:T(8,128)(2,1)}, u32[]{:S(2)}, u32[]{:S(2)}) collective-permute-start(bf16[6,384,256]{2,1,0:T(8,128)(2,1)} %get-tuple-element.32.refs_0_), channel_id=1, source_target_pairs={{0,2},{2,0},{4,6},{6,4},{10,12},{12,10},{14,8},{8,14},{1,3},{3,1},... | collective-permute-start | bytes 3538952 | tf_op jit(solution)/shard_map/ppermute | solution.py:245
  12.7 9.5 %collective-permute-start.4 = (bf16[2,384,256]{2,1,0:T(8,128)(2,1)}, bf16[2,384,256]{2,1,0:T(8,128)(2,1)}, u32[]{:S(2)}, u32[]{:S(2)}) collective-permute-start(bf16[2,384,256]{2,1,0:T(8,128)(2,1)} %get-tuple-element.38.refs_1_), channel_id=1, source_target_pairs={{0,8},{2,10},{4,12},{6,14},{8,0},{10,2},{12,4},{14,6},{1,9},{3,11}... | collective-permute-start | bytes 1179656 | tf_op jit(solution)/shard_map/ppermute | solution.py:245
  13.4 1.1 collective-permute-start.3
  22.2 43.7 %all-to-all-start = ((bf16[32,16,1024]{2,1,0:T(8,128)(2,1)}), bf16[32,16,1024]{2,1,0:T(8,128)(2,1)S(1)}, u32[]{:S(2)}, u32[]{:S(2)}) async-start(bf16[32,16,1024]{2,1,0:T(8,128)(2,1)} %bitcast.19), calls=%async_computation | async-start | bytes 2097152 | tf_op jit(solution)/shard_map/all_to_all | solution.py:290
  37.5 28.5 %copy-start.1 = (bf16[6,384,256]{2,1,0:T(8,128)(2,1)}, bf16[6,384,256]{2,1,0:T(8,128)(2,1)S(1)}, u32[]{:S(2)}) copy-start(bf16[6,384,256]{2,1,0:T(8,128)(2,1)S(1)} %collective-permute-done.5.refs_4_) | copy-start | bytes 3538948
  39.1 26.9 %collective-permute-start.7 = (bf16[6,384,256]{2,1,0:T(8,128)(2,1)S(1)}, bf16[6,384,256]{2,1,0:T(8,128)(2,1)S(1)}, u32[]{:S(2)}, u32[]{:S(2)}) collective-permute-start(bf16[6,384,256]{2,1,0:T(8,128)(2,1)S(1)} %collective-permute-done.5.refs_4_), channel_id=1, source_target_pairs={{0,2},{2,0},{4,6},{6,4},{10,12},{12,10},{14,8},{8,14},{1,3},{3,1},... | collective-permute-start | bytes 3538952 | tf_op jit(solution)/shard_map/ppermute | solution.py:245
  40.6 9.3 %collective-permute-start.8 = (bf16[2,384,256]{2,1,0:T(8,128)(2,1)}, bf16[2,384,256]{2,1,0:T(8,128)(2,1)S(1)}, u32[]{:S(2)}, u32[]{:S(2)}) collective-permute-start(bf16[2,384,256]{2,1,0:T(8,128)(2,1)} %collective-permute-done.4), channel_id=1, source_target_pairs={{2,4},{4,2},{6,0},{0,6},{8,10},{10,8},{12,14},{14,12},{3,5},{5,3},... | collective-permute-start | bytes 1179656 | tf_op jit(solution)/shard_map/ppermute | solution.py:245
  49.8 8.0 %collective-permute-start.10 = (bf16[2,384,256]{2,1,0:T(8,128)(2,1)}, bf16[2,384,256]{2,1,0:T(8,128)(2,1)S(1)}, u32[]{:S(2)}, u32[]{:S(2)}) collective-permute-start(bf16[2,384,256]{2,1,0:T(8,128)(2,1)} %get-tuple-element.44), channel_id=1, source_target_pairs={{0,6},{2,4},{4,2},{6,0},{10,8},{12,14},{14,12},{8,10},{1,7},{3,5},... | collective-permute-start | bytes 1179656 | tf_op jit(solution)/shard_map/ppermute | solution.py:245
  49.9 9.9 %collective-permute-start.9 = (bf16[2,384,256]{2,1,0:T(8,128)(2,1)S(1)}, bf16[2,384,256]{2,1,0:T(8,128)(2,1)S(1)}, u32[]{:S(2)}, u32[]{:S(2)}) collective-permute-start(bf16[2,384,256]{2,1,0:T(8,128)(2,1)S(1)} %collective-permute-done.8), channel_id=1, source_target_pairs={{0,8},{2,10},{4,12},{6,14},{8,0},{10,2},{12,4},{14,6},{1,9},{3,11}... | collective-permute-start | bytes 1179656 | tf_op jit(solution)/shard_map/ppermute | solution.py:245
  57.8 1.9 %copy-start.2 = (bf16[2,384,256]{2,1,0:T(8,128)(2,1)}, bf16[2,384,256]{2,1,0:T(8,128)(2,1)S(1)}, u32[]{:S(2)}) copy-start(bf16[2,384,256]{2,1,0:T(8,128)(2,1)S(1)} %collective-permute-done.10.refs_5_) | copy-start | bytes 1179652
  59.7 0.8 copy-start.3
  66.0 13.2 %copy-start = (bf16[6,384,256]{2,1,0:T(8,128)(2,1)}, bf16[6,384,256]{2,1,0:T(8,128)(2,1)S(1)}, u32[]{:S(2)}) copy-start(bf16[6,384,256]{2,1,0:T(8,128)(2,1)S(1)} %collective-permute-done.7.refs_0_) | copy-start | bytes 3538948
  66.0 2.7 %collective-permute-start.11 = (bf16[512,1024]{1,0:T(8,128)(2,1)S(1)}, bf16[512,1024]{1,0:T(8,128)(2,1)S(1)}, u32[]{:S(2)}, u32[]{:S(2)}) collective-permute-start(bf16[512,1024]{1,0:T(8,128)(2,1)S(1)} %bitcast.64), channel_id=1, source_target_pairs={{0,1},{1,0},{2,3},{3,2},{4,5},{5,4},{6,7},{7,6},{8,9},{9,8},{10,11... | collective-permute-start | bytes 3145736 | tf_op jit(solution)/shard_map/ppermute | solution.py:294
  66.1 13.0 %collective-permute-start.12 = (bf16[2,384,256]{2,1,0:T(8,128)(2,1)}, bf16[2,384,256]{2,1,0:T(8,128)(2,1)}, u32[]{:S(2)}, u32[]{:S(2)}) collective-permute-start(bf16[2,384,256]{2,1,0:T(8,128)(2,1)} %copy-done.2), channel_id=1, source_target_pairs={{0,2},{2,0},{4,6},{6,4},{10,12},{12,10},{14,8},{8,14},{1,3},{3,1},... | collective-permute-start | bytes 1179656 | tf_op jit(solution)/shard_map/ppermute | solution.py:245
  82.5 2.7 %collective-permute-start.13 = (bf16[512,1024]{1,0:T(8,128)(2,1)S(1)}, bf16[512,1024]{1,0:T(8,128)(2,1)S(1)}, u32[]{:S(2)}, u32[]{:S(2)}) collective-permute-start(bf16[512,1024]{1,0:T(8,128)(2,1)S(1)} %get-tuple-element.50), channel_id=1, source_target_pairs={{0,1},{1,0},{2,3},{3,2},{4,5},{5,4},{6,7},{7,6},{8,9},{9,8},{10,11... | collective-permute-start | bytes 3145736 | tf_op jit(solution)/shard_map/ppermute | solution.py:298
  86.6 11.7 %copy-start.4 = (f32[128,64]{0,1:T(8,128)S(1)}, f32[128,64]{0,1:T(8,128)}, u32[]{:S(2)}) copy-start(f32[128,64]{0,1:T(8,128)} %param.9) | copy-start | bytes 98308
  86.6 40.0 %all-to-all-start.1 = ((bf16[32,16,1024]{2,1,0:T(8,128)(2,1)}), bf16[32,16,1024]{2,1,0:T(8,128)(2,1)S(1)}, u32[]{:S(2)}, u32[]{:S(2)}) async-start(bf16[32,16,1024]{2,1,0:T(8,128)(2,1)} %bitcast.26), calls=%async_computation.1 | async-start | bytes 2097152 | tf_op jit(solution)/shard_map/all_to_all | solution.py:299
  127.2 6.3 %collective-permute-start.14 = (bf16[128,256]{1,0:T(8,128)(2,1)S(1)}, bf16[128,256]{1,0:T(8,128)(2,1)S(1)}, u32[]{:S(2)}, u32[]{:S(2)}) collective-permute-start(bf16[128,256]{1,0:T(8,128)(2,1)S(1)} %get-tuple-element.56), channel_id=1, source_target_pairs={{0,2},{2,4},{4,6},{6,0},{1,3},{3,5},{5,7},{7,1},{8,10},{10,12},{12... | collective-permute-start | bytes 196616 | tf_op jit(solution)/shard_map/ppermute | solution.py:234
  127.3 6.2 %collective-permute-start.15 = (bf16[128,256]{1,0:T(8,128)(2,1)S(1)}, bf16[128,256]{1,0:T(8,128)(2,1)S(1)}, u32[]{:S(2)}, u32[]{:S(2)}) collective-permute-start(bf16[128,256]{1,0:T(8,128)(2,1)S(1)} %get-tuple-element.58), channel_id=1, source_target_pairs={{0,4},{2,6},{4,0},{6,2},{1,5},{3,7},{5,1},{7,3},{8,12},{10,14},{12... | collective-permute-start | bytes 196616 | tf_op jit(solution)/shard_map/ppermute | solution.py:234
  130.0 4.3 %collective-permute-start.16 = (bf16[128,256]{1,0:T(8,128)(2,1)S(1)}, bf16[128,256]{1,0:T(8,128)(2,1)S(1)}, u32[]{:S(2)}, u32[]{:S(2)}) collective-permute-start(bf16[128,256]{1,0:T(8,128)(2,1)S(1)} %get-tuple-element.57), channel_id=1, source_target_pairs={{0,6},{2,0},{4,2},{6,4},{1,7},{3,1},{5,3},{7,5},{8,14},{10,8},{12,... | collective-permute-start | bytes 196616 | tf_op jit(solution)/shard_map/ppermute | solution.py:234
